TPU v7x, 256 devices: a whole 4x4x8 slice. The times are simulated.
256 devices in a mesh: gx: 16 (over z, core), gy: 16 (over x, y).
Axes of the slice: x: 4, y: 4, z: 8, core: 2. Of those that a mesh axis runs over, the one named last changes fastest.
Arguments:
- right_sides: float32 [16384, 8, 128], P(('gx', 'gy')), may hold values from -30 to 30
- diag_blocks: bfloat16 [16384, 128, 128], P(('gx', 'gy')), may hold values from -1 to 2
- face_blocks: bfloat16 [16384, 4, 128, 128], P(('gx', 'gy')), may hold values from -0.125 to 0.125
- neighbours: int32 [16384, 4], P(('gx', 'gy')), may hold values from -1 to 207, as said below
- send_slots: int32 [256, 9, 16], P(('gx', 'gy')), may hold values from -1 to 63, as said below
- counts: int32 [256], P(('gx', 'gy')), may hold values from 32 to 64, as said below
Outputs:
- solution: float32 [16384, 8, 128], P(('gx', 'gy'))
- residual: float32 [16384, 8, 128], P(('gx', 'gy'))
Inputs may be any that keep to these rules, and one draw needn't show every extreme that they name: The first counts[g] slots of group g hold its elements; some group has exactly 64. send_slots[g, d, k] is a live slot of group g whose vector group g sends, as its k-th ghost of direction d = 3 (dx + 1) + (dy + 1), to the group at grid offset (dx, dy); -1 marks no block. A list's live entries come first and are distinct; direction 4 and directions leaving the grid hold only -1; some list holds 16 live entries. neighbours[e, f] is -1 (no coupling), a live slot of the same group, or 64 + d * 16 + k naming a live entry k of direction d of the sending group at offset -(dx, dy); slots at or beyond counts hold only -1.
All inputs are finite; a program needn't handle non-finite values.
Results may differ from a plain program's by a relative error of at most 0.0075.
The roundings to bfloat16 on the way count: a program that leaves them out, or rounds other values in their place, can miss the bound.
Values may be sent and summed in bfloat16 or wider, within the bound.
No kernel may reach another device: no remote copies, remote signals or barrier semaphores. Data moves between devices by JAX's collectives and lax.ppermute only.
A program may use at most 64 MiB of HBM per device.

v0:
```python
import jax
import jax.numpy as jnp
from jax import lax
from jax.sharding import PartitionSpec as P

POWERS = 4


HIGH = lax.Precision.HIGHEST


def passed_along(block, axis, distance):
    devices = range(lax.axis_size(axis))
    route = [(i - distance, i) for i in devices if i - distance in devices]
    return lax.ppermute(block, axis, route)


def forward_solve(factor, values):
    extent = factor.shape[-1]
    result = []
    for row_at in range(extent):
        running = values[:, row_at]
        for col_at in range(row_at):
            running = running - factor[:, row_at, col_at] * result[col_at]
        result.append(running / factor[:, row_at, row_at])
    return jnp.stack(result, axis=1)


def backward_solve(factor, values):
    extent = factor.shape[-1]
    result = [None] * extent
    for row_at in reversed(range(extent)):
        running = values[:, row_at]
        for col_at in range(row_at + 1, extent):
            running = running - factor[:, col_at, row_at] * result[col_at]
        result[row_at] = running / factor[:, row_at, row_at]
    return jnp.stack(result, axis=1)


def coefficients(gram):
    factor = jnp.linalg.cholesky(gram[:, 1:, 1:])
    return backward_solve(factor, forward_solve(factor, gram[:, 1:, 0]))


def fetch_ghosts(packets):
    empty = jnp.zeros_like(packets[4])
    columns = lax.axis_size("gy")
    column = lax.axis_index("gy")
    arrived = []
    for target in range(9):
        if target == 4:
            arrived.append(empty)
        else:
            step_row = target // 3 - 1
            step_col = target % 3 - 1
            shifted = passed_along(packets[target], ("gx", "gy"), step_row * columns + step_col)
            inside = (column - step_col >= 0) & (column - step_col < columns)
            arrived.append(jnp.where(inside, shifted, jnp.zeros((), jnp.bfloat16)))
    return jnp.stack(arrived)


def per_device(right_sides, diag_blocks, face_blocks, neighbours, send_slots, counts):
    capacity = right_sides.shape[0]
    slot_ids = lax.iota(jnp.int32, capacity)
    live_mask = (slot_ids < counts[0]).astype(jnp.float32)[:, None, None]
    outgoing = send_slots[0]
    sending = outgoing >= 0
    out_index = jnp.where(sending, outgoing, 0)
    present = neighbours >= 0
    source = jnp.where(present, neighbours, 0)
    zero_half = jnp.zeros((), jnp.bfloat16)
    vectors = [right_sides * live_mask]
    for step_index in range(POWERS):
        rounded = vectors[-1].astype(jnp.bfloat16)
        packets = jnp.where(sending[:, :, None, None], rounded[out_index], zero_half)
        ghosts = fetch_ghosts(packets)
        lookup = jnp.concatenate([rounded, ghosts.reshape((-1,) + rounded.shape[1:])], axis=0)
        gathered = jnp.where(present[:, :, None, None], lookup[source], zero_half)
        own_part = jnp.einsum(
            "eij,erj->eri", diag_blocks, rounded, preferred_element_type=jnp.float32
        )
        face_part = jnp.einsum(
            "efij,efrj->eri", face_blocks, gathered, preferred_element_type=jnp.float32
        )
        vectors.append((own_part + face_part) * live_mask)
    basis = jnp.stack(vectors)
    local_gram = jnp.einsum("icrn,jcrn->rij", basis, basis, precision=HIGH)
    gram = lax.psum(local_gram, ("gx", "gy"))
    weights = coefficients(gram)
    solution = jnp.einsum("rk,kcrn->crn", weights, basis[:POWERS], precision=HIGH)
    residual = basis[0] - jnp.einsum("rk,kcrn->crn", weights, basis[1:], precision=HIGH)
    return (solution, residual)


def solution(mesh):
    in_specs = (
        P(("gx", "gy"), None, None),
        P(("gx", "gy"), None, None),
        P(("gx", "gy"), None, None, None),
        P(("gx", "gy"), None),
        P(("gx", "gy"), None, None),
        P(("gx", "gy")),
    )
    out_specs = (P(("gx", "gy"), None, None), P(("gx", "gy"), None, None))
    return jax.shard_map(
        per_device, mesh=mesh, in_specs=in_specs, out_specs=out_specs, check_vma=False
    )
```

profile of v0, /device:TPU:1, one launch (start us, length us, event | category | flops | bytes accessed | tf_op | source)
XLA Modules:
  0.0 309.1 jit_solution(4113129172325548190)
XLA Ops:
  7.9 5.2 %collective-permute-start.1 = (bf16[16,8,128]{2,1,0:T(8,128)(2,1)}, bf16[16,8,128]{2,1,0:T(8,128)(2,1)}, u32[]{:S(2)}, u32[]{:S(2)}) collective-permute-start(bf16[16,8,128]{2,1,0:T(8,128)(2,1)} %get-tuple-element.53), channel_id=1, source_target_pairs={{16,0},{17,1},{18,2},{19,3},{20,4},{21,5},{22,6},{23,7},{24,8},{25... | collective-permute-start | bytes 98312 | tf_op jit(solution)/shard_map/ppermute | solution.py:15
  13.1 1.9 collective-permute-start.2
  15.0 6.2 %collective-permute-start.3 = (bf16[16,8,128]{2,1,0:T(8,128)(2,1)}, bf16[16,8,128]{2,1,0:T(8,128)(2,1)}, u32[]{:S(2)}, u32[]{:S(2)}) collective-permute-start(bf16[16,8,128]{2,1,0:T(8,128)(2,1)} %get-tuple-element.51), channel_id=1, source_target_pairs={{1,0},{2,1},{3,2},{4,3},{5,4},{6,5},{7,6},{8,7},{9,8},{10,9},{11,1... | collective-permute-start | bytes 98312 | tf_op jit(solution)/shard_map/ppermute | solution.py:15
  21.2 1.9 collective-permute-start.4
  26.2 8.3 %collective-permute-start.5 = (bf16[16,8,128]{2,1,0:T(8,128)(2,1)}, bf16[16,8,128]{2,1,0:T(8,128)(2,1)S(1)}, u32[]{:S(2)}, u32[]{:S(2)}) collective-permute-start(bf16[16,8,128]{2,1,0:T(8,128)(2,1)} %get-tuple-element.49), channel_id=1, source_target_pairs={{0,15},{1,16},{2,17},{3,18},{4,19},{5,20},{6,21},{7,22},{8,23},{9,... | collective-permute-start | bytes 98312 | tf_op jit(solution)/shard_map/ppermute | solution.py:15
  35.3 6.7 %collective-permute-start.6 = (bf16[16,8,128]{2,1,0:T(8,128)(2,1)}, bf16[16,8,128]{2,1,0:T(8,128)(2,1)S(1)}, u32[]{:S(2)}, u32[]{:S(2)}) collective-permute-start(bf16[16,8,128]{2,1,0:T(8,128)(2,1)} %get-tuple-element.48), channel_id=1, source_target_pairs={{0,16},{1,17},{2,18},{3,19},{4,20},{5,21},{6,22},{7,23},{8,24},{9,... | collective-permute-start | bytes 98312 | tf_op jit(solution)/shard_map/ppermute | solution.py:15
  46.3 2.6 gather_fusion.1
  48.9 5.9 %convolution_bitcast_fusion.3 = f32[64,8,128]{2,1,0:T(8,128)S(1)} fusion(bf16[64,4,128,128]{3,2,1,0:T(8,128)(2,1)} %param.8, bf16[64,4,8,128]{3,2,1,0:T(8,128)(2,1)} %bitcast.295, pred[64,4]{1,0:T(8,128)(4,1)S(1)} %copy.36), kind=kOutput, calls=%fused_computation.20 | convolution fusion | flops 67371008 | bytes 9175296 | tf_op jit(solution)/shard_map/efij,efrj->eri/dot_general | solution.py:82
  60.7 1.9 collective-permute-start.9
  62.6 1.9 collective-permute-start.10
  64.5 8.1 %collective-permute-start.11 = (bf16[16,8,128]{2,1,0:T(8,128)(2,1)S(1)}, bf16[16,8,128]{2,1,0:T(8,128)(2,1)S(1)}, u32[]{:S(2)}, u32[]{:S(2)}) collective-permute-start(bf16[16,8,128]{2,1,0:T(8,128)(2,1)S(1)} %get-tuple-element.43), channel_id=1, source_target_pairs={{1,0},{2,1},{3,2},{4,3},{5,4},{6,5},{7,6},{8,7},{9,8},{10,9},{11,1... | collective-permute-start | bytes 98312 | tf_op jit(solution)/shard_map/ppermute | solution.py:15
  72.6 1.9 collective-permute-start.12
  74.6 9.5 %collective-permute-start.13 = (bf16[16,8,128]{2,1,0:T(8,128)(2,1)S(1)}, bf16[16,8,128]{2,1,0:T(8,128)(2,1)S(1)}, u32[]{:S(2)}, u32[]{:S(2)}) collective-permute-start(bf16[16,8,128]{2,1,0:T(8,128)(2,1)S(1)} %get-tuple-element.41), channel_id=1, source_target_pairs={{0,15},{1,16},{2,17},{3,18},{4,19},{5,20},{6,21},{7,22},{8,23},{9,... | collective-permute-start | bytes 98312 | tf_op jit(solution)/shard_map/ppermute | solution.py:15
  84.1 7.8 %collective-permute-start.14 = (bf16[16,8,128]{2,1,0:T(8,128)(2,1)S(1)}, bf16[16,8,128]{2,1,0:T(8,128)(2,1)S(1)}, u32[]{:S(2)}, u32[]{:S(2)}) collective-permute-start(bf16[16,8,128]{2,1,0:T(8,128)(2,1)S(1)} %get-tuple-element.40), channel_id=1, source_target_pairs={{0,16},{1,17},{2,18},{3,19},{4,20},{5,21},{6,22},{7,23},{8,24},{9,... | collective-permute-start | bytes 98312 | tf_op jit(solution)/shard_map/ppermute | solution.py:15
  95.0 2.6 gather_fusion.3
  97.6 5.9 %convolution_bitcast_fusion.2 = f32[64,8,128]{2,1,0:T(8,128)S(1)} fusion(bf16[64,4,128,128]{3,2,1,0:T(8,128)(2,1)} %param.8, bf16[64,4,8,128]{3,2,1,0:T(8,128)(2,1)} %bitcast.296, pred[64,4]{1,0:T(8,128)(4,1)S(1)} %copy.36), kind=kOutput, calls=%fused_computation.17 | convolution fusion | flops 67371008 | bytes 9175296 | tf_op jit(solution)/shard_map/efij,efrj->eri/dot_general | solution.py:82
  113.7 8.1 %collective-permute-start.19 = (bf16[16,8,128]{2,1,0:T(8,128)(2,1)S(1)}, bf16[16,8,128]{2,1,0:T(8,128)(2,1)S(1)}, u32[]{:S(2)}, u32[]{:S(2)}) collective-permute-start(bf16[16,8,128]{2,1,0:T(8,128)(2,1)S(1)} %get-tuple-element.35), channel_id=1, source_target_pairs={{1,0},{2,1},{3,2},{4,3},{5,4},{6,5},{7,6},{8,7},{9,8},{10,9},{11,1... | collective-permute-start | bytes 98312 | tf_op jit(solution)/shard_map/ppermute | solution.py:15
  123.7 9.5 %collective-permute-start.21 = (bf16[16,8,128]{2,1,0:T(8,128)(2,1)S(1)}, bf16[16,8,128]{2,1,0:T(8,128)(2,1)S(1)}, u32[]{:S(2)}, u32[]{:S(2)}) collective-permute-start(bf16[16,8,128]{2,1,0:T(8,128)(2,1)S(1)} %get-tuple-element.33), channel_id=1, source_target_pairs={{0,15},{1,16},{2,17},{3,18},{4,19},{5,20},{6,21},{7,22},{8,23},{9,... | collective-permute-start | bytes 98312 | tf_op jit(solution)/shard_map/ppermute | solution.py:15
  133.3 7.8 %collective-permute-start.22 = (bf16[16,8,128]{2,1,0:T(8,128)(2,1)S(1)}, bf16[16,8,128]{2,1,0:T(8,128)(2,1)S(1)}, u32[]{:S(2)}, u32[]{:S(2)}) collective-permute-start(bf16[16,8,128]{2,1,0:T(8,128)(2,1)S(1)} %get-tuple-element.32), channel_id=1, source_target_pairs={{0,16},{1,17},{2,18},{3,19},{4,20},{5,21},{6,22},{7,23},{8,24},{9,... | collective-permute-start | bytes 98312 | tf_op jit(solution)/shard_map/ppermute | solution.py:15
  144.3 2.6 gather_fusion.5
  146.9 5.9 %convolution_bitcast_fusion.1 = f32[64,8,128]{2,1,0:T(8,128)S(1)} fusion(bf16[64,4,128,128]{3,2,1,0:T(8,128)(2,1)} %param.8, bf16[64,4,8,128]{3,2,1,0:T(8,128)(2,1)} %bitcast.297, pred[64,4]{1,0:T(8,128)(4,1)S(1)} %copy.36), kind=kOutput, calls=%fused_computation.14 | convolution fusion | flops 67371008 | bytes 9175296 | tf_op jit(solution)/shard_map/efij,efrj->eri/dot_general | solution.py:82
  161.0 1.9 collective-permute-start.26
  162.9 8.2 %collective-permute-start.27 = (bf16[16,8,128]{2,1,0:T(8,128)(2,1)S(1)}, bf16[16,8,128]{2,1,0:T(8,128)(2,1)S(1)}, u32[]{:S(2)}, u32[]{:S(2)}) collective-permute-start(bf16[16,8,128]{2,1,0:T(8,128)(2,1)S(1)} %get-tuple-element.27), channel_id=1, source_target_pairs={{1,0},{2,1},{3,2},{4,3},{5,4},{6,5},{7,6},{8,7},{9,8},{10,9},{11,1... | collective-permute-start | bytes 98312 | tf_op jit(solution)/shard_map/ppermute | solution.py:15
  173.1 9.6 %collective-permute-start.29 = (bf16[16,8,128]{2,1,0:T(8,128)(2,1)S(1)}, bf16[16,8,128]{2,1,0:T(8,128)(2,1)S(1)}, u32[]{:S(2)}, u32[]{:S(2)}) collective-permute-start(bf16[16,8,128]{2,1,0:T(8,128)(2,1)S(1)} %get-tuple-element.25), channel_id=1, source_target_pairs={{0,15},{1,16},{2,17},{3,18},{4,19},{5,20},{6,21},{7,22},{8,23},{9,... | collective-permute-start | bytes 98312 | tf_op jit(solution)/shard_map/ppermute | solution.py:15
  182.7 7.8 %collective-permute-start.30 = (bf16[16,8,128]{2,1,0:T(8,128)(2,1)S(1)}, bf16[16,8,128]{2,1,0:T(8,128)(2,1)S(1)}, u32[]{:S(2)}, u32[]{:S(2)}) collective-permute-start(bf16[16,8,128]{2,1,0:T(8,128)(2,1)S(1)} %get-tuple-element.24), channel_id=1, source_target_pairs={{0,16},{1,17},{2,18},{3,19},{4,20},{5,21},{6,22},{7,23},{8,24},{9,... | collective-permute-start | bytes 98312 | tf_op jit(solution)/shard_map/ppermute | solution.py:15
  193.6 2.6 gather_fusion.7
  196.3 5.9 %convolution_bitcast_fusion = f32[64,8,128]{2,1,0:T(8,128)S(1)} fusion(bf16[64,4,128,128]{3,2,1,0:T(8,128)(2,1)} %param.8, bf16[64,4,8,128]{3,2,1,0:T(8,128)(2,1)} %bitcast.294, pred[64,4]{1,0:T(8,128)(4,1)S(1)} %copy.36), kind=kOutput, calls=%fused_computation.10 | convolution fusion | flops 67371008 | bytes 9175296 | tf_op jit(solution)/shard_map/efij,efrj->eri/dot_general | solution.py:82
  204.0 4.9 %fusion.7 = f32[8,5,5]{1,2,0:T(8,128)S(1)} fusion(f32[5,64,8,128]{3,2,1,0:T(8,128)S(1)} %get-tuple-element.61), kind=kOutput, calls=%fused_computation.23 | convolution fusion | flops 19660800 | bytes 1311520 | tf_op jit(solution)/shard_map/icrn,jcrn->rij/dot_general | solution.py:87
  209.0 87.5 %psum.7 = f32[8,5,5]{1,2,0:T(8,128)S(1)} all-reduce(f32[8,5,5]{1,2,0:T(8,128)S(1)} %fusion.7), channel_id=1, replica_groups=mesh['gx'=16,'gy'=16] {'gx','gy'}, use_global_device_ids=true, to_apply=%region_0.1 | all-reduce | flops 200 | bytes 1600 | tf_op jit(solution)/shard_map/psum | solution.py:88
  296.9 3.0 custom-call.4
  302.3 2.5 fusion.12
  305.7 2.5 fusion.10
  (164 shorter events, 58.4 us)
Async XLA Ops:
  6.6 19.6 %collective-permute-start = (bf16[16,8,128]{2,1,0:T(8,128)(2,1)}, bf16[16,8,128]{2,1,0:T(8,128)(2,1)}, u32[]{:S(2)}, u32[]{:S(2)}) collective-permute-start(bf16[16,8,128]{2,1,0:T(8,128)(2,1)} %get-tuple-element.54), channel_id=1, source_target_pairs={{17,0},{18,1},{19,2},{20,3},{21,4},{22,5},{23,6},{24,7},{25,8},{26... | collective-permute-start | bytes 98312 | tf_op jit(solution)/shard_map/ppermute | solution.py:15
  7.9 27.4 %collective-permute-start.1 = (bf16[16,8,128]{2,1,0:T(8,128)(2,1)}, bf16[16,8,128]{2,1,0:T(8,128)(2,1)}, u32[]{:S(2)}, u32[]{:S(2)}) collective-permute-start(bf16[16,8,128]{2,1,0:T(8,128)(2,1)} %get-tuple-element.53), channel_id=1, source_target_pairs={{16,0},{17,1},{18,2},{19,3},{20,4},{21,5},{22,6},{23,7},{24,8},{25... | collective-permute-start | bytes 98312 | tf_op jit(solution)/shard_map/ppermute | solution.py:15
  13.1 29.8 %collective-permute-start.2 = (bf16[16,8,128]{2,1,0:T(8,128)(2,1)}, bf16[16,8,128]{2,1,0:T(8,128)(2,1)}, u32[]{:S(2)}, u32[]{:S(2)}) collective-permute-start(bf16[16,8,128]{2,1,0:T(8,128)(2,1)} %get-tuple-element.52), channel_id=1, source_target_pairs={{15,0},{16,1},{17,2},{18,3},{19,4},{20,5},{21,6},{22,7},{23,8},{24... | collective-permute-start | bytes 98312 | tf_op jit(solution)/shard_map/ppermute | solution.py:15
  15.0 29.2 %collective-permute-start.3 = (bf16[16,8,128]{2,1,0:T(8,128)(2,1)}, bf16[16,8,128]{2,1,0:T(8,128)(2,1)}, u32[]{:S(2)}, u32[]{:S(2)}) collective-permute-start(bf16[16,8,128]{2,1,0:T(8,128)(2,1)} %get-tuple-element.51), channel_id=1, source_target_pairs={{1,0},{2,1},{3,2},{4,3},{5,4},{6,5},{7,6},{8,7},{9,8},{10,9},{11,1... | collective-permute-start | bytes 98312 | tf_op jit(solution)/shard_map/ppermute | solution.py:15
  21.2 23.8 %collective-permute-start.4 = (bf16[16,8,128]{2,1,0:T(8,128)(2,1)}, bf16[16,8,128]{2,1,0:T(8,128)(2,1)}, u32[]{:S(2)}, u32[]{:S(2)}) collective-permute-start(bf16[16,8,128]{2,1,0:T(8,128)(2,1)} %get-tuple-element.50), channel_id=1, source_target_pairs={{0,1},{1,2},{2,3},{3,4},{4,5},{5,6},{6,7},{7,8},{8,9},{9,10},{10,1... | collective-permute-start | bytes 98312 | tf_op jit(solution)/shard_map/ppermute | solution.py:15
  26.2 18.8 %collective-permute-start.5 = (bf16[16,8,128]{2,1,0:T(8,128)(2,1)}, bf16[16,8,128]{2,1,0:T(8,128)(2,1)S(1)}, u32[]{:S(2)}, u32[]{:S(2)}) collective-permute-start(bf16[16,8,128]{2,1,0:T(8,128)(2,1)} %get-tuple-element.49), channel_id=1, source_target_pairs={{0,15},{1,16},{2,17},{3,18},{4,19},{5,20},{6,21},{7,22},{8,23},{9,... | collective-permute-start | bytes 98312 | tf_op jit(solution)/shard_map/ppermute | solution.py:15
  35.3 9.8 %collective-permute-start.6 = (bf16[16,8,128]{2,1,0:T(8,128)(2,1)}, bf16[16,8,128]{2,1,0:T(8,128)(2,1)S(1)}, u32[]{:S(2)}, u32[]{:S(2)}) collective-permute-start(bf16[16,8,128]{2,1,0:T(8,128)(2,1)} %get-tuple-element.48), channel_id=1, source_target_pairs={{0,16},{1,17},{2,18},{3,19},{4,20},{5,21},{6,22},{7,23},{8,24},{9,... | collective-permute-start | bytes 98312 | tf_op jit(solution)/shard_map/ppermute | solution.py:15
  42.9 2.6 collective-permute-start.7
  59.4 15.2 %collective-permute-start.8 = (bf16[16,8,128]{2,1,0:T(8,128)(2,1)S(1)}, bf16[16,8,128]{2,1,0:T(8,128)(2,1)S(1)}, u32[]{:S(2)}, u32[]{:S(2)}) collective-permute-start(bf16[16,8,128]{2,1,0:T(8,128)(2,1)S(1)} %get-tuple-element.46), channel_id=1, source_target_pairs={{17,0},{18,1},{19,2},{20,3},{21,4},{22,5},{23,6},{24,7},{25,8},{26... | collective-permute-start | bytes 98312 | tf_op jit(solution)/shard_map/ppermute | solution.py:15
  60.7 23.4 %collective-permute-start.9 = (bf16[16,8,128]{2,1,0:T(8,128)(2,1)S(1)}, bf16[16,8,128]{2,1,0:T(8,128)(2,1)S(1)}, u32[]{:S(2)}, u32[]{:S(2)}) collective-permute-start(bf16[16,8,128]{2,1,0:T(8,128)(2,1)S(1)} %get-tuple-element.45), channel_id=1, source_target_pairs={{16,0},{17,1},{18,2},{19,3},{20,4},{21,5},{22,6},{23,7},{24,8},{25... | collective-permute-start | bytes 98312 | tf_op jit(solution)/shard_map/ppermute | solution.py:15
  62.6 29.3 %collective-permute-start.10 = (bf16[16,8,128]{2,1,0:T(8,128)(2,1)S(1)}, bf16[16,8,128]{2,1,0:T(8,128)(2,1)S(1)}, u32[]{:S(2)}, u32[]{:S(2)}) collective-permute-start(bf16[16,8,128]{2,1,0:T(8,128)(2,1)S(1)} %get-tuple-element.44), channel_id=1, source_target_pairs={{15,0},{16,1},{17,2},{18,3},{19,4},{20,5},{21,6},{22,7},{23,8},{24... | collective-permute-start | bytes 98312 | tf_op jit(solution)/shard_map/ppermute | solution.py:15
  64.5 28.7 %collective-permute-start.11 = (bf16[16,8,128]{2,1,0:T(8,128)(2,1)S(1)}, bf16[16,8,128]{2,1,0:T(8,128)(2,1)S(1)}, u32[]{:S(2)}, u32[]{:S(2)}) collective-permute-start(bf16[16,8,128]{2,1,0:T(8,128)(2,1)S(1)} %get-tuple-element.43), channel_id=1, source_target_pairs={{1,0},{2,1},{3,2},{4,3},{5,4},{6,5},{7,6},{8,7},{9,8},{10,9},{11,1... | collective-permute-start | bytes 98312 | tf_op jit(solution)/shard_map/ppermute | solution.py:15
  72.6 20.6 %collective-permute-start.12 = (bf16[16,8,128]{2,1,0:T(8,128)(2,1)S(1)}, bf16[16,8,128]{2,1,0:T(8,128)(2,1)S(1)}, u32[]{:S(2)}, u32[]{:S(2)}) collective-permute-start(bf16[16,8,128]{2,1,0:T(8,128)(2,1)S(1)} %get-tuple-element.42), channel_id=1, source_target_pairs={{0,1},{1,2},{2,3},{3,4},{4,5},{5,6},{6,7},{7,8},{8,9},{9,10},{10,1... | collective-permute-start | bytes 98312 | tf_op jit(solution)/shard_map/ppermute | solution.py:15
  74.6 18.7 %collective-permute-start.13 = (bf16[16,8,128]{2,1,0:T(8,128)(2,1)S(1)}, bf16[16,8,128]{2,1,0:T(8,128)(2,1)S(1)}, u32[]{:S(2)}, u32[]{:S(2)}) collective-permute-start(bf16[16,8,128]{2,1,0:T(8,128)(2,1)S(1)} %get-tuple-element.41), channel_id=1, source_target_pairs={{0,15},{1,16},{2,17},{3,18},{4,19},{5,20},{6,21},{7,22},{8,23},{9,... | collective-permute-start | bytes 98312 | tf_op jit(solution)/shard_map/ppermute | solution.py:15
  84.1 9.2 %collective-permute-start.14 = (bf16[16,8,128]{2,1,0:T(8,128)(2,1)S(1)}, bf16[16,8,128]{2,1,0:T(8,128)(2,1)S(1)}, u32[]{:S(2)}, u32[]{:S(2)}) collective-permute-start(bf16[16,8,128]{2,1,0:T(8,128)(2,1)S(1)} %get-tuple-element.40), channel_id=1, source_target_pairs={{0,16},{1,17},{2,18},{3,19},{4,20},{5,21},{6,22},{7,23},{8,24},{9,... | collective-permute-start | bytes 98312 | tf_op jit(solution)/shard_map/ppermute | solution.py:15
  91.9 2.3 collective-permute-start.15
  108.0 15.7 %collective-permute-start.16 = (bf16[16,8,128]{2,1,0:T(8,128)(2,1)S(1)}, bf16[16,8,128]{2,1,0:T(8,128)(2,1)S(1)}, u32[]{:S(2)}, u32[]{:S(2)}) collective-permute-start(bf16[16,8,128]{2,1,0:T(8,128)(2,1)S(1)} %get-tuple-element.38), channel_id=1, source_target_pairs={{17,0},{18,1},{19,2},{20,3},{21,4},{22,5},{23,6},{24,7},{25,8},{26... | collective-permute-start | bytes 98312 | tf_op jit(solution)/shard_map/ppermute | solution.py:15
  109.8 23.5 %collective-permute-start.17 = (bf16[16,8,128]{2,1,0:T(8,128)(2,1)S(1)}, bf16[16,8,128]{2,1,0:T(8,128)(2,1)S(1)}, u32[]{:S(2)}, u32[]{:S(2)}) collective-permute-start(bf16[16,8,128]{2,1,0:T(8,128)(2,1)S(1)} %get-tuple-element.37), channel_id=1, source_target_pairs={{16,0},{17,1},{18,2},{19,3},{20,4},{21,5},{22,6},{23,7},{24,8},{25... | collective-permute-start | bytes 98312 | tf_op jit(solution)/shard_map/ppermute | solution.py:15
  111.8 29.4 %collective-permute-start.18 = (bf16[16,8,128]{2,1,0:T(8,128)(2,1)S(1)}, bf16[16,8,128]{2,1,0:T(8,128)(2,1)S(1)}, u32[]{:S(2)}, u32[]{:S(2)}) collective-permute-start(bf16[16,8,128]{2,1,0:T(8,128)(2,1)S(1)} %get-tuple-element.36), channel_id=1, source_target_pairs={{15,0},{16,1},{17,2},{18,3},{19,4},{20,5},{21,6},{22,7},{23,8},{24... | collective-permute-start | bytes 98312 | tf_op jit(solution)/shard_map/ppermute | solution.py:15
  113.7 28.8 %collective-permute-start.19 = (bf16[16,8,128]{2,1,0:T(8,128)(2,1)S(1)}, bf16[16,8,128]{2,1,0:T(8,128)(2,1)S(1)}, u32[]{:S(2)}, u32[]{:S(2)}) collective-permute-start(bf16[16,8,128]{2,1,0:T(8,128)(2,1)S(1)} %get-tuple-element.35), channel_id=1, source_target_pairs={{1,0},{2,1},{3,2},{4,3},{5,4},{6,5},{7,6},{8,7},{9,8},{10,9},{11,1... | collective-permute-start | bytes 98312 | tf_op jit(solution)/shard_map/ppermute | solution.py:15
  121.8 20.7 %collective-permute-start.20 = (bf16[16,8,128]{2,1,0:T(8,128)(2,1)S(1)}, bf16[16,8,128]{2,1,0:T(8,128)(2,1)S(1)}, u32[]{:S(2)}, u32[]{:S(2)}) collective-permute-start(bf16[16,8,128]{2,1,0:T(8,128)(2,1)S(1)} %get-tuple-element.34), channel_id=1, source_target_pairs={{0,1},{1,2},{2,3},{3,4},{4,5},{5,6},{6,7},{7,8},{8,9},{9,10},{10,1... | collective-permute-start | bytes 98312 | tf_op jit(solution)/shard_map/ppermute | solution.py:15
  123.7 18.8 %collective-permute-start.21 = (bf16[16,8,128]{2,1,0:T(8,128)(2,1)S(1)}, bf16[16,8,128]{2,1,0:T(8,128)(2,1)S(1)}, u32[]{:S(2)}, u32[]{:S(2)}) collective-permute-start(bf16[16,8,128]{2,1,0:T(8,128)(2,1)S(1)} %get-tuple-element.33), channel_id=1, source_target_pairs={{0,15},{1,16},{2,17},{3,18},{4,19},{5,20},{6,21},{7,22},{8,23},{9,... | collective-permute-start | bytes 98312 | tf_op jit(solution)/shard_map/ppermute | solution.py:15
  133.3 9.3 %collective-permute-start.22 = (bf16[16,8,128]{2,1,0:T(8,128)(2,1)S(1)}, bf16[16,8,128]{2,1,0:T(8,128)(2,1)S(1)}, u32[]{:S(2)}, u32[]{:S(2)}) collective-permute-start(bf16[16,8,128]{2,1,0:T(8,128)(2,1)S(1)} %get-tuple-element.32), channel_id=1, source_target_pairs={{0,16},{1,17},{2,18},{3,19},{4,20},{5,21},{6,22},{7,23},{8,24},{9,... | collective-permute-start | bytes 98312 | tf_op jit(solution)/shard_map/ppermute | solution.py:15
  141.1 2.3 collective-permute-start.23
  157.3 15.7 %collective-permute-start.24 = (bf16[16,8,128]{2,1,0:T(8,128)(2,1)S(1)}, bf16[16,8,128]{2,1,0:T(8,128)(2,1)S(1)}, u32[]{:S(2)}, u32[]{:S(2)}) collective-permute-start(bf16[16,8,128]{2,1,0:T(8,128)(2,1)S(1)} %get-tuple-element.30), channel_id=1, source_target_pairs={{17,0},{18,1},{19,2},{20,3},{21,4},{22,5},{23,6},{24,7},{25,8},{26... | collective-permute-start | bytes 98312 | tf_op jit(solution)/shard_map/ppermute | solution.py:15
  159.1 23.6 %collective-permute-start.25 = (bf16[16,8,128]{2,1,0:T(8,128)(2,1)S(1)}, bf16[16,8,128]{2,1,0:T(8,128)(2,1)S(1)}, u32[]{:S(2)}, u32[]{:S(2)}) collective-permute-start(bf16[16,8,128]{2,1,0:T(8,128)(2,1)S(1)} %get-tuple-element.29), channel_id=1, source_target_pairs={{16,0},{17,1},{18,2},{19,3},{20,4},{21,5},{22,6},{23,7},{24,8},{25... | collective-permute-start | bytes 98312 | tf_op jit(solution)/shard_map/ppermute | solution.py:15
  161.0 29.5 %collective-permute-start.26 = (bf16[16,8,128]{2,1,0:T(8,128)(2,1)S(1)}, bf16[16,8,128]{2,1,0:T(8,128)(2,1)S(1)}, u32[]{:S(2)}, u32[]{:S(2)}) collective-permute-start(bf16[16,8,128]{2,1,0:T(8,128)(2,1)S(1)} %get-tuple-element.28), channel_id=1, source_target_pairs={{15,0},{16,1},{17,2},{18,3},{19,4},{20,5},{21,6},{22,7},{23,8},{24... | collective-permute-start | bytes 98312 | tf_op jit(solution)/shard_map/ppermute | solution.py:15
  162.9 29.1 %collective-permute-start.27 = (bf16[16,8,128]{2,1,0:T(8,128)(2,1)S(1)}, bf16[16,8,128]{2,1,0:T(8,128)(2,1)S(1)}, u32[]{:S(2)}, u32[]{:S(2)}) collective-permute-start(bf16[16,8,128]{2,1,0:T(8,128)(2,1)S(1)} %get-tuple-element.27), channel_id=1, source_target_pairs={{1,0},{2,1},{3,2},{4,3},{5,4},{6,5},{7,6},{8,7},{9,8},{10,9},{11,1... | collective-permute-start | bytes 98312 | tf_op jit(solution)/shard_map/ppermute | solution.py:15
  171.1 20.9 %collective-permute-start.28 = (bf16[16,8,128]{2,1,0:T(8,128)(2,1)S(1)}, bf16[16,8,128]{2,1,0:T(8,128)(2,1)S(1)}, u32[]{:S(2)}, u32[]{:S(2)}) collective-permute-start(bf16[16,8,128]{2,1,0:T(8,128)(2,1)S(1)} %get-tuple-element.26), channel_id=1, source_target_pairs={{0,1},{1,2},{2,3},{3,4},{4,5},{5,6},{6,7},{7,8},{8,9},{9,10},{10,1... | collective-permute-start | bytes 98312 | tf_op jit(solution)/shard_map/ppermute | solution.py:15
  173.1 19.0 %collective-permute-start.29 = (bf16[16,8,128]{2,1,0:T(8,128)(2,1)S(1)}, bf16[16,8,128]{2,1,0:T(8,128)(2,1)S(1)}, u32[]{:S(2)}, u32[]{:S(2)}) collective-permute-start(bf16[16,8,128]{2,1,0:T(8,128)(2,1)S(1)} %get-tuple-element.25), channel_id=1, source_target_pairs={{0,15},{1,16},{2,17},{3,18},{4,19},{5,20},{6,21},{7,22},{8,23},{9,... | collective-permute-start | bytes 98312 | tf_op jit(solution)/shard_map/ppermute | solution.py:15
  182.7 9.5 %collective-permute-start.30 = (bf16[16,8,128]{2,1,0:T(8,128)(2,1)S(1)}, bf16[16,8,128]{2,1,0:T(8,128)(2,1)S(1)}, u32[]{:S(2)}, u32[]{:S(2)}) collective-permute-start(bf16[16,8,128]{2,1,0:T(8,128)(2,1)S(1)} %get-tuple-element.24), channel_id=1, source_target_pairs={{0,16},{1,17},{2,18},{3,19},{4,20},{5,21},{6,22},{7,23},{8,24},{9,... | collective-permute-start | bytes 98312 | tf_op jit(solution)/shard_map/ppermute | solution.py:15
  190.5 2.3 collective-permute-start.31
  (14 other events, 341.8 us)
where the time goes:
time: 311 us; the launch traced here: 309 us
  starting transfers between devices  134 us (43%)
  blocking collectives  87.5 us (28%)
  matrix products  38.9 us (13%)
  other arithmetic  22.7 us (7%)
  local copies, waits for them, and re-layouts  20.8 us (7%)
    ppermute x32, starting transfers between devices, passed_along(): return lax.ppermute(block, axis, route)  134 us
    psum x1, blocking collectives, per_device(): gram = lax.psum(local_gram, ('gx', 'gy'))  87.5 us
    dot_general x4, matrix products, per_device(): jnp.einsum('efij,efrj->eri', face_blocks, gathered, preferred_element_typ...  23.5 us
    gather x4, local copies, waits for them, and re-layouts, per_device(): gathered = jnp.where(present[:, :, None, None], lookup[source], zero_half)  10.4 us
  transfers between devices with their start and end apart: 32, of which 4 were waited for; matrix products, arithmetic and copies ran while one was open for 2% of the time, Pallas kernels for 0%

commit v1 on v0

v1 whole, which is shorter than its diff:
```python
import functools

import jax
import jax.numpy as jnp
from jax import lax
from jax.experimental import pallas as pl
from jax.experimental.pallas import tpu as pltpu
from jax.sharding import PartitionSpec as P

POWERS = 4
CAP = 64
SEND = 16
FACES = 4
SIDE = 16
LOOKUP = CAP + 9 * SEND
NOTHING = CAP + 4 * SEND
UNROLL = 16
META_SEND = FACES * CAP
META_COUNT = META_SEND + 9 * SEND
META_SIZE = 512

ROW_BY_ROW = (((1,), (1,)), ((), ()))
IN_VMEM = pl.BlockSpec(memory_space=pltpu.VMEM)
IN_SMEM = pl.BlockSpec(memory_space=pltpu.SMEM)
UP_DIRECTIONS = (2, 5, 8)
DOWN_DIRECTIONS = (0, 3, 6)


def pair_lane(first, second):
    return 5 * first + second


def vector_shape(count, dtype):
    return jax.ShapeDtypeStruct((count, 8, 128), dtype)


def params():
    return pltpu.CompilerParams(vmem_limit_bytes=16 << 20)


def pack(meta, rounded, up, down, next_row, last_row):
    for target, directions in (
        (up, UP_DIRECTIONS),
        (down, DOWN_DIRECTIONS),
        (next_row, (7,)),
        (last_row, (1,)),
    ):
        for at, direction in enumerate(directions):
            for k in range(SEND):
                slot = jnp.maximum(meta[META_SEND + direction * SEND + k], 0)
                target[at * SEND + k] = rounded[slot]


def start_kernel(meta, right_sides, basis, rounded, up, down, next_row, last_row):
    count = meta[META_COUNT]
    element = lax.broadcasted_iota(jnp.int32, basis.shape, 0)
    live = jnp.where(element < count, right_sides[...], 0.0)
    basis[...] = live
    rounded[...] = live.astype(jnp.bfloat16)
    pack(meta, rounded, up, down, next_row, last_row)


def relay_kernel(from_down, from_up, next_row, last_row, send_next, send_last):
    send_next[0:SEND] = from_up[2 * SEND : 3 * SEND]
    send_next[SEND : 2 * SEND] = next_row[...]
    send_next[2 * SEND : 3 * SEND] = from_down[2 * SEND : 3 * SEND]
    send_last[0:SEND] = from_up[0:SEND]
    send_last[SEND : 2 * SEND] = last_row[...]
    send_last[2 * SEND : 3 * SEND] = from_down[0:SEND]


def apply_kernel(power, *refs):
    meta, diag, face, rounded, from_down, from_up, from_last, from_next = refs[:8]
    basis = refs[8 : 9 + power]
    refs = refs[9 + power :]
    last = power == POWERS - 1
    gram_in = refs[0] if power else None
    refs = refs[1:] if power else refs
    if last:
        image, gram_out, lookup = refs
    else:
        image, image_rounded, up, down, next_row, last_row, gram_out, lookup = refs
    lookup[0:CAP] = rounded[...]
    lookup[CAP : CAP + 3 * SEND] = from_next[...]
    lookup[CAP + 3 * SEND : CAP + 4 * SEND] = from_up[SEND : 2 * SEND]
    lookup[NOTHING : NOTHING + SEND] = jnp.zeros((SEND, 8, 128), jnp.bfloat16)
    lookup[CAP + 5 * SEND : CAP + 6 * SEND] = from_down[SEND : 2 * SEND]
    lookup[CAP + 6 * SEND : CAP + 9 * SEND] = from_last[...]

    def element(e, sums):
        near = [rounded[e]]
        for f in range(FACES):
            at = meta[f * CAP + e]
            near.append(lookup[jnp.where(at < 0, NOTHING, at)])
        blocks = [diag[e]] + [face[e, f] for f in range(FACES)]
        out = lax.dot_general(
            jnp.concatenate(near, axis=1),
            jnp.concatenate(blocks, axis=1),
            ROW_BY_ROW,
            preferred_element_type=jnp.float32,
        )
        image[e] = out
        if not last:
            image_rounded[e] = out.astype(jnp.bfloat16)
        others = [ref[e] for ref in basis] + [out]
        return tuple(s + out * other for s, other in zip(sums, others))

    def several(step, sums):
        for u in range(UNROLL):
            sums = element(step * UNROLL + u, sums)
        return sums

    zero = jnp.zeros((8, 128), jnp.float32)
    sums = lax.fori_loop(0, CAP // UNROLL, several, (zero,) * (power + 2))
    if not last:
        pack(meta, image_rounded, up, down, next_row, last_row)
    lane = lax.broadcasted_iota(jnp.int32, (8, 128), 1)
    gram = gram_in[...] if power else zero
    for a, s in enumerate(sums):
        total = jnp.sum(s, axis=1, keepdims=True)
        gram = jnp.where(lane == pair_lane(a, power + 1), total, gram)
    gram_out[...] = gram


def finish_kernel(gram, b0, b1, b2, b3, b4, solution, residual):
    def entry(a, b):
        at = pair_lane(min(a, b), max(a, b))
        return jnp.broadcast_to(gram[:, at : at + 1], (8, 128))

    factor = {}
    for i in range(POWERS):
        for j in range(i + 1):
            value = entry(i + 1, j + 1)
            for k in range(j):
                value = value - factor[i, k] * factor[j, k]
            factor[i, j] = jnp.sqrt(value) if i == j else value / factor[j, j]
    forward = []
    for i in range(POWERS):
        value = entry(0, i + 1)
        for k in range(i):
            value = value - factor[i, k] * forward[k]
        forward.append(value / factor[i, i])
    weights = [None] * POWERS
    for i in reversed(range(POWERS)):
        value = forward[i]
        for k in range(i + 1, POWERS):
            value = value - factor[k, i] * weights[k]
        weights[i] = value / factor[i, i]
    basis = (b0, b1, b2, b3, b4)

    def several(step, carry):
        for u in range(8):
            e = step * 8 + u
            v = [ref[e] for ref in basis]
            total = weights[0] * v[0]
            moved = weights[0] * v[1]
            for k in range(1, POWERS):
                total = total + weights[k] * v[k]
                moved = moved + weights[k] * v[k + 1]
            solution[e] = total
            residual[e] = v[0] - moved
        return carry

    lax.fori_loop(0, CAP // 8, several, 0)


def shifted(block, axis, distance):
    return lax.ppermute(block, axis, [(i, (i + distance) % SIDE) for i in range(SIDE)])


def summed(block):
    for axis in ("gx", "gy"):
        for step in (1, 4):
            other = [
                lax.ppermute(block, axis, [(i, i ^ (k * step)) for i in range(SIDE)])
                for k in (1, 2, 3)
            ]
            block = (block + other[0]) + (other[1] + other[2])
    return block


def per_device(right_sides, diag_blocks, face_blocks, neighbours, send_slots, counts):
    meta = jnp.concatenate(
        [
            neighbours.T.reshape(-1),
            send_slots.reshape(-1),
            counts,
            jnp.zeros((META_SIZE - META_COUNT - 1,), jnp.int32),
        ]
    )
    diag_blocks = pltpu.with_memory_space_constraint(diag_blocks, pltpu.VMEM)
    face_blocks = pltpu.with_memory_space_constraint(face_blocks, pltpu.VMEM)
    half = jnp.bfloat16
    packets = [vector_shape(n * SEND, half) for n in (3, 3, 1, 1)]
    full = vector_shape(CAP, jnp.float32)
    gram_shape = jax.ShapeDtypeStruct((8, 128), jnp.float32)
    first, rounded, up, down, next_row, last_row = pl.pallas_call(
        start_kernel,
        name="start",
        in_specs=[IN_SMEM, IN_VMEM],
        out_specs=[IN_VMEM] * 6,
        out_shape=[full, vector_shape(CAP, half)] + packets,
        compiler_params=params(),
    )(meta, right_sides)
    basis = [first]
    gram = []
    for power in range(POWERS):
        last = power == POWERS - 1
        from_down = shifted(up, "gy", 1)
        from_up = shifted(down, "gy", -1)
        send_next, send_last = pl.pallas_call(
            relay_kernel,
            name="relay",
            in_specs=[IN_VMEM] * 4,
            out_specs=[IN_VMEM] * 2,
            out_shape=[vector_shape(3 * SEND, half)] * 2,
            compiler_params=params(),
        )(from_down, from_up, next_row, last_row)
        from_last = shifted(send_next, "gx", 1)
        from_next = shifted(send_last, "gx", -1)
        shapes = [full] if last else [full, vector_shape(CAP, half)] + packets
        shapes = shapes + [gram_shape]
        outs = pl.pallas_call(
            functools.partial(apply_kernel, power),
            name=f"apply{power}",
            in_specs=[IN_SMEM] + [IN_VMEM] * (8 + power + len(gram)),
            out_specs=[IN_VMEM] * len(shapes),
            out_shape=shapes,
            scratch_shapes=[pltpu.VMEM((LOOKUP, 8, 128), half)],
            compiler_params=params(),
        )(
            meta, diag_blocks, face_blocks, rounded, from_down, from_up, from_last,
            from_next, *basis, *gram,
        )
        basis.append(outs[0])
        gram = [outs[-1]]
        if not last:
            rounded, up, down, next_row, last_row = outs[1:-1]
    total = summed(gram[0])
    return pl.pallas_call(
        finish_kernel,
        name="finish",
        in_specs=[IN_VMEM] * 6,
        out_specs=[IN_VMEM] * 2,
        out_shape=[full] * 2,
        compiler_params=params(),
    )(total, *basis)


def solution(mesh):
    in_specs = (
        P(("gx", "gy"), None, None),
        P(("gx", "gy"), None, None),
        P(("gx", "gy"), None, None, None),
        P(("gx", "gy"), None),
        P(("gx", "gy"), None, None),
        P(("gx", "gy")),
    )
    out_specs = (P(("gx", "gy"), None, None), P(("gx", "gy"), None, None))
    return jax.shard_map(
        per_device, mesh=mesh, in_specs=in_specs, out_specs=out_specs, check_vma=False
    )
```

time: 311 us -> 118 us (0.38)
  the two profiles are of different devices: /device:TPU:1 before, /device:TPU:4 now
where the time goes in v1:
time: 118 us
  starting transfers between devices  55 us (47%)
  waiting for transfers between devices  33.8 us (29%)
  Pallas kernels  19.9 us (17%)
  local copies, waits for them, and re-layouts  6.77 us (6%)
  between operations  1.41 us (1%)
    ppermute x16, starting transfers between devices, shifted(): lax.ppermute(block, axis, [(i, (i + distance) % SIDE) for i in range(SIDE)])  30 us
    ppermute x12, starting transfers between devices, summed(): lax.ppermute(block, axis, [(i, i ^ k * step) for i in range(SIDE)])  25 us
    ppermute x16, waiting for transfers between devices, shifted(): lax.ppermute(block, axis, [(i, (i + distance) % SIDE) for i in range(SIDE)])  19.7 us
    pallas_call x4, Pallas kernels, per_device(): pl.pallas_call(functools.partial(apply_kernel, power), name=f'apply{power...  17.9 us
    ppermute x12, waiting for transfers between devices, summed(): lax.ppermute(block, axis, [(i, i ^ k * step) for i in range(SIDE)])  14.1 us
    unnamed x8, local copies, waits for them, and re-layouts  5.93 us
  transfers between devices with their start and end apart: 28, of which 16 were waited for; matrix products, arithmetic and copies ran while one was open for 0% of the time, Pallas kernels for 0%

profile of v1, /device:TPU:4, one launch (start us, length us, event | category | flops | bytes accessed | tf_op | source)
XLA Modules:
  0.0 117.6 jit_solution(12332614506856526182)
XLA Ops:
  4.7 1.7 %collective-permute-start = (bf16[48,8,128]{2,1,0:T(8,128)(2,1)S(1)}, bf16[48,8,128]{2,1,0:T(8,128)(2,1)S(1)}, u32[]{:S(2)}, u32[]{:S(2)}) collective-permute-start(bf16[48,8,128]{2,1,0:T(8,128)(2,1)S(1)} %get-tuple-element.40), channel_id=1, source_target_pairs={{0,1},{1,2},{2,3},{3,4},{4,5},{5,6},{6,7},{7,8},{8,9},{9,10},{10,1... | collective-permute-start | bytes 294920 | tf_op jit(solution)/shard_map/ppermute | solution.py:168
  6.3 2.6 %collective-permute-start.1 = (bf16[48,8,128]{2,1,0:T(8,128)(2,1)S(1)}, bf16[48,8,128]{2,1,0:T(8,128)(2,1)S(1)}, u32[]{:S(2)}, u32[]{:S(2)}) collective-permute-start(bf16[48,8,128]{2,1,0:T(8,128)(2,1)S(1)} %get-tuple-element.41), channel_id=1, source_target_pairs={{0,15},{1,0},{2,1},{3,2},{4,3},{5,4},{6,5},{7,6},{8,7},{9,8},{10,9... | collective-permute-start | bytes 294920 | tf_op jit(solution)/shard_map/ppermute | solution.py:168
  8.9 2.6 %collective-permute-done.from_down.refs_4_ = bf16[48,8,128]{2,1,0:T(8,128)(2,1)S(1)} collective-permute-done((bf16[48,8,128]{2,1,0:T(8,128)(2,1)S(1)}, bf16[48,8,128]{2,1,0:T(8,128)(2,1)S(1)}, u32[]{:S(2)}, u32[]{:S(2)}) %collective-permute-start) | collective-permute-done | bytes 98336 | tf_op jit(solution)/shard_map/ppermute | solution.py:168
  11.5 4.2 %collective-permute-start.3 = (bf16[48,8,128]{2,1,0:T(8,128)(2,1)S(1)}, bf16[48,8,128]{2,1,0:T(8,128)(2,1)S(1)}, u32[]{:S(2)}, u32[]{:S(2)}) collective-permute-start(bf16[48,8,128]{2,1,0:T(8,128)(2,1)S(1)} %get-tuple-element.45), channel_id=1, source_target_pairs={{0,240},{16,0},{32,16},{48,32},{64,48},{80,64},{96,80},{112,96},{1... | collective-permute-start | bytes 294920 | tf_op jit(solution)/shard_map/ppermute | solution.py:168
  15.7 2.3 %collective-permute-done.2.refs_6_ = bf16[48,8,128]{2,1,0:T(8,128)(2,1)S(1)} collective-permute-done((bf16[48,8,128]{2,1,0:T(8,128)(2,1)S(1)}, bf16[48,8,128]{2,1,0:T(8,128)(2,1)S(1)}, u32[]{:S(2)}, u32[]{:S(2)}) %collective-permute-start.2) | collective-permute-done | bytes 98336 | tf_op jit(solution)/shard_map/ppermute | solution.py:168
  18.0 3.4 %copy-done = bf16[64,4,128,128]{3,2,1,0:T(8,128)(2,1)S(1)} copy-done((bf16[64,4,128,128]{3,2,1,0:T(8,128)(2,1)S(1)}, bf16[64,4,128,128]{3,2,1,0:T(8,128)(2,1)}, u32[]{:S(2)}) %copy-start) | copy-done | bytes 8388632
  21.3 1.6 %copy-done.2 = bf16[64,128,128]{2,1,0:T(8,128)(2,1)S(1)} copy-done((bf16[64,128,128]{2,1,0:T(8,128)(2,1)S(1)}, bf16[64,128,128]{2,1,0:T(8,128)(2,1)}, u32[]{:S(2)}) %copy-start.2) | copy-done | bytes 2097176
  22.9 4.5 %apply0.1 = (f32[64,8,128]{2,1,0:T(8,128)S(1)}, bf16[64,8,128]{2,1,0:T(8,128)(2,1)S(1)}, bf16[48,8,128]{2,1,0:T(8,128)(2,1)S(1)}, bf16[48,8,128]{2,1,0:T(8,128)(...) custom-call(s32[512]{0:T(512)S(1)} %pad_add_fusion.meta.refs_0_, ...), custom_call_target="tpu_custom_call" | custom-call | tf_op jit(solution)/shard_map/apply0/pallas_call | solution.py:223
  28.4 3.2 %collective-permute-start.5 = (bf16[48,8,128]{2,1,0:T(8,128)(2,1)S(1)}, bf16[48,8,128]{2,1,0:T(8,128)(2,1)S(1)}, u32[]{:S(2)}, u32[]{:S(2)}) collective-permute-start(bf16[48,8,128]{2,1,0:T(8,128)(2,1)S(1)} %get-tuple-element.49), channel_id=1, source_target_pairs={{0,15},{1,0},{2,1},{3,2},{4,3},{5,4},{6,5},{7,6},{8,7},{9,8},{10,9... | collective-permute-start | bytes 294920 | tf_op jit(solution)/shard_map/ppermute | solution.py:168
  31.6 2.8 %collective-permute-done.4.from_down.refs_4_ = bf16[48,8,128]{2,1,0:T(8,128)(2,1)S(1)} collective-permute-done((bf16[48,8,128]{2,1,0:T(8,128)(2,1)S(1)}, bf16[48,8,128]{2,1,0:T(8,128)(2,1)S(1)}, u32[]{:S(2)}, u32[]{:S(2)}) %collective-permute-start.4) | collective-permute-done | bytes 98336 | tf_op jit(solution)/shard_map/ppermute | solution.py:168
  34.5 2.9 %collective-permute-start.7 = (bf16[48,8,128]{2,1,0:T(8,128)(2,1)S(1)}, bf16[48,8,128]{2,1,0:T(8,128)(2,1)S(1)}, u32[]{:S(2)}, u32[]{:S(2)}) collective-permute-start(bf16[48,8,128]{2,1,0:T(8,128)(2,1)S(1)} %get-tuple-element.53), channel_id=1, source_target_pairs={{0,240},{16,0},{32,16},{48,32},{64,48},{80,64},{96,80},{112,96},{1... | collective-permute-start | bytes 294920 | tf_op jit(solution)/shard_map/ppermute | solution.py:168
  37.4 2.3 %collective-permute-done.6.refs_6_ = bf16[48,8,128]{2,1,0:T(8,128)(2,1)S(1)} collective-permute-done((bf16[48,8,128]{2,1,0:T(8,128)(2,1)S(1)}, bf16[48,8,128]{2,1,0:T(8,128)(2,1)S(1)}, u32[]{:S(2)}, u32[]{:S(2)}) %collective-permute-start.6) | collective-permute-done | bytes 98336 | tf_op jit(solution)/shard_map/ppermute | solution.py:168
  39.7 4.5 %apply1.1 = (f32[64,8,128]{2,1,0:T(8,128)S(1)}, bf16[64,8,128]{2,1,0:T(8,128)(2,1)S(1)}, bf16[48,8,128]{2,1,0:T(8,128)(2,1)S(1)}, bf16[48,8,128]{2,1,0:T(8,128)(...) custom-call(s32[512]{0:T(512)S(1)} %pad_add_fusion.meta.refs_0_, ...), custom_call_target="tpu_custom_call" | custom-call | tf_op jit(solution)/shard_map/apply1/pallas_call | solution.py:223
  45.2 3.3 %collective-permute-start.9 = (bf16[48,8,128]{2,1,0:T(8,128)(2,1)S(1)}, bf16[48,8,128]{2,1,0:T(8,128)(2,1)S(1)}, u32[]{:S(2)}, u32[]{:S(2)}) collective-permute-start(bf16[48,8,128]{2,1,0:T(8,128)(2,1)S(1)} %get-tuple-element.58), channel_id=1, source_target_pairs={{0,15},{1,0},{2,1},{3,2},{4,3},{5,4},{6,5},{7,6},{8,7},{9,8},{10,9... | collective-permute-start | bytes 294920 | tf_op jit(solution)/shard_map/ppermute | solution.py:168
  48.5 2.6 %collective-permute-done.8.from_down.refs_4_ = bf16[48,8,128]{2,1,0:T(8,128)(2,1)S(1)} collective-permute-done((bf16[48,8,128]{2,1,0:T(8,128)(2,1)S(1)}, bf16[48,8,128]{2,1,0:T(8,128)(2,1)S(1)}, u32[]{:S(2)}, u32[]{:S(2)}) %collective-permute-start.8) | collective-permute-done | bytes 98336 | tf_op jit(solution)/shard_map/ppermute | solution.py:168
  51.1 2.9 %collective-permute-start.11 = (bf16[48,8,128]{2,1,0:T(8,128)(2,1)S(1)}, bf16[48,8,128]{2,1,0:T(8,128)(2,1)S(1)}, u32[]{:S(2)}, u32[]{:S(2)}) collective-permute-start(bf16[48,8,128]{2,1,0:T(8,128)(2,1)S(1)} %get-tuple-element.62), channel_id=1, source_target_pairs={{0,240},{16,0},{32,16},{48,32},{64,48},{80,64},{96,80},{112,96},{1... | collective-permute-start | bytes 294920 | tf_op jit(solution)/shard_map/ppermute | solution.py:168
  54.0 2.3 %collective-permute-done.10.refs_6_ = bf16[48,8,128]{2,1,0:T(8,128)(2,1)S(1)} collective-permute-done((bf16[48,8,128]{2,1,0:T(8,128)(2,1)S(1)}, bf16[48,8,128]{2,1,0:T(8,128)(2,1)S(1)}, u32[]{:S(2)}, u32[]{:S(2)}) %collective-permute-start.10) | collective-permute-done | bytes 98336 | tf_op jit(solution)/shard_map/ppermute | solution.py:168
  56.3 4.5 %apply2.1 = (f32[64,8,128]{2,1,0:T(8,128)S(1)}, bf16[64,8,128]{2,1,0:T(8,128)(2,1)S(1)}, bf16[48,8,128]{2,1,0:T(8,128)(2,1)S(1)}, bf16[48,8,128]{2,1,0:T(8,128)(...) custom-call(s32[512]{0:T(512)S(1)} %pad_add_fusion.meta.refs_0_, ...), custom_call_target="tpu_custom_call" | custom-call | tf_op jit(solution)/shard_map/apply2/pallas_call | solution.py:223
  62.0 3.2 %collective-permute-start.13 = (bf16[48,8,128]{2,1,0:T(8,128)(2,1)S(1)}, bf16[48,8,128]{2,1,0:T(8,128)(2,1)S(1)}, u32[]{:S(2)}, u32[]{:S(2)}) collective-permute-start(bf16[48,8,128]{2,1,0:T(8,128)(2,1)S(1)} %get-tuple-element.67), channel_id=1, source_target_pairs={{0,15},{1,0},{2,1},{3,2},{4,3},{5,4},{6,5},{7,6},{8,7},{9,8},{10,9... | collective-permute-start | bytes 294920 | tf_op jit(solution)/shard_map/ppermute | solution.py:168
  65.1 2.5 %collective-permute-done.12.from_down.refs_4_ = bf16[48,8,128]{2,1,0:T(8,128)(2,1)S(1)} collective-permute-done((bf16[48,8,128]{2,1,0:T(8,128)(2,1)S(1)}, bf16[48,8,128]{2,1,0:T(8,128)(2,1)S(1)}, u32[]{:S(2)}, u32[]{:S(2)}) %collective-permute-start.12) | collective-permute-done | bytes 98336 | tf_op jit(solution)/shard_map/ppermute | solution.py:168
  67.7 2.9 %collective-permute-start.15 = (bf16[48,8,128]{2,1,0:T(8,128)(2,1)S(1)}, bf16[48,8,128]{2,1,0:T(8,128)(2,1)S(1)}, u32[]{:S(2)}, u32[]{:S(2)}) collective-permute-start(bf16[48,8,128]{2,1,0:T(8,128)(2,1)S(1)} %get-tuple-element.71), channel_id=1, source_target_pairs={{0,240},{16,0},{32,16},{48,32},{64,48},{80,64},{96,80},{112,96},{1... | collective-permute-start | bytes 294920 | tf_op jit(solution)/shard_map/ppermute | solution.py:168
  70.6 2.3 %collective-permute-done.14.refs_6_ = bf16[48,8,128]{2,1,0:T(8,128)(2,1)S(1)} collective-permute-done((bf16[48,8,128]{2,1,0:T(8,128)(2,1)S(1)}, bf16[48,8,128]{2,1,0:T(8,128)(2,1)S(1)}, u32[]{:S(2)}, u32[]{:S(2)}) %collective-permute-start.14) | collective-permute-done | bytes 98336 | tf_op jit(solution)/shard_map/ppermute | solution.py:168
  72.9 4.4 %apply3.1 = (f32[64,8,128]{2,1,0:T(8,128)S(1)}, f32[8,128]{1,0:T(8,128)S(1)}) custom-call(s32[512]{0:T(512)S(1)} %pad_add_fusion.meta.refs_0_, bf16[64,128,128]{2,1,0:T(8,128)(2,1)S(1)} %copy-done.2, bf16[64,4,128,128]{3,2,1,0:T(8,128)(2,1)S(1)} %copy-done.1, bf16[64,8,128]{2,1,0:T(8,128)(2,1)S(1)} %get-tuple-element.65.refs_3_, ...), custom_call_target="tpu_custom_call" | custom-call | tf_op jit(solution)/shard_map/apply3/pallas_call | solution.py:223
  77.5 1.7 %collective-permute-start.16 = (f32[8,128]{1,0:T(8,128)S(1)}, f32[8,128]{1,0:T(8,128)S(1)}, u32[]{:S(2)}, u32[]{:S(2)}) collective-permute-start(f32[8,128]{1,0:T(8,128)S(1)} %get-tuple-element.74), channel_id=1, source_target_pairs={{0,16},{16,0},{32,48},{48,32},{64,80},{80,64},{96,112},{112,96},{1... | collective-permute-start | bytes 12296 | tf_op jit(solution)/shard_map/ppermute | solution.py:175
  81.1 4.4 %collective-permute-start.21 = (f32[8,128]{1,0:T(8,128)S(1)}, f32[8,128]{1,0:T(8,128)S(1)}, u32[]{:S(2)}, u32[]{:S(2)}) collective-permute-start(f32[8,128]{1,0:T(8,128)S(1)} %add_add_fusion.3), channel_id=1, source_target_pairs={{0,192},{16,208},{32,224},{48,240},{64,128},{80,144},{96,160},{112... | collective-permute-start | bytes 12296 | tf_op jit(solution)/shard_map/ppermute | solution.py:175
  85.5 6.3 %collective-permute-start.20 = (f32[8,128]{1,0:T(8,128)S(1)}, f32[8,128]{1,0:T(8,128)S(1)}, u32[]{:S(2)}, u32[]{:S(2)}) collective-permute-start(f32[8,128]{1,0:T(8,128)S(1)} %add_add_fusion.3), channel_id=1, source_target_pairs={{0,128},{16,144},{32,160},{48,176},{64,192},{80,208},{96,224},{112... | collective-permute-start | bytes 12296 | tf_op jit(solution)/shard_map/ppermute | solution.py:175
  93.4 2.9 %collective-permute-done.19 = f32[8,128]{1,0:T(8,128)S(1)} collective-permute-done((f32[8,128]{1,0:T(8,128)S(1)}, f32[8,128]{1,0:T(8,128)S(1)}, u32[]{:S(2)}, u32[]{:S(2)}) %collective-permute-start.19) | collective-permute-done | bytes 4128 | tf_op jit(solution)/shard_map/ppermute | solution.py:175
  96.3 3.9 %collective-permute-start.24 = (f32[8,128]{1,0:T(8,128)S(1)}, f32[8,128]{1,0:T(8,128)S(1)}, u32[]{:S(2)}, u32[]{:S(2)}) collective-permute-start(f32[8,128]{1,0:T(8,128)S(1)} %add_add_fusion.2), channel_id=1, source_target_pairs={{0,3},{1,2},{2,1},{3,0},{4,7},{5,6},{6,5},{7,4},{8,11},{9,10},{10,... | collective-permute-start | bytes 12296 | tf_op jit(solution)/shard_map/ppermute | solution.py:175
  101.8 3.5 %collective-permute-done.23 = f32[8,128]{1,0:T(8,128)S(1)} collective-permute-done((f32[8,128]{1,0:T(8,128)S(1)}, f32[8,128]{1,0:T(8,128)S(1)}, u32[]{:S(2)}, u32[]{:S(2)}) %collective-permute-start.23) | collective-permute-done | bytes 4128 | tf_op jit(solution)/shard_map/ppermute | solution.py:175
  106.3 6.6 %collective-permute-start.26 = (f32[8,128]{1,0:T(8,128)S(1)}, f32[8,128]{1,0:T(8,128)S(1)}, u32[]{:S(2)}, u32[]{:S(2)}) collective-permute-start(f32[8,128]{1,0:T(8,128)S(1)} %add_add_fusion.1), channel_id=1, source_target_pairs={{0,8},{1,9},{2,10},{3,11},{4,12},{5,13},{6,14},{7,15},{8,0},{9,1},... | collective-permute-start | bytes 12296 | tf_op jit(solution)/shard_map/ppermute | solution.py:175
  112.9 1.6 %collective-permute-done.26 = f32[8,128]{1,0:T(8,128)S(1)} collective-permute-done((f32[8,128]{1,0:T(8,128)S(1)}, f32[8,128]{1,0:T(8,128)S(1)}, u32[]{:S(2)}, u32[]{:S(2)}) %collective-permute-start.26) | collective-permute-done | bytes 4128 | tf_op jit(solution)/shard_map/ppermute | solution.py:175
  114.5 2.0 %collective-permute-done.25 = f32[8,128]{1,0:T(8,128)S(1)} collective-permute-done((f32[8,128]{1,0:T(8,128)S(1)}, f32[8,128]{1,0:T(8,128)S(1)}, u32[]{:S(2)}, u32[]{:S(2)}) %collective-permute-start.25) | collective-permute-done | bytes 4128 | tf_op jit(solution)/shard_map/ppermute | solution.py:175
  (51 shorter events, 13.8 us)
Async XLA Ops:
  2.9 1.0 copy-start.3
  4.7 6.8 %collective-permute-start = (bf16[48,8,128]{2,1,0:T(8,128)(2,1)S(1)}, bf16[48,8,128]{2,1,0:T(8,128)(2,1)S(1)}, u32[]{:S(2)}, u32[]{:S(2)}) collective-permute-start(bf16[48,8,128]{2,1,0:T(8,128)(2,1)S(1)} %get-tuple-element.40), channel_id=1, source_target_pairs={{0,1},{1,2},{2,3},{3,4},{4,5},{5,6},{6,7},{7,8},{8,9},{9,10},{10,1... | collective-permute-start | bytes 294920 | tf_op jit(solution)/shard_map/ppermute | solution.py:168
  6.3 5.2 %collective-permute-start.1 = (bf16[48,8,128]{2,1,0:T(8,128)(2,1)S(1)}, bf16[48,8,128]{2,1,0:T(8,128)(2,1)S(1)}, u32[]{:S(2)}, u32[]{:S(2)}) collective-permute-start(bf16[48,8,128]{2,1,0:T(8,128)(2,1)S(1)} %get-tuple-element.41), channel_id=1, source_target_pairs={{0,15},{1,0},{2,1},{3,2},{4,3},{5,4},{6,5},{7,6},{8,7},{9,8},{10,9... | collective-permute-start | bytes 294920 | tf_op jit(solution)/shard_map/ppermute | solution.py:168
  11.5 6.5 %collective-permute-start.2 = (bf16[48,8,128]{2,1,0:T(8,128)(2,1)S(1)}, bf16[48,8,128]{2,1,0:T(8,128)(2,1)S(1)}, u32[]{:S(2)}, u32[]{:S(2)}) collective-permute-start(bf16[48,8,128]{2,1,0:T(8,128)(2,1)S(1)} %get-tuple-element.44), channel_id=1, source_target_pairs={{0,16},{16,32},{32,48},{48,64},{64,80},{80,96},{96,112},{112,128},... | collective-permute-start | bytes 294920 | tf_op jit(solution)/shard_map/ppermute | solution.py:168
  11.5 6.4 %collective-permute-start.3 = (bf16[48,8,128]{2,1,0:T(8,128)(2,1)S(1)}, bf16[48,8,128]{2,1,0:T(8,128)(2,1)S(1)}, u32[]{:S(2)}, u32[]{:S(2)}) collective-permute-start(bf16[48,8,128]{2,1,0:T(8,128)(2,1)S(1)} %get-tuple-element.45), channel_id=1, source_target_pairs={{0,240},{16,0},{32,16},{48,32},{64,48},{80,64},{96,80},{112,96},{1... | collective-permute-start | bytes 294920 | tf_op jit(solution)/shard_map/ppermute | solution.py:168
  18.0 3.4 %copy-start = (bf16[64,4,128,128]{3,2,1,0:T(8,128)(2,1)S(1)}, bf16[64,4,128,128]{3,2,1,0:T(8,128)(2,1)}, u32[]{:S(2)}) copy-start(bf16[64,4,128,128]{3,2,1,0:T(8,128)(2,1)} %refs_2_.7) | copy-start | bytes 25165828
  21.3 1.6 %copy-start.2 = (bf16[64,128,128]{2,1,0:T(8,128)(2,1)S(1)}, bf16[64,128,128]{2,1,0:T(8,128)(2,1)}, u32[]{:S(2)}) copy-start(bf16[64,128,128]{2,1,0:T(8,128)(2,1)} %refs_1_.7) | copy-start | bytes 6291460
  22.9 16.8 %copy-start.1 = (bf16[64,4,128,128]{3,2,1,0:T(8,128)(2,1)S(1)}, bf16[64,4,128,128]{3,2,1,0:T(8,128)(2,1)}, u32[]{:S(2)}) copy-start(bf16[64,4,128,128]{3,2,1,0:T(8,128)(2,1)} %refs_2_.7) | copy-start | bytes 25165828
  27.4 7.0 %collective-permute-start.4 = (bf16[48,8,128]{2,1,0:T(8,128)(2,1)S(1)}, bf16[48,8,128]{2,1,0:T(8,128)(2,1)S(1)}, u32[]{:S(2)}, u32[]{:S(2)}) collective-permute-start(bf16[48,8,128]{2,1,0:T(8,128)(2,1)S(1)} %get-tuple-element.48), channel_id=1, source_target_pairs={{0,1},{1,2},{2,3},{3,4},{4,5},{5,6},{6,7},{7,8},{8,9},{9,10},{10,1... | collective-permute-start | bytes 294920 | tf_op jit(solution)/shard_map/ppermute | solution.py:168
  28.4 6.0 %collective-permute-start.5 = (bf16[48,8,128]{2,1,0:T(8,128)(2,1)S(1)}, bf16[48,8,128]{2,1,0:T(8,128)(2,1)S(1)}, u32[]{:S(2)}, u32[]{:S(2)}) collective-permute-start(bf16[48,8,128]{2,1,0:T(8,128)(2,1)S(1)} %get-tuple-element.49), channel_id=1, source_target_pairs={{0,15},{1,0},{2,1},{3,2},{4,3},{5,4},{6,5},{7,6},{8,7},{9,8},{10,9... | collective-permute-start | bytes 294920 | tf_op jit(solution)/shard_map/ppermute | solution.py:168
  34.5 5.3 %collective-permute-start.6 = (bf16[48,8,128]{2,1,0:T(8,128)(2,1)S(1)}, bf16[48,8,128]{2,1,0:T(8,128)(2,1)S(1)}, u32[]{:S(2)}, u32[]{:S(2)}) collective-permute-start(bf16[48,8,128]{2,1,0:T(8,128)(2,1)S(1)} %get-tuple-element.52), channel_id=1, source_target_pairs={{0,16},{16,32},{32,48},{48,64},{64,80},{80,96},{96,112},{112,128},... | collective-permute-start | bytes 294920 | tf_op jit(solution)/shard_map/ppermute | solution.py:168
  34.5 5.2 %collective-permute-start.7 = (bf16[48,8,128]{2,1,0:T(8,128)(2,1)S(1)}, bf16[48,8,128]{2,1,0:T(8,128)(2,1)S(1)}, u32[]{:S(2)}, u32[]{:S(2)}) collective-permute-start(bf16[48,8,128]{2,1,0:T(8,128)(2,1)S(1)} %get-tuple-element.53), channel_id=1, source_target_pairs={{0,240},{16,0},{32,16},{48,32},{64,48},{80,64},{96,80},{112,96},{1... | collective-permute-start | bytes 294920 | tf_op jit(solution)/shard_map/ppermute | solution.py:168
  44.2 6.8 %collective-permute-start.8 = (bf16[48,8,128]{2,1,0:T(8,128)(2,1)S(1)}, bf16[48,8,128]{2,1,0:T(8,128)(2,1)S(1)}, u32[]{:S(2)}, u32[]{:S(2)}) collective-permute-start(bf16[48,8,128]{2,1,0:T(8,128)(2,1)S(1)} %get-tuple-element.57), channel_id=1, source_target_pairs={{0,1},{1,2},{2,3},{3,4},{4,5},{5,6},{6,7},{7,8},{8,9},{9,10},{10,1... | collective-permute-start | bytes 294920 | tf_op jit(solution)/shard_map/ppermute | solution.py:168
  45.2 5.9 %collective-permute-start.9 = (bf16[48,8,128]{2,1,0:T(8,128)(2,1)S(1)}, bf16[48,8,128]{2,1,0:T(8,128)(2,1)S(1)}, u32[]{:S(2)}, u32[]{:S(2)}) collective-permute-start(bf16[48,8,128]{2,1,0:T(8,128)(2,1)S(1)} %get-tuple-element.58), channel_id=1, source_target_pairs={{0,15},{1,0},{2,1},{3,2},{4,3},{5,4},{6,5},{7,6},{8,7},{9,8},{10,9... | collective-permute-start | bytes 294920 | tf_op jit(solution)/shard_map/ppermute | solution.py:168
  51.1 5.3 %collective-permute-start.10 = (bf16[48,8,128]{2,1,0:T(8,128)(2,1)S(1)}, bf16[48,8,128]{2,1,0:T(8,128)(2,1)S(1)}, u32[]{:S(2)}, u32[]{:S(2)}) collective-permute-start(bf16[48,8,128]{2,1,0:T(8,128)(2,1)S(1)} %get-tuple-element.61), channel_id=1, source_target_pairs={{0,16},{16,32},{32,48},{48,64},{64,80},{80,96},{96,112},{112,128},... | collective-permute-start | bytes 294920 | tf_op jit(solution)/shard_map/ppermute | solution.py:168
  51.1 5.2 %collective-permute-start.11 = (bf16[48,8,128]{2,1,0:T(8,128)(2,1)S(1)}, bf16[48,8,128]{2,1,0:T(8,128)(2,1)S(1)}, u32[]{:S(2)}, u32[]{:S(2)}) collective-permute-start(bf16[48,8,128]{2,1,0:T(8,128)(2,1)S(1)} %get-tuple-element.62), channel_id=1, source_target_pairs={{0,240},{16,0},{32,16},{48,32},{64,48},{80,64},{96,80},{112,96},{1... | collective-permute-start | bytes 294920 | tf_op jit(solution)/shard_map/ppermute | solution.py:168
  60.8 6.8 %collective-permute-start.12 = (bf16[48,8,128]{2,1,0:T(8,128)(2,1)S(1)}, bf16[48,8,128]{2,1,0:T(8,128)(2,1)S(1)}, u32[]{:S(2)}, u32[]{:S(2)}) collective-permute-start(bf16[48,8,128]{2,1,0:T(8,128)(2,1)S(1)} %get-tuple-element.66), channel_id=1, source_target_pairs={{0,1},{1,2},{2,3},{3,4},{4,5},{5,6},{6,7},{7,8},{8,9},{9,10},{10,1... | collective-permute-start | bytes 294920 | tf_op jit(solution)/shard_map/ppermute | solution.py:168
  62.0 5.7 %collective-permute-start.13 = (bf16[48,8,128]{2,1,0:T(8,128)(2,1)S(1)}, bf16[48,8,128]{2,1,0:T(8,128)(2,1)S(1)}, u32[]{:S(2)}, u32[]{:S(2)}) collective-permute-start(bf16[48,8,128]{2,1,0:T(8,128)(2,1)S(1)} %get-tuple-element.67), channel_id=1, source_target_pairs={{0,15},{1,0},{2,1},{3,2},{4,3},{5,4},{6,5},{7,6},{8,7},{9,8},{10,9... | collective-permute-start | bytes 294920 | tf_op jit(solution)/shard_map/ppermute | solution.py:168
  67.7 5.3 %collective-permute-start.14 = (bf16[48,8,128]{2,1,0:T(8,128)(2,1)S(1)}, bf16[48,8,128]{2,1,0:T(8,128)(2,1)S(1)}, u32[]{:S(2)}, u32[]{:S(2)}) collective-permute-start(bf16[48,8,128]{2,1,0:T(8,128)(2,1)S(1)} %get-tuple-element.70), channel_id=1, source_target_pairs={{0,16},{16,32},{32,48},{48,64},{64,80},{80,96},{96,112},{112,128},... | collective-permute-start | bytes 294920 | tf_op jit(solution)/shard_map/ppermute | solution.py:168
  67.7 5.2 %collective-permute-start.15 = (bf16[48,8,128]{2,1,0:T(8,128)(2,1)S(1)}, bf16[48,8,128]{2,1,0:T(8,128)(2,1)S(1)}, u32[]{:S(2)}, u32[]{:S(2)}) collective-permute-start(bf16[48,8,128]{2,1,0:T(8,128)(2,1)S(1)} %get-tuple-element.71), channel_id=1, source_target_pairs={{0,240},{16,0},{32,16},{48,32},{64,48},{80,64},{96,80},{112,96},{1... | collective-permute-start | bytes 294920 | tf_op jit(solution)/shard_map/ppermute | solution.py:168
  77.4 3.1 %collective-permute-start.18 = (f32[8,128]{1,0:T(8,128)S(1)}, f32[8,128]{1,0:T(8,128)S(1)}, u32[]{:S(2)}, u32[]{:S(2)}) collective-permute-start(f32[8,128]{1,0:T(8,128)S(1)} %get-tuple-element.74), channel_id=1, source_target_pairs={{0,48},{16,32},{32,16},{48,0},{64,112},{80,96},{96,80},{112,64},{1... | collective-permute-start | bytes 12296 | tf_op jit(solution)/shard_map/ppermute | solution.py:175
  77.4 3.7 %collective-permute-start.17 = (f32[8,128]{1,0:T(8,128)S(1)}, f32[8,128]{1,0:T(8,128)S(1)}, u32[]{:S(2)}, u32[]{:S(2)}) collective-permute-start(f32[8,128]{1,0:T(8,128)S(1)} %get-tuple-element.74), channel_id=1, source_target_pairs={{0,32},{16,48},{32,0},{48,16},{64,96},{80,112},{96,64},{112,80},{1... | collective-permute-start | bytes 12296 | tf_op jit(solution)/shard_map/ppermute | solution.py:175
  77.5 3.6 %collective-permute-start.16 = (f32[8,128]{1,0:T(8,128)S(1)}, f32[8,128]{1,0:T(8,128)S(1)}, u32[]{:S(2)}, u32[]{:S(2)}) collective-permute-start(f32[8,128]{1,0:T(8,128)S(1)} %get-tuple-element.74), channel_id=1, source_target_pairs={{0,16},{16,0},{32,48},{48,32},{64,80},{80,64},{96,112},{112,96},{1... | collective-permute-start | bytes 12296 | tf_op jit(solution)/shard_map/ppermute | solution.py:175
  81.1 10.7 %collective-permute-start.21 = (f32[8,128]{1,0:T(8,128)S(1)}, f32[8,128]{1,0:T(8,128)S(1)}, u32[]{:S(2)}, u32[]{:S(2)}) collective-permute-start(f32[8,128]{1,0:T(8,128)S(1)} %add_add_fusion.3), channel_id=1, source_target_pairs={{0,192},{16,208},{32,224},{48,240},{64,128},{80,144},{96,160},{112... | collective-permute-start | bytes 12296 | tf_op jit(solution)/shard_map/ppermute | solution.py:175
  85.5 7.9 %collective-permute-start.20 = (f32[8,128]{1,0:T(8,128)S(1)}, f32[8,128]{1,0:T(8,128)S(1)}, u32[]{:S(2)}, u32[]{:S(2)}) collective-permute-start(f32[8,128]{1,0:T(8,128)S(1)} %add_add_fusion.3), channel_id=1, source_target_pairs={{0,128},{16,144},{32,160},{48,176},{64,192},{80,208},{96,224},{112... | collective-permute-start | bytes 12296 | tf_op jit(solution)/shard_map/ppermute | solution.py:175
  91.8 4.5 %collective-permute-start.19 = (f32[8,128]{1,0:T(8,128)S(1)}, f32[8,128]{1,0:T(8,128)S(1)}, u32[]{:S(2)}, u32[]{:S(2)}) collective-permute-start(f32[8,128]{1,0:T(8,128)S(1)} %add_add_fusion.3), channel_id=1, source_target_pairs={{0,64},{16,80},{32,96},{48,112},{64,0},{80,16},{96,32},{112,48},{1... | collective-permute-start | bytes 12296 | tf_op jit(solution)/shard_map/ppermute | solution.py:175
  96.3 5.5 %collective-permute-start.24 = (f32[8,128]{1,0:T(8,128)S(1)}, f32[8,128]{1,0:T(8,128)S(1)}, u32[]{:S(2)}, u32[]{:S(2)}) collective-permute-start(f32[8,128]{1,0:T(8,128)S(1)} %add_add_fusion.2), channel_id=1, source_target_pairs={{0,3},{1,2},{2,1},{3,0},{4,7},{5,6},{6,5},{7,4},{8,11},{9,10},{10,... | collective-permute-start | bytes 12296 | tf_op jit(solution)/shard_map/ppermute | solution.py:175
  100.3 5.1 %collective-permute-start.23 = (f32[8,128]{1,0:T(8,128)S(1)}, f32[8,128]{1,0:T(8,128)S(1)}, u32[]{:S(2)}, u32[]{:S(2)}) collective-permute-start(f32[8,128]{1,0:T(8,128)S(1)} %add_add_fusion.2), channel_id=1, source_target_pairs={{0,2},{1,3},{2,0},{3,1},{4,6},{5,7},{6,4},{7,5},{8,10},{9,11},{10,... | collective-permute-start | bytes 12296 | tf_op jit(solution)/shard_map/ppermute | solution.py:175
  100.3 5.1 %collective-permute-start.22 = (f32[8,128]{1,0:T(8,128)S(1)}, f32[8,128]{1,0:T(8,128)S(1)}, u32[]{:S(2)}, u32[]{:S(2)}) collective-permute-start(f32[8,128]{1,0:T(8,128)S(1)} %add_add_fusion.2), channel_id=1, source_target_pairs={{0,1},{1,0},{2,3},{3,2},{4,5},{5,4},{6,7},{7,6},{8,9},{9,8},{10,11... | collective-permute-start | bytes 12296 | tf_op jit(solution)/shard_map/ppermute | solution.py:175
  105.4 7.5 %collective-permute-start.27 = (f32[8,128]{1,0:T(8,128)S(1)}, f32[8,128]{1,0:T(8,128)S(1)}, u32[]{:S(2)}, u32[]{:S(2)}) collective-permute-start(f32[8,128]{1,0:T(8,128)S(1)} %add_add_fusion.1), channel_id=1, source_target_pairs={{0,12},{1,13},{2,14},{3,15},{4,8},{5,9},{6,10},{7,11},{8,4},{9,5},... | collective-permute-start | bytes 12296 | tf_op jit(solution)/shard_map/ppermute | solution.py:175
  106.3 8.2 %collective-permute-start.26 = (f32[8,128]{1,0:T(8,128)S(1)}, f32[8,128]{1,0:T(8,128)S(1)}, u32[]{:S(2)}, u32[]{:S(2)}) collective-permute-start(f32[8,128]{1,0:T(8,128)S(1)} %add_add_fusion.1), channel_id=1, source_target_pairs={{0,8},{1,9},{2,10},{3,11},{4,12},{5,13},{6,14},{7,15},{8,0},{9,1},... | collective-permute-start | bytes 12296 | tf_op jit(solution)/shard_map/ppermute | solution.py:175
  112.9 3.6 %collective-permute-start.25 = (f32[8,128]{1,0:T(8,128)S(1)}, f32[8,128]{1,0:T(8,128)S(1)}, u32[]{:S(2)}, u32[]{:S(2)}) collective-permute-start(f32[8,128]{1,0:T(8,128)S(1)} %add_add_fusion.1), channel_id=1, source_target_pairs={{0,4},{1,5},{2,6},{3,7},{4,0},{5,1},{6,2},{7,3},{8,12},{9,13},{10,... | collective-permute-start | bytes 12296 | tf_op jit(solution)/shard_map/ppermute | solution.py:175

commit v2 on v1

v2 whole, which is shorter than its diff:
```python
import functools

import jax
import jax.numpy as jnp
from jax import lax
from jax.experimental import pallas as pl
from jax.experimental.pallas import tpu as pltpu
from jax.sharding import PartitionSpec as P

POWERS = 4
CAP = 64
SEND = 16
FACES = 4
SIDE = 16
GROUPS = SIDE * SIDE
ROWS = 128
LOOKUP = CAP + 9 * SEND
NOTHING = CAP + 4 * SEND
UNROLL = 16
BLOCKS = FACES + 1
CHUNK = 8
HALF_CAP = CAP // 2
CHUNKS = HALF_CAP // CHUNK

IN_VMEM = pl.BlockSpec(memory_space=pltpu.VMEM)
IN_SMEM = pl.BlockSpec(memory_space=pltpu.SMEM)
ANYWHERE = pl.BlockSpec(memory_space=pl.ANY)
IN_HBM = pl.BlockSpec(memory_space=pltpu.HBM)
UP_DIRECTIONS = (2, 5, 8)
DOWN_DIRECTIONS = (0, 3, 6)
PAIRS = [(a, b) for a in range(5) for b in range(a, 5) if b > 0]
PAIR_LANE = {pair: at for at, pair in enumerate(PAIRS)}
LANES_PER_SIDE = 16


def vector_shape(count, dtype):
    return jax.ShapeDtypeStruct((count, 8, ROWS), dtype)


def params(mebibytes=16):
    return pltpu.CompilerParams(vmem_limit_bytes=mebibytes << 20)


def pack(send_slots, rounded, up, down, next_row, last_row):
    for target, directions in (
        (up, UP_DIRECTIONS),
        (down, DOWN_DIRECTIONS),
        (next_row, (7,)),
        (last_row, (1,)),
    ):
        for at, direction in enumerate(directions):
            for k in range(SEND):
                slot = jnp.maximum(send_slots[direction, 0, k], 0)
                target[at * SEND + k] = rounded[slot]


def start_kernel(
    send_slots, counts, right_sides, basis, rounded, up, down, next_row, last_row
):
    element = lax.broadcasted_iota(jnp.int32, basis.shape, 0)
    live = jnp.where(element < counts[0], right_sides[...], 0.0)
    basis[...] = live
    rounded[...] = live.astype(jnp.bfloat16)
    pack(send_slots, rounded, up, down, next_row, last_row)


def make_plan(neighbours, order):
    local = jnp.int32(0)
    for e in range(CAP):
        farthest = neighbours[0, e]
        for f in range(1, FACES):
            farthest = jnp.maximum(farthest, neighbours[f, e])
        ghost = farthest >= CAP
        order[jnp.where(ghost, CAP - 1 - (e - local), local)] = e
        local = local + jnp.where(ghost, 0, 1)
    order[CAP] = local // UNROLL


def transpose_blocks(base, diag, face, turned, diag_here, face_here, arrived, extra):
    def fetch(c):
        here = pl.ds(c * CHUNK, CHUNK)
        there = pl.ds(base + c * CHUNK, CHUNK)
        return (
            pltpu.make_async_copy(diag.at[there], diag_here.at[here], arrived.at[c, 0]),
            pltpu.make_async_copy(face.at[there], face_here.at[here], arrived.at[c, 1]),
        )

    for c in range(CHUNKS):
        for copy in fetch(c):
            copy.start()
    extra()
    for c in range(CHUNKS):
        for copy in fetch(c):
            copy.wait()

        def element(at, carry, c=c):
            e = c * CHUNK + at
            turned[base + e, 0:ROWS] = diag_here[e].T
            for f in range(FACES):
                turned[base + e, (f + 1) * ROWS : (f + 2) * ROWS] = face_here[e, f].T
            return carry

        lax.fori_loop(0, CHUNK, element, 0, unroll=4)


def first_half_kernel(
    neighbours, diag, face, turned, order, diag_here, face_here, arrived
):
    transpose_blocks(
        0, diag, face, turned, diag_here, face_here, arrived,
        lambda: make_plan(neighbours, order),
    )


def second_half_kernel(diag, face, before, turned, diag_here, face_here, arrived):
    transpose_blocks(
        HALF_CAP, diag, face, turned, diag_here, face_here, arrived, lambda: None
    )


def relay_kernel(*refs):
    from_down, from_up, next_row, last_row = refs[:4]
    send_next, send_last = refs[-2:]
    send_next[0:SEND] = from_up[2 * SEND : 3 * SEND]
    send_next[SEND : 2 * SEND] = next_row[...]
    send_next[2 * SEND : 3 * SEND] = from_down[2 * SEND : 3 * SEND]
    send_last[0:SEND] = from_up[0:SEND]
    send_last[SEND : 2 * SEND] = last_row[...]
    send_last[2 * SEND : 3 * SEND] = from_down[0:SEND]


def fill_local(lookup, rounded):
    lookup[0:CAP] = rounded[...]
    lookup[NOTHING : NOTHING + SEND] = jnp.zeros((SEND, 8, ROWS), jnp.bfloat16)


def fill_ghosts(lookup, from_down, from_up, from_last, from_next):
    lookup[CAP : CAP + 3 * SEND] = from_next[...]
    lookup[CAP + 3 * SEND : CAP + 4 * SEND] = from_up[SEND : 2 * SEND]
    lookup[CAP + 5 * SEND : CAP + 6 * SEND] = from_down[SEND : 2 * SEND]
    lookup[CAP + 6 * SEND : CAP + 9 * SEND] = from_last[...]


def apply_runs(
    first, limit, order, neighbours, turned, lookup, basis, image, image_rounded
):
    def element(e, sums):
        near = [lookup[e]]
        for f in range(FACES):
            at = neighbours[f, e]
            near.append(lookup[jnp.where(at < 0, NOTHING, at)])
        out = jnp.dot(
            jnp.concatenate(near, axis=1),
            turned[e],
            preferred_element_type=jnp.float32,
        )
        image[e] = out
        if image_rounded is not None:
            image_rounded[e] = out.astype(jnp.bfloat16)
        others = [ref[e] for ref in basis] + [out]
        return tuple(s + out * other for s, other in zip(sums, others))

    def run(step, sums):
        for u in range(UNROLL):
            at = step * UNROLL + u
            sums = element(at if order is None else order[at], sums)
        return sums

    zero = jnp.zeros((8, ROWS), jnp.float32)
    return lax.fori_loop(first, limit, run, (zero,) * (len(basis) + 1))


def with_sums(gram, sums):
    lane = lax.broadcasted_iota(jnp.int32, (8, ROWS), 1)
    newest = len(sums) - 1
    for a, s in enumerate(sums):
        total = jnp.sum(s, axis=1, keepdims=True)
        gram = gram + jnp.where(lane == PAIR_LANE[a, newest], total, 0.0)
    return gram


def whole_kernel(
    neighbours, send_slots, turned, rounded, from_down, from_up, from_last, from_next,
    b0, image, image_rounded, up, down, next_row, last_row, gram_out, lookup,
):
    fill_local(lookup, rounded)
    fill_ghosts(lookup, from_down, from_up, from_last, from_next)
    sums = apply_runs(
        0, CAP // UNROLL, None, neighbours, turned, lookup, (b0,), image, image_rounded
    )
    pack(send_slots, image_rounded, up, down, next_row, last_row)
    gram_out[...] = with_sums(jnp.zeros((8, ROWS), jnp.float32), sums)


def local_kernel(power, *refs):
    neighbours, order, turned, rounded, gram_in = refs[:5]
    basis = refs[5 : 6 + power]
    image, image_rounded, gram_out, lookup = refs[6 + power :]
    fill_local(lookup, rounded)
    sums = apply_runs(
        0, order[CAP], order, neighbours, turned, lookup, basis, image, image_rounded
    )
    gram_out[...] = with_sums(gram_in[...], sums)


def ghost_kernel(power, *refs):
    neighbours, order, send_slots, turned, rounded = refs[:5]
    received = refs[5:9]
    gram_in = refs[9]
    basis = refs[10 : 11 + power]
    refs = refs[13 + power :]
    last = power == POWERS - 1
    if last:
        image, image_rounded, gram_out, lookup = refs
    else:
        image, image_rounded, up, down, next_row, last_row, gram_out, lookup = refs
    fill_local(lookup, rounded)
    fill_ghosts(lookup, *received)
    sums = apply_runs(
        order[CAP], CAP // UNROLL, order, neighbours, turned, lookup, basis, image,
        image_rounded,
    )
    if not last:
        pack(send_slots, image_rounded, up, down, next_row, last_row)
    gram = with_sums(gram_in[...], sums)
    if last:
        lane = lax.broadcasted_iota(jnp.int32, (8, ROWS), 1)
        side = lax.broadcasted_iota(jnp.int32, (8, ROWS), 0)
        spread = jnp.zeros((8, ROWS), jnp.float32)
        for at in range(len(PAIRS)):
            value = jnp.broadcast_to(gram[:, at : at + 1], (8, ROWS))
            spread = jnp.where(lane == side * LANES_PER_SIDE + at, value, spread)
        row = jnp.sum(spread, axis=0, keepdims=True)
        gram_out[...] = jnp.broadcast_to(row, gram_out.shape)
    else:
        gram_out[...] = gram


def finish_kernel(gram_rows, b0, b1, b2, b3, b4, solution, residual):
    lane = lax.broadcasted_iota(jnp.int32, (8, ROWS), 1)
    side = lax.broadcasted_iota(jnp.int32, (8, ROWS), 0)
    row = jnp.sum(gram_rows[...], axis=0, keepdims=True)
    spread = jnp.broadcast_to(row, (8, ROWS))

    def entry(a, b):
        at = PAIR_LANE[min(a, b), max(a, b)]
        mine = jnp.where(lane == side * LANES_PER_SIDE + at, spread, 0.0)
        total = jnp.sum(mine, axis=1, keepdims=True)
        return jnp.broadcast_to(total, (8, ROWS))

    factor = {}
    for i in range(POWERS):
        for j in range(i + 1):
            value = entry(i + 1, j + 1)
            for k in range(j):
                value = value - factor[i, k] * factor[j, k]
            factor[i, j] = jnp.sqrt(value) if i == j else value / factor[j, j]
    forward = []
    for i in range(POWERS):
        value = entry(0, i + 1)
        for k in range(i):
            value = value - factor[i, k] * forward[k]
        forward.append(value / factor[i, i])
    weights = [None] * POWERS
    for i in reversed(range(POWERS)):
        value = forward[i]
        for k in range(i + 1, POWERS):
            value = value - factor[k, i] * weights[k]
        weights[i] = value / factor[i, i]
    basis = (b0, b1, b2, b3, b4)

    def several(step, carry):
        for u in range(8):
            e = step * 8 + u
            v = [ref[e] for ref in basis]
            total = weights[0] * v[0]
            moved = weights[0] * v[1]
            for k in range(1, POWERS):
                total = total + weights[k] * v[k]
                moved = moved + weights[k] * v[k + 1]
            solution[e] = total
            residual[e] = v[0] - moved
        return carry

    lax.fori_loop(0, CAP // 8, several, 0)


def shifted(block, axis, distance):
    return lax.ppermute(block, axis, [(i, (i + distance) % SIDE) for i in range(SIDE)])


def per_device(right_sides, diag_blocks, face_blocks, neighbours, send_slots, counts):
    half = jnp.bfloat16
    neighbours = neighbours.T
    send_slots = send_slots.transpose(1, 0, 2)
    in_place = lambda array: pltpu.with_memory_space_constraint(array, pltpu.HBM)
    diag_blocks = in_place(diag_blocks)
    face_blocks = in_place(face_blocks)
    packets = [vector_shape(n * SEND, half) for n in (3, 3, 1, 1)]
    full = vector_shape(CAP, jnp.float32)
    narrow = vector_shape(CAP, half)
    gram_shape = jax.ShapeDtypeStruct((8, ROWS), jnp.float32)
    rows_shape = jax.ShapeDtypeStruct((GROUPS, ROWS), jnp.float32)
    turned_shape = pltpu.VMEM((CAP, BLOCKS * ROWS, ROWS), half)
    lookup = pltpu.VMEM((LOOKUP, 8, ROWS), half)
    landing = [
        pltpu.VMEM((HALF_CAP, ROWS, ROWS), half),
        pltpu.VMEM((HALF_CAP, FACES, ROWS, ROWS), half),
        pltpu.SemaphoreType.DMA((CHUNKS, 2)),
    ]
    first, rounded, up, down, next_row, last_row = pl.pallas_call(
        start_kernel,
        name="start",
        in_specs=[IN_SMEM, IN_SMEM, IN_VMEM],
        out_specs=[IN_VMEM] * 6,
        out_shape=[full, narrow] + packets,
        compiler_params=params(),
    )(in_place(send_slots), counts, in_place(right_sides))
    basis = [first]
    gram = None
    for power in range(POWERS):
        last = power == POWERS - 1
        from_down = shifted(up, "gy", 1)
        from_up = shifted(down, "gy", -1)
        if power == 0:
            turned, order = pl.pallas_call(
                first_half_kernel,
                name="first_half",
                in_specs=[IN_SMEM, IN_HBM, IN_HBM],
                out_specs=[IN_VMEM, IN_SMEM],
                out_shape=[turned_shape, jax.ShapeDtypeStruct((128,), jnp.int32)],
                scratch_shapes=landing,
                compiler_params=params(),
            )(neighbours, diag_blocks, face_blocks)
            after = (order,)
        else:
            after = ()
            image, image_rounded, gram = pl.pallas_call(
                functools.partial(local_kernel, power),
                name=f"local{power}",
                in_specs=[IN_SMEM] * 2 + [IN_VMEM] * (4 + power),
                out_specs=[IN_VMEM] * 3,
                out_shape=[full, narrow, gram_shape],
                scratch_shapes=[lookup],
                compiler_params=params(),
            )(neighbours, order, turned, rounded, gram, *basis)
        send_next, send_last = pl.pallas_call(
            relay_kernel,
            name="relay",
            in_specs=[IN_VMEM] * 4 + [ANYWHERE] * len(after),
            out_specs=[IN_VMEM] * 2,
            out_shape=[vector_shape(3 * SEND, half)] * 2,
            compiler_params=params(),
        )(from_down, from_up, next_row, last_row, *after)
        from_last = shifted(send_next, "gx", 1)
        from_next = shifted(send_last, "gx", -1)
        received = (from_down, from_up, from_last, from_next)
        if power == 0:
            turned = pl.pallas_call(
                second_half_kernel,
                name="second_half",
                in_specs=[IN_HBM, IN_HBM, IN_VMEM],
                out_specs=IN_VMEM,
                out_shape=turned_shape,
                scratch_shapes=landing,
                input_output_aliases={2: 0},
                compiler_params=params(),
            )(diag_blocks, face_blocks, turned)
            outs = pl.pallas_call(
                whole_kernel,
                name="whole",
                in_specs=[IN_SMEM] * 2 + [IN_VMEM] * 7,
                out_specs=[IN_VMEM] * 7,
                out_shape=[full, narrow] + packets + [gram_shape],
                scratch_shapes=[lookup],
                compiler_params=params(),
            )(neighbours, send_slots, turned, rounded, *received, first)
        else:
            shapes = [full, narrow] + ([rows_shape] if last else packets + [gram_shape])
            outs = pl.pallas_call(
                functools.partial(ghost_kernel, power),
                name=f"ghost{power}",
                in_specs=[IN_SMEM] * 3 + [IN_VMEM] * (10 + power),
                out_specs=[IN_VMEM] * len(shapes),
                out_shape=shapes,
                scratch_shapes=[lookup],
                input_output_aliases={11 + power: 0, 12 + power: 1},
                compiler_params=params(),
            )(
                neighbours, order, send_slots, turned, rounded, *received, gram, *basis,
                image, image_rounded,
            )
        basis.append(outs[0])
        rounded = outs[1]
        gram = outs[-1]
        if not last:
            up, down, next_row, last_row = outs[2:-1]
    gathered = lax.all_to_all(gram, ("gx", "gy"), 0, 0, tiled=True)
    return pl.pallas_call(
        finish_kernel,
        name="finish",
        in_specs=[IN_VMEM] * 6,
        out_specs=[IN_VMEM] * 2,
        out_shape=[full] * 2,
        compiler_params=params(),
    )(gathered, *basis)


def solution(mesh):
    in_specs = (
        P(("gx", "gy"), None, None),
        P(("gx", "gy"), None, None),
        P(("gx", "gy"), None, None, None),
        P(("gx", "gy"), None),
        P(("gx", "gy"), None, None),
        P(("gx", "gy")),
    )
    out_specs = (P(("gx", "gy"), None, None), P(("gx", "gy"), None, None))
    return jax.shard_map(
        per_device, mesh=mesh, in_specs=in_specs, out_specs=out_specs, check_vma=False
    )
```

time: 118 us -> 97.7 us (0.83)
  the two profiles are of different devices: /device:TPU:4 before, /device:TPU:1 now
where the time goes in v2:
time: 97.7 us; the launch traced here: 97.6 us
  starting transfers between devices  34.7 us (36%)
  blocking collectives  28.3 us (29%)
  Pallas kernels  23.9 us (24%)
  waiting for transfers between devices  8.54 us (9%)
  between operations  1.43 us (1%)
    ppermute x16, starting transfers between devices, shifted(): lax.ppermute(block, axis, [(i, (i + distance) % SIDE) for i in range(SIDE)])  34.7 us
    all_to_all x1, blocking collectives, per_device(): gathered = lax.all_to_all(gram, ('gx', 'gy'), 0, 0, tiled=True)  28.3 us
    ppermute x16, waiting for transfers between devices, shifted(): lax.ppermute(block, axis, [(i, (i + distance) % SIDE) for i in range(SIDE)])  8.54 us
    pallas_call x3, Pallas kernels, per_device(): pl.pallas_call(functools.partial(ghost_kernel, power), name=f'ghost{power...  5.82 us
    pallas_call x3, Pallas kernels, per_device(): pl.pallas_call(functools.partial(local_kernel, power), name=f'local{power...  5.37 us
    pallas_call x1, Pallas kernels, per_device(): pl.pallas_call(first_half_kernel, name='first_half', in_specs=[IN_SMEM, I...  4.11 us
    pallas_call x1, Pallas kernels, per_device(): pl.pallas_call(second_half_kernel, name='second_half', in_specs=[IN_HBM,...  3.2 us
    pallas_call x1, Pallas kernels, per_device(): pl.pallas_call(whole_kernel, name='whole', in_specs=[IN_SMEM] * 2 + [IN_V...  2.98 us
  transfers between devices with their start and end apart: 16, of which 6 were waited for; matrix products, arithmetic and copies ran while one was open for 0% of the time, Pallas kernels for 13%

profile of v2, /device:TPU:1, one launch (start us, length us, event | category | flops | bytes accessed | tf_op | source)
XLA Modules:
  0.0 97.6 jit_solution(12871706114637010576)
XLA Ops:
  1.3 1.2 %start.1 = (f32[64,8,128]{2,1,0:T(8,128)S(1)}, bf16[64,8,128]{2,1,0:T(8,128)(2,1)S(1)}, bf16[48,8,128]{2,1,0:T(8,128)(2,1)S(1)}, bf16[48,8,128]{2,1,0:T(8,128)(2...) custom-call(s32[9,1,16]{2,1,0:T(1,128)} %bitcast.16, s32[1]{0:T(128)S(6)} %copy.23.counts, ...), custom_call_target="tpu_custom_call" | custom-call | tf_op jit(solution)/shard_map/start/pallas_call | solution.py:311
  2.5 2.2 %collective-permute-start = (bf16[48,8,128]{2,1,0:T(8,128)(2,1)S(1)}, bf16[48,8,128]{2,1,0:T(8,128)(2,1)S(1)}, u32[]{:S(2)}, u32[]{:S(2)}) collective-permute-start(bf16[48,8,128]{2,1,0:T(8,128)(2,1)S(1)} %get-tuple-element.53), channel_id=1, source_target_pairs={{0,1},{1,2},{2,3},{3,4},{4,5},{5,6},{6,7},{7,8},{8,9},{9,10},{10,1... | collective-permute-start | bytes 294920 | tf_op jit(solution)/shard_map/ppermute | solution.py:289
  4.7 3.7 %collective-permute-start.1 = (bf16[48,8,128]{2,1,0:T(8,128)(2,1)S(1)}, bf16[48,8,128]{2,1,0:T(8,128)(2,1)S(1)}, u32[]{:S(2)}, u32[]{:S(2)}) collective-permute-start(bf16[48,8,128]{2,1,0:T(8,128)(2,1)S(1)} %get-tuple-element.54), channel_id=1, source_target_pairs={{0,15},{1,0},{2,1},{3,2},{4,3},{5,4},{6,5},{7,6},{8,7},{9,8},{10,9... | collective-permute-start | bytes 294920 | tf_op jit(solution)/shard_map/ppermute | solution.py:289
  8.4 0.7 copy-done
  9.1 4.1 %first_half.1 = (bf16[64,640,128]{2,1,0:T(8,128)(2,1)S(1)}, s32[128]{0:T(128)S(1)}) custom-call(s32[4,64]{1,0:T(4,128)S(1)} %bitcast.8, bf16[64,128,128]{2,1,0:T(8,128)(2,1)} %diag.3, bf16[64,4,128,128]{3,2,1,0:T(8,128)(2,1)} %face.3), custom_call_target="tpu_custom_call" | custom-call | tf_op jit(solution)/shard_map/first_half/pallas_call | solution.py:326
  13.2 2.5 %collective-permute-start.2 = (bf16[48,8,128]{2,1,0:T(8,128)(2,1)S(1)}, bf16[48,8,128]{2,1,0:T(8,128)(2,1)S(1)}, u32[]{:S(2)}, u32[]{:S(2)}) collective-permute-start(bf16[48,8,128]{2,1,0:T(8,128)(2,1)S(1)} %get-tuple-element.57), channel_id=1, source_target_pairs={{0,16},{16,32},{32,48},{48,64},{64,80},{80,96},{96,112},{112,128},... | collective-permute-start | bytes 294920 | tf_op jit(solution)/shard_map/ppermute | solution.py:289
  15.8 0.2 collective-permute-start.3
  16.0 3.2 %second_half.1.turned.refs_2_.refs_3_ = bf16[64,640,128]{2,1,0:T(8,128)(2,1)S(1)} custom-call(bf16[64,128,128]{2,1,0:T(8,128)(2,1)} %diag.3, bf16[64,4,128,128]{3,2,1,0:T(8,128)(2,1)} %face.3, bf16[64,640,128]{2,1,0:T(8,128)(2,1)S(1)} %get-tuple-element.51.before), custom_call_target="tpu_custom_call", output_to_operand_aliasing={{}: (2, {})} | custom-call | tf_op jit(solution)/shard_map/second_half/pallas_call | solution.py:359
  19.2 0.9 collective-permute-done.3.from_next
  20.1 3.0 %whole.1 = (f32[64,8,128]{2,1,0:T(8,128)S(1)}, bf16[64,8,128]{2,1,0:T(8,128)(2,1)S(1)}, bf16[48,8,128]{2,1,0:T(8,128)(2,1)S(1)}, bf16[48,8,128]{2,1,0:T(8,128)(2...) custom-call(s32[4,64]{1,0:T(4,128)S(1)} %bitcast.9, ...), custom_call_target="tpu_custom_call" | custom-call | tf_op jit(solution)/shard_map/whole/pallas_call | solution.py:369
  23.2 4.8 %collective-permute-start.5 = (bf16[48,8,128]{2,1,0:T(8,128)(2,1)S(1)}, bf16[48,8,128]{2,1,0:T(8,128)(2,1)S(1)}, u32[]{:S(2)}, u32[]{:S(2)}) collective-permute-start(bf16[48,8,128]{2,1,0:T(8,128)(2,1)S(1)} %get-tuple-element.62), channel_id=1, source_target_pairs={{0,15},{1,0},{2,1},{3,2},{4,3},{5,4},{6,5},{7,6},{8,7},{9,8},{10,9... | collective-permute-start | bytes 294920 | tf_op jit(solution)/shard_map/ppermute | solution.py:289
  28.0 2.0 %collective-permute-done.4.refs_0_.refs_5_ = bf16[48,8,128]{2,1,0:T(8,128)(2,1)S(1)} collective-permute-done((bf16[48,8,128]{2,1,0:T(8,128)(2,1)S(1)}, bf16[48,8,128]{2,1,0:T(8,128)(2,1)S(1)}, u32[]{:S(2)}, u32[]{:S(2)}) %collective-permute-start.4) | collective-permute-done | bytes 98336 | tf_op jit(solution)/shard_map/ppermute | solution.py:289
  30.0 2.8 %collective-permute-start.6 = (bf16[48,8,128]{2,1,0:T(8,128)(2,1)S(1)}, bf16[48,8,128]{2,1,0:T(8,128)(2,1)S(1)}, u32[]{:S(2)}, u32[]{:S(2)}) collective-permute-start(bf16[48,8,128]{2,1,0:T(8,128)(2,1)S(1)} %get-tuple-element.65), channel_id=1, source_target_pairs={{0,16},{16,32},{32,48},{48,64},{64,80},{80,96},{96,112},{112,128},... | collective-permute-start | bytes 294920 | tf_op jit(solution)/shard_map/ppermute | solution.py:289
  32.8 0.8 collective-permute-start.7
  33.6 1.7 %local1.1 = (f32[64,8,128]{2,1,0:T(8,128)S(1)}, bf16[64,8,128]{2,1,0:T(8,128)(2,1)S(1)}, f32[8,128]{1,0:T(8,128)S(1)}) custom-call(s32[4,64]{1,0:T(4,128)S(1)} %bitcast.10, s32[128]{0:T(128)S(1)} %get-tuple-element.50.refs_4_.refs_1_, bf16[64,640,128]{2,1,0:T(8,128)(2,1)S(1)} %second_half.1.turned.refs_2_.refs_3_, ...), custom_call_target="tpu_custom_call" | custom-call | tf_op jit(solution)/shard_map/local1/pallas_call | solution.py:338
  35.3 1.5 %collective-permute-done.7.refs_8_ = bf16[48,8,128]{2,1,0:T(8,128)(2,1)S(1)} collective-permute-done((bf16[48,8,128]{2,1,0:T(8,128)(2,1)S(1)}, bf16[48,8,128]{2,1,0:T(8,128)(2,1)S(1)}, u32[]{:S(2)}, u32[]{:S(2)}) %collective-permute-start.7) | collective-permute-done | bytes 98336 | tf_op jit(solution)/shard_map/ppermute | solution.py:289
  36.8 1.9 %ghost1.1 = (f32[64,8,128]{2,1,0:T(8,128)S(1)}, bf16[64,8,128]{2,1,0:T(8,128)(2,1)S(1)}, bf16[48,8,128]{2,1,0:T(8,128)(2,1)S(1)}, bf16[48,8,128]{2,1,0:T(8,128)(...) custom-call(s32[4,64]{1,0:T(4,128)S(1)} %bitcast.11, ...), custom_call_target="tpu_custom_call", output_to_operand_aliasing={{0}: (12, {}), {1}: (13, {})} | custom-call | tf_op jit(solution)/shard_map/ghost1/pallas_call | solution.py:380
  38.8 5.1 %collective-permute-start.9 = (bf16[48,8,128]{2,1,0:T(8,128)(2,1)S(1)}, bf16[48,8,128]{2,1,0:T(8,128)(2,1)S(1)}, u32[]{:S(2)}, u32[]{:S(2)}) collective-permute-start(bf16[48,8,128]{2,1,0:T(8,128)(2,1)S(1)} %get-tuple-element.74), channel_id=1, source_target_pairs={{0,15},{1,0},{2,1},{3,2},{4,3},{5,4},{6,5},{7,6},{8,7},{9,8},{10,9... | collective-permute-start | bytes 294920 | tf_op jit(solution)/shard_map/ppermute | solution.py:289
  43.9 1.9 %collective-permute-done.8.refs_0_.refs_5_ = bf16[48,8,128]{2,1,0:T(8,128)(2,1)S(1)} collective-permute-done((bf16[48,8,128]{2,1,0:T(8,128)(2,1)S(1)}, bf16[48,8,128]{2,1,0:T(8,128)(2,1)S(1)}, u32[]{:S(2)}, u32[]{:S(2)}) %collective-permute-start.8) | collective-permute-done | bytes 98336 | tf_op jit(solution)/shard_map/ppermute | solution.py:289
  45.8 0.9 collective-permute-start.10
  46.8 2.0 %collective-permute-start.11 = (bf16[48,8,128]{2,1,0:T(8,128)(2,1)S(1)}, bf16[48,8,128]{2,1,0:T(8,128)(2,1)S(1)}, u32[]{:S(2)}, u32[]{:S(2)}) collective-permute-start(bf16[48,8,128]{2,1,0:T(8,128)(2,1)S(1)} %get-tuple-element.78), channel_id=1, source_target_pairs={{0,240},{16,0},{32,16},{48,32},{64,48},{80,64},{96,80},{112,96},{1... | collective-permute-start | bytes 294920 | tf_op jit(solution)/shard_map/ppermute | solution.py:289
  48.8 1.7 %local2.1 = (f32[64,8,128]{2,1,0:T(8,128)S(1)}, bf16[64,8,128]{2,1,0:T(8,128)(2,1)S(1)}, f32[8,128]{1,0:T(8,128)S(1)}) custom-call(s32[4,64]{1,0:T(4,128)S(1)} %bitcast.12, s32[128]{0:T(128)S(1)} %get-tuple-element.50.refs_4_.refs_1_, bf16[64,640,128]{2,1,0:T(8,128)(2,1)S(1)} %second_half.1.turned.refs_2_.refs_3_, ...), custom_call_target="tpu_custom_call" | custom-call | tf_op jit(solution)/shard_map/local2/pallas_call | solution.py:338
  50.5 0.3 collective-permute-done.11.refs_8_
  50.8 1.9 %ghost2.1 = (f32[64,8,128]{2,1,0:T(8,128)S(1)}, bf16[64,8,128]{2,1,0:T(8,128)(2,1)S(1)}, bf16[48,8,128]{2,1,0:T(8,128)(2,1)S(1)}, bf16[48,8,128]{2,1,0:T(8,128)(...) custom-call(s32[4,64]{1,0:T(4,128)S(1)} %bitcast.13, ...), custom_call_target="tpu_custom_call", output_to_operand_aliasing={{0}: (13, {}), {1}: (14, {})} | custom-call | tf_op jit(solution)/shard_map/ghost2/pallas_call | solution.py:380
  52.9 5.2 %collective-permute-start.13 = (bf16[48,8,128]{2,1,0:T(8,128)(2,1)S(1)}, bf16[48,8,128]{2,1,0:T(8,128)(2,1)S(1)}, u32[]{:S(2)}, u32[]{:S(2)}) collective-permute-start(bf16[48,8,128]{2,1,0:T(8,128)(2,1)S(1)} %get-tuple-element.86), channel_id=1, source_target_pairs={{0,15},{1,0},{2,1},{3,2},{4,3},{5,4},{6,5},{7,6},{8,7},{9,8},{10,9... | collective-permute-start | bytes 294920 | tf_op jit(solution)/shard_map/ppermute | solution.py:289
  58.0 1.9 %collective-permute-done.12.refs_0_.refs_5_ = bf16[48,8,128]{2,1,0:T(8,128)(2,1)S(1)} collective-permute-done((bf16[48,8,128]{2,1,0:T(8,128)(2,1)S(1)}, bf16[48,8,128]{2,1,0:T(8,128)(2,1)S(1)}, u32[]{:S(2)}, u32[]{:S(2)}) %collective-permute-start.12) | collective-permute-done | bytes 98336 | tf_op jit(solution)/shard_map/ppermute | solution.py:289
  60.0 0.9 collective-permute-start.14
  60.8 3.3 %collective-permute-start.15 = (bf16[48,8,128]{2,1,0:T(8,128)(2,1)S(1)}, bf16[48,8,128]{2,1,0:T(8,128)(2,1)S(1)}, u32[]{:S(2)}, u32[]{:S(2)}) collective-permute-start(bf16[48,8,128]{2,1,0:T(8,128)(2,1)S(1)} %get-tuple-element.90), channel_id=1, source_target_pairs={{0,240},{16,0},{32,16},{48,32},{64,48},{80,64},{96,80},{112,96},{1... | collective-permute-start | bytes 294920 | tf_op jit(solution)/shard_map/ppermute | solution.py:289
  64.1 1.9 %local3.1 = (f32[64,8,128]{2,1,0:T(8,128)S(1)}, bf16[64,8,128]{2,1,0:T(8,128)(2,1)S(1)}, f32[8,128]{1,0:T(8,128)S(1)}) custom-call(s32[4,64]{1,0:T(4,128)S(1)} %bitcast.14, s32[128]{0:T(128)S(1)} %get-tuple-element.50.refs_4_.refs_1_, bf16[64,640,128]{2,1,0:T(8,128)(2,1)S(1)} %second_half.1.turned.refs_2_.refs_3_, ...), custom_call_target="tpu_custom_call" | custom-call | tf_op jit(solution)/shard_map/local3/pallas_call | solution.py:338
  66.1 2.0 %ghost3.1 = (f32[64,8,128]{2,1,0:T(8,128)S(1)}, bf16[64,8,128]{2,1,0:T(8,128)(2,1)S(1)}, f32[256,128]{1,0:T(8,128)S(1)}) custom-call(s32[4,64]{1,0:T(4,128)S(1)} %bitcast.15, s32[128]{0:T(128)S(1)} %get-tuple-element.50.refs_4_.refs_1_, s32[9,1,16]{2,1,0:T(1,128)S(1)} %bitcast.20, ...), custom_call_target="tpu_custom_call", output_to_operand_aliasing={{0}: (14, {}), {1}: (15, {})} | custom-call | tf_op jit(solution)/shard_map/ghost3/pallas_call | solution.py:380
  68.1 28.3 %all_to_all.11 = f32[256,1,128]{2,1,0:T(1,128)S(1)} all-to-all(f32[256,1,128]{2,1,0:T(1,128)S(1)} %bitcast.7), channel_id=1, replica_groups=mesh['gx'=16,'gy'=16] {'gx','gy'}, dimensions={0} | all-to-all | bytes 262144 | tf_op jit(solution)/shard_map/all_to_all | solution.py:398
  96.4 1.2 %finish.1 = (f32[64,8,128]{2,1,0:T(8,128)}, f32[64,8,128]{2,1,0:T(8,128)}) custom-call(f32[256,128]{1,0:T(8,128)S(1)} %bitcast.6, f32[64,8,128]{2,1,0:T(8,128)S(1)} %get-tuple-element.59.b0.refs_5_.refs_10_, f32[64,8,128]{2,1,0:T(8,128)S(1)} %get-tuple-element.68.refs_6_.refs_11_.b1, f32[64,8,128]{2,1,0:T(8,128)S(1)} %get-tuple-element.80.refs_7_.refs_12_.b2, ...), custom_call_target="tpu_custom_call" | custom-call | tf_op jit(solution)/shard_map/finish/pallas_call | solution.py:399
  (22 shorter events, 0.3 us)
Async XLA Ops:
  2.5 10.7 %collective-permute-start = (bf16[48,8,128]{2,1,0:T(8,128)(2,1)S(1)}, bf16[48,8,128]{2,1,0:T(8,128)(2,1)S(1)}, u32[]{:S(2)}, u32[]{:S(2)}) collective-permute-start(bf16[48,8,128]{2,1,0:T(8,128)(2,1)S(1)} %get-tuple-element.53), channel_id=1, source_target_pairs={{0,1},{1,2},{2,3},{3,4},{4,5},{5,6},{6,7},{7,8},{8,9},{9,10},{10,1... | collective-permute-start | bytes 294920 | tf_op jit(solution)/shard_map/ppermute | solution.py:289
  4.7 8.5 %collective-permute-start.1 = (bf16[48,8,128]{2,1,0:T(8,128)(2,1)S(1)}, bf16[48,8,128]{2,1,0:T(8,128)(2,1)S(1)}, u32[]{:S(2)}, u32[]{:S(2)}) collective-permute-start(bf16[48,8,128]{2,1,0:T(8,128)(2,1)S(1)} %get-tuple-element.54), channel_id=1, source_target_pairs={{0,15},{1,0},{2,1},{3,2},{4,3},{5,4},{6,5},{7,6},{8,7},{9,8},{10,9... | collective-permute-start | bytes 294920 | tf_op jit(solution)/shard_map/ppermute | solution.py:289
  8.4 0.7 copy-start
  13.2 6.0 %collective-permute-start.2 = (bf16[48,8,128]{2,1,0:T(8,128)(2,1)S(1)}, bf16[48,8,128]{2,1,0:T(8,128)(2,1)S(1)}, u32[]{:S(2)}, u32[]{:S(2)}) collective-permute-start(bf16[48,8,128]{2,1,0:T(8,128)(2,1)S(1)} %get-tuple-element.57), channel_id=1, source_target_pairs={{0,16},{16,32},{32,48},{48,64},{64,80},{80,96},{96,112},{112,128},... | collective-permute-start | bytes 294920 | tf_op jit(solution)/shard_map/ppermute | solution.py:289
  15.8 4.3 %collective-permute-start.3 = (bf16[48,8,128]{2,1,0:T(8,128)(2,1)S(1)}, bf16[48,8,128]{2,1,0:T(8,128)(2,1)S(1)}, u32[]{:S(2)}, u32[]{:S(2)}) collective-permute-start(bf16[48,8,128]{2,1,0:T(8,128)(2,1)S(1)} %get-tuple-element.58), channel_id=1, source_target_pairs={{0,240},{16,0},{32,16},{48,32},{64,48},{80,64},{96,80},{112,96},{1... | collective-permute-start | bytes 294920 | tf_op jit(solution)/shard_map/ppermute | solution.py:289
  16.0 4.1 %copy-start.1 = (s32[64,4]{0,1:T(4,128)S(1)}, s32[64,4]{0,1:T(4,128)}, u32[]{:S(2)}) copy-start(s32[64,4]{0,1:T(4,128)} %param.9) | copy-start | bytes 3076
  16.0 4.1 %copy-start.2 = (s32[1,9,16]{2,0,1:T(1,128)S(1)}, s32[1,9,16]{2,0,1:T(1,128)}, u32[]{:S(2)}) copy-start(s32[1,9,16]{2,0,1:T(1,128)} %param.10) | copy-start | bytes 1732
  23.1 6.9 %collective-permute-start.4 = (bf16[48,8,128]{2,1,0:T(8,128)(2,1)S(1)}, bf16[48,8,128]{2,1,0:T(8,128)(2,1)S(1)}, u32[]{:S(2)}, u32[]{:S(2)}) collective-permute-start(bf16[48,8,128]{2,1,0:T(8,128)(2,1)S(1)} %get-tuple-element.61), channel_id=1, source_target_pairs={{0,1},{1,2},{2,3},{3,4},{4,5},{5,6},{6,7},{7,8},{8,9},{9,10},{10,1... | collective-permute-start | bytes 294920 | tf_op jit(solution)/shard_map/ppermute | solution.py:289
  23.2 6.8 %collective-permute-start.5 = (bf16[48,8,128]{2,1,0:T(8,128)(2,1)S(1)}, bf16[48,8,128]{2,1,0:T(8,128)(2,1)S(1)}, u32[]{:S(2)}, u32[]{:S(2)}) collective-permute-start(bf16[48,8,128]{2,1,0:T(8,128)(2,1)S(1)} %get-tuple-element.62), channel_id=1, source_target_pairs={{0,15},{1,0},{2,1},{3,2},{4,3},{5,4},{6,5},{7,6},{8,7},{9,8},{10,9... | collective-permute-start | bytes 294920 | tf_op jit(solution)/shard_map/ppermute | solution.py:289
  30.0 5.3 %collective-permute-start.6 = (bf16[48,8,128]{2,1,0:T(8,128)(2,1)S(1)}, bf16[48,8,128]{2,1,0:T(8,128)(2,1)S(1)}, u32[]{:S(2)}, u32[]{:S(2)}) collective-permute-start(bf16[48,8,128]{2,1,0:T(8,128)(2,1)S(1)} %get-tuple-element.65), channel_id=1, source_target_pairs={{0,16},{16,32},{32,48},{48,64},{64,80},{80,96},{96,112},{112,128},... | collective-permute-start | bytes 294920 | tf_op jit(solution)/shard_map/ppermute | solution.py:289
  32.8 4.0 %collective-permute-start.7 = (bf16[48,8,128]{2,1,0:T(8,128)(2,1)S(1)}, bf16[48,8,128]{2,1,0:T(8,128)(2,1)S(1)}, u32[]{:S(2)}, u32[]{:S(2)}) collective-permute-start(bf16[48,8,128]{2,1,0:T(8,128)(2,1)S(1)} %get-tuple-element.66), channel_id=1, source_target_pairs={{0,240},{16,0},{32,16},{48,32},{64,48},{80,64},{96,80},{112,96},{1... | collective-permute-start | bytes 294920 | tf_op jit(solution)/shard_map/ppermute | solution.py:289
  38.7 7.1 %collective-permute-start.8 = (bf16[48,8,128]{2,1,0:T(8,128)(2,1)S(1)}, bf16[48,8,128]{2,1,0:T(8,128)(2,1)S(1)}, u32[]{:S(2)}, u32[]{:S(2)}) collective-permute-start(bf16[48,8,128]{2,1,0:T(8,128)(2,1)S(1)} %get-tuple-element.73), channel_id=1, source_target_pairs={{0,1},{1,2},{2,3},{3,4},{4,5},{5,6},{6,7},{7,8},{8,9},{9,10},{10,1... | collective-permute-start | bytes 294920 | tf_op jit(solution)/shard_map/ppermute | solution.py:289
  38.8 7.0 %collective-permute-start.9 = (bf16[48,8,128]{2,1,0:T(8,128)(2,1)S(1)}, bf16[48,8,128]{2,1,0:T(8,128)(2,1)S(1)}, u32[]{:S(2)}, u32[]{:S(2)}) collective-permute-start(bf16[48,8,128]{2,1,0:T(8,128)(2,1)S(1)} %get-tuple-element.74), channel_id=1, source_target_pairs={{0,15},{1,0},{2,1},{3,2},{4,3},{5,4},{6,5},{7,6},{8,7},{9,8},{10,9... | collective-permute-start | bytes 294920 | tf_op jit(solution)/shard_map/ppermute | solution.py:289
  45.8 4.7 %collective-permute-start.10 = (bf16[48,8,128]{2,1,0:T(8,128)(2,1)S(1)}, bf16[48,8,128]{2,1,0:T(8,128)(2,1)S(1)}, u32[]{:S(2)}, u32[]{:S(2)}) collective-permute-start(bf16[48,8,128]{2,1,0:T(8,128)(2,1)S(1)} %get-tuple-element.77), channel_id=1, source_target_pairs={{0,16},{16,32},{32,48},{48,64},{64,80},{80,96},{96,112},{112,128},... | collective-permute-start | bytes 294920 | tf_op jit(solution)/shard_map/ppermute | solution.py:289
  46.8 4.0 %collective-permute-start.11 = (bf16[48,8,128]{2,1,0:T(8,128)(2,1)S(1)}, bf16[48,8,128]{2,1,0:T(8,128)(2,1)S(1)}, u32[]{:S(2)}, u32[]{:S(2)}) collective-permute-start(bf16[48,8,128]{2,1,0:T(8,128)(2,1)S(1)} %get-tuple-element.78), channel_id=1, source_target_pairs={{0,240},{16,0},{32,16},{48,32},{64,48},{80,64},{96,80},{112,96},{1... | collective-permute-start | bytes 294920 | tf_op jit(solution)/shard_map/ppermute | solution.py:289
  52.8 7.2 %collective-permute-start.12 = (bf16[48,8,128]{2,1,0:T(8,128)(2,1)S(1)}, bf16[48,8,128]{2,1,0:T(8,128)(2,1)S(1)}, u32[]{:S(2)}, u32[]{:S(2)}) collective-permute-start(bf16[48,8,128]{2,1,0:T(8,128)(2,1)S(1)} %get-tuple-element.85), channel_id=1, source_target_pairs={{0,1},{1,2},{2,3},{3,4},{4,5},{5,6},{6,7},{7,8},{8,9},{9,10},{10,1... | collective-permute-start | bytes 294920 | tf_op jit(solution)/shard_map/ppermute | solution.py:289
  52.9 7.1 %collective-permute-start.13 = (bf16[48,8,128]{2,1,0:T(8,128)(2,1)S(1)}, bf16[48,8,128]{2,1,0:T(8,128)(2,1)S(1)}, u32[]{:S(2)}, u32[]{:S(2)}) collective-permute-start(bf16[48,8,128]{2,1,0:T(8,128)(2,1)S(1)} %get-tuple-element.86), channel_id=1, source_target_pairs={{0,15},{1,0},{2,1},{3,2},{4,3},{5,4},{6,5},{7,6},{8,7},{9,8},{10,9... | collective-permute-start | bytes 294920 | tf_op jit(solution)/shard_map/ppermute | solution.py:289
  60.0 6.1 %collective-permute-start.14 = (bf16[48,8,128]{2,1,0:T(8,128)(2,1)S(1)}, bf16[48,8,128]{2,1,0:T(8,128)(2,1)S(1)}, u32[]{:S(2)}, u32[]{:S(2)}) collective-permute-start(bf16[48,8,128]{2,1,0:T(8,128)(2,1)S(1)} %get-tuple-element.89), channel_id=1, source_target_pairs={{0,16},{16,32},{32,48},{48,64},{64,80},{80,96},{96,112},{112,128},... | collective-permute-start | bytes 294920 | tf_op jit(solution)/shard_map/ppermute | solution.py:289
  60.8 5.2 %collective-permute-start.15 = (bf16[48,8,128]{2,1,0:T(8,128)(2,1)S(1)}, bf16[48,8,128]{2,1,0:T(8,128)(2,1)S(1)}, u32[]{:S(2)}, u32[]{:S(2)}) collective-permute-start(bf16[48,8,128]{2,1,0:T(8,128)(2,1)S(1)} %get-tuple-element.90), channel_id=1, source_target_pairs={{0,240},{16,0},{32,16},{48,32},{64,48},{80,64},{96,80},{112,96},{1... | collective-permute-start | bytes 294920 | tf_op jit(solution)/shard_map/ppermute | solution.py:289

commit v3 on v2

--- a/solution.py
+++ b/solution.py
@@ -28,6 +28,10 @@
 IN_HBM = pl.BlockSpec(memory_space=pltpu.HBM)
 UP_DIRECTIONS = (2, 5, 8)
 DOWN_DIRECTIONS = (0, 3, 6)
+LOCAL_RUNS = CAP
+PLACES = 2 * CAP
+SLOTS = PLACES + FACES * CAP
+TABLE = SLOTS + 2 * CAP + 2 * SEND
 PAIRS = [(a, b) for a in range(5) for b in range(a, 5) if b > 0]
 PAIR_LANE = {pair: at for at, pair in enumerate(PAIRS)}
 LANES_PER_SIDE = 16
@@ -41,7 +45,7 @@
     return pltpu.CompilerParams(vmem_limit_bytes=mebibytes << 20)
 
 
-def pack(send_slots, rounded, up, down, next_row, last_row):
+def pack(slot_of, rounded, up, down, next_row, last_row):
     for target, directions in (
         (up, UP_DIRECTIONS),
         (down, DOWN_DIRECTIONS),
@@ -50,8 +54,15 @@
     ):
         for at, direction in enumerate(directions):
             for k in range(SEND):
-                slot = jnp.maximum(send_slots[direction, 0, k], 0)
-                target[at * SEND + k] = rounded[slot]
+                target[at * SEND + k] = rounded[slot_of(direction, k)]
+
+
+def listed(send_slots):
+    return lambda direction, k: jnp.maximum(send_slots[direction, 0, k], 0)
+
+
+def planned(table):
+    return lambda direction, k: table[SLOTS + direction * SEND + k]
 
 
 def start_kernel(
@@ -61,22 +72,29 @@
     live = jnp.where(element < counts[0], right_sides[...], 0.0)
     basis[...] = live
     rounded[...] = live.astype(jnp.bfloat16)
-    pack(send_slots, rounded, up, down, next_row, last_row)
-
-
-def make_plan(neighbours, order):
+    pack(listed(send_slots), rounded, up, down, next_row, last_row)
+
+
+def plan_kernel(neighbours, send_slots, table, done):
     local = jnp.int32(0)
     for e in range(CAP):
-        farthest = neighbours[0, e]
-        for f in range(1, FACES):
-            farthest = jnp.maximum(farthest, neighbours[f, e])
+        at = [neighbours[f, e] for f in range(FACES)]
+        farthest = jnp.maximum(jnp.maximum(at[0], at[1]), jnp.maximum(at[2], at[3]))
         ghost = farthest >= CAP
-        order[jnp.where(ghost, CAP - 1 - (e - local), local)] = e
+        place = jnp.where(ghost, CAP - 1 - (e - local), local)
+        table[place] = e
+        for f in range(FACES):
+            table[PLACES + f * CAP + place] = jnp.where(at[f] < 0, NOTHING, at[f])
         local = local + jnp.where(ghost, 0, 1)
-    order[CAP] = local // UNROLL
-
-
-def transpose_blocks(base, diag, face, turned, diag_here, face_here, arrived, extra):
+    table[LOCAL_RUNS] = local // UNROLL
+    for direction in range(9):
+        for k in range(SEND):
+            slot = listed(send_slots)(direction, k)
+            table[SLOTS + direction * SEND + k] = slot
+    done[...] = jnp.zeros_like(done)
+
+
+def transpose_blocks(base, diag, face, turned, diag_here, face_here, arrived):
     def fetch(c):
         here = pl.ds(c * CHUNK, CHUNK)
         there = pl.ds(base + c * CHUNK, CHUNK)
@@ -88,7 +106,6 @@
     for c in range(CHUNKS):
         for copy in fetch(c):
             copy.start()
-    extra()
     for c in range(CHUNKS):
         for copy in fetch(c):
             copy.wait()
@@ -103,19 +120,13 @@
         lax.fori_loop(0, CHUNK, element, 0, unroll=4)
 
 
-def first_half_kernel(
-    neighbours, diag, face, turned, order, diag_here, face_here, arrived
-):
-    transpose_blocks(
-        0, diag, face, turned, diag_here, face_here, arrived,
-        lambda: make_plan(neighbours, order),
-    )
+def first_half_kernel(diag, face, turned, done, diag_here, face_here, arrived):
+    transpose_blocks(0, diag, face, turned, diag_here, face_here, arrived)
+    done[...] = jnp.zeros_like(done)
 
 
 def second_half_kernel(diag, face, before, turned, diag_here, face_here, arrived):
-    transpose_blocks(
-        HALF_CAP, diag, face, turned, diag_here, face_here, arrived, lambda: None
-    )
+    transpose_blocks(HALF_CAP, diag, face, turned, diag_here, face_here, arrived)
 
 
 def relay_kernel(*refs):
@@ -141,29 +152,30 @@
     lookup[CAP + 6 * SEND : CAP + 9 * SEND] = from_last[...]
 
 
-def apply_runs(
-    first, limit, order, neighbours, turned, lookup, basis, image, image_rounded
-):
-    def element(e, sums):
-        near = [lookup[e]]
-        for f in range(FACES):
-            at = neighbours[f, e]
-            near.append(lookup[jnp.where(at < 0, NOTHING, at)])
-        out = jnp.dot(
-            jnp.concatenate(near, axis=1),
-            turned[e],
+def apply_runs(first, limit, find, turned, lookup, basis, image, image_rounded):
+    def near(found):
+        vectors = jnp.concatenate([lookup[at] for at in found], axis=1)
+        return vectors.astype(jnp.float32)
+
+    def two(found, sums):
+        elements = [places[0] for places in found]
+        both = jnp.dot(
+            jnp.concatenate([near(f) for f in found], axis=0).astype(jnp.bfloat16),
+            jnp.concatenate([turned[e] for e in elements], axis=1),
             preferred_element_type=jnp.float32,
         )
-        image[e] = out
-        if image_rounded is not None:
+        for at, e in enumerate(elements):
+            out = both[8 * at : 8 * at + 8, ROWS * at : ROWS * at + ROWS]
+            image[e] = out
             image_rounded[e] = out.astype(jnp.bfloat16)
-        others = [ref[e] for ref in basis] + [out]
-        return tuple(s + out * other for s, other in zip(sums, others))
+            others = [ref[e] for ref in basis] + [out]
+            sums = tuple(s + out * other for s, other in zip(sums, others))
+        return sums
 
     def run(step, sums):
-        for u in range(UNROLL):
+        for u in range(0, UNROLL, 2):
             at = step * UNROLL + u
-            sums = element(at if order is None else order[at], sums)
+            sums = two([find(at), find(at + 1)], sums)
         return sums
 
     zero = jnp.zeros((8, ROWS), jnp.float32)
@@ -185,30 +197,39 @@
 ):
     fill_local(lookup, rounded)
     fill_ghosts(lookup, from_down, from_up, from_last, from_next)
+
+    def find(e):
+        at = [neighbours[f, e] for f in range(FACES)]
+        return [e] + [jnp.where(a < 0, NOTHING, a) for a in at]
+
     sums = apply_runs(
-        0, CAP // UNROLL, None, neighbours, turned, lookup, (b0,), image, image_rounded
+        0, CAP // UNROLL, find, turned, lookup, (b0,), image, image_rounded
     )
-    pack(send_slots, image_rounded, up, down, next_row, last_row)
+    pack(listed(send_slots), image_rounded, up, down, next_row, last_row)
     gram_out[...] = with_sums(jnp.zeros((8, ROWS), jnp.float32), sums)
 
 
+def find_in(table):
+    return lambda at: [table[at]] + [table[PLACES + f * CAP + at] for f in range(FACES)]
+
+
 def local_kernel(power, *refs):
-    neighbours, order, turned, rounded, gram_in = refs[:5]
-    basis = refs[5 : 6 + power]
-    image, image_rounded, gram_out, lookup = refs[6 + power :]
+    table, turned, rounded, gram_in = refs[:4]
+    basis = refs[4 : 5 + power]
+    image, image_rounded, gram_out, lookup = refs[5 + power :]
     fill_local(lookup, rounded)
     sums = apply_runs(
-        0, order[CAP], order, neighbours, turned, lookup, basis, image, image_rounded
+        0, table[LOCAL_RUNS], find_in(table), turned, lookup, basis, image, image_rounded
     )
     gram_out[...] = with_sums(gram_in[...], sums)
 
 
 def ghost_kernel(power, *refs):
-    neighbours, order, send_slots, turned, rounded = refs[:5]
-    received = refs[5:9]
-    gram_in = refs[9]
-    basis = refs[10 : 11 + power]
-    refs = refs[13 + power :]
+    table, turned, rounded = refs[:3]
+    received = refs[3:7]
+    gram_in = refs[7]
+    basis = refs[8 : 9 + power]
+    refs = refs[11 + power :]
     last = power == POWERS - 1
     if last:
         image, image_rounded, gram_out, lookup = refs
@@ -217,11 +238,11 @@
     fill_local(lookup, rounded)
     fill_ghosts(lookup, *received)
     sums = apply_runs(
-        order[CAP], CAP // UNROLL, order, neighbours, turned, lookup, basis, image,
+        table[LOCAL_RUNS], CAP // UNROLL, find_in(table), turned, lookup, basis, image,
         image_rounded,
     )
     if not last:
-        pack(send_slots, image_rounded, up, down, next_row, last_row)
+        pack(planned(table), image_rounded, up, down, next_row, last_row)
     gram = with_sums(gram_in[...], sums)
     if last:
         lane = lax.broadcasted_iota(jnp.int32, (8, ROWS), 1)
@@ -322,28 +343,38 @@
         last = power == POWERS - 1
         from_down = shifted(up, "gy", 1)
         from_up = shifted(down, "gy", -1)
+        after = ()
         if power == 0:
-            turned, order = pl.pallas_call(
+            turned, done = pl.pallas_call(
                 first_half_kernel,
                 name="first_half",
-                in_specs=[IN_SMEM, IN_HBM, IN_HBM],
-                out_specs=[IN_VMEM, IN_SMEM],
-                out_shape=[turned_shape, jax.ShapeDtypeStruct((128,), jnp.int32)],
+                in_specs=[IN_HBM] * 2,
+                out_specs=[IN_VMEM] * 2,
+                out_shape=[turned_shape, gram_shape],
                 scratch_shapes=landing,
                 compiler_params=params(),
-            )(neighbours, diag_blocks, face_blocks)
-            after = (order,)
-        else:
-            after = ()
+            )(diag_blocks, face_blocks)
+            after = (done,)
+        elif power == 1:
+            table, done = pl.pallas_call(
+                plan_kernel,
+                name="plan",
+                in_specs=[IN_SMEM] * 2,
+                out_specs=[IN_SMEM, IN_VMEM],
+                out_shape=[pltpu.SMEM((TABLE,), jnp.int32), gram_shape],
+                compiler_params=params(),
+            )(neighbours, send_slots)
+            after = (done,)
+        if power > 0:
             image, image_rounded, gram = pl.pallas_call(
                 functools.partial(local_kernel, power),
                 name=f"local{power}",
-                in_specs=[IN_SMEM] * 2 + [IN_VMEM] * (4 + power),
+                in_specs=[IN_SMEM] + [IN_VMEM] * (4 + power),
                 out_specs=[IN_VMEM] * 3,
                 out_shape=[full, narrow, gram_shape],
                 scratch_shapes=[lookup],
                 compiler_params=params(),
-            )(neighbours, order, turned, rounded, gram, *basis)
+            )(table, turned, rounded, gram, *basis)
         send_next, send_last = pl.pallas_call(
             relay_kernel,
             name="relay",
@@ -380,15 +411,14 @@
             outs = pl.pallas_call(
                 functools.partial(ghost_kernel, power),
                 name=f"ghost{power}",
-                in_specs=[IN_SMEM] * 3 + [IN_VMEM] * (10 + power),
+                in_specs=[IN_SMEM] + [IN_VMEM] * (10 + power),
                 out_specs=[IN_VMEM] * len(shapes),
                 out_shape=shapes,
                 scratch_shapes=[lookup],
-                input_output_aliases={11 + power: 0, 12 + power: 1},
+                input_output_aliases={9 + power: 0, 10 + power: 1},
                 compiler_params=params(),
             )(
-                neighbours, order, send_slots, turned, rounded, *received, gram, *basis,
-                image, image_rounded,
+                table, turned, rounded, *received, gram, *basis, image, image_rounded,
             )
         basis.append(outs[0])
         rounded = outs[1]

time: 97.7 us -> 93.5 us (0.957)
  Pallas kernels: 23.9 us -> 19.6 us
    pallas_call x3, Pallas kernels: 5.82 us -> 3.49 us  [per_device(): pl.pallas_call(functools.partial(ghost_kernel, power), name=f'ghost{power...]
    pallas_call x3, Pallas kernels: 5.37 us -> 3.14 us  [per_device(): pl.pallas_call(functools.partial(local_kernel, power), name=f'local{power...]
    pallas_call x1 -> x2, Pallas kernels: 4.11 us -> 4.64 us  [the longest x1 3.18 us: per_device(): pl.pallas_call(first_half_kernel, name='first_half', in_specs=[IN_HBM] *...]
  transfers between devices with their start and end apart: 16 -> 16, of which waited for: 6 -> 6; matrix products, arithmetic and copies ran while one was open for 0% -> 0% of each run, Pallas kernels for 13% -> 12%
where the time goes in v3:
time: 93.5 us; the launch traced here: 93.3 us
  starting transfers between devices  34.7 us (37%)
  blocking collectives  29.2 us (31%)
  Pallas kernels  19.6 us (21%)
  waiting for transfers between devices  8.42 us (9%)
  between operations  1.43 us (2%)
    ppermute x16, starting transfers between devices, shifted(): lax.ppermute(block, axis, [(i, (i + distance) % SIDE) for i in range(SIDE)])  34.7 us
    all_to_all x1, blocking collectives, per_device(): gathered = lax.all_to_all(gram, ('gx', 'gy'), 0, 0, tiled=True)  29.2 us
    ppermute x16, waiting for transfers between devices, shifted(): lax.ppermute(block, axis, [(i, (i + distance) % SIDE) for i in range(SIDE)])  8.42 us
    pallas_call x3, Pallas kernels, per_device(): pl.pallas_call(functools.partial(ghost_kernel, power), name=f'ghost{power...  3.49 us
    pallas_call x1, Pallas kernels, per_device(): pl.pallas_call(second_half_kernel, name='second_half', in_specs=[IN_HBM,...  3.2 us
    pallas_call x1, Pallas kernels, per_device(): pl.pallas_call(first_half_kernel, name='first_half', in_specs=[IN_HBM] *...  3.18 us
    pallas_call x3, Pallas kernels, per_device(): pl.pallas_call(functools.partial(local_kernel, power), name=f'local{power...  3.14 us
    pallas_call x1, Pallas kernels, per_device(): pl.pallas_call(whole_kernel, name='whole', in_specs=[IN_SMEM] * 2 + [IN_V...  2.69 us
  transfers between devices with their start and end apart: 16, of which 6 were waited for; matrix products, arithmetic and copies ran while one was open for 0% of the time, Pallas kernels for 12%

profile of v3, /device:TPU:1, one launch (start us, length us, event | category | flops | bytes accessed | tf_op | source)
XLA Modules:
  0.0 93.3 jit_solution(11440273611477665884)
XLA Ops:
  1.3 1.2 %start.1 = (f32[64,8,128]{2,1,0:T(8,128)S(1)}, bf16[64,8,128]{2,1,0:T(8,128)(2,1)S(1)}, bf16[48,8,128]{2,1,0:T(8,128)(2,1)S(1)}, bf16[48,8,128]{2,1,0:T(8,128)(2...) custom-call(s32[9,1,16]{2,1,0:T(1,128)} %bitcast.8, s32[1]{0:T(128)S(6)} %copy.23.counts, ...), custom_call_target="tpu_custom_call" | custom-call | tf_op jit(solution)/shard_map/start/pallas_call | solution.py:332
  2.5 2.2 %collective-permute-start = (bf16[48,8,128]{2,1,0:T(8,128)(2,1)S(1)}, bf16[48,8,128]{2,1,0:T(8,128)(2,1)S(1)}, u32[]{:S(2)}, u32[]{:S(2)}) collective-permute-start(bf16[48,8,128]{2,1,0:T(8,128)(2,1)S(1)} %get-tuple-element.55), channel_id=1, source_target_pairs={{0,1},{1,2},{2,3},{3,4},{4,5},{5,6},{6,7},{7,8},{8,9},{9,10},{10,1... | collective-permute-start | bytes 294920 | tf_op jit(solution)/shard_map/ppermute | solution.py:310
  4.7 3.7 %collective-permute-start.1 = (bf16[48,8,128]{2,1,0:T(8,128)(2,1)S(1)}, bf16[48,8,128]{2,1,0:T(8,128)(2,1)S(1)}, u32[]{:S(2)}, u32[]{:S(2)}) collective-permute-start(bf16[48,8,128]{2,1,0:T(8,128)(2,1)S(1)} %get-tuple-element.56), channel_id=1, source_target_pairs={{0,15},{1,0},{2,1},{3,2},{4,3},{5,4},{6,5},{7,6},{8,7},{9,8},{10,9... | collective-permute-start | bytes 294920 | tf_op jit(solution)/shard_map/ppermute | solution.py:310
  8.4 3.2 %first_half.1 = (bf16[64,640,128]{2,1,0:T(8,128)(2,1)S(1)}, f32[8,128]{1,0:T(8,128)S(1)}) custom-call(bf16[64,128,128]{2,1,0:T(8,128)(2,1)} %diag.3, bf16[64,4,128,128]{3,2,1,0:T(8,128)(2,1)} %face.3), custom_call_target="tpu_custom_call" | custom-call | tf_op jit(solution)/shard_map/first_half/pallas_call | solution.py:348
  11.6 2.5 %collective-permute-start.2 = (bf16[48,8,128]{2,1,0:T(8,128)(2,1)S(1)}, bf16[48,8,128]{2,1,0:T(8,128)(2,1)S(1)}, u32[]{:S(2)}, u32[]{:S(2)}) collective-permute-start(bf16[48,8,128]{2,1,0:T(8,128)(2,1)S(1)} %get-tuple-element.60), channel_id=1, source_target_pairs={{0,16},{16,32},{32,48},{48,64},{64,80},{80,96},{96,112},{112,128},... | collective-permute-start | bytes 294920 | tf_op jit(solution)/shard_map/ppermute | solution.py:310
  14.2 0.2 collective-permute-start.3
  14.4 3.2 %second_half.1.turned.refs_1_ = bf16[64,640,128]{2,1,0:T(8,128)(2,1)S(1)} custom-call(bf16[64,128,128]{2,1,0:T(8,128)(2,1)} %diag.3, bf16[64,4,128,128]{3,2,1,0:T(8,128)(2,1)} %face.3, bf16[64,640,128]{2,1,0:T(8,128)(2,1)S(1)} %get-tuple-element.53.before), custom_call_target="tpu_custom_call", output_to_operand_aliasing={{}: (2, {})} | custom-call | tf_op jit(solution)/shard_map/second_half/pallas_call | solution.py:390
  17.6 0.9 collective-permute-done.3.from_next
  18.5 2.7 %whole.1 = (f32[64,8,128]{2,1,0:T(8,128)S(1)}, bf16[64,8,128]{2,1,0:T(8,128)(2,1)S(1)}, bf16[48,8,128]{2,1,0:T(8,128)(2,1)S(1)}, bf16[48,8,128]{2,1,0:T(8,128)(2...) custom-call(s32[4,64]{1,0:T(4,128)S(1)} %bitcast.11, ...), custom_call_target="tpu_custom_call" | custom-call | tf_op jit(solution)/shard_map/whole/pallas_call | solution.py:400
  21.3 4.8 %collective-permute-start.5 = (bf16[48,8,128]{2,1,0:T(8,128)(2,1)S(1)}, bf16[48,8,128]{2,1,0:T(8,128)(2,1)S(1)}, u32[]{:S(2)}, u32[]{:S(2)}) collective-permute-start(bf16[48,8,128]{2,1,0:T(8,128)(2,1)S(1)} %get-tuple-element.65), channel_id=1, source_target_pairs={{0,15},{1,0},{2,1},{3,2},{4,3},{5,4},{6,5},{7,6},{8,7},{9,8},{10,9... | collective-permute-start | bytes 294920 | tf_op jit(solution)/shard_map/ppermute | solution.py:310
  26.1 1.5 %plan.1 = (s32[544]{0:T(1024)S(4)}, f32[8,128]{1,0:T(8,128)S(1)}) custom-call(s32[4,64]{1,0:T(4,128)S(1)} %bitcast.12, s32[9,1,16]{2,1,0:T(1,128)S(1)} %bitcast.10), custom_call_target="tpu_custom_call" | custom-call | tf_op jit(solution)/shard_map/plan/pallas_call | solution.py:359
  27.5 0.5 collective-permute-done.4.refs_0_.refs_3_
  28.1 2.8 %collective-permute-start.6 = (bf16[48,8,128]{2,1,0:T(8,128)(2,1)S(1)}, bf16[48,8,128]{2,1,0:T(8,128)(2,1)S(1)}, u32[]{:S(2)}, u32[]{:S(2)}) collective-permute-start(bf16[48,8,128]{2,1,0:T(8,128)(2,1)S(1)} %get-tuple-element.69), channel_id=1, source_target_pairs={{0,16},{16,32},{32,48},{48,64},{64,80},{80,96},{96,112},{112,128},... | collective-permute-start | bytes 294920 | tf_op jit(solution)/shard_map/ppermute | solution.py:310
  30.9 0.8 collective-permute-start.7
  31.7 1.0 %local1.1 = (f32[64,8,128]{2,1,0:T(8,128)S(1)}, bf16[64,8,128]{2,1,0:T(8,128)(2,1)S(1)}, f32[8,128]{1,0:T(8,128)S(1)}) custom-call(s32[544]{0:T(1024)S(4)} %get-tuple-element.52.refs_0_, bf16[64,640,128]{2,1,0:T(8,128)(2,1)S(1)} %second_half.1.turned.refs_1_, bf16[64,8,128]{2,1,0:T(8,128)(2,1)S(1)} %get-tuple-element.63.refs_2_, ...), custom_call_target="tpu_custom_call" | custom-call | tf_op jit(solution)/shard_map/local1/pallas_call | solution.py:369
  32.7 2.2 %collective-permute-done.7.refs_6_ = bf16[48,8,128]{2,1,0:T(8,128)(2,1)S(1)} collective-permute-done((bf16[48,8,128]{2,1,0:T(8,128)(2,1)S(1)}, bf16[48,8,128]{2,1,0:T(8,128)(2,1)S(1)}, u32[]{:S(2)}, u32[]{:S(2)}) %collective-permute-start.7) | collective-permute-done | bytes 98336 | tf_op jit(solution)/shard_map/ppermute | solution.py:310
  34.9 1.1 %ghost1.1 = (f32[64,8,128]{2,1,0:T(8,128)S(1)}, bf16[64,8,128]{2,1,0:T(8,128)(2,1)S(1)}, bf16[48,8,128]{2,1,0:T(8,128)(2,1)S(1)}, bf16[48,8,128]{2,1,0:T(8,128)(...) custom-call(s32[544]{0:T(1024)S(4)} %get-tuple-element.52.refs_0_, ...), custom_call_target="tpu_custom_call", output_to_operand_aliasing={{0}: (10, {}), {1}: (11, {})} | custom-call | tf_op jit(solution)/shard_map/ghost1/pallas_call | solution.py:411
  36.1 5.1 %collective-permute-start.9 = (bf16[48,8,128]{2,1,0:T(8,128)(2,1)S(1)}, bf16[48,8,128]{2,1,0:T(8,128)(2,1)S(1)}, u32[]{:S(2)}, u32[]{:S(2)}) collective-permute-start(bf16[48,8,128]{2,1,0:T(8,128)(2,1)S(1)} %get-tuple-element.78), channel_id=1, source_target_pairs={{0,15},{1,0},{2,1},{3,2},{4,3},{5,4},{6,5},{7,6},{8,7},{9,8},{10,9... | collective-permute-start | bytes 294920 | tf_op jit(solution)/shard_map/ppermute | solution.py:310
  41.2 1.9 %collective-permute-done.8.refs_0_.refs_3_ = bf16[48,8,128]{2,1,0:T(8,128)(2,1)S(1)} collective-permute-done((bf16[48,8,128]{2,1,0:T(8,128)(2,1)S(1)}, bf16[48,8,128]{2,1,0:T(8,128)(2,1)S(1)}, u32[]{:S(2)}, u32[]{:S(2)}) %collective-permute-start.8) | collective-permute-done | bytes 98336 | tf_op jit(solution)/shard_map/ppermute | solution.py:310
  43.1 0.9 %collective-permute-start.10 = (bf16[48,8,128]{2,1,0:T(8,128)(2,1)S(1)}, bf16[48,8,128]{2,1,0:T(8,128)(2,1)S(1)}, u32[]{:S(2)}, u32[]{:S(2)}) collective-permute-start(bf16[48,8,128]{2,1,0:T(8,128)(2,1)S(1)} %get-tuple-element.81), channel_id=1, source_target_pairs={{0,16},{16,32},{32,48},{48,64},{64,80},{80,96},{96,112},{112,128},... | collective-permute-start | bytes 294920 | tf_op jit(solution)/shard_map/ppermute | solution.py:310
  44.1 2.0 %collective-permute-start.11 = (bf16[48,8,128]{2,1,0:T(8,128)(2,1)S(1)}, bf16[48,8,128]{2,1,0:T(8,128)(2,1)S(1)}, u32[]{:S(2)}, u32[]{:S(2)}) collective-permute-start(bf16[48,8,128]{2,1,0:T(8,128)(2,1)S(1)} %get-tuple-element.82), channel_id=1, source_target_pairs={{0,240},{16,0},{32,16},{48,32},{64,48},{80,64},{96,80},{112,96},{1... | collective-permute-start | bytes 294920 | tf_op jit(solution)/shard_map/ppermute | solution.py:310
  46.1 1.0 %local2.1 = (f32[64,8,128]{2,1,0:T(8,128)S(1)}, bf16[64,8,128]{2,1,0:T(8,128)(2,1)S(1)}, f32[8,128]{1,0:T(8,128)S(1)}) custom-call(s32[544]{0:T(1024)S(4)} %get-tuple-element.52.refs_0_, bf16[64,640,128]{2,1,0:T(8,128)(2,1)S(1)} %second_half.1.turned.refs_1_, bf16[64,8,128]{2,1,0:T(8,128)(2,1)S(1)} %get-tuple-element.76.refs_2_, ...), custom_call_target="tpu_custom_call" | custom-call | tf_op jit(solution)/shard_map/local2/pallas_call | solution.py:369
  47.2 1.0 %collective-permute-done.11.refs_6_ = bf16[48,8,128]{2,1,0:T(8,128)(2,1)S(1)} collective-permute-done((bf16[48,8,128]{2,1,0:T(8,128)(2,1)S(1)}, bf16[48,8,128]{2,1,0:T(8,128)(2,1)S(1)}, u32[]{:S(2)}, u32[]{:S(2)}) %collective-permute-start.11) | collective-permute-done | bytes 98336 | tf_op jit(solution)/shard_map/ppermute | solution.py:310
  48.1 1.1 %ghost2.1 = (f32[64,8,128]{2,1,0:T(8,128)S(1)}, bf16[64,8,128]{2,1,0:T(8,128)(2,1)S(1)}, bf16[48,8,128]{2,1,0:T(8,128)(2,1)S(1)}, bf16[48,8,128]{2,1,0:T(8,128)(...) custom-call(s32[544]{0:T(1024)S(4)} %get-tuple-element.52.refs_0_, ...), custom_call_target="tpu_custom_call", output_to_operand_aliasing={{0}: (11, {}), {1}: (12, {})} | custom-call | tf_op jit(solution)/shard_map/ghost2/pallas_call | solution.py:411
  49.4 5.2 %collective-permute-start.13 = (bf16[48,8,128]{2,1,0:T(8,128)(2,1)S(1)}, bf16[48,8,128]{2,1,0:T(8,128)(2,1)S(1)}, u32[]{:S(2)}, u32[]{:S(2)}) collective-permute-start(bf16[48,8,128]{2,1,0:T(8,128)(2,1)S(1)} %get-tuple-element.90), channel_id=1, source_target_pairs={{0,15},{1,0},{2,1},{3,2},{4,3},{5,4},{6,5},{7,6},{8,7},{9,8},{10,9... | collective-permute-start | bytes 294920 | tf_op jit(solution)/shard_map/ppermute | solution.py:310
  54.5 1.9 %collective-permute-done.12.refs_0_.refs_3_ = bf16[48,8,128]{2,1,0:T(8,128)(2,1)S(1)} collective-permute-done((bf16[48,8,128]{2,1,0:T(8,128)(2,1)S(1)}, bf16[48,8,128]{2,1,0:T(8,128)(2,1)S(1)}, u32[]{:S(2)}, u32[]{:S(2)}) %collective-permute-start.12) | collective-permute-done | bytes 98336 | tf_op jit(solution)/shard_map/ppermute | solution.py:310
  56.5 0.9 collective-permute-start.14
  57.4 3.3 %collective-permute-start.15 = (bf16[48,8,128]{2,1,0:T(8,128)(2,1)S(1)}, bf16[48,8,128]{2,1,0:T(8,128)(2,1)S(1)}, u32[]{:S(2)}, u32[]{:S(2)}) collective-permute-start(bf16[48,8,128]{2,1,0:T(8,128)(2,1)S(1)} %get-tuple-element.94), channel_id=1, source_target_pairs={{0,240},{16,0},{32,16},{48,32},{64,48},{80,64},{96,80},{112,96},{1... | collective-permute-start | bytes 294920 | tf_op jit(solution)/shard_map/ppermute | solution.py:310
  60.6 1.1 %local3.1 = (f32[64,8,128]{2,1,0:T(8,128)S(1)}, bf16[64,8,128]{2,1,0:T(8,128)(2,1)S(1)}, f32[8,128]{1,0:T(8,128)S(1)}) custom-call(s32[544]{0:T(1024)S(4)} %get-tuple-element.52.refs_0_, bf16[64,640,128]{2,1,0:T(8,128)(2,1)S(1)} %second_half.1.turned.refs_1_, bf16[64,8,128]{2,1,0:T(8,128)(2,1)S(1)} %get-tuple-element.88.refs_2_, ...), custom_call_target="tpu_custom_call" | custom-call | tf_op jit(solution)/shard_map/local3/pallas_call | solution.py:369
  61.7 1.2 %ghost3.1 = (f32[64,8,128]{2,1,0:T(8,128)S(1)}, bf16[64,8,128]{2,1,0:T(8,128)(2,1)S(1)}, f32[256,128]{1,0:T(8,128)S(1)}) custom-call(s32[544]{0:T(1024)S(4)} %get-tuple-element.52.refs_0_, bf16[64,640,128]{2,1,0:T(8,128)(2,1)S(1)} %second_half.1.turned.refs_1_, ...), custom_call_target="tpu_custom_call", output_to_operand_aliasing={{0}: (12, {}), {1}: (13, {})} | custom-call | tf_op jit(solution)/shard_map/ghost3/pallas_call | solution.py:411
  62.9 29.2 %all_to_all.11 = f32[256,1,128]{2,1,0:T(1,128)S(1)} all-to-all(f32[256,1,128]{2,1,0:T(1,128)S(1)} %bitcast.7), channel_id=1, replica_groups=mesh['gx'=16,'gy'=16] {'gx','gy'}, dimensions={0} | all-to-all | bytes 262144 | tf_op jit(solution)/shard_map/all_to_all | solution.py:428
  92.2 1.2 %finish.1 = (f32[64,8,128]{2,1,0:T(8,128)}, f32[64,8,128]{2,1,0:T(8,128)}) custom-call(f32[256,128]{1,0:T(8,128)S(1)} %bitcast.6, f32[64,8,128]{2,1,0:T(8,128)S(1)} %get-tuple-element.62.b0.refs_4_.refs_8_, f32[64,8,128]{2,1,0:T(8,128)S(1)} %get-tuple-element.72.refs_5_.refs_9_.b1, f32[64,8,128]{2,1,0:T(8,128)S(1)} %get-tuple-element.84.refs_6_.refs_10_.b2, ...), custom_call_target="tpu_custom_call" | custom-call | tf_op jit(solution)/shard_map/finish/pallas_call | solution.py:429
  (21 shorter events, 0.3 us)
Async XLA Ops:
  2.5 9.1 %collective-permute-start = (bf16[48,8,128]{2,1,0:T(8,128)(2,1)S(1)}, bf16[48,8,128]{2,1,0:T(8,128)(2,1)S(1)}, u32[]{:S(2)}, u32[]{:S(2)}) collective-permute-start(bf16[48,8,128]{2,1,0:T(8,128)(2,1)S(1)} %get-tuple-element.55), channel_id=1, source_target_pairs={{0,1},{1,2},{2,3},{3,4},{4,5},{5,6},{6,7},{7,8},{8,9},{9,10},{10,1... | collective-permute-start | bytes 294920 | tf_op jit(solution)/shard_map/ppermute | solution.py:310
  4.7 6.9 %collective-permute-start.1 = (bf16[48,8,128]{2,1,0:T(8,128)(2,1)S(1)}, bf16[48,8,128]{2,1,0:T(8,128)(2,1)S(1)}, u32[]{:S(2)}, u32[]{:S(2)}) collective-permute-start(bf16[48,8,128]{2,1,0:T(8,128)(2,1)S(1)} %get-tuple-element.56), channel_id=1, source_target_pairs={{0,15},{1,0},{2,1},{3,2},{4,3},{5,4},{6,5},{7,6},{8,7},{9,8},{10,9... | collective-permute-start | bytes 294920 | tf_op jit(solution)/shard_map/ppermute | solution.py:310
  11.6 6.0 %collective-permute-start.2 = (bf16[48,8,128]{2,1,0:T(8,128)(2,1)S(1)}, bf16[48,8,128]{2,1,0:T(8,128)(2,1)S(1)}, u32[]{:S(2)}, u32[]{:S(2)}) collective-permute-start(bf16[48,8,128]{2,1,0:T(8,128)(2,1)S(1)} %get-tuple-element.60), channel_id=1, source_target_pairs={{0,16},{16,32},{32,48},{48,64},{64,80},{80,96},{96,112},{112,128},... | collective-permute-start | bytes 294920 | tf_op jit(solution)/shard_map/ppermute | solution.py:310
  14.2 4.3 %collective-permute-start.3 = (bf16[48,8,128]{2,1,0:T(8,128)(2,1)S(1)}, bf16[48,8,128]{2,1,0:T(8,128)(2,1)S(1)}, u32[]{:S(2)}, u32[]{:S(2)}) collective-permute-start(bf16[48,8,128]{2,1,0:T(8,128)(2,1)S(1)} %get-tuple-element.61), channel_id=1, source_target_pairs={{0,240},{16,0},{32,16},{48,32},{64,48},{80,64},{96,80},{112,96},{1... | collective-permute-start | bytes 294920 | tf_op jit(solution)/shard_map/ppermute | solution.py:310
  14.4 4.1 %copy-start = (s32[1,9,16]{2,0,1:T(1,128)S(1)}, s32[1,9,16]{2,0,1:T(1,128)}, u32[]{:S(2)}) copy-start(s32[1,9,16]{2,0,1:T(1,128)} %param.10) | copy-start | bytes 1732
  14.4 4.1 %copy-start.1 = (s32[64,4]{0,1:T(4,128)S(1)}, s32[64,4]{0,1:T(4,128)}, u32[]{:S(2)}) copy-start(s32[64,4]{0,1:T(4,128)} %param.9) | copy-start | bytes 3076
  21.2 6.9 %collective-permute-start.4 = (bf16[48,8,128]{2,1,0:T(8,128)(2,1)S(1)}, bf16[48,8,128]{2,1,0:T(8,128)(2,1)S(1)}, u32[]{:S(2)}, u32[]{:S(2)}) collective-permute-start(bf16[48,8,128]{2,1,0:T(8,128)(2,1)S(1)} %get-tuple-element.64), channel_id=1, source_target_pairs={{0,1},{1,2},{2,3},{3,4},{4,5},{5,6},{6,7},{7,8},{8,9},{9,10},{10,1... | collective-permute-start | bytes 294920 | tf_op jit(solution)/shard_map/ppermute | solution.py:310
  21.3 6.8 %collective-permute-start.5 = (bf16[48,8,128]{2,1,0:T(8,128)(2,1)S(1)}, bf16[48,8,128]{2,1,0:T(8,128)(2,1)S(1)}, u32[]{:S(2)}, u32[]{:S(2)}) collective-permute-start(bf16[48,8,128]{2,1,0:T(8,128)(2,1)S(1)} %get-tuple-element.65), channel_id=1, source_target_pairs={{0,15},{1,0},{2,1},{3,2},{4,3},{5,4},{6,5},{7,6},{8,7},{9,8},{10,9... | collective-permute-start | bytes 294920 | tf_op jit(solution)/shard_map/ppermute | solution.py:310
  28.1 4.6 %collective-permute-start.6 = (bf16[48,8,128]{2,1,0:T(8,128)(2,1)S(1)}, bf16[48,8,128]{2,1,0:T(8,128)(2,1)S(1)}, u32[]{:S(2)}, u32[]{:S(2)}) collective-permute-start(bf16[48,8,128]{2,1,0:T(8,128)(2,1)S(1)} %get-tuple-element.69), channel_id=1, source_target_pairs={{0,16},{16,32},{32,48},{48,64},{64,80},{80,96},{96,112},{112,128},... | collective-permute-start | bytes 294920 | tf_op jit(solution)/shard_map/ppermute | solution.py:310
  30.9 4.0 %collective-permute-start.7 = (bf16[48,8,128]{2,1,0:T(8,128)(2,1)S(1)}, bf16[48,8,128]{2,1,0:T(8,128)(2,1)S(1)}, u32[]{:S(2)}, u32[]{:S(2)}) collective-permute-start(bf16[48,8,128]{2,1,0:T(8,128)(2,1)S(1)} %get-tuple-element.70), channel_id=1, source_target_pairs={{0,240},{16,0},{32,16},{48,32},{64,48},{80,64},{96,80},{112,96},{1... | collective-permute-start | bytes 294920 | tf_op jit(solution)/shard_map/ppermute | solution.py:310
  36.0 7.1 %collective-permute-start.8 = (bf16[48,8,128]{2,1,0:T(8,128)(2,1)S(1)}, bf16[48,8,128]{2,1,0:T(8,128)(2,1)S(1)}, u32[]{:S(2)}, u32[]{:S(2)}) collective-permute-start(bf16[48,8,128]{2,1,0:T(8,128)(2,1)S(1)} %get-tuple-element.77), channel_id=1, source_target_pairs={{0,1},{1,2},{2,3},{3,4},{4,5},{5,6},{6,7},{7,8},{8,9},{9,10},{10,1... | collective-permute-start | bytes 294920 | tf_op jit(solution)/shard_map/ppermute | solution.py:310
  36.1 7.0 %collective-permute-start.9 = (bf16[48,8,128]{2,1,0:T(8,128)(2,1)S(1)}, bf16[48,8,128]{2,1,0:T(8,128)(2,1)S(1)}, u32[]{:S(2)}, u32[]{:S(2)}) collective-permute-start(bf16[48,8,128]{2,1,0:T(8,128)(2,1)S(1)} %get-tuple-element.78), channel_id=1, source_target_pairs={{0,15},{1,0},{2,1},{3,2},{4,3},{5,4},{6,5},{7,6},{8,7},{9,8},{10,9... | collective-permute-start | bytes 294920 | tf_op jit(solution)/shard_map/ppermute | solution.py:310
  43.1 4.0 %collective-permute-start.10 = (bf16[48,8,128]{2,1,0:T(8,128)(2,1)S(1)}, bf16[48,8,128]{2,1,0:T(8,128)(2,1)S(1)}, u32[]{:S(2)}, u32[]{:S(2)}) collective-permute-start(bf16[48,8,128]{2,1,0:T(8,128)(2,1)S(1)} %get-tuple-element.81), channel_id=1, source_target_pairs={{0,16},{16,32},{32,48},{48,64},{64,80},{80,96},{96,112},{112,128},... | collective-permute-start | bytes 294920 | tf_op jit(solution)/shard_map/ppermute | solution.py:310
  44.1 4.0 %collective-permute-start.11 = (bf16[48,8,128]{2,1,0:T(8,128)(2,1)S(1)}, bf16[48,8,128]{2,1,0:T(8,128)(2,1)S(1)}, u32[]{:S(2)}, u32[]{:S(2)}) collective-permute-start(bf16[48,8,128]{2,1,0:T(8,128)(2,1)S(1)} %get-tuple-element.82), channel_id=1, source_target_pairs={{0,240},{16,0},{32,16},{48,32},{64,48},{80,64},{96,80},{112,96},{1... | collective-permute-start | bytes 294920 | tf_op jit(solution)/shard_map/ppermute | solution.py:310
  49.3 7.2 %collective-permute-start.12 = (bf16[48,8,128]{2,1,0:T(8,128)(2,1)S(1)}, bf16[48,8,128]{2,1,0:T(8,128)(2,1)S(1)}, u32[]{:S(2)}, u32[]{:S(2)}) collective-permute-start(bf16[48,8,128]{2,1,0:T(8,128)(2,1)S(1)} %get-tuple-element.89), channel_id=1, source_target_pairs={{0,1},{1,2},{2,3},{3,4},{4,5},{5,6},{6,7},{7,8},{8,9},{9,10},{10,1... | collective-permute-start | bytes 294920 | tf_op jit(solution)/shard_map/ppermute | solution.py:310
  49.4 7.1 %collective-permute-start.13 = (bf16[48,8,128]{2,1,0:T(8,128)(2,1)S(1)}, bf16[48,8,128]{2,1,0:T(8,128)(2,1)S(1)}, u32[]{:S(2)}, u32[]{:S(2)}) collective-permute-start(bf16[48,8,128]{2,1,0:T(8,128)(2,1)S(1)} %get-tuple-element.90), channel_id=1, source_target_pairs={{0,15},{1,0},{2,1},{3,2},{4,3},{5,4},{6,5},{7,6},{8,7},{9,8},{10,9... | collective-permute-start | bytes 294920 | tf_op jit(solution)/shard_map/ppermute | solution.py:310
  56.5 5.2 %collective-permute-start.14 = (bf16[48,8,128]{2,1,0:T(8,128)(2,1)S(1)}, bf16[48,8,128]{2,1,0:T(8,128)(2,1)S(1)}, u32[]{:S(2)}, u32[]{:S(2)}) collective-permute-start(bf16[48,8,128]{2,1,0:T(8,128)(2,1)S(1)} %get-tuple-element.93), channel_id=1, source_target_pairs={{0,16},{16,32},{32,48},{48,64},{64,80},{80,96},{96,112},{112,128},... | collective-permute-start | bytes 294920 | tf_op jit(solution)/shard_map/ppermute | solution.py:310
  57.4 4.3 %collective-permute-start.15 = (bf16[48,8,128]{2,1,0:T(8,128)(2,1)S(1)}, bf16[48,8,128]{2,1,0:T(8,128)(2,1)S(1)}, u32[]{:S(2)}, u32[]{:S(2)}) collective-permute-start(bf16[48,8,128]{2,1,0:T(8,128)(2,1)S(1)} %get-tuple-element.94), channel_id=1, source_target_pairs={{0,240},{16,0},{32,16},{48,32},{64,48},{80,64},{96,80},{112,96},{1... | collective-permute-start | bytes 294920 | tf_op jit(solution)/shard_map/ppermute | solution.py:310

commit v4 on v3

--- a/solution.py
+++ b/solution.py
@@ -18,9 +18,7 @@
 NOTHING = CAP + 4 * SEND
 UNROLL = 16
 BLOCKS = FACES + 1
-CHUNK = 8
-HALF_CAP = CAP // 2
-CHUNKS = HALF_CAP // CHUNK
+QUARTER = CAP // 4
 
 IN_VMEM = pl.BlockSpec(memory_space=pltpu.VMEM)
 IN_SMEM = pl.BlockSpec(memory_space=pltpu.SMEM)
@@ -66,13 +64,19 @@
 
 
 def start_kernel(
-    send_slots, counts, right_sides, basis, rounded, up, down, next_row, last_row
+    send_slots, counts, right_sides, diag, face, basis, rounded, up, down, next_row,
+    last_row, diag_first, face_first, arrived,
 ):
+    first = fetching(0, diag, face, diag_first, face_first, arrived)
+    for copy in first:
+        copy.start()
     element = lax.broadcasted_iota(jnp.int32, basis.shape, 0)
     live = jnp.where(element < counts[0], right_sides[...], 0.0)
     basis[...] = live
     rounded[...] = live.astype(jnp.bfloat16)
     pack(listed(send_slots), rounded, up, down, next_row, last_row)
+    for copy in first:
+        copy.wait()
 
 
 def plan_kernel(neighbours, send_slots, table, done):
@@ -94,39 +98,52 @@
     done[...] = jnp.zeros_like(done)
 
 
-def transpose_blocks(base, diag, face, turned, diag_here, face_here, arrived):
-    def fetch(c):
-        here = pl.ds(c * CHUNK, CHUNK)
-        there = pl.ds(base + c * CHUNK, CHUNK)
-        return (
-            pltpu.make_async_copy(diag.at[there], diag_here.at[here], arrived.at[c, 0]),
-            pltpu.make_async_copy(face.at[there], face_here.at[here], arrived.at[c, 1]),
-        )
-
-    for c in range(CHUNKS):
-        for copy in fetch(c):
-            copy.start()
-    for c in range(CHUNKS):
-        for copy in fetch(c):
-            copy.wait()
-
-        def element(at, carry, c=c):
-            e = c * CHUNK + at
-            turned[base + e, 0:ROWS] = diag_here[e].T
-            for f in range(FACES):
-                turned[base + e, (f + 1) * ROWS : (f + 2) * ROWS] = face_here[e, f].T
-            return carry
-
-        lax.fori_loop(0, CHUNK, element, 0, unroll=4)
-
-
-def first_half_kernel(diag, face, turned, done, diag_here, face_here, arrived):
-    transpose_blocks(0, diag, face, turned, diag_here, face_here, arrived)
+def fetching(first, diag, face, diag_here, face_here, arrived):
+    there = pl.ds(first, QUARTER)
+    return (
+        pltpu.make_async_copy(diag.at[there], diag_here, arrived.at[0]),
+        pltpu.make_async_copy(face.at[there], face_here, arrived.at[1]),
+    )
+
+
+def transpose_quarter(first, diag_here, face_here, turned):
+    def element(at, carry):
+        e = first + at
+        turned[e, 0:ROWS] = diag_here[at].T
+        for f in range(FACES):
+            turned[e, (f + 1) * ROWS : (f + 2) * ROWS] = face_here[at, f].T
+        return carry
+
+    lax.fori_loop(0, QUARTER, element, 0, unroll=8)
+
+
+def first_half_kernel(
+    diag, face, diag_first, face_first, turned, diag_third, face_third, done,
+    diag_here, face_here, arrived, arrived_third,
+):
+    second = fetching(QUARTER, diag, face, diag_here, face_here, arrived)
+    third = fetching(2 * QUARTER, diag, face, diag_third, face_third, arrived_third)
+    for copy in second + third:
+        copy.start()
+    transpose_quarter(0, diag_first, face_first, turned)
+    for copy in second:
+        copy.wait()
+    transpose_quarter(QUARTER, diag_here, face_here, turned)
     done[...] = jnp.zeros_like(done)
-
-
-def second_half_kernel(diag, face, before, turned, diag_here, face_here, arrived):
-    transpose_blocks(HALF_CAP, diag, face, turned, diag_here, face_here, arrived)
+    for copy in third:
+        copy.wait()
+
+
+def second_half_kernel(
+    diag, face, diag_third, face_third, before, turned, diag_here, face_here, arrived
+):
+    fourth = fetching(3 * QUARTER, diag, face, diag_here, face_here, arrived)
+    for copy in fourth:
+        copy.start()
+    transpose_quarter(2 * QUARTER, diag_third, face_third, turned)
+    for copy in fourth:
+        copy.wait()
+    transpose_quarter(3 * QUARTER, diag_here, face_here, turned)
 
 
 def relay_kernel(*refs):
@@ -270,24 +287,28 @@
         return jnp.broadcast_to(total, (8, ROWS))
 
     factor = {}
+    inverse = []
     for i in range(POWERS):
         for j in range(i + 1):
             value = entry(i + 1, j + 1)
             for k in range(j):
                 value = value - factor[i, k] * factor[j, k]
-            factor[i, j] = jnp.sqrt(value) if i == j else value / factor[j, j]
+            if i == j:
+                inverse.append(1.0 / jnp.sqrt(value))
+            else:
+                factor[i, j] = value * inverse[j]
     forward = []
     for i in range(POWERS):
         value = entry(0, i + 1)
         for k in range(i):
             value = value - factor[i, k] * forward[k]
-        forward.append(value / factor[i, i])
+        forward.append(value * inverse[i])
     weights = [None] * POWERS
     for i in reversed(range(POWERS)):
         value = forward[i]
         for k in range(i + 1, POWERS):
             value = value - factor[k, i] * weights[k]
-        weights[i] = value / factor[i, i]
+        weights[i] = value * inverse[i]
     basis = (b0, b1, b2, b3, b4)
 
     def several(step, carry):
@@ -324,19 +345,20 @@
     rows_shape = jax.ShapeDtypeStruct((GROUPS, ROWS), jnp.float32)
     turned_shape = pltpu.VMEM((CAP, BLOCKS * ROWS, ROWS), half)
     lookup = pltpu.VMEM((LOOKUP, 8, ROWS), half)
-    landing = [
-        pltpu.VMEM((HALF_CAP, ROWS, ROWS), half),
-        pltpu.VMEM((HALF_CAP, FACES, ROWS, ROWS), half),
-        pltpu.SemaphoreType.DMA((CHUNKS, 2)),
+    quarter = [
+        pltpu.VMEM((QUARTER, ROWS, ROWS), half),
+        pltpu.VMEM((QUARTER, FACES, ROWS, ROWS), half),
     ]
-    first, rounded, up, down, next_row, last_row = pl.pallas_call(
+    arrived = pltpu.SemaphoreType.DMA((2,))
+    first, rounded, up, down, next_row, last_row, *blocks = pl.pallas_call(
         start_kernel,
         name="start",
-        in_specs=[IN_SMEM, IN_SMEM, IN_VMEM],
-        out_specs=[IN_VMEM] * 6,
-        out_shape=[full, narrow] + packets,
+        in_specs=[IN_SMEM, IN_SMEM, IN_VMEM, IN_HBM, IN_HBM],
+        out_specs=[IN_VMEM] * 8,
+        out_shape=[full, narrow] + packets + quarter,
+        scratch_shapes=[arrived],
         compiler_params=params(),
-    )(in_place(send_slots), counts, in_place(right_sides))
+    )(in_place(send_slots), counts, in_place(right_sides), diag_blocks, face_blocks)
     basis = [first]
     gram = None
     for power in range(POWERS):
@@ -345,15 +367,15 @@
         from_up = shifted(down, "gy", -1)
         after = ()
         if power == 0:
-            turned, done = pl.pallas_call(
+            turned, *blocks, done = pl.pallas_call(
                 first_half_kernel,
                 name="first_half",
-                in_specs=[IN_HBM] * 2,
-                out_specs=[IN_VMEM] * 2,
-                out_shape=[turned_shape, gram_shape],
-                scratch_shapes=landing,
-                compiler_params=params(),
-            )(diag_blocks, face_blocks)
+                in_specs=[IN_HBM] * 2 + [IN_VMEM] * 2,
+                out_specs=[IN_VMEM] * 4,
+                out_shape=[turned_shape] + quarter + [gram_shape],
+                scratch_shapes=quarter + [arrived, arrived],
+                compiler_params=params(),
+            )(diag_blocks, face_blocks, *blocks)
             after = (done,)
         elif power == 1:
             table, done = pl.pallas_call(
@@ -390,13 +412,13 @@
             turned = pl.pallas_call(
                 second_half_kernel,
                 name="second_half",
-                in_specs=[IN_HBM, IN_HBM, IN_VMEM],
+                in_specs=[IN_HBM] * 2 + [IN_VMEM] * 3,
                 out_specs=IN_VMEM,
                 out_shape=turned_shape,
-                scratch_shapes=landing,
-                input_output_aliases={2: 0},
-                compiler_params=params(),
-            )(diag_blocks, face_blocks, turned)
+                scratch_shapes=quarter + [arrived],
+                input_output_aliases={4: 0},
+                compiler_params=params(),
+            )(diag_blocks, face_blocks, *blocks, turned)
             outs = pl.pallas_call(
                 whole_kernel,
                 name="whole",

time: 93.5 us -> 94 us (level)
    pallas_call x1, Pallas kernels: 1.18 us -> 2.75 us  [per_device(): pl.pallas_call(start_kernel, name='start', in_specs=[IN_SMEM, IN_SMEM, IN...]
  transfers between devices with their start and end apart: 16 -> 16, of which waited for: 6 -> 6; matrix products, arithmetic and copies ran while one was open for 0% -> 0% of each run, Pallas kernels for 12% -> 11%
where the time goes in v4:
time: 94 us; the launch traced here: 93.8 us
  starting transfers between devices  35.3 us (38%)
  blocking collectives  29.2 us (31%)
  Pallas kernels  20.1 us (21%)
  waiting for transfers between devices  7.81 us (8%)
  between operations  1.43 us (2%)
    ppermute x16, starting transfers between devices, shifted(): lax.ppermute(block, axis, [(i, (i + distance) % SIDE) for i in range(SIDE)])  35.3 us
    all_to_all x1, blocking collectives, per_device(): gathered = lax.all_to_all(gram, ('gx', 'gy'), 0, 0, tiled=True)  29.2 us
    ppermute x16, waiting for transfers between devices, shifted(): lax.ppermute(block, axis, [(i, (i + distance) % SIDE) for i in range(SIDE)])  7.81 us
    pallas_call x3, Pallas kernels, per_device(): pl.pallas_call(functools.partial(ghost_kernel, power), name=f'ghost{power...  3.48 us
    pallas_call x3, Pallas kernels, per_device(): pl.pallas_call(functools.partial(local_kernel, power), name=f'local{power...  3.14 us
    pallas_call x1, Pallas kernels, per_device(): pl.pallas_call(start_kernel, name='start', in_specs=[IN_SMEM, IN_SMEM, IN...  2.75 us
    pallas_call x1, Pallas kernels, per_device(): pl.pallas_call(first_half_kernel, name='first_half', in_specs=[IN_HBM] *...  2.75 us
    pallas_call x1, Pallas kernels, per_device(): pl.pallas_call(whole_kernel, name='whole', in_specs=[IN_SMEM] * 2 + [IN_V...  2.69 us
  transfers between devices with their start and end apart: 16, of which 6 were waited for; matrix products, arithmetic and copies ran while one was open for 0% of the time, Pallas kernels for 11%

profile of v4, /device:TPU:1, one launch (start us, length us, event | category | flops | bytes accessed | tf_op | source)
XLA Modules:
  0.0 93.8 jit_solution(14573301727686733379)
XLA Ops:
  1.3 2.7 %start.1 = (f32[64,8,128]{2,1,0:T(8,128)S(1)}, bf16[64,8,128]{2,1,0:T(8,128)(2,1)S(1)}, bf16[48,8,128]{2,1,0:T(8,128)(2,1)S(1)}, bf16[48,8,128]{2,1,0:T(8,128)(2...) custom-call(s32[9,1,16]{2,1,0:T(1,128)} %bitcast.8, ...), custom_call_target="tpu_custom_call" | custom-call | tf_op jit(solution)/shard_map/start/pallas_call | solution.py:353
  4.0 2.2 %collective-permute-start = (bf16[48,8,128]{2,1,0:T(8,128)(2,1)S(1)}, bf16[48,8,128]{2,1,0:T(8,128)(2,1)S(1)}, u32[]{:S(2)}, u32[]{:S(2)}) collective-permute-start(bf16[48,8,128]{2,1,0:T(8,128)(2,1)S(1)} %get-tuple-element.63), channel_id=1, source_target_pairs={{0,1},{1,2},{2,3},{3,4},{4,5},{5,6},{6,7},{7,8},{8,9},{9,10},{10,1... | collective-permute-start | bytes 294920 | tf_op jit(solution)/shard_map/ppermute | solution.py:331
  6.2 3.7 %collective-permute-start.1 = (bf16[48,8,128]{2,1,0:T(8,128)(2,1)S(1)}, bf16[48,8,128]{2,1,0:T(8,128)(2,1)S(1)}, u32[]{:S(2)}, u32[]{:S(2)}) collective-permute-start(bf16[48,8,128]{2,1,0:T(8,128)(2,1)S(1)} %get-tuple-element.64), channel_id=1, source_target_pairs={{0,15},{1,0},{2,1},{3,2},{4,3},{5,4},{6,5},{7,6},{8,7},{9,8},{10,9... | collective-permute-start | bytes 294920 | tf_op jit(solution)/shard_map/ppermute | solution.py:331
  10.0 2.7 %first_half.1 = (bf16[64,640,128]{2,1,0:T(8,128)(2,1)S(1)}, bf16[16,128,128]{2,1,0:T(8,128)(2,1)S(1)}, bf16[16,4,128,128]{3,2,1,0:T(8,128)(2,1)S(1)}, f32[8,128]{1,0:T(8,128)S(1)}) custom-call(bf16[64,128,128]{2,1,0:T(8,128)(2,1)} %diag.5, bf16[64,4,128,128]{3,2,1,0:T(8,128)(2,1)} %face.5, bf16[16,128,128]{2,1,0:T(8,128)(2,1)S(1)} %get-tuple-element.57.diag_first, ...), custom_call_target="tpu_custom_call" | custom-call | tf_op jit(solution)/shard_map/first_half/pallas_call | solution.py:370
  12.8 2.5 %collective-permute-start.2 = (bf16[48,8,128]{2,1,0:T(8,128)(2,1)S(1)}, bf16[48,8,128]{2,1,0:T(8,128)(2,1)S(1)}, u32[]{:S(2)}, u32[]{:S(2)}) collective-permute-start(bf16[48,8,128]{2,1,0:T(8,128)(2,1)S(1)} %get-tuple-element.68), channel_id=1, source_target_pairs={{0,16},{16,32},{32,48},{48,64},{64,80},{80,96},{96,112},{112,128},... | collective-permute-start | bytes 294920 | tf_op jit(solution)/shard_map/ppermute | solution.py:331
  15.3 0.2 collective-permute-start.3
  15.5 2.6 %second_half.1.turned.refs_1_ = bf16[64,640,128]{2,1,0:T(8,128)(2,1)S(1)} custom-call(bf16[64,128,128]{2,1,0:T(8,128)(2,1)} %diag.5, bf16[64,4,128,128]{3,2,1,0:T(8,128)(2,1)} %face.5, bf16[16,128,128]{2,1,0:T(8,128)(2,1)S(1)} %get-tuple-element.59.diag_third, ...), custom_call_target="tpu_custom_call", output_to_operand_aliasing={{}: (4, {})} | custom-call | tf_op jit(solution)/shard_map/second_half/pallas_call | solution.py:412
  18.1 1.5 %collective-permute-done.3.from_next = bf16[48,8,128]{2,1,0:T(8,128)(2,1)S(1)} collective-permute-done((bf16[48,8,128]{2,1,0:T(8,128)(2,1)S(1)}, bf16[48,8,128]{2,1,0:T(8,128)(2,1)S(1)}, u32[]{:S(2)}, u32[]{:S(2)}) %collective-permute-start.3) | collective-permute-done | bytes 98336 | tf_op jit(solution)/shard_map/ppermute | solution.py:331
  19.6 2.7 %whole.1 = (f32[64,8,128]{2,1,0:T(8,128)S(1)}, bf16[64,8,128]{2,1,0:T(8,128)(2,1)S(1)}, bf16[48,8,128]{2,1,0:T(8,128)(2,1)S(1)}, bf16[48,8,128]{2,1,0:T(8,128)(2...) custom-call(s32[4,64]{1,0:T(4,128)S(1)} %bitcast.11, ...), custom_call_target="tpu_custom_call" | custom-call | tf_op jit(solution)/shard_map/whole/pallas_call | solution.py:422
  22.4 5.0 %collective-permute-start.5 = (bf16[48,8,128]{2,1,0:T(8,128)(2,1)S(1)}, bf16[48,8,128]{2,1,0:T(8,128)(2,1)S(1)}, u32[]{:S(2)}, u32[]{:S(2)}) collective-permute-start(bf16[48,8,128]{2,1,0:T(8,128)(2,1)S(1)} %get-tuple-element.73), channel_id=1, source_target_pairs={{0,15},{1,0},{2,1},{3,2},{4,3},{5,4},{6,5},{7,6},{8,7},{9,8},{10,9... | collective-permute-start | bytes 294920 | tf_op jit(solution)/shard_map/ppermute | solution.py:331
  27.4 1.5 %plan.1 = (s32[544]{0:T(1024)S(4)}, f32[8,128]{1,0:T(8,128)S(1)}) custom-call(s32[4,64]{1,0:T(4,128)S(1)} %bitcast.12, s32[9,1,16]{2,1,0:T(1,128)S(1)} %bitcast.10), custom_call_target="tpu_custom_call" | custom-call | tf_op jit(solution)/shard_map/plan/pallas_call | solution.py:381
  28.9 0.4 collective-permute-done.4.refs_0_.refs_3_
  29.3 1.4 %collective-permute-start.6 = (bf16[48,8,128]{2,1,0:T(8,128)(2,1)S(1)}, bf16[48,8,128]{2,1,0:T(8,128)(2,1)S(1)}, u32[]{:S(2)}, u32[]{:S(2)}) collective-permute-start(bf16[48,8,128]{2,1,0:T(8,128)(2,1)S(1)} %get-tuple-element.77), channel_id=1, source_target_pairs={{0,16},{16,32},{32,48},{48,64},{64,80},{80,96},{96,112},{112,128},... | collective-permute-start | bytes 294920 | tf_op jit(solution)/shard_map/ppermute | solution.py:331
  30.7 1.5 %collective-permute-start.7 = (bf16[48,8,128]{2,1,0:T(8,128)(2,1)S(1)}, bf16[48,8,128]{2,1,0:T(8,128)(2,1)S(1)}, u32[]{:S(2)}, u32[]{:S(2)}) collective-permute-start(bf16[48,8,128]{2,1,0:T(8,128)(2,1)S(1)} %get-tuple-element.78), channel_id=1, source_target_pairs={{0,240},{16,0},{32,16},{48,32},{64,48},{80,64},{96,80},{112,96},{1... | collective-permute-start | bytes 294920 | tf_op jit(solution)/shard_map/ppermute | solution.py:331
  32.2 1.0 %local1.1 = (f32[64,8,128]{2,1,0:T(8,128)S(1)}, bf16[64,8,128]{2,1,0:T(8,128)(2,1)S(1)}, f32[8,128]{1,0:T(8,128)S(1)}) custom-call(s32[544]{0:T(1024)S(4)} %get-tuple-element.56.refs_0_, bf16[64,640,128]{2,1,0:T(8,128)(2,1)S(1)} %second_half.1.turned.refs_1_, bf16[64,8,128]{2,1,0:T(8,128)(2,1)S(1)} %get-tuple-element.71.refs_2_, ...), custom_call_target="tpu_custom_call" | custom-call | tf_op jit(solution)/shard_map/local1/pallas_call | solution.py:391
  33.2 1.5 %collective-permute-done.7.refs_6_ = bf16[48,8,128]{2,1,0:T(8,128)(2,1)S(1)} collective-permute-done((bf16[48,8,128]{2,1,0:T(8,128)(2,1)S(1)}, bf16[48,8,128]{2,1,0:T(8,128)(2,1)S(1)}, u32[]{:S(2)}, u32[]{:S(2)}) %collective-permute-start.7) | collective-permute-done | bytes 98336 | tf_op jit(solution)/shard_map/ppermute | solution.py:331
  34.7 1.1 %ghost1.1 = (f32[64,8,128]{2,1,0:T(8,128)S(1)}, bf16[64,8,128]{2,1,0:T(8,128)(2,1)S(1)}, bf16[48,8,128]{2,1,0:T(8,128)(2,1)S(1)}, bf16[48,8,128]{2,1,0:T(8,128)(...) custom-call(s32[544]{0:T(1024)S(4)} %get-tuple-element.56.refs_0_, ...), custom_call_target="tpu_custom_call", output_to_operand_aliasing={{0}: (10, {}), {1}: (11, {})} | custom-call | tf_op jit(solution)/shard_map/ghost1/pallas_call | solution.py:433
  36.0 5.4 %collective-permute-start.9 = (bf16[48,8,128]{2,1,0:T(8,128)(2,1)S(1)}, bf16[48,8,128]{2,1,0:T(8,128)(2,1)S(1)}, u32[]{:S(2)}, u32[]{:S(2)}) collective-permute-start(bf16[48,8,128]{2,1,0:T(8,128)(2,1)S(1)} %get-tuple-element.86), channel_id=1, source_target_pairs={{0,15},{1,0},{2,1},{3,2},{4,3},{5,4},{6,5},{7,6},{8,7},{9,8},{10,9... | collective-permute-start | bytes 294920 | tf_op jit(solution)/shard_map/ppermute | solution.py:331
  41.3 1.9 %collective-permute-done.8.refs_0_.refs_3_ = bf16[48,8,128]{2,1,0:T(8,128)(2,1)S(1)} collective-permute-done((bf16[48,8,128]{2,1,0:T(8,128)(2,1)S(1)}, bf16[48,8,128]{2,1,0:T(8,128)(2,1)S(1)}, u32[]{:S(2)}, u32[]{:S(2)}) %collective-permute-start.8) | collective-permute-done | bytes 98336 | tf_op jit(solution)/shard_map/ppermute | solution.py:331
  43.3 0.9 collective-permute-start.10
  44.2 2.5 %collective-permute-start.11 = (bf16[48,8,128]{2,1,0:T(8,128)(2,1)S(1)}, bf16[48,8,128]{2,1,0:T(8,128)(2,1)S(1)}, u32[]{:S(2)}, u32[]{:S(2)}) collective-permute-start(bf16[48,8,128]{2,1,0:T(8,128)(2,1)S(1)} %get-tuple-element.90), channel_id=1, source_target_pairs={{0,240},{16,0},{32,16},{48,32},{64,48},{80,64},{96,80},{112,96},{1... | collective-permute-start | bytes 294920 | tf_op jit(solution)/shard_map/ppermute | solution.py:331
  46.6 1.0 %local2.1 = (f32[64,8,128]{2,1,0:T(8,128)S(1)}, bf16[64,8,128]{2,1,0:T(8,128)(2,1)S(1)}, f32[8,128]{1,0:T(8,128)S(1)}) custom-call(s32[544]{0:T(1024)S(4)} %get-tuple-element.56.refs_0_, bf16[64,640,128]{2,1,0:T(8,128)(2,1)S(1)} %second_half.1.turned.refs_1_, bf16[64,8,128]{2,1,0:T(8,128)(2,1)S(1)} %get-tuple-element.84.refs_2_, ...), custom_call_target="tpu_custom_call" | custom-call | tf_op jit(solution)/shard_map/local2/pallas_call | solution.py:391
  47.7 0.5 collective-permute-done.11.refs_6_
  48.2 1.1 %ghost2.1 = (f32[64,8,128]{2,1,0:T(8,128)S(1)}, bf16[64,8,128]{2,1,0:T(8,128)(2,1)S(1)}, bf16[48,8,128]{2,1,0:T(8,128)(2,1)S(1)}, bf16[48,8,128]{2,1,0:T(8,128)(...) custom-call(s32[544]{0:T(1024)S(4)} %get-tuple-element.56.refs_0_, ...), custom_call_target="tpu_custom_call", output_to_operand_aliasing={{0}: (11, {}), {1}: (12, {})} | custom-call | tf_op jit(solution)/shard_map/ghost2/pallas_call | solution.py:433
  49.4 5.2 %collective-permute-start.13 = (bf16[48,8,128]{2,1,0:T(8,128)(2,1)S(1)}, bf16[48,8,128]{2,1,0:T(8,128)(2,1)S(1)}, u32[]{:S(2)}, u32[]{:S(2)}) collective-permute-start(bf16[48,8,128]{2,1,0:T(8,128)(2,1)S(1)} %get-tuple-element.98), channel_id=1, source_target_pairs={{0,15},{1,0},{2,1},{3,2},{4,3},{5,4},{6,5},{7,6},{8,7},{9,8},{10,9... | collective-permute-start | bytes 294920 | tf_op jit(solution)/shard_map/ppermute | solution.py:331
  54.7 1.9 %collective-permute-done.12.refs_0_.refs_3_ = bf16[48,8,128]{2,1,0:T(8,128)(2,1)S(1)} collective-permute-done((bf16[48,8,128]{2,1,0:T(8,128)(2,1)S(1)}, bf16[48,8,128]{2,1,0:T(8,128)(2,1)S(1)}, u32[]{:S(2)}, u32[]{:S(2)}) %collective-permute-start.12) | collective-permute-done | bytes 98336 | tf_op jit(solution)/shard_map/ppermute | solution.py:331
  56.6 0.9 collective-permute-start.14
  57.5 3.7 %collective-permute-start.15 = (bf16[48,8,128]{2,1,0:T(8,128)(2,1)S(1)}, bf16[48,8,128]{2,1,0:T(8,128)(2,1)S(1)}, u32[]{:S(2)}, u32[]{:S(2)}) collective-permute-start(bf16[48,8,128]{2,1,0:T(8,128)(2,1)S(1)} %get-tuple-element.102), channel_id=1, source_target_pairs={{0,240},{16,0},{32,16},{48,32},{64,48},{80,64},{96,80},{112,96},{1... | collective-permute-start | bytes 294920 | tf_op jit(solution)/shard_map/ppermute | solution.py:331
  61.2 1.1 %local3.1 = (f32[64,8,128]{2,1,0:T(8,128)S(1)}, bf16[64,8,128]{2,1,0:T(8,128)(2,1)S(1)}, f32[8,128]{1,0:T(8,128)S(1)}) custom-call(s32[544]{0:T(1024)S(4)} %get-tuple-element.56.refs_0_, bf16[64,640,128]{2,1,0:T(8,128)(2,1)S(1)} %second_half.1.turned.refs_1_, bf16[64,8,128]{2,1,0:T(8,128)(2,1)S(1)} %get-tuple-element.96.refs_2_, ...), custom_call_target="tpu_custom_call" | custom-call | tf_op jit(solution)/shard_map/local3/pallas_call | solution.py:391
  62.2 1.2 %ghost3.1 = (f32[64,8,128]{2,1,0:T(8,128)S(1)}, bf16[64,8,128]{2,1,0:T(8,128)(2,1)S(1)}, f32[256,128]{1,0:T(8,128)S(1)}) custom-call(s32[544]{0:T(1024)S(4)} %get-tuple-element.56.refs_0_, bf16[64,640,128]{2,1,0:T(8,128)(2,1)S(1)} %second_half.1.turned.refs_1_, ...), custom_call_target="tpu_custom_call", output_to_operand_aliasing={{0}: (12, {}), {1}: (13, {})} | custom-call | tf_op jit(solution)/shard_map/ghost3/pallas_call | solution.py:433
  63.5 29.2 %all_to_all.11 = f32[256,1,128]{2,1,0:T(1,128)S(1)} all-to-all(f32[256,1,128]{2,1,0:T(1,128)S(1)} %bitcast.7), channel_id=1, replica_groups=mesh['gx'=16,'gy'=16] {'gx','gy'}, dimensions={0} | all-to-all | bytes 262144 | tf_op jit(solution)/shard_map/all_to_all | solution.py:450
  92.7 1.2 %finish.1 = (f32[64,8,128]{2,1,0:T(8,128)}, f32[64,8,128]{2,1,0:T(8,128)}) custom-call(f32[256,128]{1,0:T(8,128)S(1)} %bitcast.6, f32[64,8,128]{2,1,0:T(8,128)S(1)} %get-tuple-element.70.b0.refs_4_.refs_8_, f32[64,8,128]{2,1,0:T(8,128)S(1)} %get-tuple-element.80.refs_5_.refs_9_.b1, f32[64,8,128]{2,1,0:T(8,128)S(1)} %get-tuple-element.92.refs_6_.refs_10_.b2, ...), custom_call_target="tpu_custom_call" | custom-call | tf_op jit(solution)/shard_map/finish/pallas_call | solution.py:451
  (21 shorter events, 0.3 us)
Async XLA Ops:
  4.0 8.7 %collective-permute-start = (bf16[48,8,128]{2,1,0:T(8,128)(2,1)S(1)}, bf16[48,8,128]{2,1,0:T(8,128)(2,1)S(1)}, u32[]{:S(2)}, u32[]{:S(2)}) collective-permute-start(bf16[48,8,128]{2,1,0:T(8,128)(2,1)S(1)} %get-tuple-element.63), channel_id=1, source_target_pairs={{0,1},{1,2},{2,3},{3,4},{4,5},{5,6},{6,7},{7,8},{8,9},{9,10},{10,1... | collective-permute-start | bytes 294920 | tf_op jit(solution)/shard_map/ppermute | solution.py:331
  6.2 6.5 %collective-permute-start.1 = (bf16[48,8,128]{2,1,0:T(8,128)(2,1)S(1)}, bf16[48,8,128]{2,1,0:T(8,128)(2,1)S(1)}, u32[]{:S(2)}, u32[]{:S(2)}) collective-permute-start(bf16[48,8,128]{2,1,0:T(8,128)(2,1)S(1)} %get-tuple-element.64), channel_id=1, source_target_pairs={{0,15},{1,0},{2,1},{3,2},{4,3},{5,4},{6,5},{7,6},{8,7},{9,8},{10,9... | collective-permute-start | bytes 294920 | tf_op jit(solution)/shard_map/ppermute | solution.py:331
  12.8 5.4 %collective-permute-start.2 = (bf16[48,8,128]{2,1,0:T(8,128)(2,1)S(1)}, bf16[48,8,128]{2,1,0:T(8,128)(2,1)S(1)}, u32[]{:S(2)}, u32[]{:S(2)}) collective-permute-start(bf16[48,8,128]{2,1,0:T(8,128)(2,1)S(1)} %get-tuple-element.68), channel_id=1, source_target_pairs={{0,16},{16,32},{32,48},{48,64},{64,80},{80,96},{96,112},{112,128},... | collective-permute-start | bytes 294920 | tf_op jit(solution)/shard_map/ppermute | solution.py:331
  15.3 4.3 %collective-permute-start.3 = (bf16[48,8,128]{2,1,0:T(8,128)(2,1)S(1)}, bf16[48,8,128]{2,1,0:T(8,128)(2,1)S(1)}, u32[]{:S(2)}, u32[]{:S(2)}) collective-permute-start(bf16[48,8,128]{2,1,0:T(8,128)(2,1)S(1)} %get-tuple-element.69), channel_id=1, source_target_pairs={{0,240},{16,0},{32,16},{48,32},{64,48},{80,64},{96,80},{112,96},{1... | collective-permute-start | bytes 294920 | tf_op jit(solution)/shard_map/ppermute | solution.py:331
  15.5 4.1 %copy-start = (s32[1,9,16]{2,0,1:T(1,128)S(1)}, s32[1,9,16]{2,0,1:T(1,128)}, u32[]{:S(2)}) copy-start(s32[1,9,16]{2,0,1:T(1,128)} %param.10) | copy-start | bytes 1732
  15.5 4.1 %copy-start.1 = (s32[64,4]{0,1:T(4,128)S(1)}, s32[64,4]{0,1:T(4,128)}, u32[]{:S(2)}) copy-start(s32[64,4]{0,1:T(4,128)} %param.9) | copy-start | bytes 3076
  22.3 7.0 %collective-permute-start.4 = (bf16[48,8,128]{2,1,0:T(8,128)(2,1)S(1)}, bf16[48,8,128]{2,1,0:T(8,128)(2,1)S(1)}, u32[]{:S(2)}, u32[]{:S(2)}) collective-permute-start(bf16[48,8,128]{2,1,0:T(8,128)(2,1)S(1)} %get-tuple-element.72), channel_id=1, source_target_pairs={{0,1},{1,2},{2,3},{3,4},{4,5},{5,6},{6,7},{7,8},{8,9},{9,10},{10,1... | collective-permute-start | bytes 294920 | tf_op jit(solution)/shard_map/ppermute | solution.py:331
  22.4 6.9 %collective-permute-start.5 = (bf16[48,8,128]{2,1,0:T(8,128)(2,1)S(1)}, bf16[48,8,128]{2,1,0:T(8,128)(2,1)S(1)}, u32[]{:S(2)}, u32[]{:S(2)}) collective-permute-start(bf16[48,8,128]{2,1,0:T(8,128)(2,1)S(1)} %get-tuple-element.73), channel_id=1, source_target_pairs={{0,15},{1,0},{2,1},{3,2},{4,3},{5,4},{6,5},{7,6},{8,7},{9,8},{10,9... | collective-permute-start | bytes 294920 | tf_op jit(solution)/shard_map/ppermute | solution.py:331
  29.3 3.9 %collective-permute-start.6 = (bf16[48,8,128]{2,1,0:T(8,128)(2,1)S(1)}, bf16[48,8,128]{2,1,0:T(8,128)(2,1)S(1)}, u32[]{:S(2)}, u32[]{:S(2)}) collective-permute-start(bf16[48,8,128]{2,1,0:T(8,128)(2,1)S(1)} %get-tuple-element.77), channel_id=1, source_target_pairs={{0,16},{16,32},{32,48},{48,64},{64,80},{80,96},{96,112},{112,128},... | collective-permute-start | bytes 294920 | tf_op jit(solution)/shard_map/ppermute | solution.py:331
  30.7 4.0 %collective-permute-start.7 = (bf16[48,8,128]{2,1,0:T(8,128)(2,1)S(1)}, bf16[48,8,128]{2,1,0:T(8,128)(2,1)S(1)}, u32[]{:S(2)}, u32[]{:S(2)}) collective-permute-start(bf16[48,8,128]{2,1,0:T(8,128)(2,1)S(1)} %get-tuple-element.78), channel_id=1, source_target_pairs={{0,240},{16,0},{32,16},{48,32},{64,48},{80,64},{96,80},{112,96},{1... | collective-permute-start | bytes 294920 | tf_op jit(solution)/shard_map/ppermute | solution.py:331
  35.9 7.4 %collective-permute-start.8 = (bf16[48,8,128]{2,1,0:T(8,128)(2,1)S(1)}, bf16[48,8,128]{2,1,0:T(8,128)(2,1)S(1)}, u32[]{:S(2)}, u32[]{:S(2)}) collective-permute-start(bf16[48,8,128]{2,1,0:T(8,128)(2,1)S(1)} %get-tuple-element.85), channel_id=1, source_target_pairs={{0,1},{1,2},{2,3},{3,4},{4,5},{5,6},{6,7},{7,8},{8,9},{9,10},{10,1... | collective-permute-start | bytes 294920 | tf_op jit(solution)/shard_map/ppermute | solution.py:331
  36.0 7.3 %collective-permute-start.9 = (bf16[48,8,128]{2,1,0:T(8,128)(2,1)S(1)}, bf16[48,8,128]{2,1,0:T(8,128)(2,1)S(1)}, u32[]{:S(2)}, u32[]{:S(2)}) collective-permute-start(bf16[48,8,128]{2,1,0:T(8,128)(2,1)S(1)} %get-tuple-element.86), channel_id=1, source_target_pairs={{0,15},{1,0},{2,1},{3,2},{4,3},{5,4},{6,5},{7,6},{8,7},{9,8},{10,9... | collective-permute-start | bytes 294920 | tf_op jit(solution)/shard_map/ppermute | solution.py:331
  43.3 4.4 %collective-permute-start.10 = (bf16[48,8,128]{2,1,0:T(8,128)(2,1)S(1)}, bf16[48,8,128]{2,1,0:T(8,128)(2,1)S(1)}, u32[]{:S(2)}, u32[]{:S(2)}) collective-permute-start(bf16[48,8,128]{2,1,0:T(8,128)(2,1)S(1)} %get-tuple-element.89), channel_id=1, source_target_pairs={{0,16},{16,32},{32,48},{48,64},{64,80},{80,96},{96,112},{112,128},... | collective-permute-start | bytes 294920 | tf_op jit(solution)/shard_map/ppermute | solution.py:331
  44.2 4.0 %collective-permute-start.11 = (bf16[48,8,128]{2,1,0:T(8,128)(2,1)S(1)}, bf16[48,8,128]{2,1,0:T(8,128)(2,1)S(1)}, u32[]{:S(2)}, u32[]{:S(2)}) collective-permute-start(bf16[48,8,128]{2,1,0:T(8,128)(2,1)S(1)} %get-tuple-element.90), channel_id=1, source_target_pairs={{0,240},{16,0},{32,16},{48,32},{64,48},{80,64},{96,80},{112,96},{1... | collective-permute-start | bytes 294920 | tf_op jit(solution)/shard_map/ppermute | solution.py:331
  49.3 7.2 %collective-permute-start.12 = (bf16[48,8,128]{2,1,0:T(8,128)(2,1)S(1)}, bf16[48,8,128]{2,1,0:T(8,128)(2,1)S(1)}, u32[]{:S(2)}, u32[]{:S(2)}) collective-permute-start(bf16[48,8,128]{2,1,0:T(8,128)(2,1)S(1)} %get-tuple-element.97), channel_id=1, source_target_pairs={{0,1},{1,2},{2,3},{3,4},{4,5},{5,6},{6,7},{7,8},{8,9},{9,10},{10,1... | collective-permute-start | bytes 294920 | tf_op jit(solution)/shard_map/ppermute | solution.py:331
  49.4 7.1 %collective-permute-start.13 = (bf16[48,8,128]{2,1,0:T(8,128)(2,1)S(1)}, bf16[48,8,128]{2,1,0:T(8,128)(2,1)S(1)}, u32[]{:S(2)}, u32[]{:S(2)}) collective-permute-start(bf16[48,8,128]{2,1,0:T(8,128)(2,1)S(1)} %get-tuple-element.98), channel_id=1, source_target_pairs={{0,15},{1,0},{2,1},{3,2},{4,3},{5,4},{6,5},{7,6},{8,7},{9,8},{10,9... | collective-permute-start | bytes 294920 | tf_op jit(solution)/shard_map/ppermute | solution.py:331
  56.6 5.6 %collective-permute-start.14 = (bf16[48,8,128]{2,1,0:T(8,128)(2,1)S(1)}, bf16[48,8,128]{2,1,0:T(8,128)(2,1)S(1)}, u32[]{:S(2)}, u32[]{:S(2)}) collective-permute-start(bf16[48,8,128]{2,1,0:T(8,128)(2,1)S(1)} %get-tuple-element.101), channel_id=1, source_target_pairs={{0,16},{16,32},{32,48},{48,64},{64,80},{80,96},{96,112},{112,128},... | collective-permute-start | bytes 294920 | tf_op jit(solution)/shard_map/ppermute | solution.py:331
  57.5 4.7 %collective-permute-start.15 = (bf16[48,8,128]{2,1,0:T(8,128)(2,1)S(1)}, bf16[48,8,128]{2,1,0:T(8,128)(2,1)S(1)}, u32[]{:S(2)}, u32[]{:S(2)}) collective-permute-start(bf16[48,8,128]{2,1,0:T(8,128)(2,1)S(1)} %get-tuple-element.102), channel_id=1, source_target_pairs={{0,240},{16,0},{32,16},{48,32},{64,48},{80,64},{96,80},{112,96},{1... | collective-permute-start | bytes 294920 | tf_op jit(solution)/shard_map/ppermute | solution.py:331

commit v5 on v4

--- a/solution.py
+++ b/solution.py
@@ -19,6 +19,7 @@
 UNROLL = 16
 BLOCKS = FACES + 1
 QUARTER = CAP // 4
+EIGHTH = CAP // 8
 
 IN_VMEM = pl.BlockSpec(memory_space=pltpu.VMEM)
 IN_SMEM = pl.BlockSpec(memory_space=pltpu.SMEM)
@@ -64,19 +65,13 @@
 
 
 def start_kernel(
-    send_slots, counts, right_sides, diag, face, basis, rounded, up, down, next_row,
-    last_row, diag_first, face_first, arrived,
+    send_slots, counts, right_sides, basis, rounded, up, down, next_row, last_row
 ):
-    first = fetching(0, diag, face, diag_first, face_first, arrived)
-    for copy in first:
-        copy.start()
     element = lax.broadcasted_iota(jnp.int32, basis.shape, 0)
     live = jnp.where(element < counts[0], right_sides[...], 0.0)
     basis[...] = live
     rounded[...] = live.astype(jnp.bfloat16)
     pack(listed(send_slots), rounded, up, down, next_row, last_row)
-    for copy in first:
-        copy.wait()
 
 
 def plan_kernel(neighbours, send_slots, table, done):
@@ -99,51 +94,94 @@
 
 
 def fetching(first, diag, face, diag_here, face_here, arrived):
-    there = pl.ds(first, QUARTER)
+    there = pl.ds(first, diag_here.shape[0])
     return (
         pltpu.make_async_copy(diag.at[there], diag_here, arrived.at[0]),
         pltpu.make_async_copy(face.at[there], face_here, arrived.at[1]),
     )
 
 
-def transpose_quarter(first, diag_here, face_here, turned):
+def transpose_some(first, diag_here, face_here, turned, also=lambda at: None):
     def element(at, carry):
         e = first + at
         turned[e, 0:ROWS] = diag_here[at].T
         for f in range(FACES):
             turned[e, (f + 1) * ROWS : (f + 2) * ROWS] = face_here[at, f].T
+        also(at)
         return carry
 
-    lax.fori_loop(0, QUARTER, element, 0, unroll=8)
+    lax.fori_loop(0, diag_here.shape[0], element, 0, unroll=8)
 
 
 def first_half_kernel(
-    diag, face, diag_first, face_first, turned, diag_third, face_third, done,
-    diag_here, face_here, arrived, arrived_third,
+    diag, face, turned, diag_third, face_third, done, diag_here, face_here, arrived
 ):
-    second = fetching(QUARTER, diag, face, diag_here, face_here, arrived)
-    third = fetching(2 * QUARTER, diag, face, diag_third, face_third, arrived_third)
-    for copy in second + third:
+    parts = []
+    for at in range(0, 2 * QUARTER, EIGHTH):
+        here = pl.ds(at, EIGHTH)
+        place = diag_here.at[here], face_here.at[here]
+        parts.append((at, place, fetching(at, diag, face, *place, arrived.at[at // EIGHTH])))
+    third = fetching(2 * QUARTER, diag, face, diag_third, face_third, arrived.at[4])
+    for _, _, copies in parts:
+        for copy in copies:
+            copy.start()
+    for copy in third:
         copy.start()
-    transpose_quarter(0, diag_first, face_first, turned)
-    for copy in second:
-        copy.wait()
-    transpose_quarter(QUARTER, diag_here, face_here, turned)
+    for at, place, copies in parts:
+        for copy in copies:
+            copy.wait()
+        transpose_some(at, *place, turned)
     done[...] = jnp.zeros_like(done)
     for copy in third:
         copy.wait()
 
 
 def second_half_kernel(
-    diag, face, diag_third, face_third, before, turned, diag_here, face_here, arrived
+    neighbours, diag, face, diag_third, face_third, rounded, before, turned, image,
+    image_rounded, ghostly, diag_here, face_here, arrived, lookup,
 ):
     fourth = fetching(3 * QUARTER, diag, face, diag_here, face_here, arrived)
     for copy in fourth:
         copy.start()
-    transpose_quarter(2 * QUARTER, diag_third, face_third, turned)
+    fill_local(lookup, rounded)
+
+    def apply_from(first, diag_of, face_of):
+        def apply(at):
+            e = first + at
+            vectors = [lookup[e]]
+            for f in range(FACES):
+                near = neighbours[f, e]
+                vectors.append(
+                    lookup[jnp.where((near < 0) | (near >= CAP), NOTHING, near)]
+                )
+            blocks = [diag_of[at]] + [face_of[at, f] for f in range(FACES)]
+            out = lax.dot_general(
+                jnp.concatenate(vectors, axis=1),
+                jnp.concatenate(blocks, axis=1),
+                (((1,), (1,)), ((), ())),
+                preferred_element_type=jnp.float32,
+            )
+            image[e] = out
+            image_rounded[e] = out.astype(jnp.bfloat16)
+
+        return apply
+
+    transpose_some(
+        2 * QUARTER, diag_third, face_third, turned,
+        apply_from(2 * QUARTER, diag_third, face_third),
+    )
+    for run in (2, 3):
+        farthest = jnp.int32(-1)
+        for e in range(run * UNROLL, (run + 1) * UNROLL):
+            for f in range(FACES):
+                farthest = jnp.maximum(farthest, neighbours[f, e])
+        ghostly[run] = farthest
     for copy in fourth:
         copy.wait()
-    transpose_quarter(3 * QUARTER, diag_here, face_here, turned)
+    transpose_some(
+        3 * QUARTER, diag_here, face_here, turned,
+        apply_from(3 * QUARTER, diag_here, face_here),
+    )
 
 
 def relay_kernel(*refs):
@@ -209,8 +247,9 @@
 
 
 def whole_kernel(
-    neighbours, send_slots, turned, rounded, from_down, from_up, from_last, from_next,
-    b0, image, image_rounded, up, down, next_row, last_row, gram_out, lookup,
+    neighbours, send_slots, ghostly, turned, rounded, from_down, from_up, from_last,
+    from_next, b0, before, before_rounded, image, image_rounded, up, down, next_row,
+    last_row, gram_out, lookup,
 ):
     fill_local(lookup, rounded)
     fill_ghosts(lookup, from_down, from_up, from_last, from_next)
@@ -219,11 +258,23 @@
         at = [neighbours[f, e] for f in range(FACES)]
         return [e] + [jnp.where(a < 0, NOTHING, a) for a in at]
 
-    sums = apply_runs(
-        0, CAP // UNROLL, find, turned, lookup, (b0,), image, image_rounded
-    )
+    def again(first, limit):
+        apply_runs(first, limit, find, turned, lookup, (), image, image_rounded)
+
+    again(0, 2)
+    for run in (2, 3):
+        pl.when(ghostly[run] >= CAP)(functools.partial(again, run, run + 1))
     pack(listed(send_slots), image_rounded, up, down, next_row, last_row)
-    gram_out[...] = with_sums(jnp.zeros((8, ROWS), jnp.float32), sums)
+
+    def products(step, sums):
+        for u in range(UNROLL):
+            out = image[step * UNROLL + u]
+            sums = sums[0] + b0[step * UNROLL + u] * out, sums[1] + out * out
+        return sums
+
+    zero = jnp.zeros((8, ROWS), jnp.float32)
+    sums = lax.fori_loop(0, CAP // UNROLL, products, (zero, zero))
+    gram_out[...] = with_sums(zero, sums)
 
 
 def find_in(table):
@@ -350,15 +401,14 @@
         pltpu.VMEM((QUARTER, FACES, ROWS, ROWS), half),
     ]
     arrived = pltpu.SemaphoreType.DMA((2,))
-    first, rounded, up, down, next_row, last_row, *blocks = pl.pallas_call(
+    first, rounded, up, down, next_row, last_row = pl.pallas_call(
         start_kernel,
         name="start",
-        in_specs=[IN_SMEM, IN_SMEM, IN_VMEM, IN_HBM, IN_HBM],
-        out_specs=[IN_VMEM] * 8,
-        out_shape=[full, narrow] + packets + quarter,
-        scratch_shapes=[arrived],
+        in_specs=[IN_SMEM, IN_SMEM, IN_VMEM],
+        out_specs=[IN_VMEM] * 6,
+        out_shape=[full, narrow] + packets,
         compiler_params=params(),
-    )(in_place(send_slots), counts, in_place(right_sides), diag_blocks, face_blocks)
+    )(in_place(send_slots), counts, in_place(right_sides))
     basis = [first]
     gram = None
     for power in range(POWERS):
@@ -370,12 +420,16 @@
             turned, *blocks, done = pl.pallas_call(
                 first_half_kernel,
                 name="first_half",
-                in_specs=[IN_HBM] * 2 + [IN_VMEM] * 2,
+                in_specs=[IN_HBM] * 2,
                 out_specs=[IN_VMEM] * 4,
                 out_shape=[turned_shape] + quarter + [gram_shape],
-                scratch_shapes=quarter + [arrived, arrived],
+                scratch_shapes=[
+                    pltpu.VMEM((2 * QUARTER, ROWS, ROWS), half),
+                    pltpu.VMEM((2 * QUARTER, FACES, ROWS, ROWS), half),
+                    pltpu.SemaphoreType.DMA((5, 2)),
+                ],
                 compiler_params=params(),
-            )(diag_blocks, face_blocks, *blocks)
+            )(diag_blocks, face_blocks)
             after = (done,)
         elif power == 1:
             table, done = pl.pallas_call(
@@ -409,25 +463,29 @@
         from_next = shifted(send_last, "gx", -1)
         received = (from_down, from_up, from_last, from_next)
         if power == 0:
-            turned = pl.pallas_call(
+            turned, image, image_rounded, ghostly = pl.pallas_call(
                 second_half_kernel,
                 name="second_half",
-                in_specs=[IN_HBM] * 2 + [IN_VMEM] * 3,
-                out_specs=IN_VMEM,
-                out_shape=turned_shape,
-                scratch_shapes=quarter + [arrived],
-                input_output_aliases={4: 0},
+                in_specs=[IN_SMEM] + [IN_HBM] * 2 + [IN_VMEM] * 4,
+                out_specs=[IN_VMEM] * 3 + [IN_SMEM],
+                out_shape=[turned_shape, full, narrow, pltpu.SMEM((8,), jnp.int32)],
+                scratch_shapes=quarter + [arrived, lookup],
+                input_output_aliases={6: 0},
                 compiler_params=params(),
-            )(diag_blocks, face_blocks, *blocks, turned)
+            )(neighbours, diag_blocks, face_blocks, *blocks, rounded, turned)
             outs = pl.pallas_call(
                 whole_kernel,
                 name="whole",
-                in_specs=[IN_SMEM] * 2 + [IN_VMEM] * 7,
+                in_specs=[IN_SMEM] * 3 + [IN_VMEM] * 9,
                 out_specs=[IN_VMEM] * 7,
                 out_shape=[full, narrow] + packets + [gram_shape],
                 scratch_shapes=[lookup],
+                input_output_aliases={10: 0, 11: 1},
                 compiler_params=params(),
-            )(neighbours, send_slots, turned, rounded, *received, first)
+            )(
+                neighbours, send_slots, ghostly, turned, rounded, *received, first,
+                image, image_rounded,
+            )
         else:
             shapes = [full, narrow] + ([rows_shape] if last else packets + [gram_shape])
             outs = pl.pallas_call(

time: 94 us -> 93.3 us (level)
    pallas_call x1, Pallas kernels: 2.75 us -> 1.18 us  [per_device(): pl.pallas_call(start_kernel, name='start', in_specs=[IN_SMEM, IN_SMEM, IN...]
  transfers between devices with their start and end apart: 16 -> 16, of which waited for: 6 -> 6; matrix products, arithmetic and copies ran while one was open for 0% -> 0% of each run, Pallas kernels for 11% -> 12%
where the time goes in v5:
time: 93.3 us; the launch traced here: 93.1 us
  starting transfers between devices  35 us (38%)
  blocking collectives  29.2 us (31%)
  Pallas kernels  19.2 us (21%)
  waiting for transfers between devices  8.26 us (9%)
  between operations  1.44 us (2%)
    ppermute x16, starting transfers between devices, shifted(): lax.ppermute(block, axis, [(i, (i + distance) % SIDE) for i in range(SIDE)])  35 us
    all_to_all x1, blocking collectives, per_device(): gathered = lax.all_to_all(gram, ('gx', 'gy'), 0, 0, tiled=True)  29.2 us
    ppermute x16, waiting for transfers between devices, shifted(): lax.ppermute(block, axis, [(i, (i + distance) % SIDE) for i in range(SIDE)])  8.26 us
    pallas_call x3, Pallas kernels, per_device(): pl.pallas_call(functools.partial(ghost_kernel, power), name=f'ghost{power...  3.48 us
    pallas_call x1, Pallas kernels, per_device(): pl.pallas_call(first_half_kernel, name='first_half', in_specs=[IN_HBM] *...  3.42 us
    pallas_call x1, Pallas kernels, per_device(): pl.pallas_call(second_half_kernel, name='second_half', in_specs=[IN_SMEM]...  3.4 us
    pallas_call x3, Pallas kernels, per_device(): pl.pallas_call(functools.partial(local_kernel, power), name=f'local{power...  3.14 us
    pallas_call x1, Pallas kernels, per_device(): pl.pallas_call(whole_kernel, name='whole', in_specs=[IN_SMEM] * 3 + [IN_V...  1.92 us
  transfers between devices with their start and end apart: 16, of which 6 were waited for; matrix products, arithmetic and copies ran while one was open for 0% of the time, Pallas kernels for 12%

profile of v5, /device:TPU:1, one launch (start us, length us, event | category | flops | bytes accessed | tf_op | source)
XLA Modules:
  0.0 93.1 jit_solution(16579366038063359199)
XLA Ops:
  1.3 1.2 %start.1 = (f32[64,8,128]{2,1,0:T(8,128)S(1)}, bf16[64,8,128]{2,1,0:T(8,128)(2,1)S(1)}, bf16[48,8,128]{2,1,0:T(8,128)(2,1)S(1)}, bf16[48,8,128]{2,1,0:T(8,128)(2...) custom-call(s32[9,1,16]{2,1,0:T(1,128)} %bitcast.8, s32[1]{0:T(128)S(6)} %copy.27.counts, ...), custom_call_target="tpu_custom_call" | custom-call | tf_op jit(solution)/shard_map/start/pallas_call | solution.py:404
  2.5 2.2 %collective-permute-start = (bf16[48,8,128]{2,1,0:T(8,128)(2,1)S(1)}, bf16[48,8,128]{2,1,0:T(8,128)(2,1)S(1)}, u32[]{:S(2)}, u32[]{:S(2)}) collective-permute-start(bf16[48,8,128]{2,1,0:T(8,128)(2,1)S(1)} %get-tuple-element.65), channel_id=1, source_target_pairs={{0,1},{1,2},{2,3},{3,4},{4,5},{5,6},{6,7},{7,8},{8,9},{9,10},{10,1... | collective-permute-start | bytes 294920 | tf_op jit(solution)/shard_map/ppermute | solution.py:382
  4.7 3.7 %collective-permute-start.1 = (bf16[48,8,128]{2,1,0:T(8,128)(2,1)S(1)}, bf16[48,8,128]{2,1,0:T(8,128)(2,1)S(1)}, u32[]{:S(2)}, u32[]{:S(2)}) collective-permute-start(bf16[48,8,128]{2,1,0:T(8,128)(2,1)S(1)} %get-tuple-element.66), channel_id=1, source_target_pairs={{0,15},{1,0},{2,1},{3,2},{4,3},{5,4},{6,5},{7,6},{8,7},{9,8},{10,9... | collective-permute-start | bytes 294920 | tf_op jit(solution)/shard_map/ppermute | solution.py:382
  8.4 3.4 %first_half.1 = (bf16[64,640,128]{2,1,0:T(8,128)(2,1)S(1)}, bf16[16,128,128]{2,1,0:T(8,128)(2,1)S(1)}, bf16[16,4,128,128]{3,2,1,0:T(8,128)(2,1)S(1)}, f32[8,128]{1,0:T(8,128)S(1)}) custom-call(bf16[64,128,128]{2,1,0:T(8,128)(2,1)} %diag.3, bf16[64,4,128,128]{3,2,1,0:T(8,128)(2,1)} %face.3), custom_call_target="tpu_custom_call" | custom-call | tf_op jit(solution)/shard_map/first_half/pallas_call | solution.py:420
  11.9 2.5 %collective-permute-start.2 = (bf16[48,8,128]{2,1,0:T(8,128)(2,1)S(1)}, bf16[48,8,128]{2,1,0:T(8,128)(2,1)S(1)}, u32[]{:S(2)}, u32[]{:S(2)}) collective-permute-start(bf16[48,8,128]{2,1,0:T(8,128)(2,1)S(1)} %get-tuple-element.70), channel_id=1, source_target_pairs={{0,16},{16,32},{32,48},{48,64},{64,80},{80,96},{96,112},{112,128},... | collective-permute-start | bytes 294920 | tf_op jit(solution)/shard_map/ppermute | solution.py:382
  14.7 3.4 %second_half.1 = (bf16[64,640,128]{2,1,0:T(8,128)(2,1)S(1)}, f32[64,8,128]{2,1,0:T(8,128)S(1)}, bf16[64,8,128]{2,1,0:T(8,128)(2,1)S(1)}, s32[8]{0:T(128)S(4)}) custom-call(s32[4,64]{1,0:T(4,128)S(1)} %bitcast.11, bf16[64,128,128]{2,1,0:T(8,128)(2,1)} %diag.3, bf16[64,4,128,128]{3,2,1,0:T(8,128)(2,1)} %face.3, ...), custom_call_target="tpu_custom_call", output_to_operand_aliasing={{0}: (6, {})} | custom-call | tf_op jit(solution)/shard_map/second_half/pallas_call | solution.py:466
  18.1 0.7 collective-permute-done.3.from_next
  18.8 1.9 %whole.1 = (f32[64,8,128]{2,1,0:T(8,128)S(1)}, bf16[64,8,128]{2,1,0:T(8,128)(2,1)S(1)}, bf16[48,8,128]{2,1,0:T(8,128)(2,1)S(1)}, bf16[48,8,128]{2,1,0:T(8,128)(2...) custom-call(s32[4,64]{1,0:T(4,128)S(1)} %bitcast.12, ...), custom_call_target="tpu_custom_call", output_to_operand_aliasing={{0}: (10, {}), {1}: (11, {})} | custom-call | tf_op jit(solution)/shard_map/whole/pallas_call | solution.py:476
  20.7 4.8 %collective-permute-start.5 = (bf16[48,8,128]{2,1,0:T(8,128)(2,1)S(1)}, bf16[48,8,128]{2,1,0:T(8,128)(2,1)S(1)}, u32[]{:S(2)}, u32[]{:S(2)}) collective-permute-start(bf16[48,8,128]{2,1,0:T(8,128)(2,1)S(1)} %get-tuple-element.77), channel_id=1, source_target_pairs={{0,15},{1,0},{2,1},{3,2},{4,3},{5,4},{6,5},{7,6},{8,7},{9,8},{10,9... | collective-permute-start | bytes 294920 | tf_op jit(solution)/shard_map/ppermute | solution.py:382
  25.5 1.5 %plan.1 = (s32[544]{0:T(1024)S(4)}, f32[8,128]{1,0:T(8,128)S(1)}) custom-call(s32[4,64]{1,0:T(4,128)S(1)} %bitcast.13, s32[9,1,16]{2,1,0:T(1,128)S(1)} %bitcast.10), custom_call_target="tpu_custom_call" | custom-call | tf_op jit(solution)/shard_map/plan/pallas_call | solution.py:435
  27.0 0.5 collective-permute-done.4.refs_0_.refs_3_
  27.5 3.0 %collective-permute-start.6 = (bf16[48,8,128]{2,1,0:T(8,128)(2,1)S(1)}, bf16[48,8,128]{2,1,0:T(8,128)(2,1)S(1)}, u32[]{:S(2)}, u32[]{:S(2)}) collective-permute-start(bf16[48,8,128]{2,1,0:T(8,128)(2,1)S(1)} %get-tuple-element.81), channel_id=1, source_target_pairs={{0,16},{16,32},{32,48},{48,64},{64,80},{80,96},{96,112},{112,128},... | collective-permute-start | bytes 294920 | tf_op jit(solution)/shard_map/ppermute | solution.py:382
  30.5 0.8 collective-permute-start.7
  31.3 1.0 %local1.1 = (f32[64,8,128]{2,1,0:T(8,128)S(1)}, bf16[64,8,128]{2,1,0:T(8,128)(2,1)S(1)}, f32[8,128]{1,0:T(8,128)S(1)}) custom-call(s32[544]{0:T(1024)S(4)} %get-tuple-element.58.refs_0_, bf16[64,640,128]{2,1,0:T(8,128)(2,1)S(1)} %get-tuple-element.63.turned.refs_1_, bf16[64,8,128]{2,1,0:T(8,128)(2,1)S(1)} %get-tuple-element.75.refs_2_, ...), custom_call_target="tpu_custom_call" | custom-call | tf_op jit(solution)/shard_map/local1/pallas_call | solution.py:445
  32.3 2.2 %collective-permute-done.7.refs_6_ = bf16[48,8,128]{2,1,0:T(8,128)(2,1)S(1)} collective-permute-done((bf16[48,8,128]{2,1,0:T(8,128)(2,1)S(1)}, bf16[48,8,128]{2,1,0:T(8,128)(2,1)S(1)}, u32[]{:S(2)}, u32[]{:S(2)}) %collective-permute-start.7) | collective-permute-done | bytes 98336 | tf_op jit(solution)/shard_map/ppermute | solution.py:382
  34.5 1.1 %ghost1.1 = (f32[64,8,128]{2,1,0:T(8,128)S(1)}, bf16[64,8,128]{2,1,0:T(8,128)(2,1)S(1)}, bf16[48,8,128]{2,1,0:T(8,128)(2,1)S(1)}, bf16[48,8,128]{2,1,0:T(8,128)(...) custom-call(s32[544]{0:T(1024)S(4)} %get-tuple-element.58.refs_0_, ...), custom_call_target="tpu_custom_call", output_to_operand_aliasing={{0}: (10, {}), {1}: (11, {})} | custom-call | tf_op jit(solution)/shard_map/ghost1/pallas_call | solution.py:491
  35.8 4.9 %collective-permute-start.9 = (bf16[48,8,128]{2,1,0:T(8,128)(2,1)S(1)}, bf16[48,8,128]{2,1,0:T(8,128)(2,1)S(1)}, u32[]{:S(2)}, u32[]{:S(2)}) collective-permute-start(bf16[48,8,128]{2,1,0:T(8,128)(2,1)S(1)} %get-tuple-element.90), channel_id=1, source_target_pairs={{0,15},{1,0},{2,1},{3,2},{4,3},{5,4},{6,5},{7,6},{8,7},{9,8},{10,9... | collective-permute-start | bytes 294920 | tf_op jit(solution)/shard_map/ppermute | solution.py:382
  40.6 1.9 %collective-permute-done.8.refs_0_.refs_3_ = bf16[48,8,128]{2,1,0:T(8,128)(2,1)S(1)} collective-permute-done((bf16[48,8,128]{2,1,0:T(8,128)(2,1)S(1)}, bf16[48,8,128]{2,1,0:T(8,128)(2,1)S(1)}, u32[]{:S(2)}, u32[]{:S(2)}) %collective-permute-start.8) | collective-permute-done | bytes 98336 | tf_op jit(solution)/shard_map/ppermute | solution.py:382
  42.6 1.2 %collective-permute-start.10 = (bf16[48,8,128]{2,1,0:T(8,128)(2,1)S(1)}, bf16[48,8,128]{2,1,0:T(8,128)(2,1)S(1)}, u32[]{:S(2)}, u32[]{:S(2)}) collective-permute-start(bf16[48,8,128]{2,1,0:T(8,128)(2,1)S(1)} %get-tuple-element.93), channel_id=1, source_target_pairs={{0,16},{16,32},{32,48},{48,64},{64,80},{80,96},{96,112},{112,128},... | collective-permute-start | bytes 294920 | tf_op jit(solution)/shard_map/ppermute | solution.py:382
  43.7 2.0 %collective-permute-start.11 = (bf16[48,8,128]{2,1,0:T(8,128)(2,1)S(1)}, bf16[48,8,128]{2,1,0:T(8,128)(2,1)S(1)}, u32[]{:S(2)}, u32[]{:S(2)}) collective-permute-start(bf16[48,8,128]{2,1,0:T(8,128)(2,1)S(1)} %get-tuple-element.94), channel_id=1, source_target_pairs={{0,240},{16,0},{32,16},{48,32},{64,48},{80,64},{96,80},{112,96},{1... | collective-permute-start | bytes 294920 | tf_op jit(solution)/shard_map/ppermute | solution.py:382
  45.7 1.0 %local2.1 = (f32[64,8,128]{2,1,0:T(8,128)S(1)}, bf16[64,8,128]{2,1,0:T(8,128)(2,1)S(1)}, f32[8,128]{1,0:T(8,128)S(1)}) custom-call(s32[544]{0:T(1024)S(4)} %get-tuple-element.58.refs_0_, bf16[64,640,128]{2,1,0:T(8,128)(2,1)S(1)} %get-tuple-element.63.turned.refs_1_, bf16[64,8,128]{2,1,0:T(8,128)(2,1)S(1)} %get-tuple-element.88.refs_2_, ...), custom_call_target="tpu_custom_call" | custom-call | tf_op jit(solution)/shard_map/local2/pallas_call | solution.py:445
  46.8 1.0 %collective-permute-done.11.refs_6_ = bf16[48,8,128]{2,1,0:T(8,128)(2,1)S(1)} collective-permute-done((bf16[48,8,128]{2,1,0:T(8,128)(2,1)S(1)}, bf16[48,8,128]{2,1,0:T(8,128)(2,1)S(1)}, u32[]{:S(2)}, u32[]{:S(2)}) %collective-permute-start.11) | collective-permute-done | bytes 98336 | tf_op jit(solution)/shard_map/ppermute | solution.py:382
  47.8 1.1 %ghost2.1 = (f32[64,8,128]{2,1,0:T(8,128)S(1)}, bf16[64,8,128]{2,1,0:T(8,128)(2,1)S(1)}, bf16[48,8,128]{2,1,0:T(8,128)(2,1)S(1)}, bf16[48,8,128]{2,1,0:T(8,128)(...) custom-call(s32[544]{0:T(1024)S(4)} %get-tuple-element.58.refs_0_, ...), custom_call_target="tpu_custom_call", output_to_operand_aliasing={{0}: (11, {}), {1}: (12, {})} | custom-call | tf_op jit(solution)/shard_map/ghost2/pallas_call | solution.py:491
  48.9 0.3 collective-permute-start.12
  49.2 5.3 %collective-permute-start.13 = (bf16[48,8,128]{2,1,0:T(8,128)(2,1)S(1)}, bf16[48,8,128]{2,1,0:T(8,128)(2,1)S(1)}, u32[]{:S(2)}, u32[]{:S(2)}) collective-permute-start(bf16[48,8,128]{2,1,0:T(8,128)(2,1)S(1)} %get-tuple-element.102), channel_id=1, source_target_pairs={{0,15},{1,0},{2,1},{3,2},{4,3},{5,4},{6,5},{7,6},{8,7},{9,8},{10,9... | collective-permute-start | bytes 294920 | tf_op jit(solution)/shard_map/ppermute | solution.py:382
  54.5 1.9 %collective-permute-done.12.refs_0_.refs_3_ = bf16[48,8,128]{2,1,0:T(8,128)(2,1)S(1)} collective-permute-done((bf16[48,8,128]{2,1,0:T(8,128)(2,1)S(1)}, bf16[48,8,128]{2,1,0:T(8,128)(2,1)S(1)}, u32[]{:S(2)}, u32[]{:S(2)}) %collective-permute-start.12) | collective-permute-done | bytes 98336 | tf_op jit(solution)/shard_map/ppermute | solution.py:382
  56.5 0.9 collective-permute-start.14
  57.3 3.1 %collective-permute-start.15 = (bf16[48,8,128]{2,1,0:T(8,128)(2,1)S(1)}, bf16[48,8,128]{2,1,0:T(8,128)(2,1)S(1)}, u32[]{:S(2)}, u32[]{:S(2)}) collective-permute-start(bf16[48,8,128]{2,1,0:T(8,128)(2,1)S(1)} %get-tuple-element.106), channel_id=1, source_target_pairs={{0,240},{16,0},{32,16},{48,32},{64,48},{80,64},{96,80},{112,96},{1... | collective-permute-start | bytes 294920 | tf_op jit(solution)/shard_map/ppermute | solution.py:382
  60.4 1.1 %local3.1 = (f32[64,8,128]{2,1,0:T(8,128)S(1)}, bf16[64,8,128]{2,1,0:T(8,128)(2,1)S(1)}, f32[8,128]{1,0:T(8,128)S(1)}) custom-call(s32[544]{0:T(1024)S(4)} %get-tuple-element.58.refs_0_, bf16[64,640,128]{2,1,0:T(8,128)(2,1)S(1)} %get-tuple-element.63.turned.refs_1_, bf16[64,8,128]{2,1,0:T(8,128)(2,1)S(1)} %get-tuple-element.100.refs_2_, ...), custom_call_target="tpu_custom_call" | custom-call | tf_op jit(solution)/shard_map/local3/pallas_call | solution.py:445
  61.5 1.2 %ghost3.1 = (f32[64,8,128]{2,1,0:T(8,128)S(1)}, bf16[64,8,128]{2,1,0:T(8,128)(2,1)S(1)}, f32[256,128]{1,0:T(8,128)S(1)}) custom-call(s32[544]{0:T(1024)S(4)} %get-tuple-element.58.refs_0_, bf16[64,640,128]{2,1,0:T(8,128)(2,1)S(1)} %get-tuple-element.63.turned.refs_1_, ...), custom_call_target="tpu_custom_call", output_to_operand_aliasing={{0}: (12, {}), {1}: (13, {})} | custom-call | tf_op jit(solution)/shard_map/ghost3/pallas_call | solution.py:491
  62.7 29.2 %all_to_all.11 = f32[256,1,128]{2,1,0:T(1,128)S(1)} all-to-all(f32[256,1,128]{2,1,0:T(1,128)S(1)} %bitcast.7), channel_id=1, replica_groups=mesh['gx'=16,'gy'=16] {'gx','gy'}, dimensions={0} | all-to-all | bytes 262144 | tf_op jit(solution)/shard_map/all_to_all | solution.py:508
  92.0 1.2 %finish.1 = (f32[64,8,128]{2,1,0:T(8,128)}, f32[64,8,128]{2,1,0:T(8,128)}) custom-call(f32[256,128]{1,0:T(8,128)S(1)} %bitcast.6, f32[64,8,128]{2,1,0:T(8,128)S(1)} %get-tuple-element.72.b0.refs_4_.refs_8_, f32[64,8,128]{2,1,0:T(8,128)S(1)} %get-tuple-element.84.refs_5_.refs_9_.b1, f32[64,8,128]{2,1,0:T(8,128)S(1)} %get-tuple-element.96.refs_6_.refs_10_.b2, ...), custom_call_target="tpu_custom_call" | custom-call | tf_op jit(solution)/shard_map/finish/pallas_call | solution.py:509
  (21 shorter events, 0.4 us)
Async XLA Ops:
  0.6 14.0 %copy-start.1 = (s32[64,4]{0,1:T(4,128)S(1)}, s32[64,4]{0,1:T(4,128)}, u32[]{:S(2)}) copy-start(s32[64,4]{0,1:T(4,128)} %param.9) | copy-start | bytes 3076
  2.5 9.4 %collective-permute-start = (bf16[48,8,128]{2,1,0:T(8,128)(2,1)S(1)}, bf16[48,8,128]{2,1,0:T(8,128)(2,1)S(1)}, u32[]{:S(2)}, u32[]{:S(2)}) collective-permute-start(bf16[48,8,128]{2,1,0:T(8,128)(2,1)S(1)} %get-tuple-element.65), channel_id=1, source_target_pairs={{0,1},{1,2},{2,3},{3,4},{4,5},{5,6},{6,7},{7,8},{8,9},{9,10},{10,1... | collective-permute-start | bytes 294920 | tf_op jit(solution)/shard_map/ppermute | solution.py:382
  4.7 7.2 %collective-permute-start.1 = (bf16[48,8,128]{2,1,0:T(8,128)(2,1)S(1)}, bf16[48,8,128]{2,1,0:T(8,128)(2,1)S(1)}, u32[]{:S(2)}, u32[]{:S(2)}) collective-permute-start(bf16[48,8,128]{2,1,0:T(8,128)(2,1)S(1)} %get-tuple-element.66), channel_id=1, source_target_pairs={{0,15},{1,0},{2,1},{3,2},{4,3},{5,4},{6,5},{7,6},{8,7},{9,8},{10,9... | collective-permute-start | bytes 294920 | tf_op jit(solution)/shard_map/ppermute | solution.py:382
  11.9 6.2 %collective-permute-start.2 = (bf16[48,8,128]{2,1,0:T(8,128)(2,1)S(1)}, bf16[48,8,128]{2,1,0:T(8,128)(2,1)S(1)}, u32[]{:S(2)}, u32[]{:S(2)}) collective-permute-start(bf16[48,8,128]{2,1,0:T(8,128)(2,1)S(1)} %get-tuple-element.70), channel_id=1, source_target_pairs={{0,16},{16,32},{32,48},{48,64},{64,80},{80,96},{96,112},{112,128},... | collective-permute-start | bytes 294920 | tf_op jit(solution)/shard_map/ppermute | solution.py:382
  14.4 4.3 %collective-permute-start.3 = (bf16[48,8,128]{2,1,0:T(8,128)(2,1)S(1)}, bf16[48,8,128]{2,1,0:T(8,128)(2,1)S(1)}, u32[]{:S(2)}, u32[]{:S(2)}) collective-permute-start(bf16[48,8,128]{2,1,0:T(8,128)(2,1)S(1)} %get-tuple-element.71), channel_id=1, source_target_pairs={{0,240},{16,0},{32,16},{48,32},{64,48},{80,64},{96,80},{112,96},{1... | collective-permute-start | bytes 294920 | tf_op jit(solution)/shard_map/ppermute | solution.py:382
  14.7 4.1 %copy-start = (s32[1,9,16]{2,0,1:T(1,128)S(1)}, s32[1,9,16]{2,0,1:T(1,128)}, u32[]{:S(2)}) copy-start(s32[1,9,16]{2,0,1:T(1,128)} %param.10) | copy-start | bytes 1732
  20.7 6.8 %collective-permute-start.4 = (bf16[48,8,128]{2,1,0:T(8,128)(2,1)S(1)}, bf16[48,8,128]{2,1,0:T(8,128)(2,1)S(1)}, u32[]{:S(2)}, u32[]{:S(2)}) collective-permute-start(bf16[48,8,128]{2,1,0:T(8,128)(2,1)S(1)} %get-tuple-element.76), channel_id=1, source_target_pairs={{0,1},{1,2},{2,3},{3,4},{4,5},{5,6},{6,7},{7,8},{8,9},{9,10},{10,1... | collective-permute-start | bytes 294920 | tf_op jit(solution)/shard_map/ppermute | solution.py:382
  20.7 6.8 %collective-permute-start.5 = (bf16[48,8,128]{2,1,0:T(8,128)(2,1)S(1)}, bf16[48,8,128]{2,1,0:T(8,128)(2,1)S(1)}, u32[]{:S(2)}, u32[]{:S(2)}) collective-permute-start(bf16[48,8,128]{2,1,0:T(8,128)(2,1)S(1)} %get-tuple-element.77), channel_id=1, source_target_pairs={{0,15},{1,0},{2,1},{3,2},{4,3},{5,4},{6,5},{7,6},{8,7},{9,8},{10,9... | collective-permute-start | bytes 294920 | tf_op jit(solution)/shard_map/ppermute | solution.py:382
  27.5 4.8 %collective-permute-start.6 = (bf16[48,8,128]{2,1,0:T(8,128)(2,1)S(1)}, bf16[48,8,128]{2,1,0:T(8,128)(2,1)S(1)}, u32[]{:S(2)}, u32[]{:S(2)}) collective-permute-start(bf16[48,8,128]{2,1,0:T(8,128)(2,1)S(1)} %get-tuple-element.81), channel_id=1, source_target_pairs={{0,16},{16,32},{32,48},{48,64},{64,80},{80,96},{96,112},{112,128},... | collective-permute-start | bytes 294920 | tf_op jit(solution)/shard_map/ppermute | solution.py:382
  30.5 4.0 %collective-permute-start.7 = (bf16[48,8,128]{2,1,0:T(8,128)(2,1)S(1)}, bf16[48,8,128]{2,1,0:T(8,128)(2,1)S(1)}, u32[]{:S(2)}, u32[]{:S(2)}) collective-permute-start(bf16[48,8,128]{2,1,0:T(8,128)(2,1)S(1)} %get-tuple-element.82), channel_id=1, source_target_pairs={{0,240},{16,0},{32,16},{48,32},{64,48},{80,64},{96,80},{112,96},{1... | collective-permute-start | bytes 294920 | tf_op jit(solution)/shard_map/ppermute | solution.py:382
  35.7 6.9 %collective-permute-start.8 = (bf16[48,8,128]{2,1,0:T(8,128)(2,1)S(1)}, bf16[48,8,128]{2,1,0:T(8,128)(2,1)S(1)}, u32[]{:S(2)}, u32[]{:S(2)}) collective-permute-start(bf16[48,8,128]{2,1,0:T(8,128)(2,1)S(1)} %get-tuple-element.89), channel_id=1, source_target_pairs={{0,1},{1,2},{2,3},{3,4},{4,5},{5,6},{6,7},{7,8},{8,9},{9,10},{10,1... | collective-permute-start | bytes 294920 | tf_op jit(solution)/shard_map/ppermute | solution.py:382
  35.8 6.8 %collective-permute-start.9 = (bf16[48,8,128]{2,1,0:T(8,128)(2,1)S(1)}, bf16[48,8,128]{2,1,0:T(8,128)(2,1)S(1)}, u32[]{:S(2)}, u32[]{:S(2)}) collective-permute-start(bf16[48,8,128]{2,1,0:T(8,128)(2,1)S(1)} %get-tuple-element.90), channel_id=1, source_target_pairs={{0,15},{1,0},{2,1},{3,2},{4,3},{5,4},{6,5},{7,6},{8,7},{9,8},{10,9... | collective-permute-start | bytes 294920 | tf_op jit(solution)/shard_map/ppermute | solution.py:382
  42.6 4.2 %collective-permute-start.10 = (bf16[48,8,128]{2,1,0:T(8,128)(2,1)S(1)}, bf16[48,8,128]{2,1,0:T(8,128)(2,1)S(1)}, u32[]{:S(2)}, u32[]{:S(2)}) collective-permute-start(bf16[48,8,128]{2,1,0:T(8,128)(2,1)S(1)} %get-tuple-element.93), channel_id=1, source_target_pairs={{0,16},{16,32},{32,48},{48,64},{64,80},{80,96},{96,112},{112,128},... | collective-permute-start | bytes 294920 | tf_op jit(solution)/shard_map/ppermute | solution.py:382
  43.7 4.0 %collective-permute-start.11 = (bf16[48,8,128]{2,1,0:T(8,128)(2,1)S(1)}, bf16[48,8,128]{2,1,0:T(8,128)(2,1)S(1)}, u32[]{:S(2)}, u32[]{:S(2)}) collective-permute-start(bf16[48,8,128]{2,1,0:T(8,128)(2,1)S(1)} %get-tuple-element.94), channel_id=1, source_target_pairs={{0,240},{16,0},{32,16},{48,32},{64,48},{80,64},{96,80},{112,96},{1... | collective-permute-start | bytes 294920 | tf_op jit(solution)/shard_map/ppermute | solution.py:382
  48.9 7.5 %collective-permute-start.12 = (bf16[48,8,128]{2,1,0:T(8,128)(2,1)S(1)}, bf16[48,8,128]{2,1,0:T(8,128)(2,1)S(1)}, u32[]{:S(2)}, u32[]{:S(2)}) collective-permute-start(bf16[48,8,128]{2,1,0:T(8,128)(2,1)S(1)} %get-tuple-element.101), channel_id=1, source_target_pairs={{0,1},{1,2},{2,3},{3,4},{4,5},{5,6},{6,7},{7,8},{8,9},{9,10},{10,1... | collective-permute-start | bytes 294920 | tf_op jit(solution)/shard_map/ppermute | solution.py:382
  49.2 7.3 %collective-permute-start.13 = (bf16[48,8,128]{2,1,0:T(8,128)(2,1)S(1)}, bf16[48,8,128]{2,1,0:T(8,128)(2,1)S(1)}, u32[]{:S(2)}, u32[]{:S(2)}) collective-permute-start(bf16[48,8,128]{2,1,0:T(8,128)(2,1)S(1)} %get-tuple-element.102), channel_id=1, source_target_pairs={{0,15},{1,0},{2,1},{3,2},{4,3},{5,4},{6,5},{7,6},{8,7},{9,8},{10,9... | collective-permute-start | bytes 294920 | tf_op jit(solution)/shard_map/ppermute | solution.py:382
  56.5 5.0 %collective-permute-start.14 = (bf16[48,8,128]{2,1,0:T(8,128)(2,1)S(1)}, bf16[48,8,128]{2,1,0:T(8,128)(2,1)S(1)}, u32[]{:S(2)}, u32[]{:S(2)}) collective-permute-start(bf16[48,8,128]{2,1,0:T(8,128)(2,1)S(1)} %get-tuple-element.105), channel_id=1, source_target_pairs={{0,16},{16,32},{32,48},{48,64},{64,80},{80,96},{96,112},{112,128},... | collective-permute-start | bytes 294920 | tf_op jit(solution)/shard_map/ppermute | solution.py:382
  57.3 4.2 %collective-permute-start.15 = (bf16[48,8,128]{2,1,0:T(8,128)(2,1)S(1)}, bf16[48,8,128]{2,1,0:T(8,128)(2,1)S(1)}, u32[]{:S(2)}, u32[]{:S(2)}) collective-permute-start(bf16[48,8,128]{2,1,0:T(8,128)(2,1)S(1)} %get-tuple-element.106), channel_id=1, source_target_pairs={{0,240},{16,0},{32,16},{48,32},{64,48},{80,64},{96,80},{112,96},{1... | collective-permute-start | bytes 294920 | tf_op jit(solution)/shard_map/ppermute | solution.py:382

commit v6 on v5

--- a/solution.py
+++ b/solution.py
@@ -451,6 +451,7 @@
                 scratch_shapes=[lookup],
                 compiler_params=params(),
             )(table, turned, rounded, gram, *basis)
+            after = (gram,)
         send_next, send_last = pl.pallas_call(
             relay_kernel,
             name="relay",

time: 93.3 us -> 93.7 us (level)
  transfers between devices with their start and end apart: 16 -> 16, of which waited for: 6 -> 9; matrix products, arithmetic and copies ran while one was open for 0% -> 0% of each run, Pallas kernels for 12% -> 13%
where the time goes in v6:
time: 93.7 us; the launch traced here: 93.5 us
  starting transfers between devices  35.3 us (38%)
  blocking collectives  29.3 us (31%)
  Pallas kernels  19.8 us (21%)
  waiting for transfers between devices  7.62 us (8%)
  between operations  1.44 us (2%)
    ppermute x16, starting transfers between devices, shifted(): lax.ppermute(block, axis, [(i, (i + distance) % SIDE) for i in range(SIDE)])  35.3 us
    all_to_all x1, blocking collectives, per_device(): gathered = lax.all_to_all(gram, ('gx', 'gy'), 0, 0, tiled=True)  29.3 us
    ppermute x16, waiting for transfers between devices, shifted(): lax.ppermute(block, axis, [(i, (i + distance) % SIDE) for i in range(SIDE)])  7.62 us
    pallas_call x3, Pallas kernels, per_device(): pl.pallas_call(functools.partial(ghost_kernel, power), name=f'ghost{power...  3.47 us
    pallas_call x1, Pallas kernels, per_device(): pl.pallas_call(first_half_kernel, name='first_half', in_specs=[IN_HBM] *...  3.42 us
    pallas_call x1, Pallas kernels, per_device(): pl.pallas_call(second_half_kernel, name='second_half', in_specs=[IN_SMEM]...  3.4 us
    pallas_call x3, Pallas kernels, per_device(): pl.pallas_call(functools.partial(local_kernel, power), name=f'local{power...  3.13 us
    pallas_call x1, Pallas kernels, per_device(): pl.pallas_call(plan_kernel, name='plan', in_specs=[IN_SMEM] * 2, out_spec...  2.06 us
  transfers between devices with their start and end apart: 16, of which 9 were waited for; matrix products, arithmetic and copies ran while one was open for 0% of the time, Pallas kernels for 13%

profile of v6, /device:TPU:1, one launch (start us, length us, event | category | flops | bytes accessed | tf_op | source)
XLA Modules:
  0.0 93.5 jit_solution(15528674486504168506)
XLA Ops:
  1.3 1.2 %start.1 = (f32[64,8,128]{2,1,0:T(8,128)S(1)}, bf16[64,8,128]{2,1,0:T(8,128)(2,1)S(1)}, bf16[48,8,128]{2,1,0:T(8,128)(2,1)S(1)}, bf16[48,8,128]{2,1,0:T(8,128)(2...) custom-call(s32[9,1,16]{2,1,0:T(1,128)} %bitcast.8, s32[1]{0:T(128)S(6)} %copy.27.counts, ...), custom_call_target="tpu_custom_call" | custom-call | tf_op jit(solution)/shard_map/start/pallas_call | solution.py:404
  2.5 2.2 %collective-permute-start = (bf16[48,8,128]{2,1,0:T(8,128)(2,1)S(1)}, bf16[48,8,128]{2,1,0:T(8,128)(2,1)S(1)}, u32[]{:S(2)}, u32[]{:S(2)}) collective-permute-start(bf16[48,8,128]{2,1,0:T(8,128)(2,1)S(1)} %get-tuple-element.64), channel_id=1, source_target_pairs={{0,1},{1,2},{2,3},{3,4},{4,5},{5,6},{6,7},{7,8},{8,9},{9,10},{10,1... | collective-permute-start | bytes 294920 | tf_op jit(solution)/shard_map/ppermute | solution.py:382
  4.7 3.7 %collective-permute-start.1 = (bf16[48,8,128]{2,1,0:T(8,128)(2,1)S(1)}, bf16[48,8,128]{2,1,0:T(8,128)(2,1)S(1)}, u32[]{:S(2)}, u32[]{:S(2)}) collective-permute-start(bf16[48,8,128]{2,1,0:T(8,128)(2,1)S(1)} %get-tuple-element.65), channel_id=1, source_target_pairs={{0,15},{1,0},{2,1},{3,2},{4,3},{5,4},{6,5},{7,6},{8,7},{9,8},{10,9... | collective-permute-start | bytes 294920 | tf_op jit(solution)/shard_map/ppermute | solution.py:382
  8.4 3.4 %first_half.1 = (bf16[64,640,128]{2,1,0:T(8,128)(2,1)S(1)}, bf16[16,128,128]{2,1,0:T(8,128)(2,1)S(1)}, bf16[16,4,128,128]{3,2,1,0:T(8,128)(2,1)S(1)}, f32[8,128]{1,0:T(8,128)S(1)}) custom-call(bf16[64,128,128]{2,1,0:T(8,128)(2,1)} %diag.3, bf16[64,4,128,128]{3,2,1,0:T(8,128)(2,1)} %face.3), custom_call_target="tpu_custom_call" | custom-call | tf_op jit(solution)/shard_map/first_half/pallas_call | solution.py:420
  11.9 2.5 %collective-permute-start.2 = (bf16[48,8,128]{2,1,0:T(8,128)(2,1)S(1)}, bf16[48,8,128]{2,1,0:T(8,128)(2,1)S(1)}, u32[]{:S(2)}, u32[]{:S(2)}) collective-permute-start(bf16[48,8,128]{2,1,0:T(8,128)(2,1)S(1)} %get-tuple-element.69), channel_id=1, source_target_pairs={{0,16},{16,32},{32,48},{48,64},{64,80},{80,96},{96,112},{112,128},... | collective-permute-start | bytes 294920 | tf_op jit(solution)/shard_map/ppermute | solution.py:382
  14.7 3.4 %second_half.1 = (bf16[64,640,128]{2,1,0:T(8,128)(2,1)S(1)}, f32[64,8,128]{2,1,0:T(8,128)S(1)}, bf16[64,8,128]{2,1,0:T(8,128)(2,1)S(1)}, s32[8]{0:T(128)S(4)}) custom-call(s32[4,64]{1,0:T(4,128)S(1)} %bitcast.11, bf16[64,128,128]{2,1,0:T(8,128)(2,1)} %diag.3, bf16[64,4,128,128]{3,2,1,0:T(8,128)(2,1)} %face.3, ...), custom_call_target="tpu_custom_call", output_to_operand_aliasing={{0}: (6, {})} | custom-call | tf_op jit(solution)/shard_map/second_half/pallas_call | solution.py:467
  18.8 1.9 %whole.1 = (f32[64,8,128]{2,1,0:T(8,128)S(1)}, bf16[64,8,128]{2,1,0:T(8,128)(2,1)S(1)}, bf16[48,8,128]{2,1,0:T(8,128)(2,1)S(1)}, bf16[48,8,128]{2,1,0:T(8,128)(2...) custom-call(s32[4,64]{1,0:T(4,128)S(1)} %bitcast.12, ...), custom_call_target="tpu_custom_call", output_to_operand_aliasing={{0}: (10, {}), {1}: (11, {})} | custom-call | tf_op jit(solution)/shard_map/whole/pallas_call | solution.py:477
  20.7 4.8 %collective-permute-start.5 = (bf16[48,8,128]{2,1,0:T(8,128)(2,1)S(1)}, bf16[48,8,128]{2,1,0:T(8,128)(2,1)S(1)}, u32[]{:S(2)}, u32[]{:S(2)}) collective-permute-start(bf16[48,8,128]{2,1,0:T(8,128)(2,1)S(1)} %get-tuple-element.76), channel_id=1, source_target_pairs={{0,15},{1,0},{2,1},{3,2},{4,3},{5,4},{6,5},{7,6},{8,7},{9,8},{10,9... | collective-permute-start | bytes 294920 | tf_op jit(solution)/shard_map/ppermute | solution.py:382
  25.5 2.1 %plan.1 = (s32[544]{0:T(1024)S(4)}, f32[8,128]{1,0:T(8,128)}) custom-call(s32[4,64]{1,0:T(4,128)S(1)} %bitcast.13, s32[9,1,16]{2,1,0:T(1,128)S(1)} %bitcast.10), custom_call_target="tpu_custom_call" | custom-call | tf_op jit(solution)/shard_map/plan/pallas_call | solution.py:435
  27.5 1.0 %local1.1 = (f32[64,8,128]{2,1,0:T(8,128)S(1)}, bf16[64,8,128]{2,1,0:T(8,128)(2,1)S(1)}, f32[8,128]{1,0:T(8,128)S(1)}) custom-call(s32[544]{0:T(1024)S(4)} %get-tuple-element.57.refs_0_, bf16[64,640,128]{2,1,0:T(8,128)(2,1)S(1)} %get-tuple-element.62.turned.refs_1_, bf16[64,8,128]{2,1,0:T(8,128)(2,1)S(1)} %get-tuple-element.74.refs_2_, ...), custom_call_target="tpu_custom_call" | custom-call | tf_op jit(solution)/shard_map/local1/pallas_call | solution.py:445
  28.6 1.9 %collective-permute-start.6 = (bf16[48,8,128]{2,1,0:T(8,128)(2,1)S(1)}, bf16[48,8,128]{2,1,0:T(8,128)(2,1)S(1)}, u32[]{:S(2)}, u32[]{:S(2)}) collective-permute-start(bf16[48,8,128]{2,1,0:T(8,128)(2,1)S(1)} %get-tuple-element.82), channel_id=1, source_target_pairs={{0,16},{16,32},{32,48},{48,64},{64,80},{80,96},{96,112},{112,128},... | collective-permute-start | bytes 294920 | tf_op jit(solution)/shard_map/ppermute | solution.py:382
  30.5 1.3 %collective-permute-start.7 = (bf16[48,8,128]{2,1,0:T(8,128)(2,1)S(1)}, bf16[48,8,128]{2,1,0:T(8,128)(2,1)S(1)}, u32[]{:S(2)}, u32[]{:S(2)}) collective-permute-start(bf16[48,8,128]{2,1,0:T(8,128)(2,1)S(1)} %get-tuple-element.83), channel_id=1, source_target_pairs={{0,240},{16,0},{32,16},{48,32},{64,48},{80,64},{96,80},{112,96},{1... | collective-permute-start | bytes 294920 | tf_op jit(solution)/shard_map/ppermute | solution.py:382
  31.8 0.8 collective-permute-done.6.refs_5_
  32.6 2.0 %collective-permute-done.7.refs_6_ = bf16[48,8,128]{2,1,0:T(8,128)(2,1)S(1)} collective-permute-done((bf16[48,8,128]{2,1,0:T(8,128)(2,1)S(1)}, bf16[48,8,128]{2,1,0:T(8,128)(2,1)S(1)}, u32[]{:S(2)}, u32[]{:S(2)}) %collective-permute-start.7) | collective-permute-done | bytes 98336 | tf_op jit(solution)/shard_map/ppermute | solution.py:382
  34.5 1.1 %ghost1.1 = (f32[64,8,128]{2,1,0:T(8,128)S(1)}, bf16[64,8,128]{2,1,0:T(8,128)(2,1)S(1)}, bf16[48,8,128]{2,1,0:T(8,128)(2,1)S(1)}, bf16[48,8,128]{2,1,0:T(8,128)(...) custom-call(s32[544]{0:T(1024)S(4)} %get-tuple-element.57.refs_0_, ...), custom_call_target="tpu_custom_call", output_to_operand_aliasing={{0}: (10, {}), {1}: (11, {})} | custom-call | tf_op jit(solution)/shard_map/ghost1/pallas_call | solution.py:492
  35.8 4.9 %collective-permute-start.9 = (bf16[48,8,128]{2,1,0:T(8,128)(2,1)S(1)}, bf16[48,8,128]{2,1,0:T(8,128)(2,1)S(1)}, u32[]{:S(2)}, u32[]{:S(2)}) collective-permute-start(bf16[48,8,128]{2,1,0:T(8,128)(2,1)S(1)} %get-tuple-element.88), channel_id=1, source_target_pairs={{0,15},{1,0},{2,1},{3,2},{4,3},{5,4},{6,5},{7,6},{8,7},{9,8},{10,9... | collective-permute-start | bytes 294920 | tf_op jit(solution)/shard_map/ppermute | solution.py:382
  40.6 1.0 %local2.1 = (f32[64,8,128]{2,1,0:T(8,128)S(1)}, bf16[64,8,128]{2,1,0:T(8,128)(2,1)S(1)}, f32[8,128]{1,0:T(8,128)S(1)}) custom-call(s32[544]{0:T(1024)S(4)} %get-tuple-element.57.refs_0_, bf16[64,640,128]{2,1,0:T(8,128)(2,1)S(1)} %get-tuple-element.62.turned.refs_1_, bf16[64,8,128]{2,1,0:T(8,128)(2,1)S(1)} %get-tuple-element.86.refs_2_, ...), custom_call_target="tpu_custom_call" | custom-call | tf_op jit(solution)/shard_map/local2/pallas_call | solution.py:445
  41.7 0.9 collective-permute-done.8.refs_0_.refs_3_
  42.6 1.2 %collective-permute-start.10 = (bf16[48,8,128]{2,1,0:T(8,128)(2,1)S(1)}, bf16[48,8,128]{2,1,0:T(8,128)(2,1)S(1)}, u32[]{:S(2)}, u32[]{:S(2)}) collective-permute-start(bf16[48,8,128]{2,1,0:T(8,128)(2,1)S(1)} %get-tuple-element.94), channel_id=1, source_target_pairs={{0,16},{16,32},{32,48},{48,64},{64,80},{80,96},{96,112},{112,128},... | collective-permute-start | bytes 294920 | tf_op jit(solution)/shard_map/ppermute | solution.py:382
  43.7 2.5 %collective-permute-start.11 = (bf16[48,8,128]{2,1,0:T(8,128)(2,1)S(1)}, bf16[48,8,128]{2,1,0:T(8,128)(2,1)S(1)}, u32[]{:S(2)}, u32[]{:S(2)}) collective-permute-start(bf16[48,8,128]{2,1,0:T(8,128)(2,1)S(1)} %get-tuple-element.95), channel_id=1, source_target_pairs={{0,240},{16,0},{32,16},{48,32},{64,48},{80,64},{96,80},{112,96},{1... | collective-permute-start | bytes 294920 | tf_op jit(solution)/shard_map/ppermute | solution.py:382
  46.2 0.8 collective-permute-done.10.refs_5_
  47.0 0.7 collective-permute-done.11.refs_6_
  47.8 1.1 %ghost2.1 = (f32[64,8,128]{2,1,0:T(8,128)S(1)}, bf16[64,8,128]{2,1,0:T(8,128)(2,1)S(1)}, bf16[48,8,128]{2,1,0:T(8,128)(2,1)S(1)}, bf16[48,8,128]{2,1,0:T(8,128)(...) custom-call(s32[544]{0:T(1024)S(4)} %get-tuple-element.57.refs_0_, ...), custom_call_target="tpu_custom_call", output_to_operand_aliasing={{0}: (11, {}), {1}: (12, {})} | custom-call | tf_op jit(solution)/shard_map/ghost2/pallas_call | solution.py:492
  49.2 5.3 %collective-permute-start.13 = (bf16[48,8,128]{2,1,0:T(8,128)(2,1)S(1)}, bf16[48,8,128]{2,1,0:T(8,128)(2,1)S(1)}, u32[]{:S(2)}, u32[]{:S(2)}) collective-permute-start(bf16[48,8,128]{2,1,0:T(8,128)(2,1)S(1)} %get-tuple-element.100), channel_id=1, source_target_pairs={{0,15},{1,0},{2,1},{3,2},{4,3},{5,4},{6,5},{7,6},{8,7},{9,8},{10,9... | collective-permute-start | bytes 294920 | tf_op jit(solution)/shard_map/ppermute | solution.py:382
  54.5 1.1 %local3.1 = (f32[64,8,128]{2,1,0:T(8,128)S(1)}, bf16[64,8,128]{2,1,0:T(8,128)(2,1)S(1)}, f32[8,128]{1,0:T(8,128)S(1)}) custom-call(s32[544]{0:T(1024)S(4)} %get-tuple-element.57.refs_0_, bf16[64,640,128]{2,1,0:T(8,128)(2,1)S(1)} %get-tuple-element.62.turned.refs_1_, bf16[64,8,128]{2,1,0:T(8,128)(2,1)S(1)} %get-tuple-element.98.refs_2_, ...), custom_call_target="tpu_custom_call" | custom-call | tf_op jit(solution)/shard_map/local3/pallas_call | solution.py:445
  55.6 0.9 collective-permute-done.12.refs_0_.refs_3_
  56.5 0.9 collective-permute-start.14
  57.4 3.5 %collective-permute-start.15 = (bf16[48,8,128]{2,1,0:T(8,128)(2,1)S(1)}, bf16[48,8,128]{2,1,0:T(8,128)(2,1)S(1)}, u32[]{:S(2)}, u32[]{:S(2)}) collective-permute-start(bf16[48,8,128]{2,1,0:T(8,128)(2,1)S(1)} %get-tuple-element.107), channel_id=1, source_target_pairs={{0,240},{16,0},{32,16},{48,32},{64,48},{80,64},{96,80},{112,96},{1... | collective-permute-start | bytes 294920 | tf_op jit(solution)/shard_map/ppermute | solution.py:382
  60.9 0.8 collective-permute-done.14.refs_5_
  61.8 1.2 %ghost3.1 = (f32[64,8,128]{2,1,0:T(8,128)S(1)}, bf16[64,8,128]{2,1,0:T(8,128)(2,1)S(1)}, f32[256,128]{1,0:T(8,128)S(1)}) custom-call(s32[544]{0:T(1024)S(4)} %get-tuple-element.57.refs_0_, bf16[64,640,128]{2,1,0:T(8,128)(2,1)S(1)} %get-tuple-element.62.turned.refs_1_, ...), custom_call_target="tpu_custom_call", output_to_operand_aliasing={{0}: (12, {}), {1}: (13, {})} | custom-call | tf_op jit(solution)/shard_map/ghost3/pallas_call | solution.py:492
  63.0 29.3 %all_to_all.11 = f32[256,1,128]{2,1,0:T(1,128)S(1)} all-to-all(f32[256,1,128]{2,1,0:T(1,128)S(1)} %bitcast.7), channel_id=1, replica_groups=mesh['gx'=16,'gy'=16] {'gx','gy'}, dimensions={0} | all-to-all | bytes 262144 | tf_op jit(solution)/shard_map/all_to_all | solution.py:509
  92.4 1.2 %finish.1 = (f32[64,8,128]{2,1,0:T(8,128)}, f32[64,8,128]{2,1,0:T(8,128)}) custom-call(f32[256,128]{1,0:T(8,128)S(1)} %bitcast.6, f32[64,8,128]{2,1,0:T(8,128)S(1)} %get-tuple-element.71.b0.refs_4_.refs_8_, f32[64,8,128]{2,1,0:T(8,128)S(1)} %get-tuple-element.80.refs_5_.refs_9_.b1, f32[64,8,128]{2,1,0:T(8,128)S(1)} %get-tuple-element.92.refs_6_.refs_10_.b2, ...), custom_call_target="tpu_custom_call" | custom-call | tf_op jit(solution)/shard_map/finish/pallas_call | solution.py:510
  (21 shorter events, 1.5 us)
Async XLA Ops:
  0.6 14.0 %copy-start.1 = (s32[64,4]{0,1:T(4,128)S(1)}, s32[64,4]{0,1:T(4,128)}, u32[]{:S(2)}) copy-start(s32[64,4]{0,1:T(4,128)} %param.9) | copy-start | bytes 3076
  2.5 9.4 %collective-permute-start = (bf16[48,8,128]{2,1,0:T(8,128)(2,1)S(1)}, bf16[48,8,128]{2,1,0:T(8,128)(2,1)S(1)}, u32[]{:S(2)}, u32[]{:S(2)}) collective-permute-start(bf16[48,8,128]{2,1,0:T(8,128)(2,1)S(1)} %get-tuple-element.64), channel_id=1, source_target_pairs={{0,1},{1,2},{2,3},{3,4},{4,5},{5,6},{6,7},{7,8},{8,9},{9,10},{10,1... | collective-permute-start | bytes 294920 | tf_op jit(solution)/shard_map/ppermute | solution.py:382
  4.7 7.2 %collective-permute-start.1 = (bf16[48,8,128]{2,1,0:T(8,128)(2,1)S(1)}, bf16[48,8,128]{2,1,0:T(8,128)(2,1)S(1)}, u32[]{:S(2)}, u32[]{:S(2)}) collective-permute-start(bf16[48,8,128]{2,1,0:T(8,128)(2,1)S(1)} %get-tuple-element.65), channel_id=1, source_target_pairs={{0,15},{1,0},{2,1},{3,2},{4,3},{5,4},{6,5},{7,6},{8,7},{9,8},{10,9... | collective-permute-start | bytes 294920 | tf_op jit(solution)/shard_map/ppermute | solution.py:382
  11.9 6.2 %collective-permute-start.2 = (bf16[48,8,128]{2,1,0:T(8,128)(2,1)S(1)}, bf16[48,8,128]{2,1,0:T(8,128)(2,1)S(1)}, u32[]{:S(2)}, u32[]{:S(2)}) collective-permute-start(bf16[48,8,128]{2,1,0:T(8,128)(2,1)S(1)} %get-tuple-element.69), channel_id=1, source_target_pairs={{0,16},{16,32},{32,48},{48,64},{64,80},{80,96},{96,112},{112,128},... | collective-permute-start | bytes 294920 | tf_op jit(solution)/shard_map/ppermute | solution.py:382
  14.4 4.3 %collective-permute-start.3 = (bf16[48,8,128]{2,1,0:T(8,128)(2,1)S(1)}, bf16[48,8,128]{2,1,0:T(8,128)(2,1)S(1)}, u32[]{:S(2)}, u32[]{:S(2)}) collective-permute-start(bf16[48,8,128]{2,1,0:T(8,128)(2,1)S(1)} %get-tuple-element.70), channel_id=1, source_target_pairs={{0,240},{16,0},{32,16},{48,32},{64,48},{80,64},{96,80},{112,96},{1... | collective-permute-start | bytes 294920 | tf_op jit(solution)/shard_map/ppermute | solution.py:382
  14.7 4.1 %copy-start = (s32[1,9,16]{2,0,1:T(1,128)S(1)}, s32[1,9,16]{2,0,1:T(1,128)}, u32[]{:S(2)}) copy-start(s32[1,9,16]{2,0,1:T(1,128)} %param.10) | copy-start | bytes 1732
  20.7 7.9 %collective-permute-start.4 = (bf16[48,8,128]{2,1,0:T(8,128)(2,1)S(1)}, bf16[48,8,128]{2,1,0:T(8,128)(2,1)S(1)}, u32[]{:S(2)}, u32[]{:S(2)}) collective-permute-start(bf16[48,8,128]{2,1,0:T(8,128)(2,1)S(1)} %get-tuple-element.75), channel_id=1, source_target_pairs={{0,1},{1,2},{2,3},{3,4},{4,5},{5,6},{6,7},{7,8},{8,9},{9,10},{10,1... | collective-permute-start | bytes 294920 | tf_op jit(solution)/shard_map/ppermute | solution.py:382
  20.7 7.9 %collective-permute-start.5 = (bf16[48,8,128]{2,1,0:T(8,128)(2,1)S(1)}, bf16[48,8,128]{2,1,0:T(8,128)(2,1)S(1)}, u32[]{:S(2)}, u32[]{:S(2)}) collective-permute-start(bf16[48,8,128]{2,1,0:T(8,128)(2,1)S(1)} %get-tuple-element.76), channel_id=1, source_target_pairs={{0,15},{1,0},{2,1},{3,2},{4,3},{5,4},{6,5},{7,6},{8,7},{9,8},{10,9... | collective-permute-start | bytes 294920 | tf_op jit(solution)/shard_map/ppermute | solution.py:382
  28.6 4.0 %collective-permute-start.6 = (bf16[48,8,128]{2,1,0:T(8,128)(2,1)S(1)}, bf16[48,8,128]{2,1,0:T(8,128)(2,1)S(1)}, u32[]{:S(2)}, u32[]{:S(2)}) collective-permute-start(bf16[48,8,128]{2,1,0:T(8,128)(2,1)S(1)} %get-tuple-element.82), channel_id=1, source_target_pairs={{0,16},{16,32},{32,48},{48,64},{64,80},{80,96},{96,112},{112,128},... | collective-permute-start | bytes 294920 | tf_op jit(solution)/shard_map/ppermute | solution.py:382
  30.5 4.0 %collective-permute-start.7 = (bf16[48,8,128]{2,1,0:T(8,128)(2,1)S(1)}, bf16[48,8,128]{2,1,0:T(8,128)(2,1)S(1)}, u32[]{:S(2)}, u32[]{:S(2)}) collective-permute-start(bf16[48,8,128]{2,1,0:T(8,128)(2,1)S(1)} %get-tuple-element.83), channel_id=1, source_target_pairs={{0,240},{16,0},{32,16},{48,32},{64,48},{80,64},{96,80},{112,96},{1... | collective-permute-start | bytes 294920 | tf_op jit(solution)/shard_map/ppermute | solution.py:382
  35.7 6.9 %collective-permute-start.8 = (bf16[48,8,128]{2,1,0:T(8,128)(2,1)S(1)}, bf16[48,8,128]{2,1,0:T(8,128)(2,1)S(1)}, u32[]{:S(2)}, u32[]{:S(2)}) collective-permute-start(bf16[48,8,128]{2,1,0:T(8,128)(2,1)S(1)} %get-tuple-element.87), channel_id=1, source_target_pairs={{0,1},{1,2},{2,3},{3,4},{4,5},{5,6},{6,7},{7,8},{8,9},{9,10},{10,1... | collective-permute-start | bytes 294920 | tf_op jit(solution)/shard_map/ppermute | solution.py:382
  35.8 6.8 %collective-permute-start.9 = (bf16[48,8,128]{2,1,0:T(8,128)(2,1)S(1)}, bf16[48,8,128]{2,1,0:T(8,128)(2,1)S(1)}, u32[]{:S(2)}, u32[]{:S(2)}) collective-permute-start(bf16[48,8,128]{2,1,0:T(8,128)(2,1)S(1)} %get-tuple-element.88), channel_id=1, source_target_pairs={{0,15},{1,0},{2,1},{3,2},{4,3},{5,4},{6,5},{7,6},{8,7},{9,8},{10,9... | collective-permute-start | bytes 294920 | tf_op jit(solution)/shard_map/ppermute | solution.py:382
  42.6 4.5 %collective-permute-start.10 = (bf16[48,8,128]{2,1,0:T(8,128)(2,1)S(1)}, bf16[48,8,128]{2,1,0:T(8,128)(2,1)S(1)}, u32[]{:S(2)}, u32[]{:S(2)}) collective-permute-start(bf16[48,8,128]{2,1,0:T(8,128)(2,1)S(1)} %get-tuple-element.94), channel_id=1, source_target_pairs={{0,16},{16,32},{32,48},{48,64},{64,80},{80,96},{96,112},{112,128},... | collective-permute-start | bytes 294920 | tf_op jit(solution)/shard_map/ppermute | solution.py:382
  43.7 4.0 %collective-permute-start.11 = (bf16[48,8,128]{2,1,0:T(8,128)(2,1)S(1)}, bf16[48,8,128]{2,1,0:T(8,128)(2,1)S(1)}, u32[]{:S(2)}, u32[]{:S(2)}) collective-permute-start(bf16[48,8,128]{2,1,0:T(8,128)(2,1)S(1)} %get-tuple-element.95), channel_id=1, source_target_pairs={{0,240},{16,0},{32,16},{48,32},{64,48},{80,64},{96,80},{112,96},{1... | collective-permute-start | bytes 294920 | tf_op jit(solution)/shard_map/ppermute | solution.py:382
  48.9 7.5 %collective-permute-start.12 = (bf16[48,8,128]{2,1,0:T(8,128)(2,1)S(1)}, bf16[48,8,128]{2,1,0:T(8,128)(2,1)S(1)}, u32[]{:S(2)}, u32[]{:S(2)}) collective-permute-start(bf16[48,8,128]{2,1,0:T(8,128)(2,1)S(1)} %get-tuple-element.99), channel_id=1, source_target_pairs={{0,1},{1,2},{2,3},{3,4},{4,5},{5,6},{6,7},{7,8},{8,9},{9,10},{10,1... | collective-permute-start | bytes 294920 | tf_op jit(solution)/shard_map/ppermute | solution.py:382
  49.2 7.3 %collective-permute-start.13 = (bf16[48,8,128]{2,1,0:T(8,128)(2,1)S(1)}, bf16[48,8,128]{2,1,0:T(8,128)(2,1)S(1)}, u32[]{:S(2)}, u32[]{:S(2)}) collective-permute-start(bf16[48,8,128]{2,1,0:T(8,128)(2,1)S(1)} %get-tuple-element.100), channel_id=1, source_target_pairs={{0,15},{1,0},{2,1},{3,2},{4,3},{5,4},{6,5},{7,6},{8,7},{9,8},{10,9... | collective-permute-start | bytes 294920 | tf_op jit(solution)/shard_map/ppermute | solution.py:382
  56.5 5.2 %collective-permute-start.14 = (bf16[48,8,128]{2,1,0:T(8,128)(2,1)S(1)}, bf16[48,8,128]{2,1,0:T(8,128)(2,1)S(1)}, u32[]{:S(2)}, u32[]{:S(2)}) collective-permute-start(bf16[48,8,128]{2,1,0:T(8,128)(2,1)S(1)} %get-tuple-element.106), channel_id=1, source_target_pairs={{0,16},{16,32},{32,48},{48,64},{64,80},{80,96},{96,112},{112,128},... | collective-permute-start | bytes 294920 | tf_op jit(solution)/shard_map/ppermute | solution.py:382
  57.4 4.5 %collective-permute-start.15 = (bf16[48,8,128]{2,1,0:T(8,128)(2,1)S(1)}, bf16[48,8,128]{2,1,0:T(8,128)(2,1)S(1)}, u32[]{:S(2)}, u32[]{:S(2)}) collective-permute-start(bf16[48,8,128]{2,1,0:T(8,128)(2,1)S(1)} %get-tuple-element.107), channel_id=1, source_target_pairs={{0,240},{16,0},{32,16},{48,32},{64,48},{80,64},{96,80},{112,96},{1... | collective-permute-start | bytes 294920 | tf_op jit(solution)/shard_map/ppermute | solution.py:382

commit v7 on v5

--- a/solution.py
+++ b/solution.py
@@ -65,12 +65,21 @@
 
 
 def start_kernel(
-    send_slots, counts, right_sides, basis, rounded, up, down, next_row, last_row
+    neighbours_from, slots_from, counts, right_sides, basis, rounded, up, down,
+    next_row, last_row, neighbours, send_slots, arrived,
 ):
+    tables = (
+        pltpu.make_async_copy(slots_from, send_slots, arrived.at[0]),
+        pltpu.make_async_copy(neighbours_from, neighbours, arrived.at[1]),
+    )
+    for copy in tables:
+        copy.start()
     element = lax.broadcasted_iota(jnp.int32, basis.shape, 0)
     live = jnp.where(element < counts[0], right_sides[...], 0.0)
     basis[...] = live
     rounded[...] = live.astype(jnp.bfloat16)
+    for copy in tables:
+        copy.wait()
     pack(listed(send_slots), rounded, up, down, next_row, last_row)
 
 
@@ -325,7 +334,9 @@
         gram_out[...] = gram
 
 
-def finish_kernel(gram_rows, b0, b1, b2, b3, b4, solution, residual):
+def finish_kernel(
+    gram_rows, b0, b1, b2, b3, b4, solution_out, residual_out, solution, residual, left
+):
     lane = lax.broadcasted_iota(jnp.int32, (8, ROWS), 1)
     side = lax.broadcasted_iota(jnp.int32, (8, ROWS), 0)
     row = jnp.sum(gram_rows[...], axis=0, keepdims=True)
@@ -375,7 +386,18 @@
             residual[e] = v[0] - moved
         return carry
 
-    lax.fori_loop(0, CAP // 8, several, 0)
+    leaving = []
+    for part in range(4):
+        lax.fori_loop(part * QUARTER // 8, (part + 1) * QUARTER // 8, several, 0)
+        rows = pl.ds(part * QUARTER, QUARTER)
+        for at, (here, there) in enumerate(
+            ((solution, solution_out), (residual, residual_out))
+        ):
+            copy = pltpu.make_async_copy(here.at[rows], there.at[rows], left.at[part, at])
+            copy.start()
+            leaving.append(copy)
+    for copy in leaving:
+        copy.wait()
 
 
 def shifted(block, axis, distance):
@@ -401,14 +423,17 @@
         pltpu.VMEM((QUARTER, FACES, ROWS, ROWS), half),
     ]
     arrived = pltpu.SemaphoreType.DMA((2,))
-    first, rounded, up, down, next_row, last_row = pl.pallas_call(
+    *outs, neighbours, send_slots = pl.pallas_call(
         start_kernel,
         name="start",
-        in_specs=[IN_SMEM, IN_SMEM, IN_VMEM],
-        out_specs=[IN_VMEM] * 6,
-        out_shape=[full, narrow] + packets,
+        in_specs=[IN_HBM, IN_HBM, IN_SMEM, IN_VMEM],
+        out_specs=[IN_VMEM] * 6 + [IN_SMEM] * 2,
+        out_shape=[full, narrow] + packets
+        + [pltpu.SMEM(table.shape, jnp.int32) for table in (neighbours, send_slots)],
+        scratch_shapes=[arrived],
         compiler_params=params(),
-    )(in_place(send_slots), counts, in_place(right_sides))
+    )(in_place(neighbours), in_place(send_slots), counts, in_place(right_sides))
+    first, rounded, up, down, next_row, last_row = outs
     basis = [first]
     gram = None
     for power in range(POWERS):
@@ -510,8 +535,10 @@
         finish_kernel,
         name="finish",
         in_specs=[IN_VMEM] * 6,
-        out_specs=[IN_VMEM] * 2,
+        out_specs=[IN_HBM] * 2,
         out_shape=[full] * 2,
+        scratch_shapes=[pltpu.VMEM((CAP, 8, ROWS), jnp.float32)] * 2
+        + [pltpu.SemaphoreType.DMA((4, 2))],
         compiler_params=params(),
     )(gathered, *basis)
 

time: 93.3 us -> 92.9 us (level)
  Pallas kernels: 19.2 us -> 17.3 us
  waiting for transfers between devices: 8.26 us -> 9.89 us
    ppermute x16, waiting for transfers between devices: 8.26 us -> 9.89 us  [shifted(): lax.ppermute(block, axis, [(i, (i + distance) % SIDE) for i in range(SIDE)])]
    pallas_call x1, Pallas kernels: 1.47 us -> 0.01 us  [per_device(): pl.pallas_call(plan_kernel, name='plan', in_specs=[IN_SMEM] * 2, out_spec...]
  transfers between devices with their start and end apart: 16 -> 16, of which waited for: 6 -> 6; matrix products, arithmetic and copies ran while one was open for 0% -> 0% of each run, Pallas kernels for 12% -> 10%
where the time goes in v7:
time: 92.9 us; the launch traced here: 92.6 us
  starting transfers between devices  34.6 us (37%)
  blocking collectives  29.2 us (31%)
  Pallas kernels  17.3 us (19%)
  waiting for transfers between devices  9.89 us (11%)
  between operations  1.58 us (2%)
    ppermute x16, starting transfers between devices, shifted(): lax.ppermute(block, axis, [(i, (i + distance) % SIDE) for i in range(SIDE)])  34.6 us
    all_to_all x1, blocking collectives, per_device(): gathered = lax.all_to_all(gram, ('gx', 'gy'), 0, 0, tiled=True)  29.2 us
    ppermute x16, waiting for transfers between devices, shifted(): lax.ppermute(block, axis, [(i, (i + distance) % SIDE) for i in range(SIDE)])  9.89 us
    pallas_call x3, Pallas kernels, per_device(): pl.pallas_call(functools.partial(ghost_kernel, power), name=f'ghost{power...  3.58 us
    pallas_call x1, Pallas kernels, per_device(): pl.pallas_call(first_half_kernel, name='first_half', in_specs=[IN_HBM] *...  3.42 us
    pallas_call x3, Pallas kernels, per_device(): pl.pallas_call(functools.partial(local_kernel, power), name=f'local{power...  3.11 us
    pallas_call x1, Pallas kernels, per_device(): pl.pallas_call(second_half_kernel, name='second_half', in_specs=[IN_SMEM]...  2.83 us
    pallas_call x1, Pallas kernels, per_device(): pl.pallas_call(start_kernel, name='start', in_specs=[IN_HBM, IN_HBM, IN_S...  1.94 us
  transfers between devices with their start and end apart: 16, of which 6 were waited for; matrix products, arithmetic and copies ran while one was open for 0% of the time, Pallas kernels for 10%

profile of v7, /device:TPU:1, one launch (start us, length us, event | category | flops | bytes accessed | tf_op | source)
XLA Modules:
  0.0 92.6 jit_solution(15229482905143729658)
XLA Ops:
  1.3 1.9 %start.1 = (f32[64,8,128]{2,1,0:T(8,128)S(1)}, bf16[64,8,128]{2,1,0:T(8,128)(2,1)S(1)}, bf16[48,8,128]{2,1,0:T(8,128)(2,1)S(1)}, bf16[48,8,128]{2,1,0:T(8,128)(2...) custom-call(s32[4,64]{1,0:T(4,128)} %bitcast.9, ...), custom_call_target="tpu_custom_call" | custom-call | tf_op jit(solution)/shard_map/start/pallas_call | solution.py:426
  3.2 2.2 %collective-permute-start = (bf16[48,8,128]{2,1,0:T(8,128)(2,1)S(1)}, bf16[48,8,128]{2,1,0:T(8,128)(2,1)S(1)}, u32[]{:S(2)}, u32[]{:S(2)}) collective-permute-start(bf16[48,8,128]{2,1,0:T(8,128)(2,1)S(1)} %get-tuple-element.69), channel_id=1, source_target_pairs={{0,1},{1,2},{2,3},{3,4},{4,5},{5,6},{6,7},{7,8},{8,9},{9,10},{10,1... | collective-permute-start | bytes 294920 | tf_op jit(solution)/shard_map/ppermute | solution.py:404
  5.4 3.7 %collective-permute-start.1 = (bf16[48,8,128]{2,1,0:T(8,128)(2,1)S(1)}, bf16[48,8,128]{2,1,0:T(8,128)(2,1)S(1)}, u32[]{:S(2)}, u32[]{:S(2)}) collective-permute-start(bf16[48,8,128]{2,1,0:T(8,128)(2,1)S(1)} %get-tuple-element.70), channel_id=1, source_target_pairs={{0,15},{1,0},{2,1},{3,2},{4,3},{5,4},{6,5},{7,6},{8,7},{9,8},{10,9... | collective-permute-start | bytes 294920 | tf_op jit(solution)/shard_map/ppermute | solution.py:404
  9.1 3.4 %first_half.1 = (bf16[64,640,128]{2,1,0:T(8,128)(2,1)S(1)}, bf16[16,128,128]{2,1,0:T(8,128)(2,1)S(1)}, bf16[16,4,128,128]{3,2,1,0:T(8,128)(2,1)S(1)}, f32[8,128]{1,0:T(8,128)S(1)}) custom-call(bf16[64,128,128]{2,1,0:T(8,128)(2,1)} %diag.3, bf16[64,4,128,128]{3,2,1,0:T(8,128)(2,1)} %face.3), custom_call_target="tpu_custom_call" | custom-call | tf_op jit(solution)/shard_map/first_half/pallas_call | solution.py:445
  12.6 2.5 %collective-permute-start.2 = (bf16[48,8,128]{2,1,0:T(8,128)(2,1)S(1)}, bf16[48,8,128]{2,1,0:T(8,128)(2,1)S(1)}, u32[]{:S(2)}, u32[]{:S(2)}) collective-permute-start(bf16[48,8,128]{2,1,0:T(8,128)(2,1)S(1)} %get-tuple-element.74), channel_id=1, source_target_pairs={{0,16},{16,32},{32,48},{48,64},{64,80},{80,96},{96,112},{112,128},... | collective-permute-start | bytes 294920 | tf_op jit(solution)/shard_map/ppermute | solution.py:404
  15.2 0.2 collective-permute-start.3
  15.4 2.8 %second_half.1 = (bf16[64,640,128]{2,1,0:T(8,128)(2,1)S(1)}, f32[64,8,128]{2,1,0:T(8,128)S(1)}, bf16[64,8,128]{2,1,0:T(8,128)(2,1)S(1)}, s32[8]{0:T(128)S(4)}) custom-call(s32[4,64]{1,0:T(4,128)S(4)} %get-tuple-element.60.neighbours, bf16[64,128,128]{2,1,0:T(8,128)(2,1)} %diag.3, bf16[64,4,128,128]{3,2,1,0:T(8,128)(2,1)} %face.3, ...), custom_call_target="tpu_custom_call", output_to_operand_aliasing={{0}: (6, {})} | custom-call | tf_op jit(solution)/shard_map/second_half/pallas_call | solution.py:491
  18.3 1.2 %collective-permute-done.3.from_next = bf16[48,8,128]{2,1,0:T(8,128)(2,1)S(1)} collective-permute-done((bf16[48,8,128]{2,1,0:T(8,128)(2,1)S(1)}, bf16[48,8,128]{2,1,0:T(8,128)(2,1)S(1)}, u32[]{:S(2)}, u32[]{:S(2)}) %collective-permute-start.3) | collective-permute-done | bytes 98336 | tf_op jit(solution)/shard_map/ppermute | solution.py:404
  19.5 1.3 %whole.1 = (f32[64,8,128]{2,1,0:T(8,128)S(1)}, bf16[64,8,128]{2,1,0:T(8,128)(2,1)S(1)}, bf16[48,8,128]{2,1,0:T(8,128)(2,1)S(1)}, bf16[48,8,128]{2,1,0:T(8,128)(2...) custom-call(s32[4,64]{1,0:T(4,128)S(4)} %get-tuple-element.60.neighb, ...), custom_call_target="tpu_custom_call", output_to_operand_aliasing={{0}: (10, {}), {1}: (11, {})} | custom-call | tf_op jit(solution)/shard_map/whole/pallas_call | solution.py:501
  20.8 4.8 %collective-permute-start.5 = (bf16[48,8,128]{2,1,0:T(8,128)(2,1)S(1)}, bf16[48,8,128]{2,1,0:T(8,128)(2,1)S(1)}, u32[]{:S(2)}, u32[]{:S(2)}) collective-permute-start(bf16[48,8,128]{2,1,0:T(8,128)(2,1)S(1)} %get-tuple-element.81), channel_id=1, source_target_pairs={{0,15},{1,0},{2,1},{3,2},{4,3},{5,4},{6,5},{7,6},{8,7},{9,8},{10,9... | collective-permute-start | bytes 294920 | tf_op jit(solution)/shard_map/ppermute | solution.py:404
  25.6 2.0 %collective-permute-done.4.refs_0_.refs_3_ = bf16[48,8,128]{2,1,0:T(8,128)(2,1)S(1)} collective-permute-done((bf16[48,8,128]{2,1,0:T(8,128)(2,1)S(1)}, bf16[48,8,128]{2,1,0:T(8,128)(2,1)S(1)}, u32[]{:S(2)}, u32[]{:S(2)}) %collective-permute-start.4) | collective-permute-done | bytes 98336 | tf_op jit(solution)/shard_map/ppermute | solution.py:404
  27.6 2.1 %collective-permute-start.6 = (bf16[48,8,128]{2,1,0:T(8,128)(2,1)S(1)}, bf16[48,8,128]{2,1,0:T(8,128)(2,1)S(1)}, u32[]{:S(2)}, u32[]{:S(2)}) collective-permute-start(bf16[48,8,128]{2,1,0:T(8,128)(2,1)S(1)} %get-tuple-element.85), channel_id=1, source_target_pairs={{0,16},{16,32},{32,48},{48,64},{64,80},{80,96},{96,112},{112,128},... | collective-permute-start | bytes 294920 | tf_op jit(solution)/shard_map/ppermute | solution.py:404
  29.7 1.1 %collective-permute-start.7 = (bf16[48,8,128]{2,1,0:T(8,128)(2,1)S(1)}, bf16[48,8,128]{2,1,0:T(8,128)(2,1)S(1)}, u32[]{:S(2)}, u32[]{:S(2)}) collective-permute-start(bf16[48,8,128]{2,1,0:T(8,128)(2,1)S(1)} %get-tuple-element.86), channel_id=1, source_target_pairs={{0,240},{16,0},{32,16},{48,32},{64,48},{80,64},{96,80},{112,96},{1... | collective-permute-start | bytes 294920 | tf_op jit(solution)/shard_map/ppermute | solution.py:404
  30.8 1.0 %local1.1 = (f32[64,8,128]{2,1,0:T(8,128)S(1)}, bf16[64,8,128]{2,1,0:T(8,128)(2,1)S(1)}, f32[8,128]{1,0:T(8,128)S(1)}) custom-call(s32[544]{0:T(1024)S(4)} %get-tuple-element.62.refs_0_, bf16[64,640,128]{2,1,0:T(8,128)(2,1)S(1)} %get-tuple-element.67.turned.refs_1_, bf16[64,8,128]{2,1,0:T(8,128)(2,1)S(1)} %get-tuple-element.79.refs_2_, ...), custom_call_target="tpu_custom_call" | custom-call | tf_op jit(solution)/shard_map/local1/pallas_call | solution.py:470
  31.9 1.9 %collective-permute-done.7.refs_6_ = bf16[48,8,128]{2,1,0:T(8,128)(2,1)S(1)} collective-permute-done((bf16[48,8,128]{2,1,0:T(8,128)(2,1)S(1)}, bf16[48,8,128]{2,1,0:T(8,128)(2,1)S(1)}, u32[]{:S(2)}, u32[]{:S(2)}) %collective-permute-start.7) | collective-permute-done | bytes 98336 | tf_op jit(solution)/shard_map/ppermute | solution.py:404
  33.8 1.1 %ghost1.1 = (f32[64,8,128]{2,1,0:T(8,128)S(1)}, bf16[64,8,128]{2,1,0:T(8,128)(2,1)S(1)}, bf16[48,8,128]{2,1,0:T(8,128)(2,1)S(1)}, bf16[48,8,128]{2,1,0:T(8,128)(...) custom-call(s32[544]{0:T(1024)S(4)} %get-tuple-element.62.refs_0_, ...), custom_call_target="tpu_custom_call", output_to_operand_aliasing={{0}: (10, {}), {1}: (11, {})} | custom-call | tf_op jit(solution)/shard_map/ghost1/pallas_call | solution.py:516
  34.9 0.1 collective-permute-start.8
  35.0 5.3 %collective-permute-start.9 = (bf16[48,8,128]{2,1,0:T(8,128)(2,1)S(1)}, bf16[48,8,128]{2,1,0:T(8,128)(2,1)S(1)}, u32[]{:S(2)}, u32[]{:S(2)}) collective-permute-start(bf16[48,8,128]{2,1,0:T(8,128)(2,1)S(1)} %get-tuple-element.94), channel_id=1, source_target_pairs={{0,15},{1,0},{2,1},{3,2},{4,3},{5,4},{6,5},{7,6},{8,7},{9,8},{10,9... | collective-permute-start | bytes 294920 | tf_op jit(solution)/shard_map/ppermute | solution.py:404
  40.3 1.9 %collective-permute-done.8.refs_0_.refs_3_ = bf16[48,8,128]{2,1,0:T(8,128)(2,1)S(1)} collective-permute-done((bf16[48,8,128]{2,1,0:T(8,128)(2,1)S(1)}, bf16[48,8,128]{2,1,0:T(8,128)(2,1)S(1)}, u32[]{:S(2)}, u32[]{:S(2)}) %collective-permute-start.8) | collective-permute-done | bytes 98336 | tf_op jit(solution)/shard_map/ppermute | solution.py:404
  42.3 0.9 collective-permute-start.10
  43.1 2.1 %collective-permute-start.11 = (bf16[48,8,128]{2,1,0:T(8,128)(2,1)S(1)}, bf16[48,8,128]{2,1,0:T(8,128)(2,1)S(1)}, u32[]{:S(2)}, u32[]{:S(2)}) collective-permute-start(bf16[48,8,128]{2,1,0:T(8,128)(2,1)S(1)} %get-tuple-element.98), channel_id=1, source_target_pairs={{0,240},{16,0},{32,16},{48,32},{64,48},{80,64},{96,80},{112,96},{1... | collective-permute-start | bytes 294920 | tf_op jit(solution)/shard_map/ppermute | solution.py:404
  45.3 1.0 %local2.1 = (f32[64,8,128]{2,1,0:T(8,128)S(1)}, bf16[64,8,128]{2,1,0:T(8,128)(2,1)S(1)}, f32[8,128]{1,0:T(8,128)S(1)}) custom-call(s32[544]{0:T(1024)S(4)} %get-tuple-element.62.refs_0_, bf16[64,640,128]{2,1,0:T(8,128)(2,1)S(1)} %get-tuple-element.67.turned.refs_1_, bf16[64,8,128]{2,1,0:T(8,128)(2,1)S(1)} %get-tuple-element.92.refs_2_, ...), custom_call_target="tpu_custom_call" | custom-call | tf_op jit(solution)/shard_map/local2/pallas_call | solution.py:470
  46.3 0.9 collective-permute-done.11.refs_6_
  47.2 1.2 %ghost2.1 = (f32[64,8,128]{2,1,0:T(8,128)S(1)}, bf16[64,8,128]{2,1,0:T(8,128)(2,1)S(1)}, bf16[48,8,128]{2,1,0:T(8,128)(2,1)S(1)}, bf16[48,8,128]{2,1,0:T(8,128)(...) custom-call(s32[544]{0:T(1024)S(4)} %get-tuple-element.62.refs_0_, ...), custom_call_target="tpu_custom_call", output_to_operand_aliasing={{0}: (11, {}), {1}: (12, {})} | custom-call | tf_op jit(solution)/shard_map/ghost2/pallas_call | solution.py:516
  48.5 5.2 %collective-permute-start.13 = (bf16[48,8,128]{2,1,0:T(8,128)(2,1)S(1)}, bf16[48,8,128]{2,1,0:T(8,128)(2,1)S(1)}, u32[]{:S(2)}, u32[]{:S(2)}) collective-permute-start(bf16[48,8,128]{2,1,0:T(8,128)(2,1)S(1)} %get-tuple-element.106), channel_id=1, source_target_pairs={{0,15},{1,0},{2,1},{3,2},{4,3},{5,4},{6,5},{7,6},{8,7},{9,8},{10,9... | collective-permute-start | bytes 294920 | tf_op jit(solution)/shard_map/ppermute | solution.py:404
  53.7 1.9 %collective-permute-done.12.refs_0_.refs_3_ = bf16[48,8,128]{2,1,0:T(8,128)(2,1)S(1)} collective-permute-done((bf16[48,8,128]{2,1,0:T(8,128)(2,1)S(1)}, bf16[48,8,128]{2,1,0:T(8,128)(2,1)S(1)}, u32[]{:S(2)}, u32[]{:S(2)}) %collective-permute-start.12) | collective-permute-done | bytes 98336 | tf_op jit(solution)/shard_map/ppermute | solution.py:404
  55.7 0.9 collective-permute-start.14
  56.6 3.3 %collective-permute-start.15 = (bf16[48,8,128]{2,1,0:T(8,128)(2,1)S(1)}, bf16[48,8,128]{2,1,0:T(8,128)(2,1)S(1)}, u32[]{:S(2)}, u32[]{:S(2)}) collective-permute-start(bf16[48,8,128]{2,1,0:T(8,128)(2,1)S(1)} %get-tuple-element.110), channel_id=1, source_target_pairs={{0,240},{16,0},{32,16},{48,32},{64,48},{80,64},{96,80},{112,96},{1... | collective-permute-start | bytes 294920 | tf_op jit(solution)/shard_map/ppermute | solution.py:404
  59.9 1.0 %local3.1 = (f32[64,8,128]{2,1,0:T(8,128)S(1)}, bf16[64,8,128]{2,1,0:T(8,128)(2,1)S(1)}, f32[8,128]{1,0:T(8,128)S(1)}) custom-call(s32[544]{0:T(1024)S(4)} %get-tuple-element.62.refs_0_, bf16[64,640,128]{2,1,0:T(8,128)(2,1)S(1)} %get-tuple-element.67.turned.refs_1_, bf16[64,8,128]{2,1,0:T(8,128)(2,1)S(1)} %get-tuple-element.104.refs_2_, ...), custom_call_target="tpu_custom_call" | custom-call | tf_op jit(solution)/shard_map/local3/pallas_call | solution.py:470
  61.0 1.2 %ghost3.1 = (f32[64,8,128]{2,1,0:T(8,128)S(1)}, bf16[64,8,128]{2,1,0:T(8,128)(2,1)S(1)}, f32[256,128]{1,0:T(8,128)S(1)}) custom-call(s32[544]{0:T(1024)S(4)} %get-tuple-element.62.refs_0_, bf16[64,640,128]{2,1,0:T(8,128)(2,1)S(1)} %get-tuple-element.67.turned.refs_1_, ...), custom_call_target="tpu_custom_call", output_to_operand_aliasing={{0}: (12, {}), {1}: (13, {})} | custom-call | tf_op jit(solution)/shard_map/ghost3/pallas_call | solution.py:516
  62.2 29.2 %all_to_all.11 = f32[256,1,128]{2,1,0:T(1,128)S(1)} all-to-all(f32[256,1,128]{2,1,0:T(1,128)S(1)} %bitcast.7), channel_id=1, replica_groups=mesh['gx'=16,'gy'=16] {'gx','gy'}, dimensions={0} | all-to-all | bytes 262144 | tf_op jit(solution)/shard_map/all_to_all | solution.py:533
  91.4 1.1 %finish.1 = (f32[64,8,128]{2,1,0:T(8,128)}, f32[64,8,128]{2,1,0:T(8,128)}) custom-call(f32[256,128]{1,0:T(8,128)S(1)} %bitcast.6, f32[64,8,128]{2,1,0:T(8,128)S(1)} %get-tuple-element.76.b0.refs_4_.refs_8_, f32[64,8,128]{2,1,0:T(8,128)S(1)} %get-tuple-element.88.refs_5_.refs_9_.b1, f32[64,8,128]{2,1,0:T(8,128)S(1)} %get-tuple-element.100.refs_6_.refs_10_.b2, ...), custom_call_target="tpu_custom_call" | custom-call | tf_op jit(solution)/shard_map/finish/pallas_call | solution.py:534
  (17 shorter events, 0.2 us)
Async XLA Ops:
  3.2 9.4 %collective-permute-start = (bf16[48,8,128]{2,1,0:T(8,128)(2,1)S(1)}, bf16[48,8,128]{2,1,0:T(8,128)(2,1)S(1)}, u32[]{:S(2)}, u32[]{:S(2)}) collective-permute-start(bf16[48,8,128]{2,1,0:T(8,128)(2,1)S(1)} %get-tuple-element.69), channel_id=1, source_target_pairs={{0,1},{1,2},{2,3},{3,4},{4,5},{5,6},{6,7},{7,8},{8,9},{9,10},{10,1... | collective-permute-start | bytes 294920 | tf_op jit(solution)/shard_map/ppermute | solution.py:404
  5.4 7.2 %collective-permute-start.1 = (bf16[48,8,128]{2,1,0:T(8,128)(2,1)S(1)}, bf16[48,8,128]{2,1,0:T(8,128)(2,1)S(1)}, u32[]{:S(2)}, u32[]{:S(2)}) collective-permute-start(bf16[48,8,128]{2,1,0:T(8,128)(2,1)S(1)} %get-tuple-element.70), channel_id=1, source_target_pairs={{0,15},{1,0},{2,1},{3,2},{4,3},{5,4},{6,5},{7,6},{8,7},{9,8},{10,9... | collective-permute-start | bytes 294920 | tf_op jit(solution)/shard_map/ppermute | solution.py:404
  12.6 5.6 %collective-permute-start.2 = (bf16[48,8,128]{2,1,0:T(8,128)(2,1)S(1)}, bf16[48,8,128]{2,1,0:T(8,128)(2,1)S(1)}, u32[]{:S(2)}, u32[]{:S(2)}) collective-permute-start(bf16[48,8,128]{2,1,0:T(8,128)(2,1)S(1)} %get-tuple-element.74), channel_id=1, source_target_pairs={{0,16},{16,32},{32,48},{48,64},{64,80},{80,96},{96,112},{112,128},... | collective-permute-start | bytes 294920 | tf_op jit(solution)/shard_map/ppermute | solution.py:404
  15.2 4.3 %collective-permute-start.3 = (bf16[48,8,128]{2,1,0:T(8,128)(2,1)S(1)}, bf16[48,8,128]{2,1,0:T(8,128)(2,1)S(1)}, u32[]{:S(2)}, u32[]{:S(2)}) collective-permute-start(bf16[48,8,128]{2,1,0:T(8,128)(2,1)S(1)} %get-tuple-element.75), channel_id=1, source_target_pairs={{0,240},{16,0},{32,16},{48,32},{64,48},{80,64},{96,80},{112,96},{1... | collective-permute-start | bytes 294920 | tf_op jit(solution)/shard_map/ppermute | solution.py:404
  20.8 6.8 %collective-permute-start.4 = (bf16[48,8,128]{2,1,0:T(8,128)(2,1)S(1)}, bf16[48,8,128]{2,1,0:T(8,128)(2,1)S(1)}, u32[]{:S(2)}, u32[]{:S(2)}) collective-permute-start(bf16[48,8,128]{2,1,0:T(8,128)(2,1)S(1)} %get-tuple-element.80), channel_id=1, source_target_pairs={{0,1},{1,2},{2,3},{3,4},{4,5},{5,6},{6,7},{7,8},{8,9},{9,10},{10,1... | collective-permute-start | bytes 294920 | tf_op jit(solution)/shard_map/ppermute | solution.py:404
  20.8 6.8 %collective-permute-start.5 = (bf16[48,8,128]{2,1,0:T(8,128)(2,1)S(1)}, bf16[48,8,128]{2,1,0:T(8,128)(2,1)S(1)}, u32[]{:S(2)}, u32[]{:S(2)}) collective-permute-start(bf16[48,8,128]{2,1,0:T(8,128)(2,1)S(1)} %get-tuple-element.81), channel_id=1, source_target_pairs={{0,15},{1,0},{2,1},{3,2},{4,3},{5,4},{6,5},{7,6},{8,7},{9,8},{10,9... | collective-permute-start | bytes 294920 | tf_op jit(solution)/shard_map/ppermute | solution.py:404
  27.6 4.2 %collective-permute-start.6 = (bf16[48,8,128]{2,1,0:T(8,128)(2,1)S(1)}, bf16[48,8,128]{2,1,0:T(8,128)(2,1)S(1)}, u32[]{:S(2)}, u32[]{:S(2)}) collective-permute-start(bf16[48,8,128]{2,1,0:T(8,128)(2,1)S(1)} %get-tuple-element.85), channel_id=1, source_target_pairs={{0,16},{16,32},{32,48},{48,64},{64,80},{80,96},{96,112},{112,128},... | collective-permute-start | bytes 294920 | tf_op jit(solution)/shard_map/ppermute | solution.py:404
  29.7 4.0 %collective-permute-start.7 = (bf16[48,8,128]{2,1,0:T(8,128)(2,1)S(1)}, bf16[48,8,128]{2,1,0:T(8,128)(2,1)S(1)}, u32[]{:S(2)}, u32[]{:S(2)}) collective-permute-start(bf16[48,8,128]{2,1,0:T(8,128)(2,1)S(1)} %get-tuple-element.86), channel_id=1, source_target_pairs={{0,240},{16,0},{32,16},{48,32},{64,48},{80,64},{96,80},{112,96},{1... | collective-permute-start | bytes 294920 | tf_op jit(solution)/shard_map/ppermute | solution.py:404
  34.9 7.3 %collective-permute-start.8 = (bf16[48,8,128]{2,1,0:T(8,128)(2,1)S(1)}, bf16[48,8,128]{2,1,0:T(8,128)(2,1)S(1)}, u32[]{:S(2)}, u32[]{:S(2)}) collective-permute-start(bf16[48,8,128]{2,1,0:T(8,128)(2,1)S(1)} %get-tuple-element.93), channel_id=1, source_target_pairs={{0,1},{1,2},{2,3},{3,4},{4,5},{5,6},{6,7},{7,8},{8,9},{9,10},{10,1... | collective-permute-start | bytes 294920 | tf_op jit(solution)/shard_map/ppermute | solution.py:404
  35.0 7.3 %collective-permute-start.9 = (bf16[48,8,128]{2,1,0:T(8,128)(2,1)S(1)}, bf16[48,8,128]{2,1,0:T(8,128)(2,1)S(1)}, u32[]{:S(2)}, u32[]{:S(2)}) collective-permute-start(bf16[48,8,128]{2,1,0:T(8,128)(2,1)S(1)} %get-tuple-element.94), channel_id=1, source_target_pairs={{0,15},{1,0},{2,1},{3,2},{4,3},{5,4},{6,5},{7,6},{8,7},{9,8},{10,9... | collective-permute-start | bytes 294920 | tf_op jit(solution)/shard_map/ppermute | solution.py:404
  42.3 4.0 %collective-permute-start.10 = (bf16[48,8,128]{2,1,0:T(8,128)(2,1)S(1)}, bf16[48,8,128]{2,1,0:T(8,128)(2,1)S(1)}, u32[]{:S(2)}, u32[]{:S(2)}) collective-permute-start(bf16[48,8,128]{2,1,0:T(8,128)(2,1)S(1)} %get-tuple-element.97), channel_id=1, source_target_pairs={{0,16},{16,32},{32,48},{48,64},{64,80},{80,96},{96,112},{112,128},... | collective-permute-start | bytes 294920 | tf_op jit(solution)/shard_map/ppermute | solution.py:404
  43.1 4.0 %collective-permute-start.11 = (bf16[48,8,128]{2,1,0:T(8,128)(2,1)S(1)}, bf16[48,8,128]{2,1,0:T(8,128)(2,1)S(1)}, u32[]{:S(2)}, u32[]{:S(2)}) collective-permute-start(bf16[48,8,128]{2,1,0:T(8,128)(2,1)S(1)} %get-tuple-element.98), channel_id=1, source_target_pairs={{0,240},{16,0},{32,16},{48,32},{64,48},{80,64},{96,80},{112,96},{1... | collective-permute-start | bytes 294920 | tf_op jit(solution)/shard_map/ppermute | solution.py:404
  48.4 7.2 %collective-permute-start.12 = (bf16[48,8,128]{2,1,0:T(8,128)(2,1)S(1)}, bf16[48,8,128]{2,1,0:T(8,128)(2,1)S(1)}, u32[]{:S(2)}, u32[]{:S(2)}) collective-permute-start(bf16[48,8,128]{2,1,0:T(8,128)(2,1)S(1)} %get-tuple-element.105), channel_id=1, source_target_pairs={{0,1},{1,2},{2,3},{3,4},{4,5},{5,6},{6,7},{7,8},{8,9},{9,10},{10,1... | collective-permute-start | bytes 294920 | tf_op jit(solution)/shard_map/ppermute | solution.py:404
  48.5 7.1 %collective-permute-start.13 = (bf16[48,8,128]{2,1,0:T(8,128)(2,1)S(1)}, bf16[48,8,128]{2,1,0:T(8,128)(2,1)S(1)}, u32[]{:S(2)}, u32[]{:S(2)}) collective-permute-start(bf16[48,8,128]{2,1,0:T(8,128)(2,1)S(1)} %get-tuple-element.106), channel_id=1, source_target_pairs={{0,15},{1,0},{2,1},{3,2},{4,3},{5,4},{6,5},{7,6},{8,7},{9,8},{10,9... | collective-permute-start | bytes 294920 | tf_op jit(solution)/shard_map/ppermute | solution.py:404
  55.7 5.3 %collective-permute-start.14 = (bf16[48,8,128]{2,1,0:T(8,128)(2,1)S(1)}, bf16[48,8,128]{2,1,0:T(8,128)(2,1)S(1)}, u32[]{:S(2)}, u32[]{:S(2)}) collective-permute-start(bf16[48,8,128]{2,1,0:T(8,128)(2,1)S(1)} %get-tuple-element.109), channel_id=1, source_target_pairs={{0,16},{16,32},{32,48},{48,64},{64,80},{80,96},{96,112},{112,128},... | collective-permute-start | bytes 294920 | tf_op jit(solution)/shard_map/ppermute | solution.py:404
  56.6 4.4 %collective-permute-start.15 = (bf16[48,8,128]{2,1,0:T(8,128)(2,1)S(1)}, bf16[48,8,128]{2,1,0:T(8,128)(2,1)S(1)}, u32[]{:S(2)}, u32[]{:S(2)}) collective-permute-start(bf16[48,8,128]{2,1,0:T(8,128)(2,1)S(1)} %get-tuple-element.110), channel_id=1, source_target_pairs={{0,240},{16,0},{32,16},{48,32},{64,48},{80,64},{96,80},{112,96},{1... | collective-permute-start | bytes 294920 | tf_op jit(solution)/shard_map/ppermute | solution.py:404

commit v8 on v7

--- a/solution.py
+++ b/solution.py
@@ -65,15 +65,18 @@
 
 
 def start_kernel(
-    neighbours_from, slots_from, counts, right_sides, basis, rounded, up, down,
-    next_row, last_row, neighbours, send_slots, arrived,
+    neighbours_from, slots_from, counts, right_sides_from, basis, rounded, up, down,
+    next_row, last_row, neighbours, send_slots, right_sides, arrived,
 ):
+    vectors = pltpu.make_async_copy(right_sides_from, right_sides, arrived.at[2])
     tables = (
         pltpu.make_async_copy(slots_from, send_slots, arrived.at[0]),
         pltpu.make_async_copy(neighbours_from, neighbours, arrived.at[1]),
     )
+    vectors.start()
     for copy in tables:
         copy.start()
+    vectors.wait()
     element = lax.broadcasted_iota(jnp.int32, basis.shape, 0)
     live = jnp.where(element < counts[0], right_sides[...], 0.0)
     basis[...] = live
@@ -122,36 +125,41 @@
     lax.fori_loop(0, diag_here.shape[0], element, 0, unroll=8)
 
 
-def first_half_kernel(
-    diag, face, turned, diag_third, face_third, done, diag_here, face_here, arrived
-):
+def fetch_parts(first, count, diag, face, diag_here, face_here, arrived):
     parts = []
-    for at in range(0, 2 * QUARTER, EIGHTH):
+    for at in range(0, count, EIGHTH):
         here = pl.ds(at, EIGHTH)
         place = diag_here.at[here], face_here.at[here]
-        parts.append((at, place, fetching(at, diag, face, *place, arrived.at[at // EIGHTH])))
-    third = fetching(2 * QUARTER, diag, face, diag_third, face_third, arrived.at[4])
-    for _, _, copies in parts:
+        copies = fetching(first + at, diag, face, *place, arrived.at[at // EIGHTH])
+        parts.append((first + at, place, copies))
         for copy in copies:
             copy.start()
-    for copy in third:
+    return parts
+
+
+def first_half_kernel(
+    diag, face, turned, diag_next, face_next, done, diag_here, face_here, arrived
+):
+    parts = fetch_parts(0, CAP // 2, diag, face, diag_here, face_here, arrived)
+    ahead = fetching(CAP // 2, diag, face, diag_next, face_next, arrived.at[4])
+    for copy in ahead:
         copy.start()
     for at, place, copies in parts:
         for copy in copies:
             copy.wait()
         transpose_some(at, *place, turned)
     done[...] = jnp.zeros_like(done)
-    for copy in third:
+    for copy in ahead:
         copy.wait()
 
 
 def second_half_kernel(
-    neighbours, diag, face, diag_third, face_third, rounded, before, turned, image,
+    neighbours, diag, face, diag_next, face_next, rounded, before, turned, image,
     image_rounded, ghostly, diag_here, face_here, arrived, lookup,
 ):
-    fourth = fetching(3 * QUARTER, diag, face, diag_here, face_here, arrived)
-    for copy in fourth:
-        copy.start()
+    parts = fetch_parts(
+        CAP // 2 + EIGHTH, 3 * EIGHTH, diag, face, diag_here, face_here, arrived
+    )
     fill_local(lookup, rounded)
 
     def apply_from(first, diag_of, face_of):
@@ -175,22 +183,18 @@
 
         return apply
 
-    transpose_some(
-        2 * QUARTER, diag_third, face_third, turned,
-        apply_from(2 * QUARTER, diag_third, face_third),
-    )
+    place = diag_next, face_next
+    transpose_some(CAP // 2, *place, turned, apply_from(CAP // 2, *place))
     for run in (2, 3):
         farthest = jnp.int32(-1)
         for e in range(run * UNROLL, (run + 1) * UNROLL):
             for f in range(FACES):
                 farthest = jnp.maximum(farthest, neighbours[f, e])
         ghostly[run] = farthest
-    for copy in fourth:
-        copy.wait()
-    transpose_some(
-        3 * QUARTER, diag_here, face_here, turned,
-        apply_from(3 * QUARTER, diag_here, face_here),
-    )
+    for at, place, copies in parts:
+        for copy in copies:
+            copy.wait()
+        transpose_some(at, *place, turned, apply_from(at, *place))
 
 
 def relay_kernel(*refs):
@@ -418,19 +422,24 @@
     rows_shape = jax.ShapeDtypeStruct((GROUPS, ROWS), jnp.float32)
     turned_shape = pltpu.VMEM((CAP, BLOCKS * ROWS, ROWS), half)
     lookup = pltpu.VMEM((LOOKUP, 8, ROWS), half)
-    quarter = [
-        pltpu.VMEM((QUARTER, ROWS, ROWS), half),
-        pltpu.VMEM((QUARTER, FACES, ROWS, ROWS), half),
-    ]
-    arrived = pltpu.SemaphoreType.DMA((2,))
+
+    def room(count):
+        return [
+            pltpu.VMEM((count, ROWS, ROWS), half),
+            pltpu.VMEM((count, FACES, ROWS, ROWS), half),
+        ]
+
     *outs, neighbours, send_slots = pl.pallas_call(
         start_kernel,
         name="start",
-        in_specs=[IN_HBM, IN_HBM, IN_SMEM, IN_VMEM],
+        in_specs=[IN_HBM, IN_HBM, IN_SMEM, IN_HBM],
         out_specs=[IN_VMEM] * 6 + [IN_SMEM] * 2,
         out_shape=[full, narrow] + packets
         + [pltpu.SMEM(table.shape, jnp.int32) for table in (neighbours, send_slots)],
-        scratch_shapes=[arrived],
+        scratch_shapes=[
+            pltpu.VMEM(right_sides.shape, jnp.float32),
+            pltpu.SemaphoreType.DMA((3,)),
+        ],
         compiler_params=params(),
     )(in_place(neighbours), in_place(send_slots), counts, in_place(right_sides))
     first, rounded, up, down, next_row, last_row = outs
@@ -447,12 +456,8 @@
                 name="first_half",
                 in_specs=[IN_HBM] * 2,
                 out_specs=[IN_VMEM] * 4,
-                out_shape=[turned_shape] + quarter + [gram_shape],
-                scratch_shapes=[
-                    pltpu.VMEM((2 * QUARTER, ROWS, ROWS), half),
-                    pltpu.VMEM((2 * QUARTER, FACES, ROWS, ROWS), half),
-                    pltpu.SemaphoreType.DMA((5, 2)),
-                ],
+                out_shape=[turned_shape] + room(EIGHTH) + [gram_shape],
+                scratch_shapes=room(CAP // 2) + [pltpu.SemaphoreType.DMA((5, 2))],
                 compiler_params=params(),
             )(diag_blocks, face_blocks)
             after = (done,)
@@ -494,7 +499,8 @@
                 in_specs=[IN_SMEM] + [IN_HBM] * 2 + [IN_VMEM] * 4,
                 out_specs=[IN_VMEM] * 3 + [IN_SMEM],
                 out_shape=[turned_shape, full, narrow, pltpu.SMEM((8,), jnp.int32)],
-                scratch_shapes=quarter + [arrived, lookup],
+                scratch_shapes=room(3 * EIGHTH)
+                + [pltpu.SemaphoreType.DMA((3, 2)), lookup],
                 input_output_aliases={6: 0},
                 compiler_params=params(),
             )(neighbours, diag_blocks, face_blocks, *blocks, rounded, turned)

time: 92.9 us -> 92.1 us (level)
  transfers between devices with their start and end apart: 16 -> 16, of which waited for: 6 -> 6; matrix products, arithmetic and copies ran while one was open for 0% -> 0% of each run, Pallas kernels for 10% -> 11%
where the time goes in v8:
time: 92.1 us; the launch traced here: 92 us
  starting transfers between devices  34.7 us (38%)
  blocking collectives  29.2 us (32%)
  Pallas kernels  16.9 us (18%)
  waiting for transfers between devices  9.66 us (10%)
  between operations  1.58 us (2%)
    ppermute x16, starting transfers between devices, shifted(): lax.ppermute(block, axis, [(i, (i + distance) % SIDE) for i in range(SIDE)])  34.7 us
    all_to_all x1, blocking collectives, per_device(): gathered = lax.all_to_all(gram, ('gx', 'gy'), 0, 0, tiled=True)  29.2 us
    ppermute x16, waiting for transfers between devices, shifted(): lax.ppermute(block, axis, [(i, (i + distance) % SIDE) for i in range(SIDE)])  9.66 us
    pallas_call x3, Pallas kernels, per_device(): pl.pallas_call(functools.partial(ghost_kernel, power), name=f'ghost{power...  3.49 us
    pallas_call x1, Pallas kernels, per_device(): pl.pallas_call(second_half_kernel, name='second_half', in_specs=[IN_SMEM]...  3.38 us
    pallas_call x3, Pallas kernels, per_device(): pl.pallas_call(functools.partial(local_kernel, power), name=f'local{power...  3.3 us
    pallas_call x1, Pallas kernels, per_device(): pl.pallas_call(first_half_kernel, name='first_half', in_specs=[IN_HBM] *...  2.98 us
  transfers between devices with their start and end apart: 16, of which 6 were waited for; matrix products, arithmetic and copies ran while one was open for 0% of the time, Pallas kernels for 11%

profile of v8, /device:TPU:1, one launch (start us, length us, event | category | flops | bytes accessed | tf_op | source)
XLA Modules:
  0.0 92.0 jit_solution(13615922266698097619)
XLA Ops:
  1.3 1.3 %start.1 = (f32[64,8,128]{2,1,0:T(8,128)S(1)}, bf16[64,8,128]{2,1,0:T(8,128)(2,1)S(1)}, bf16[48,8,128]{2,1,0:T(8,128)(2,1)S(1)}, bf16[48,8,128]{2,1,0:T(8,128)(2...) custom-call(s32[4,64]{1,0:T(4,128)} %bitcast.9, ...), custom_call_target="tpu_custom_call" | custom-call | tf_op jit(solution)/shard_map/start/pallas_call | solution.py:432
  2.5 2.2 %collective-permute-start = (bf16[48,8,128]{2,1,0:T(8,128)(2,1)S(1)}, bf16[48,8,128]{2,1,0:T(8,128)(2,1)S(1)}, u32[]{:S(2)}, u32[]{:S(2)}) collective-permute-start(bf16[48,8,128]{2,1,0:T(8,128)(2,1)S(1)} %get-tuple-element.69), channel_id=1, source_target_pairs={{0,1},{1,2},{2,3},{3,4},{4,5},{5,6},{6,7},{7,8},{8,9},{9,10},{10,1... | collective-permute-start | bytes 294920 | tf_op jit(solution)/shard_map/ppermute | solution.py:408
  4.7 3.7 %collective-permute-start.1 = (bf16[48,8,128]{2,1,0:T(8,128)(2,1)S(1)}, bf16[48,8,128]{2,1,0:T(8,128)(2,1)S(1)}, u32[]{:S(2)}, u32[]{:S(2)}) collective-permute-start(bf16[48,8,128]{2,1,0:T(8,128)(2,1)S(1)} %get-tuple-element.70), channel_id=1, source_target_pairs={{0,15},{1,0},{2,1},{3,2},{4,3},{5,4},{6,5},{7,6},{8,7},{9,8},{10,9... | collective-permute-start | bytes 294920 | tf_op jit(solution)/shard_map/ppermute | solution.py:408
  8.5 3.0 %first_half.1 = (bf16[64,640,128]{2,1,0:T(8,128)(2,1)S(1)}, bf16[8,128,128]{2,1,0:T(8,128)(2,1)S(1)}, bf16[8,4,128,128]{3,2,1,0:T(8,128)(2,1)S(1)}, f32[8,128]{1,0:T(8,128)S(1)}) custom-call(bf16[64,128,128]{2,1,0:T(8,128)(2,1)} %diag.3, bf16[64,4,128,128]{3,2,1,0:T(8,128)(2,1)} %face.3), custom_call_target="tpu_custom_call" | custom-call | tf_op jit(solution)/shard_map/first_half/pallas_call | solution.py:454
  11.5 2.5 %collective-permute-start.2 = (bf16[48,8,128]{2,1,0:T(8,128)(2,1)S(1)}, bf16[48,8,128]{2,1,0:T(8,128)(2,1)S(1)}, u32[]{:S(2)}, u32[]{:S(2)}) collective-permute-start(bf16[48,8,128]{2,1,0:T(8,128)(2,1)S(1)} %get-tuple-element.74), channel_id=1, source_target_pairs={{0,16},{16,32},{32,48},{48,64},{64,80},{80,96},{96,112},{112,128},... | collective-permute-start | bytes 294920 | tf_op jit(solution)/shard_map/ppermute | solution.py:408
  14.0 0.2 collective-permute-start.3
  14.3 3.4 %second_half.1 = (bf16[64,640,128]{2,1,0:T(8,128)(2,1)S(1)}, f32[64,8,128]{2,1,0:T(8,128)S(1)}, bf16[64,8,128]{2,1,0:T(8,128)(2,1)S(1)}, s32[8]{0:T(128)S(4)}) custom-call(s32[4,64]{1,0:T(4,128)S(4)} %get-tuple-element.60.neighbours, bf16[64,128,128]{2,1,0:T(8,128)(2,1)} %diag.3, bf16[64,4,128,128]{3,2,1,0:T(8,128)(2,1)} %face.3, ...), custom_call_target="tpu_custom_call", output_to_operand_aliasing={{0}: (6, {})} | custom-call | tf_op jit(solution)/shard_map/second_half/pallas_call | solution.py:496
  17.7 0.7 collective-permute-done.3.from_next
  18.4 1.3 %whole.1 = (f32[64,8,128]{2,1,0:T(8,128)S(1)}, bf16[64,8,128]{2,1,0:T(8,128)(2,1)S(1)}, bf16[48,8,128]{2,1,0:T(8,128)(2,1)S(1)}, bf16[48,8,128]{2,1,0:T(8,128)(2...) custom-call(s32[4,64]{1,0:T(4,128)S(4)} %get-tuple-element.60.neighb, ...), custom_call_target="tpu_custom_call", output_to_operand_aliasing={{0}: (10, {}), {1}: (11, {})} | custom-call | tf_op jit(solution)/shard_map/whole/pallas_call | solution.py:507
  19.7 4.8 %collective-permute-start.5 = (bf16[48,8,128]{2,1,0:T(8,128)(2,1)S(1)}, bf16[48,8,128]{2,1,0:T(8,128)(2,1)S(1)}, u32[]{:S(2)}, u32[]{:S(2)}) collective-permute-start(bf16[48,8,128]{2,1,0:T(8,128)(2,1)S(1)} %get-tuple-element.81), channel_id=1, source_target_pairs={{0,15},{1,0},{2,1},{3,2},{4,3},{5,4},{6,5},{7,6},{8,7},{9,8},{10,9... | collective-permute-start | bytes 294920 | tf_op jit(solution)/shard_map/ppermute | solution.py:408
  24.5 2.0 %collective-permute-done.4.refs_0_.refs_3_ = bf16[48,8,128]{2,1,0:T(8,128)(2,1)S(1)} collective-permute-done((bf16[48,8,128]{2,1,0:T(8,128)(2,1)S(1)}, bf16[48,8,128]{2,1,0:T(8,128)(2,1)S(1)}, u32[]{:S(2)}, u32[]{:S(2)}) %collective-permute-start.4) | collective-permute-done | bytes 98336 | tf_op jit(solution)/shard_map/ppermute | solution.py:408
  26.5 3.0 %collective-permute-start.6 = (bf16[48,8,128]{2,1,0:T(8,128)(2,1)S(1)}, bf16[48,8,128]{2,1,0:T(8,128)(2,1)S(1)}, u32[]{:S(2)}, u32[]{:S(2)}) collective-permute-start(bf16[48,8,128]{2,1,0:T(8,128)(2,1)S(1)} %get-tuple-element.85), channel_id=1, source_target_pairs={{0,16},{16,32},{32,48},{48,64},{64,80},{80,96},{96,112},{112,128},... | collective-permute-start | bytes 294920 | tf_op jit(solution)/shard_map/ppermute | solution.py:408
  29.5 0.8 collective-permute-start.7
  30.2 1.0 %local1.1 = (f32[64,8,128]{2,1,0:T(8,128)S(1)}, bf16[64,8,128]{2,1,0:T(8,128)(2,1)S(1)}, f32[8,128]{1,0:T(8,128)S(1)}) custom-call(s32[544]{0:T(1024)S(4)} %get-tuple-element.62.refs_0_, bf16[64,640,128]{2,1,0:T(8,128)(2,1)S(1)} %get-tuple-element.67.turned.refs_1_, bf16[64,8,128]{2,1,0:T(8,128)(2,1)S(1)} %get-tuple-element.79.refs_2_, ...), custom_call_target="tpu_custom_call" | custom-call | tf_op jit(solution)/shard_map/local1/pallas_call | solution.py:475
  31.3 2.2 %collective-permute-done.7.refs_6_ = bf16[48,8,128]{2,1,0:T(8,128)(2,1)S(1)} collective-permute-done((bf16[48,8,128]{2,1,0:T(8,128)(2,1)S(1)}, bf16[48,8,128]{2,1,0:T(8,128)(2,1)S(1)}, u32[]{:S(2)}, u32[]{:S(2)}) %collective-permute-start.7) | collective-permute-done | bytes 98336 | tf_op jit(solution)/shard_map/ppermute | solution.py:408
  33.5 1.1 %ghost1.1 = (f32[64,8,128]{2,1,0:T(8,128)S(1)}, bf16[64,8,128]{2,1,0:T(8,128)(2,1)S(1)}, bf16[48,8,128]{2,1,0:T(8,128)(2,1)S(1)}, bf16[48,8,128]{2,1,0:T(8,128)(...) custom-call(s32[544]{0:T(1024)S(4)} %get-tuple-element.62.refs_0_, ...), custom_call_target="tpu_custom_call", output_to_operand_aliasing={{0}: (10, {}), {1}: (11, {})} | custom-call | tf_op jit(solution)/shard_map/ghost1/pallas_call | solution.py:522
  34.7 0.1 collective-permute-start.8
  34.8 4.9 %collective-permute-start.9 = (bf16[48,8,128]{2,1,0:T(8,128)(2,1)S(1)}, bf16[48,8,128]{2,1,0:T(8,128)(2,1)S(1)}, u32[]{:S(2)}, u32[]{:S(2)}) collective-permute-start(bf16[48,8,128]{2,1,0:T(8,128)(2,1)S(1)} %get-tuple-element.94), channel_id=1, source_target_pairs={{0,15},{1,0},{2,1},{3,2},{4,3},{5,4},{6,5},{7,6},{8,7},{9,8},{10,9... | collective-permute-start | bytes 294920 | tf_op jit(solution)/shard_map/ppermute | solution.py:408
  39.6 1.9 %collective-permute-done.8.refs_0_.refs_3_ = bf16[48,8,128]{2,1,0:T(8,128)(2,1)S(1)} collective-permute-done((bf16[48,8,128]{2,1,0:T(8,128)(2,1)S(1)}, bf16[48,8,128]{2,1,0:T(8,128)(2,1)S(1)}, u32[]{:S(2)}, u32[]{:S(2)}) %collective-permute-start.8) | collective-permute-done | bytes 98336 | tf_op jit(solution)/shard_map/ppermute | solution.py:408
  41.6 1.2 %collective-permute-start.10 = (bf16[48,8,128]{2,1,0:T(8,128)(2,1)S(1)}, bf16[48,8,128]{2,1,0:T(8,128)(2,1)S(1)}, u32[]{:S(2)}, u32[]{:S(2)}) collective-permute-start(bf16[48,8,128]{2,1,0:T(8,128)(2,1)S(1)} %get-tuple-element.97), channel_id=1, source_target_pairs={{0,16},{16,32},{32,48},{48,64},{64,80},{80,96},{96,112},{112,128},... | collective-permute-start | bytes 294920 | tf_op jit(solution)/shard_map/ppermute | solution.py:408
  42.7 2.0 %collective-permute-start.11 = (bf16[48,8,128]{2,1,0:T(8,128)(2,1)S(1)}, bf16[48,8,128]{2,1,0:T(8,128)(2,1)S(1)}, u32[]{:S(2)}, u32[]{:S(2)}) collective-permute-start(bf16[48,8,128]{2,1,0:T(8,128)(2,1)S(1)} %get-tuple-element.98), channel_id=1, source_target_pairs={{0,240},{16,0},{32,16},{48,32},{64,48},{80,64},{96,80},{112,96},{1... | collective-permute-start | bytes 294920 | tf_op jit(solution)/shard_map/ppermute | solution.py:408
  44.7 1.2 %local2.1 = (f32[64,8,128]{2,1,0:T(8,128)S(1)}, bf16[64,8,128]{2,1,0:T(8,128)(2,1)S(1)}, f32[8,128]{1,0:T(8,128)S(1)}) custom-call(s32[544]{0:T(1024)S(4)} %get-tuple-element.62.refs_0_, bf16[64,640,128]{2,1,0:T(8,128)(2,1)S(1)} %get-tuple-element.67.turned.refs_1_, bf16[64,8,128]{2,1,0:T(8,128)(2,1)S(1)} %get-tuple-element.92.refs_2_, ...), custom_call_target="tpu_custom_call" | custom-call | tf_op jit(solution)/shard_map/local2/pallas_call | solution.py:475
  45.9 0.9 collective-permute-done.11.refs_6_
  46.8 1.1 %ghost2.1 = (f32[64,8,128]{2,1,0:T(8,128)S(1)}, bf16[64,8,128]{2,1,0:T(8,128)(2,1)S(1)}, bf16[48,8,128]{2,1,0:T(8,128)(2,1)S(1)}, bf16[48,8,128]{2,1,0:T(8,128)(...) custom-call(s32[544]{0:T(1024)S(4)} %get-tuple-element.62.refs_0_, ...), custom_call_target="tpu_custom_call", output_to_operand_aliasing={{0}: (11, {}), {1}: (12, {})} | custom-call | tf_op jit(solution)/shard_map/ghost2/pallas_call | solution.py:522
  48.0 5.3 %collective-permute-start.13 = (bf16[48,8,128]{2,1,0:T(8,128)(2,1)S(1)}, bf16[48,8,128]{2,1,0:T(8,128)(2,1)S(1)}, u32[]{:S(2)}, u32[]{:S(2)}) collective-permute-start(bf16[48,8,128]{2,1,0:T(8,128)(2,1)S(1)} %get-tuple-element.106), channel_id=1, source_target_pairs={{0,15},{1,0},{2,1},{3,2},{4,3},{5,4},{6,5},{7,6},{8,7},{9,8},{10,9... | collective-permute-start | bytes 294920 | tf_op jit(solution)/shard_map/ppermute | solution.py:408
  53.3 1.9 %collective-permute-done.12.refs_0_.refs_3_ = bf16[48,8,128]{2,1,0:T(8,128)(2,1)S(1)} collective-permute-done((bf16[48,8,128]{2,1,0:T(8,128)(2,1)S(1)}, bf16[48,8,128]{2,1,0:T(8,128)(2,1)S(1)}, u32[]{:S(2)}, u32[]{:S(2)}) %collective-permute-start.12) | collective-permute-done | bytes 98336 | tf_op jit(solution)/shard_map/ppermute | solution.py:408
  55.3 0.9 collective-permute-start.14
  56.2 3.1 %collective-permute-start.15 = (bf16[48,8,128]{2,1,0:T(8,128)(2,1)S(1)}, bf16[48,8,128]{2,1,0:T(8,128)(2,1)S(1)}, u32[]{:S(2)}, u32[]{:S(2)}) collective-permute-start(bf16[48,8,128]{2,1,0:T(8,128)(2,1)S(1)} %get-tuple-element.110), channel_id=1, source_target_pairs={{0,240},{16,0},{32,16},{48,32},{64,48},{80,64},{96,80},{112,96},{1... | collective-permute-start | bytes 294920 | tf_op jit(solution)/shard_map/ppermute | solution.py:408
  59.2 1.0 %local3.1 = (f32[64,8,128]{2,1,0:T(8,128)S(1)}, bf16[64,8,128]{2,1,0:T(8,128)(2,1)S(1)}, f32[8,128]{1,0:T(8,128)S(1)}) custom-call(s32[544]{0:T(1024)S(4)} %get-tuple-element.62.refs_0_, bf16[64,640,128]{2,1,0:T(8,128)(2,1)S(1)} %get-tuple-element.67.turned.refs_1_, bf16[64,8,128]{2,1,0:T(8,128)(2,1)S(1)} %get-tuple-element.104.refs_2_, ...), custom_call_target="tpu_custom_call" | custom-call | tf_op jit(solution)/shard_map/local3/pallas_call | solution.py:475
  60.3 1.2 %ghost3.1 = (f32[64,8,128]{2,1,0:T(8,128)S(1)}, bf16[64,8,128]{2,1,0:T(8,128)(2,1)S(1)}, f32[256,128]{1,0:T(8,128)S(1)}) custom-call(s32[544]{0:T(1024)S(4)} %get-tuple-element.62.refs_0_, bf16[64,640,128]{2,1,0:T(8,128)(2,1)S(1)} %get-tuple-element.67.turned.refs_1_, ...), custom_call_target="tpu_custom_call", output_to_operand_aliasing={{0}: (12, {}), {1}: (13, {})} | custom-call | tf_op jit(solution)/shard_map/ghost3/pallas_call | solution.py:522
  61.5 29.2 %all_to_all.11 = f32[256,1,128]{2,1,0:T(1,128)S(1)} all-to-all(f32[256,1,128]{2,1,0:T(1,128)S(1)} %bitcast.7), channel_id=1, replica_groups=mesh['gx'=16,'gy'=16] {'gx','gy'}, dimensions={0} | all-to-all | bytes 262144 | tf_op jit(solution)/shard_map/all_to_all | solution.py:539
  90.7 1.1 %finish.1 = (f32[64,8,128]{2,1,0:T(8,128)}, f32[64,8,128]{2,1,0:T(8,128)}) custom-call(f32[256,128]{1,0:T(8,128)S(1)} %bitcast.6, f32[64,8,128]{2,1,0:T(8,128)S(1)} %get-tuple-element.76.b0.refs_4_.refs_8_, f32[64,8,128]{2,1,0:T(8,128)S(1)} %get-tuple-element.88.refs_5_.refs_9_.b1, f32[64,8,128]{2,1,0:T(8,128)S(1)} %get-tuple-element.100.refs_6_.refs_10_.b2, ...), custom_call_target="tpu_custom_call" | custom-call | tf_op jit(solution)/shard_map/finish/pallas_call | solution.py:540
  (17 shorter events, 0.2 us)
Async XLA Ops:
  2.5 8.9 %collective-permute-start = (bf16[48,8,128]{2,1,0:T(8,128)(2,1)S(1)}, bf16[48,8,128]{2,1,0:T(8,128)(2,1)S(1)}, u32[]{:S(2)}, u32[]{:S(2)}) collective-permute-start(bf16[48,8,128]{2,1,0:T(8,128)(2,1)S(1)} %get-tuple-element.69), channel_id=1, source_target_pairs={{0,1},{1,2},{2,3},{3,4},{4,5},{5,6},{6,7},{7,8},{8,9},{9,10},{10,1... | collective-permute-start | bytes 294920 | tf_op jit(solution)/shard_map/ppermute | solution.py:408
  4.7 6.7 %collective-permute-start.1 = (bf16[48,8,128]{2,1,0:T(8,128)(2,1)S(1)}, bf16[48,8,128]{2,1,0:T(8,128)(2,1)S(1)}, u32[]{:S(2)}, u32[]{:S(2)}) collective-permute-start(bf16[48,8,128]{2,1,0:T(8,128)(2,1)S(1)} %get-tuple-element.70), channel_id=1, source_target_pairs={{0,15},{1,0},{2,1},{3,2},{4,3},{5,4},{6,5},{7,6},{8,7},{9,8},{10,9... | collective-permute-start | bytes 294920 | tf_op jit(solution)/shard_map/ppermute | solution.py:408
  11.5 6.2 %collective-permute-start.2 = (bf16[48,8,128]{2,1,0:T(8,128)(2,1)S(1)}, bf16[48,8,128]{2,1,0:T(8,128)(2,1)S(1)}, u32[]{:S(2)}, u32[]{:S(2)}) collective-permute-start(bf16[48,8,128]{2,1,0:T(8,128)(2,1)S(1)} %get-tuple-element.74), channel_id=1, source_target_pairs={{0,16},{16,32},{32,48},{48,64},{64,80},{80,96},{96,112},{112,128},... | collective-permute-start | bytes 294920 | tf_op jit(solution)/shard_map/ppermute | solution.py:408
  14.0 4.3 %collective-permute-start.3 = (bf16[48,8,128]{2,1,0:T(8,128)(2,1)S(1)}, bf16[48,8,128]{2,1,0:T(8,128)(2,1)S(1)}, u32[]{:S(2)}, u32[]{:S(2)}) collective-permute-start(bf16[48,8,128]{2,1,0:T(8,128)(2,1)S(1)} %get-tuple-element.75), channel_id=1, source_target_pairs={{0,240},{16,0},{32,16},{48,32},{64,48},{80,64},{96,80},{112,96},{1... | collective-permute-start | bytes 294920 | tf_op jit(solution)/shard_map/ppermute | solution.py:408
  19.7 6.8 %collective-permute-start.4 = (bf16[48,8,128]{2,1,0:T(8,128)(2,1)S(1)}, bf16[48,8,128]{2,1,0:T(8,128)(2,1)S(1)}, u32[]{:S(2)}, u32[]{:S(2)}) collective-permute-start(bf16[48,8,128]{2,1,0:T(8,128)(2,1)S(1)} %get-tuple-element.80), channel_id=1, source_target_pairs={{0,1},{1,2},{2,3},{3,4},{4,5},{5,6},{6,7},{7,8},{8,9},{9,10},{10,1... | collective-permute-start | bytes 294920 | tf_op jit(solution)/shard_map/ppermute | solution.py:408
  19.7 6.8 %collective-permute-start.5 = (bf16[48,8,128]{2,1,0:T(8,128)(2,1)S(1)}, bf16[48,8,128]{2,1,0:T(8,128)(2,1)S(1)}, u32[]{:S(2)}, u32[]{:S(2)}) collective-permute-start(bf16[48,8,128]{2,1,0:T(8,128)(2,1)S(1)} %get-tuple-element.81), channel_id=1, source_target_pairs={{0,15},{1,0},{2,1},{3,2},{4,3},{5,4},{6,5},{7,6},{8,7},{9,8},{10,9... | collective-permute-start | bytes 294920 | tf_op jit(solution)/shard_map/ppermute | solution.py:408
  26.5 4.8 %collective-permute-start.6 = (bf16[48,8,128]{2,1,0:T(8,128)(2,1)S(1)}, bf16[48,8,128]{2,1,0:T(8,128)(2,1)S(1)}, u32[]{:S(2)}, u32[]{:S(2)}) collective-permute-start(bf16[48,8,128]{2,1,0:T(8,128)(2,1)S(1)} %get-tuple-element.85), channel_id=1, source_target_pairs={{0,16},{16,32},{32,48},{48,64},{64,80},{80,96},{96,112},{112,128},... | collective-permute-start | bytes 294920 | tf_op jit(solution)/shard_map/ppermute | solution.py:408
  29.5 4.0 %collective-permute-start.7 = (bf16[48,8,128]{2,1,0:T(8,128)(2,1)S(1)}, bf16[48,8,128]{2,1,0:T(8,128)(2,1)S(1)}, u32[]{:S(2)}, u32[]{:S(2)}) collective-permute-start(bf16[48,8,128]{2,1,0:T(8,128)(2,1)S(1)} %get-tuple-element.86), channel_id=1, source_target_pairs={{0,240},{16,0},{32,16},{48,32},{64,48},{80,64},{96,80},{112,96},{1... | collective-permute-start | bytes 294920 | tf_op jit(solution)/shard_map/ppermute | solution.py:408
  34.7 6.9 %collective-permute-start.8 = (bf16[48,8,128]{2,1,0:T(8,128)(2,1)S(1)}, bf16[48,8,128]{2,1,0:T(8,128)(2,1)S(1)}, u32[]{:S(2)}, u32[]{:S(2)}) collective-permute-start(bf16[48,8,128]{2,1,0:T(8,128)(2,1)S(1)} %get-tuple-element.93), channel_id=1, source_target_pairs={{0,1},{1,2},{2,3},{3,4},{4,5},{5,6},{6,7},{7,8},{8,9},{9,10},{10,1... | collective-permute-start | bytes 294920 | tf_op jit(solution)/shard_map/ppermute | solution.py:408
  34.8 6.8 %collective-permute-start.9 = (bf16[48,8,128]{2,1,0:T(8,128)(2,1)S(1)}, bf16[48,8,128]{2,1,0:T(8,128)(2,1)S(1)}, u32[]{:S(2)}, u32[]{:S(2)}) collective-permute-start(bf16[48,8,128]{2,1,0:T(8,128)(2,1)S(1)} %get-tuple-element.94), channel_id=1, source_target_pairs={{0,15},{1,0},{2,1},{3,2},{4,3},{5,4},{6,5},{7,6},{8,7},{9,8},{10,9... | collective-permute-start | bytes 294920 | tf_op jit(solution)/shard_map/ppermute | solution.py:408
  41.6 4.4 %collective-permute-start.10 = (bf16[48,8,128]{2,1,0:T(8,128)(2,1)S(1)}, bf16[48,8,128]{2,1,0:T(8,128)(2,1)S(1)}, u32[]{:S(2)}, u32[]{:S(2)}) collective-permute-start(bf16[48,8,128]{2,1,0:T(8,128)(2,1)S(1)} %get-tuple-element.97), channel_id=1, source_target_pairs={{0,16},{16,32},{32,48},{48,64},{64,80},{80,96},{96,112},{112,128},... | collective-permute-start | bytes 294920 | tf_op jit(solution)/shard_map/ppermute | solution.py:408
  42.7 4.0 %collective-permute-start.11 = (bf16[48,8,128]{2,1,0:T(8,128)(2,1)S(1)}, bf16[48,8,128]{2,1,0:T(8,128)(2,1)S(1)}, u32[]{:S(2)}, u32[]{:S(2)}) collective-permute-start(bf16[48,8,128]{2,1,0:T(8,128)(2,1)S(1)} %get-tuple-element.98), channel_id=1, source_target_pairs={{0,240},{16,0},{32,16},{48,32},{64,48},{80,64},{96,80},{112,96},{1... | collective-permute-start | bytes 294920 | tf_op jit(solution)/shard_map/ppermute | solution.py:408
  47.9 7.4 %collective-permute-start.12 = (bf16[48,8,128]{2,1,0:T(8,128)(2,1)S(1)}, bf16[48,8,128]{2,1,0:T(8,128)(2,1)S(1)}, u32[]{:S(2)}, u32[]{:S(2)}) collective-permute-start(bf16[48,8,128]{2,1,0:T(8,128)(2,1)S(1)} %get-tuple-element.105), channel_id=1, source_target_pairs={{0,1},{1,2},{2,3},{3,4},{4,5},{5,6},{6,7},{7,8},{8,9},{9,10},{10,1... | collective-permute-start | bytes 294920 | tf_op jit(solution)/shard_map/ppermute | solution.py:408
  48.0 7.3 %collective-permute-start.13 = (bf16[48,8,128]{2,1,0:T(8,128)(2,1)S(1)}, bf16[48,8,128]{2,1,0:T(8,128)(2,1)S(1)}, u32[]{:S(2)}, u32[]{:S(2)}) collective-permute-start(bf16[48,8,128]{2,1,0:T(8,128)(2,1)S(1)} %get-tuple-element.106), channel_id=1, source_target_pairs={{0,15},{1,0},{2,1},{3,2},{4,3},{5,4},{6,5},{7,6},{8,7},{9,8},{10,9... | collective-permute-start | bytes 294920 | tf_op jit(solution)/shard_map/ppermute | solution.py:408
  55.3 5.0 %collective-permute-start.14 = (bf16[48,8,128]{2,1,0:T(8,128)(2,1)S(1)}, bf16[48,8,128]{2,1,0:T(8,128)(2,1)S(1)}, u32[]{:S(2)}, u32[]{:S(2)}) collective-permute-start(bf16[48,8,128]{2,1,0:T(8,128)(2,1)S(1)} %get-tuple-element.109), channel_id=1, source_target_pairs={{0,16},{16,32},{32,48},{48,64},{64,80},{80,96},{96,112},{112,128},... | collective-permute-start | bytes 294920 | tf_op jit(solution)/shard_map/ppermute | solution.py:408
  56.2 4.1 %collective-permute-start.15 = (bf16[48,8,128]{2,1,0:T(8,128)(2,1)S(1)}, bf16[48,8,128]{2,1,0:T(8,128)(2,1)S(1)}, u32[]{:S(2)}, u32[]{:S(2)}) collective-permute-start(bf16[48,8,128]{2,1,0:T(8,128)(2,1)S(1)} %get-tuple-element.110), channel_id=1, source_target_pairs={{0,240},{16,0},{32,16},{48,32},{64,48},{80,64},{96,80},{112,96},{1... | collective-permute-start | bytes 294920 | tf_op jit(solution)/shard_map/ppermute | solution.py:408

commit v9 on v8

--- a/solution.py
+++ b/solution.py
@@ -113,13 +113,12 @@
     )
 
 
-def transpose_some(first, diag_here, face_here, turned, also=lambda at: None):
+def transpose_some(first, diag_here, face_here, turned):
     def element(at, carry):
         e = first + at
         turned[e, 0:ROWS] = diag_here[at].T
         for f in range(FACES):
             turned[e, (f + 1) * ROWS : (f + 2) * ROWS] = face_here[at, f].T
-        also(at)
         return carry
 
     lax.fori_loop(0, diag_here.shape[0], element, 0, unroll=8)
@@ -153,48 +152,56 @@
         copy.wait()
 
 
+def apply_as_is(e, vectors, diag_block, face_rows, image, image_rounded):
+    out = lax.dot_general(
+        jnp.concatenate(vectors, axis=1),
+        jnp.concatenate([diag_block] + face_rows, axis=1),
+        (((1,), (1,)), ((), ())),
+        preferred_element_type=jnp.float32,
+    )
+    image[e] = out
+    image_rounded[e] = out.astype(jnp.bfloat16)
+
+
 def second_half_kernel(
-    neighbours, diag, face, diag_next, face_next, rounded, before, turned, image,
-    image_rounded, ghostly, diag_here, face_here, arrived, lookup,
+    neighbours, diag, face, diag_next, face_next, rounded, image, image_rounded,
+    diag_rest, face_rest, ghostly, arrived, lookup,
 ):
+    first = CAP // 2
     parts = fetch_parts(
-        CAP // 2 + EIGHTH, 3 * EIGHTH, diag, face, diag_here, face_here, arrived
+        first + EIGHTH, 3 * EIGHTH, diag, face, diag_rest, face_rest, arrived
     )
     fill_local(lookup, rounded)
 
-    def apply_from(first, diag_of, face_of):
-        def apply(at):
-            e = first + at
+    def apply_some(begin, diag_of, face_of):
+        for at in range(EIGHTH):
+            e = begin + at
             vectors = [lookup[e]]
             for f in range(FACES):
                 near = neighbours[f, e]
                 vectors.append(
                     lookup[jnp.where((near < 0) | (near >= CAP), NOTHING, near)]
                 )
-            blocks = [diag_of[at]] + [face_of[at, f] for f in range(FACES)]
-            out = lax.dot_general(
-                jnp.concatenate(vectors, axis=1),
-                jnp.concatenate(blocks, axis=1),
-                (((1,), (1,)), ((), ())),
-                preferred_element_type=jnp.float32,
-            )
-            image[e] = out
-            image_rounded[e] = out.astype(jnp.bfloat16)
-
-        return apply
-
-    place = diag_next, face_next
-    transpose_some(CAP // 2, *place, turned, apply_from(CAP // 2, *place))
+            rows = [face_of[at, f] for f in range(FACES)]
+            apply_as_is(e, vectors, diag_of[at], rows, image, image_rounded)
+
+    apply_some(first, diag_next, face_next)
     for run in (2, 3):
         farthest = jnp.int32(-1)
         for e in range(run * UNROLL, (run + 1) * UNROLL):
             for f in range(FACES):
                 farthest = jnp.maximum(farthest, neighbours[f, e])
         ghostly[run] = farthest
-    for at, place, copies in parts:
+    for begin, place, copies in parts:
         for copy in copies:
             copy.wait()
-        transpose_some(at, *place, turned, apply_from(at, *place))
+        apply_some(begin, *place)
+
+
+def late_kernel(diag_next, face_next, diag_rest, face_rest, before, turned, done):
+    transpose_some(CAP // 2, diag_next, face_next, turned)
+    transpose_some(CAP // 2 + EIGHTH, diag_rest, face_rest, turned)
+    done[...] = jnp.zeros_like(done)
 
 
 def relay_kernel(*refs):
@@ -260,9 +267,9 @@
 
 
 def whole_kernel(
-    neighbours, send_slots, ghostly, turned, rounded, from_down, from_up, from_last,
-    from_next, b0, before, before_rounded, image, image_rounded, up, down, next_row,
-    last_row, gram_out, lookup,
+    neighbours, send_slots, ghostly, turned, diag_next, face_next, diag_rest, face_rest,
+    rounded, from_down, from_up, from_last, from_next, b0, before, before_rounded,
+    image, image_rounded, up, down, next_row, last_row, gram_out, lookup,
 ):
     fill_local(lookup, rounded)
     fill_ghosts(lookup, from_down, from_up, from_last, from_next)
@@ -271,12 +278,19 @@
         at = [neighbours[f, e] for f in range(FACES)]
         return [e] + [jnp.where(a < 0, NOTHING, a) for a in at]
 
-    def again(first, limit):
-        apply_runs(first, limit, find, turned, lookup, (), image, image_rounded)
-
-    again(0, 2)
+    def again(run):
+        for e in range(run * UNROLL, (run + 1) * UNROLL):
+            at = e - CAP // 2
+            diag_of, face_of = diag_next, face_next
+            if at >= EIGHTH:
+                at, diag_of, face_of = at - EIGHTH, diag_rest, face_rest
+            vectors = [lookup[place] for place in find(e)]
+            rows = [face_of[at, f] for f in range(FACES)]
+            apply_as_is(e, vectors, diag_of[at], rows, image, image_rounded)
+
+    apply_runs(0, 2, find, turned, lookup, (), image, image_rounded)
     for run in (2, 3):
-        pl.when(ghostly[run] >= CAP)(functools.partial(again, run, run + 1))
+        pl.when(ghostly[run] >= CAP)(functools.partial(again, run))
     pack(listed(send_slots), image_rounded, up, down, next_row, last_row)
 
     def products(step, sums):
@@ -470,7 +484,16 @@
                 out_shape=[pltpu.SMEM((TABLE,), jnp.int32), gram_shape],
                 compiler_params=params(),
             )(neighbours, send_slots)
-            after = (done,)
+            turned, turned_done = pl.pallas_call(
+                late_kernel,
+                name="late",
+                in_specs=[IN_VMEM] * 5,
+                out_specs=[IN_VMEM] * 2,
+                out_shape=[turned_shape, gram_shape],
+                input_output_aliases={4: 0},
+                compiler_params=params(),
+            )(*blocks, turned)
+            after = (done, turned_done)
         if power > 0:
             image, image_rounded, gram = pl.pallas_call(
                 functools.partial(local_kernel, power),
@@ -493,29 +516,29 @@
         from_next = shifted(send_last, "gx", -1)
         received = (from_down, from_up, from_last, from_next)
         if power == 0:
-            turned, image, image_rounded, ghostly = pl.pallas_call(
+            image, image_rounded, *rest, ghostly = pl.pallas_call(
                 second_half_kernel,
                 name="second_half",
-                in_specs=[IN_SMEM] + [IN_HBM] * 2 + [IN_VMEM] * 4,
-                out_specs=[IN_VMEM] * 3 + [IN_SMEM],
-                out_shape=[turned_shape, full, narrow, pltpu.SMEM((8,), jnp.int32)],
-                scratch_shapes=room(3 * EIGHTH)
-                + [pltpu.SemaphoreType.DMA((3, 2)), lookup],
-                input_output_aliases={6: 0},
-                compiler_params=params(),
-            )(neighbours, diag_blocks, face_blocks, *blocks, rounded, turned)
+                in_specs=[IN_SMEM] + [IN_HBM] * 2 + [IN_VMEM] * 3,
+                out_specs=[IN_VMEM] * 4 + [IN_SMEM],
+                out_shape=[full, narrow] + room(3 * EIGHTH)
+                + [pltpu.SMEM((8,), jnp.int32)],
+                scratch_shapes=[pltpu.SemaphoreType.DMA((3, 2)), lookup],
+                compiler_params=params(),
+            )(neighbours, diag_blocks, face_blocks, *blocks, rounded)
+            blocks = blocks + rest
             outs = pl.pallas_call(
                 whole_kernel,
                 name="whole",
-                in_specs=[IN_SMEM] * 3 + [IN_VMEM] * 9,
+                in_specs=[IN_SMEM] * 3 + [IN_VMEM] * 13,
                 out_specs=[IN_VMEM] * 7,
                 out_shape=[full, narrow] + packets + [gram_shape],
                 scratch_shapes=[lookup],
-                input_output_aliases={10: 0, 11: 1},
+                input_output_aliases={14: 0, 15: 1},
                 compiler_params=params(),
             )(
-                neighbours, send_slots, ghostly, turned, rounded, *received, first,
-                image, image_rounded,
+                neighbours, send_slots, ghostly, turned, *blocks, rounded, *received,
+                first, image, image_rounded,
             )
         else:
             shapes = [full, narrow] + ([rows_shape] if last else packets + [gram_shape])

time: 92.1 us -> 92.3 us (level)
  waiting for transfers between devices: 9.66 us -> 8.2 us
  Pallas kernels: 16.9 us -> 18.2 us
    pallas_call x0 -> x1, Pallas kernels: none -> 1.56 us  [per_device(): pl.pallas_call(late_kernel, name='late', in_specs=[IN_VMEM] * 5, out_spec...]
    ppermute x16, waiting for transfers between devices: 9.66 us -> 8.2 us  [shifted(): lax.ppermute(block, axis, [(i, (i + distance) % SIDE) for i in range(SIDE)])]
  transfers between devices with their start and end apart: 16 -> 16, of which waited for: 6 -> 6; matrix products, arithmetic and copies ran while one was open for 0% -> 0% of each run, Pallas kernels for 11% -> 12%
where the time goes in v9:
time: 92.3 us; the launch traced here: 92.1 us
  starting transfers between devices  34.9 us (38%)
  blocking collectives  29.2 us (32%)
  Pallas kernels  18.2 us (20%)
  waiting for transfers between devices  8.2 us (9%)
  between operations  1.58 us (2%)
    ppermute x16, starting transfers between devices, shifted(): lax.ppermute(block, axis, [(i, (i + distance) % SIDE) for i in range(SIDE)])  34.9 us
    all_to_all x1, blocking collectives, per_device(): gathered = lax.all_to_all(gram, ('gx', 'gy'), 0, 0, tiled=True)  29.2 us
    ppermute x16, waiting for transfers between devices, shifted(): lax.ppermute(block, axis, [(i, (i + distance) % SIDE) for i in range(SIDE)])  8.2 us
    pallas_call x3, Pallas kernels, per_device(): pl.pallas_call(functools.partial(ghost_kernel, power), name=f'ghost{power...  3.48 us
    pallas_call x1, Pallas kernels, per_device(): pl.pallas_call(second_half_kernel, name='second_half', in_specs=[IN_SMEM]...  3.34 us
    pallas_call x3, Pallas kernels, per_device(): pl.pallas_call(functools.partial(local_kernel, power), name=f'local{power...  3.13 us
    pallas_call x1, Pallas kernels, per_device(): pl.pallas_call(first_half_kernel, name='first_half', in_specs=[IN_HBM] *...  2.98 us
  transfers between devices with their start and end apart: 16, of which 6 were waited for; matrix products, arithmetic and copies ran while one was open for 0% of the time, Pallas kernels for 12%

profile of v9, /device:TPU:1, one launch (start us, length us, event | category | flops | bytes accessed | tf_op | source)
XLA Modules:
  0.0 92.1 jit_solution(16380820318050899096)
XLA Ops:
  1.3 1.3 %start.1 = (f32[64,8,128]{2,1,0:T(8,128)S(1)}, bf16[64,8,128]{2,1,0:T(8,128)(2,1)S(1)}, bf16[48,8,128]{2,1,0:T(8,128)(2,1)S(1)}, bf16[48,8,128]{2,1,0:T(8,128)(2...) custom-call(s32[4,64]{1,0:T(4,128)} %bitcast.9, ...), custom_call_target="tpu_custom_call" | custom-call | tf_op jit(solution)/shard_map/start/pallas_call | solution.py:446
  2.5 2.2 %collective-permute-start = (bf16[48,8,128]{2,1,0:T(8,128)(2,1)S(1)}, bf16[48,8,128]{2,1,0:T(8,128)(2,1)S(1)}, u32[]{:S(2)}, u32[]{:S(2)}) collective-permute-start(bf16[48,8,128]{2,1,0:T(8,128)(2,1)S(1)} %get-tuple-element.74), channel_id=1, source_target_pairs={{0,1},{1,2},{2,3},{3,4},{4,5},{5,6},{6,7},{7,8},{8,9},{9,10},{10,1... | collective-permute-start | bytes 294920 | tf_op jit(solution)/shard_map/ppermute | solution.py:422
  4.7 3.7 %collective-permute-start.1 = (bf16[48,8,128]{2,1,0:T(8,128)(2,1)S(1)}, bf16[48,8,128]{2,1,0:T(8,128)(2,1)S(1)}, u32[]{:S(2)}, u32[]{:S(2)}) collective-permute-start(bf16[48,8,128]{2,1,0:T(8,128)(2,1)S(1)} %get-tuple-element.75), channel_id=1, source_target_pairs={{0,15},{1,0},{2,1},{3,2},{4,3},{5,4},{6,5},{7,6},{8,7},{9,8},{10,9... | collective-permute-start | bytes 294920 | tf_op jit(solution)/shard_map/ppermute | solution.py:422
  8.5 3.0 %first_half.1 = (bf16[64,640,128]{2,1,0:T(8,128)(2,1)S(1)}, bf16[8,128,128]{2,1,0:T(8,128)(2,1)S(1)}, bf16[8,4,128,128]{3,2,1,0:T(8,128)(2,1)S(1)}, f32[8,128]{1,0:T(8,128)S(1)}) custom-call(bf16[64,128,128]{2,1,0:T(8,128)(2,1)} %diag.3, bf16[64,4,128,128]{3,2,1,0:T(8,128)(2,1)} %face.3), custom_call_target="tpu_custom_call" | custom-call | tf_op jit(solution)/shard_map/first_half/pallas_call | solution.py:468
  11.5 2.5 %collective-permute-start.2 = (bf16[48,8,128]{2,1,0:T(8,128)(2,1)S(1)}, bf16[48,8,128]{2,1,0:T(8,128)(2,1)S(1)}, u32[]{:S(2)}, u32[]{:S(2)}) collective-permute-start(bf16[48,8,128]{2,1,0:T(8,128)(2,1)S(1)} %get-tuple-element.79), channel_id=1, source_target_pairs={{0,16},{16,32},{32,48},{48,64},{64,80},{80,96},{96,112},{112,128},... | collective-permute-start | bytes 294920 | tf_op jit(solution)/shard_map/ppermute | solution.py:422
  14.0 0.2 collective-permute-start.3
  14.3 3.3 %second_half.1 = (f32[64,8,128]{2,1,0:T(8,128)S(1)}, bf16[64,8,128]{2,1,0:T(8,128)(2,1)S(1)}, bf16[24,128,128]{2,1,0:T(8,128)(2,1)S(1)}, bf16[24,4,128,128]{3,2,1,0:T(8,128)(2,1)S(1)}, s32[8]{0:T(128)S(4)}) custom-call(s32[4,64]{1,0:T(4,128)S(4)} %get-tuple-element.63.neighbours, bf16[64,128,128]{2,1,0:T(8,128)(2,1)} %diag.3, ...), custom_call_target="tpu_custom_call" | custom-call | tf_op jit(solution)/shard_map/second_half/pallas_call | solution.py:519
  17.6 0.7 collective-permute-done.3.from_next
  18.4 1.3 %whole.1 = (f32[64,8,128]{2,1,0:T(8,128)S(1)}, bf16[64,8,128]{2,1,0:T(8,128)(2,1)S(1)}, bf16[48,8,128]{2,1,0:T(8,128)(2,1)S(1)}, bf16[48,8,128]{2,1,0:T(8,128)(2...) custom-call(s32[4,64]{1,0:T(4,128)S(4)} %get-tuple-element.63.neighb, ...), custom_call_target="tpu_custom_call", output_to_operand_aliasing={{0}: (14, {}), {1}: (15, {})} | custom-call | tf_op jit(solution)/shard_map/whole/pallas_call | solution.py:530
  19.7 4.8 %collective-permute-start.5 = (bf16[48,8,128]{2,1,0:T(8,128)(2,1)S(1)}, bf16[48,8,128]{2,1,0:T(8,128)(2,1)S(1)}, u32[]{:S(2)}, u32[]{:S(2)}) collective-permute-start(bf16[48,8,128]{2,1,0:T(8,128)(2,1)S(1)} %get-tuple-element.86), channel_id=1, source_target_pairs={{0,15},{1,0},{2,1},{3,2},{4,3},{5,4},{6,5},{7,6},{8,7},{9,8},{10,9... | collective-permute-start | bytes 294920 | tf_op jit(solution)/shard_map/ppermute | solution.py:422
  24.5 1.6 %late.1 = (bf16[64,640,128]{2,1,0:T(8,128)(2,1)S(1)}, f32[8,128]{1,0:T(8,128)S(1)}) custom-call(bf16[8,128,128]{2,1,0:T(8,128)(2,1)S(1)} %get-tuple-element.66.diag_next, bf16[8,4,128,128]{3,2,1,0:T(8,128)(2,1)S(1)} %get-tuple-element.67.face_next, bf16[24,128,128]{2,1,0:T(8,128)(2,1)S(1)} %get-tuple-element.69.diag_rest, ...), custom_call_target="tpu_custom_call", output_to_operand_aliasing={{0}: (4, {})} | custom-call | tf_op jit(solution)/shard_map/late/pallas_call | solution.py:487
  26.1 0.4 collective-permute-done.4.refs_0_.refs_3_
  26.5 3.0 %collective-permute-start.6 = (bf16[48,8,128]{2,1,0:T(8,128)(2,1)S(1)}, bf16[48,8,128]{2,1,0:T(8,128)(2,1)S(1)}, u32[]{:S(2)}, u32[]{:S(2)}) collective-permute-start(bf16[48,8,128]{2,1,0:T(8,128)(2,1)S(1)} %get-tuple-element.91), channel_id=1, source_target_pairs={{0,16},{16,32},{32,48},{48,64},{64,80},{80,96},{96,112},{112,128},... | collective-permute-start | bytes 294920 | tf_op jit(solution)/shard_map/ppermute | solution.py:422
  29.5 0.7 collective-permute-start.7
  30.2 1.0 %local1.1 = (f32[64,8,128]{2,1,0:T(8,128)S(1)}, bf16[64,8,128]{2,1,0:T(8,128)(2,1)S(1)}, f32[8,128]{1,0:T(8,128)S(1)}) custom-call(s32[544]{0:T(1024)S(4)} %get-tuple-element.65.refs_0_, bf16[64,640,128]{2,1,0:T(8,128)(2,1)S(1)} %get-tuple-element.72.refs_1_, bf16[64,8,128]{2,1,0:T(8,128)(2,1)S(1)} %get-tuple-element.84.refs_2_, ...), custom_call_target="tpu_custom_call" | custom-call | tf_op jit(solution)/shard_map/local1/pallas_call | solution.py:498
  31.2 2.3 %collective-permute-done.7.refs_6_ = bf16[48,8,128]{2,1,0:T(8,128)(2,1)S(1)} collective-permute-done((bf16[48,8,128]{2,1,0:T(8,128)(2,1)S(1)}, bf16[48,8,128]{2,1,0:T(8,128)(2,1)S(1)}, u32[]{:S(2)}, u32[]{:S(2)}) %collective-permute-start.7) | collective-permute-done | bytes 98336 | tf_op jit(solution)/shard_map/ppermute | solution.py:422
  33.5 1.1 %ghost1.1 = (f32[64,8,128]{2,1,0:T(8,128)S(1)}, bf16[64,8,128]{2,1,0:T(8,128)(2,1)S(1)}, bf16[48,8,128]{2,1,0:T(8,128)(2,1)S(1)}, bf16[48,8,128]{2,1,0:T(8,128)(...) custom-call(s32[544]{0:T(1024)S(4)} %get-tuple-element.65.refs_0_, ...), custom_call_target="tpu_custom_call", output_to_operand_aliasing={{0}: (10, {}), {1}: (11, {})} | custom-call | tf_op jit(solution)/shard_map/ghost1/pallas_call | solution.py:545
  34.8 5.0 %collective-permute-start.9 = (bf16[48,8,128]{2,1,0:T(8,128)(2,1)S(1)}, bf16[48,8,128]{2,1,0:T(8,128)(2,1)S(1)}, u32[]{:S(2)}, u32[]{:S(2)}) collective-permute-start(bf16[48,8,128]{2,1,0:T(8,128)(2,1)S(1)} %get-tuple-element.100), channel_id=1, source_target_pairs={{0,15},{1,0},{2,1},{3,2},{4,3},{5,4},{6,5},{7,6},{8,7},{9,8},{10,9... | collective-permute-start | bytes 294920 | tf_op jit(solution)/shard_map/ppermute | solution.py:422
  39.8 1.7 %collective-permute-done.8.refs_0_.refs_3_ = bf16[48,8,128]{2,1,0:T(8,128)(2,1)S(1)} collective-permute-done((bf16[48,8,128]{2,1,0:T(8,128)(2,1)S(1)}, bf16[48,8,128]{2,1,0:T(8,128)(2,1)S(1)}, u32[]{:S(2)}, u32[]{:S(2)}) %collective-permute-start.8) | collective-permute-done | bytes 98336 | tf_op jit(solution)/shard_map/ppermute | solution.py:422
  41.6 1.2 %collective-permute-start.10 = (bf16[48,8,128]{2,1,0:T(8,128)(2,1)S(1)}, bf16[48,8,128]{2,1,0:T(8,128)(2,1)S(1)}, u32[]{:S(2)}, u32[]{:S(2)}) collective-permute-start(bf16[48,8,128]{2,1,0:T(8,128)(2,1)S(1)} %get-tuple-element.103), channel_id=1, source_target_pairs={{0,16},{16,32},{32,48},{48,64},{64,80},{80,96},{96,112},{112,128},... | collective-permute-start | bytes 294920 | tf_op jit(solution)/shard_map/ppermute | solution.py:422
  42.7 1.9 %collective-permute-start.11 = (bf16[48,8,128]{2,1,0:T(8,128)(2,1)S(1)}, bf16[48,8,128]{2,1,0:T(8,128)(2,1)S(1)}, u32[]{:S(2)}, u32[]{:S(2)}) collective-permute-start(bf16[48,8,128]{2,1,0:T(8,128)(2,1)S(1)} %get-tuple-element.104), channel_id=1, source_target_pairs={{0,240},{16,0},{32,16},{48,32},{64,48},{80,64},{96,80},{112,96},{1... | collective-permute-start | bytes 294920 | tf_op jit(solution)/shard_map/ppermute | solution.py:422
  44.6 1.0 %local2.1 = (f32[64,8,128]{2,1,0:T(8,128)S(1)}, bf16[64,8,128]{2,1,0:T(8,128)(2,1)S(1)}, f32[8,128]{1,0:T(8,128)S(1)}) custom-call(s32[544]{0:T(1024)S(4)} %get-tuple-element.65.refs_0_, bf16[64,640,128]{2,1,0:T(8,128)(2,1)S(1)} %get-tuple-element.72.refs_1_, bf16[64,8,128]{2,1,0:T(8,128)(2,1)S(1)} %get-tuple-element.98.refs_2_, ...), custom_call_target="tpu_custom_call" | custom-call | tf_op jit(solution)/shard_map/local2/pallas_call | solution.py:498
  45.7 1.1 %collective-permute-done.11.refs_6_ = bf16[48,8,128]{2,1,0:T(8,128)(2,1)S(1)} collective-permute-done((bf16[48,8,128]{2,1,0:T(8,128)(2,1)S(1)}, bf16[48,8,128]{2,1,0:T(8,128)(2,1)S(1)}, u32[]{:S(2)}, u32[]{:S(2)}) %collective-permute-start.11) | collective-permute-done | bytes 98336 | tf_op jit(solution)/shard_map/ppermute | solution.py:422
  46.8 1.1 %ghost2.1 = (f32[64,8,128]{2,1,0:T(8,128)S(1)}, bf16[64,8,128]{2,1,0:T(8,128)(2,1)S(1)}, bf16[48,8,128]{2,1,0:T(8,128)(2,1)S(1)}, bf16[48,8,128]{2,1,0:T(8,128)(...) custom-call(s32[544]{0:T(1024)S(4)} %get-tuple-element.65.refs_0_, ...), custom_call_target="tpu_custom_call", output_to_operand_aliasing={{0}: (11, {}), {1}: (12, {})} | custom-call | tf_op jit(solution)/shard_map/ghost2/pallas_call | solution.py:545
  48.0 5.1 %collective-permute-start.13 = (bf16[48,8,128]{2,1,0:T(8,128)(2,1)S(1)}, bf16[48,8,128]{2,1,0:T(8,128)(2,1)S(1)}, u32[]{:S(2)}, u32[]{:S(2)}) collective-permute-start(bf16[48,8,128]{2,1,0:T(8,128)(2,1)S(1)} %get-tuple-element.112), channel_id=1, source_target_pairs={{0,15},{1,0},{2,1},{3,2},{4,3},{5,4},{6,5},{7,6},{8,7},{9,8},{10,9... | collective-permute-start | bytes 294920 | tf_op jit(solution)/shard_map/ppermute | solution.py:422
  53.1 1.9 %collective-permute-done.12.refs_0_.refs_3_ = bf16[48,8,128]{2,1,0:T(8,128)(2,1)S(1)} collective-permute-done((bf16[48,8,128]{2,1,0:T(8,128)(2,1)S(1)}, bf16[48,8,128]{2,1,0:T(8,128)(2,1)S(1)}, u32[]{:S(2)}, u32[]{:S(2)}) %collective-permute-start.12) | collective-permute-done | bytes 98336 | tf_op jit(solution)/shard_map/ppermute | solution.py:422
  55.1 0.9 collective-permute-start.14
  56.0 3.4 %collective-permute-start.15 = (bf16[48,8,128]{2,1,0:T(8,128)(2,1)S(1)}, bf16[48,8,128]{2,1,0:T(8,128)(2,1)S(1)}, u32[]{:S(2)}, u32[]{:S(2)}) collective-permute-start(bf16[48,8,128]{2,1,0:T(8,128)(2,1)S(1)} %get-tuple-element.116), channel_id=1, source_target_pairs={{0,240},{16,0},{32,16},{48,32},{64,48},{80,64},{96,80},{112,96},{1... | collective-permute-start | bytes 294920 | tf_op jit(solution)/shard_map/ppermute | solution.py:422
  59.4 1.1 %local3.1 = (f32[64,8,128]{2,1,0:T(8,128)S(1)}, bf16[64,8,128]{2,1,0:T(8,128)(2,1)S(1)}, f32[8,128]{1,0:T(8,128)S(1)}) custom-call(s32[544]{0:T(1024)S(4)} %get-tuple-element.65.refs_0_, bf16[64,640,128]{2,1,0:T(8,128)(2,1)S(1)} %get-tuple-element.72.refs_1_, bf16[64,8,128]{2,1,0:T(8,128)(2,1)S(1)} %get-tuple-element.110.refs_2_, ...), custom_call_target="tpu_custom_call" | custom-call | tf_op jit(solution)/shard_map/local3/pallas_call | solution.py:498
  60.4 1.2 %ghost3.1 = (f32[64,8,128]{2,1,0:T(8,128)S(1)}, bf16[64,8,128]{2,1,0:T(8,128)(2,1)S(1)}, f32[256,128]{1,0:T(8,128)S(1)}) custom-call(s32[544]{0:T(1024)S(4)} %get-tuple-element.65.refs_0_, bf16[64,640,128]{2,1,0:T(8,128)(2,1)S(1)} %get-tuple-element.72.refs_1_, ...), custom_call_target="tpu_custom_call", output_to_operand_aliasing={{0}: (12, {}), {1}: (13, {})} | custom-call | tf_op jit(solution)/shard_map/ghost3/pallas_call | solution.py:545
  61.7 29.2 %all_to_all.11 = f32[256,1,128]{2,1,0:T(1,128)S(1)} all-to-all(f32[256,1,128]{2,1,0:T(1,128)S(1)} %bitcast.7), channel_id=1, replica_groups=mesh['gx'=16,'gy'=16] {'gx','gy'}, dimensions={0} | all-to-all | bytes 262144 | tf_op jit(solution)/shard_map/all_to_all | solution.py:562
  90.9 1.1 %finish.1 = (f32[64,8,128]{2,1,0:T(8,128)}, f32[64,8,128]{2,1,0:T(8,128)}) custom-call(f32[256,128]{1,0:T(8,128)S(1)} %bitcast.6, f32[64,8,128]{2,1,0:T(8,128)S(1)} %get-tuple-element.81.b0.refs_4_.refs_8_, f32[64,8,128]{2,1,0:T(8,128)S(1)} %get-tuple-element.94.refs_5_.refs_9_.b1, f32[64,8,128]{2,1,0:T(8,128)S(1)} %get-tuple-element.106.refs_6_.refs_10_.b2, ...), custom_call_target="tpu_custom_call" | custom-call | tf_op jit(solution)/shard_map/finish/pallas_call | solution.py:563
  (18 shorter events, 0.3 us)
Async XLA Ops:
  2.5 8.9 %collective-permute-start = (bf16[48,8,128]{2,1,0:T(8,128)(2,1)S(1)}, bf16[48,8,128]{2,1,0:T(8,128)(2,1)S(1)}, u32[]{:S(2)}, u32[]{:S(2)}) collective-permute-start(bf16[48,8,128]{2,1,0:T(8,128)(2,1)S(1)} %get-tuple-element.74), channel_id=1, source_target_pairs={{0,1},{1,2},{2,3},{3,4},{4,5},{5,6},{6,7},{7,8},{8,9},{9,10},{10,1... | collective-permute-start | bytes 294920 | tf_op jit(solution)/shard_map/ppermute | solution.py:422
  4.7 6.7 %collective-permute-start.1 = (bf16[48,8,128]{2,1,0:T(8,128)(2,1)S(1)}, bf16[48,8,128]{2,1,0:T(8,128)(2,1)S(1)}, u32[]{:S(2)}, u32[]{:S(2)}) collective-permute-start(bf16[48,8,128]{2,1,0:T(8,128)(2,1)S(1)} %get-tuple-element.75), channel_id=1, source_target_pairs={{0,15},{1,0},{2,1},{3,2},{4,3},{5,4},{6,5},{7,6},{8,7},{9,8},{10,9... | collective-permute-start | bytes 294920 | tf_op jit(solution)/shard_map/ppermute | solution.py:422
  11.5 6.1 %collective-permute-start.2 = (bf16[48,8,128]{2,1,0:T(8,128)(2,1)S(1)}, bf16[48,8,128]{2,1,0:T(8,128)(2,1)S(1)}, u32[]{:S(2)}, u32[]{:S(2)}) collective-permute-start(bf16[48,8,128]{2,1,0:T(8,128)(2,1)S(1)} %get-tuple-element.79), channel_id=1, source_target_pairs={{0,16},{16,32},{32,48},{48,64},{64,80},{80,96},{96,112},{112,128},... | collective-permute-start | bytes 294920 | tf_op jit(solution)/shard_map/ppermute | solution.py:422
  14.0 4.3 %collective-permute-start.3 = (bf16[48,8,128]{2,1,0:T(8,128)(2,1)S(1)}, bf16[48,8,128]{2,1,0:T(8,128)(2,1)S(1)}, u32[]{:S(2)}, u32[]{:S(2)}) collective-permute-start(bf16[48,8,128]{2,1,0:T(8,128)(2,1)S(1)} %get-tuple-element.80), channel_id=1, source_target_pairs={{0,240},{16,0},{32,16},{48,32},{64,48},{80,64},{96,80},{112,96},{1... | collective-permute-start | bytes 294920 | tf_op jit(solution)/shard_map/ppermute | solution.py:422
  19.7 6.8 %collective-permute-start.4 = (bf16[48,8,128]{2,1,0:T(8,128)(2,1)S(1)}, bf16[48,8,128]{2,1,0:T(8,128)(2,1)S(1)}, u32[]{:S(2)}, u32[]{:S(2)}) collective-permute-start(bf16[48,8,128]{2,1,0:T(8,128)(2,1)S(1)} %get-tuple-element.85), channel_id=1, source_target_pairs={{0,1},{1,2},{2,3},{3,4},{4,5},{5,6},{6,7},{7,8},{8,9},{9,10},{10,1... | collective-permute-start | bytes 294920 | tf_op jit(solution)/shard_map/ppermute | solution.py:422
  19.7 6.8 %collective-permute-start.5 = (bf16[48,8,128]{2,1,0:T(8,128)(2,1)S(1)}, bf16[48,8,128]{2,1,0:T(8,128)(2,1)S(1)}, u32[]{:S(2)}, u32[]{:S(2)}) collective-permute-start(bf16[48,8,128]{2,1,0:T(8,128)(2,1)S(1)} %get-tuple-element.86), channel_id=1, source_target_pairs={{0,15},{1,0},{2,1},{3,2},{4,3},{5,4},{6,5},{7,6},{8,7},{9,8},{10,9... | collective-permute-start | bytes 294920 | tf_op jit(solution)/shard_map/ppermute | solution.py:422
  26.5 4.7 %collective-permute-start.6 = (bf16[48,8,128]{2,1,0:T(8,128)(2,1)S(1)}, bf16[48,8,128]{2,1,0:T(8,128)(2,1)S(1)}, u32[]{:S(2)}, u32[]{:S(2)}) collective-permute-start(bf16[48,8,128]{2,1,0:T(8,128)(2,1)S(1)} %get-tuple-element.91), channel_id=1, source_target_pairs={{0,16},{16,32},{32,48},{48,64},{64,80},{80,96},{96,112},{112,128},... | collective-permute-start | bytes 294920 | tf_op jit(solution)/shard_map/ppermute | solution.py:422
  29.5 4.0 %collective-permute-start.7 = (bf16[48,8,128]{2,1,0:T(8,128)(2,1)S(1)}, bf16[48,8,128]{2,1,0:T(8,128)(2,1)S(1)}, u32[]{:S(2)}, u32[]{:S(2)}) collective-permute-start(bf16[48,8,128]{2,1,0:T(8,128)(2,1)S(1)} %get-tuple-element.92), channel_id=1, source_target_pairs={{0,240},{16,0},{32,16},{48,32},{64,48},{80,64},{96,80},{112,96},{1... | collective-permute-start | bytes 294920 | tf_op jit(solution)/shard_map/ppermute | solution.py:422
  34.7 6.9 %collective-permute-start.8 = (bf16[48,8,128]{2,1,0:T(8,128)(2,1)S(1)}, bf16[48,8,128]{2,1,0:T(8,128)(2,1)S(1)}, u32[]{:S(2)}, u32[]{:S(2)}) collective-permute-start(bf16[48,8,128]{2,1,0:T(8,128)(2,1)S(1)} %get-tuple-element.99), channel_id=1, source_target_pairs={{0,1},{1,2},{2,3},{3,4},{4,5},{5,6},{6,7},{7,8},{8,9},{9,10},{10,1... | collective-permute-start | bytes 294920 | tf_op jit(solution)/shard_map/ppermute | solution.py:422
  34.8 6.8 %collective-permute-start.9 = (bf16[48,8,128]{2,1,0:T(8,128)(2,1)S(1)}, bf16[48,8,128]{2,1,0:T(8,128)(2,1)S(1)}, u32[]{:S(2)}, u32[]{:S(2)}) collective-permute-start(bf16[48,8,128]{2,1,0:T(8,128)(2,1)S(1)} %get-tuple-element.100), channel_id=1, source_target_pairs={{0,15},{1,0},{2,1},{3,2},{4,3},{5,4},{6,5},{7,6},{8,7},{9,8},{10,9... | collective-permute-start | bytes 294920 | tf_op jit(solution)/shard_map/ppermute | solution.py:422
  41.6 4.1 %collective-permute-start.10 = (bf16[48,8,128]{2,1,0:T(8,128)(2,1)S(1)}, bf16[48,8,128]{2,1,0:T(8,128)(2,1)S(1)}, u32[]{:S(2)}, u32[]{:S(2)}) collective-permute-start(bf16[48,8,128]{2,1,0:T(8,128)(2,1)S(1)} %get-tuple-element.103), channel_id=1, source_target_pairs={{0,16},{16,32},{32,48},{48,64},{64,80},{80,96},{96,112},{112,128},... | collective-permute-start | bytes 294920 | tf_op jit(solution)/shard_map/ppermute | solution.py:422
  42.7 4.0 %collective-permute-start.11 = (bf16[48,8,128]{2,1,0:T(8,128)(2,1)S(1)}, bf16[48,8,128]{2,1,0:T(8,128)(2,1)S(1)}, u32[]{:S(2)}, u32[]{:S(2)}) collective-permute-start(bf16[48,8,128]{2,1,0:T(8,128)(2,1)S(1)} %get-tuple-element.104), channel_id=1, source_target_pairs={{0,240},{16,0},{32,16},{48,32},{64,48},{80,64},{96,80},{112,96},{1... | collective-permute-start | bytes 294920 | tf_op jit(solution)/shard_map/ppermute | solution.py:422
  47.9 7.2 %collective-permute-start.12 = (bf16[48,8,128]{2,1,0:T(8,128)(2,1)S(1)}, bf16[48,8,128]{2,1,0:T(8,128)(2,1)S(1)}, u32[]{:S(2)}, u32[]{:S(2)}) collective-permute-start(bf16[48,8,128]{2,1,0:T(8,128)(2,1)S(1)} %get-tuple-element.111), channel_id=1, source_target_pairs={{0,1},{1,2},{2,3},{3,4},{4,5},{5,6},{6,7},{7,8},{8,9},{9,10},{10,1... | collective-permute-start | bytes 294920 | tf_op jit(solution)/shard_map/ppermute | solution.py:422
  48.0 7.1 %collective-permute-start.13 = (bf16[48,8,128]{2,1,0:T(8,128)(2,1)S(1)}, bf16[48,8,128]{2,1,0:T(8,128)(2,1)S(1)}, u32[]{:S(2)}, u32[]{:S(2)}) collective-permute-start(bf16[48,8,128]{2,1,0:T(8,128)(2,1)S(1)} %get-tuple-element.112), channel_id=1, source_target_pairs={{0,15},{1,0},{2,1},{3,2},{4,3},{5,4},{6,5},{7,6},{8,7},{9,8},{10,9... | collective-permute-start | bytes 294920 | tf_op jit(solution)/shard_map/ppermute | solution.py:422
  55.1 5.3 %collective-permute-start.14 = (bf16[48,8,128]{2,1,0:T(8,128)(2,1)S(1)}, bf16[48,8,128]{2,1,0:T(8,128)(2,1)S(1)}, u32[]{:S(2)}, u32[]{:S(2)}) collective-permute-start(bf16[48,8,128]{2,1,0:T(8,128)(2,1)S(1)} %get-tuple-element.115), channel_id=1, source_target_pairs={{0,16},{16,32},{32,48},{48,64},{64,80},{80,96},{96,112},{112,128},... | collective-permute-start | bytes 294920 | tf_op jit(solution)/shard_map/ppermute | solution.py:422
  56.0 4.5 %collective-permute-start.15 = (bf16[48,8,128]{2,1,0:T(8,128)(2,1)S(1)}, bf16[48,8,128]{2,1,0:T(8,128)(2,1)S(1)}, u32[]{:S(2)}, u32[]{:S(2)}) collective-permute-start(bf16[48,8,128]{2,1,0:T(8,128)(2,1)S(1)} %get-tuple-element.116), channel_id=1, source_target_pairs={{0,240},{16,0},{32,16},{48,32},{64,48},{80,64},{96,80},{112,96},{1... | collective-permute-start | bytes 294920 | tf_op jit(solution)/shard_map/ppermute | solution.py:422

commit v10 on v9

--- a/solution.py
+++ b/solution.py
@@ -136,20 +136,13 @@
     return parts
 
 
-def first_half_kernel(
-    diag, face, turned, diag_next, face_next, done, diag_here, face_here, arrived
-):
+def first_half_kernel(diag, face, turned, done, diag_here, face_here, arrived):
     parts = fetch_parts(0, CAP // 2, diag, face, diag_here, face_here, arrived)
-    ahead = fetching(CAP // 2, diag, face, diag_next, face_next, arrived.at[4])
-    for copy in ahead:
-        copy.start()
     for at, place, copies in parts:
         for copy in copies:
             copy.wait()
         transpose_some(at, *place, turned)
     done[...] = jnp.zeros_like(done)
-    for copy in ahead:
-        copy.wait()
 
 
 def apply_as_is(e, vectors, diag_block, face_rows, image, image_rounded):
@@ -164,43 +157,29 @@
 
 
 def second_half_kernel(
-    neighbours, diag, face, diag_next, face_next, rounded, image, image_rounded,
-    diag_rest, face_rest, ghostly, arrived, lookup,
+    neighbours, diag, face, rounded, image, image_rounded, ghostly, lookup
 ):
-    first = CAP // 2
-    parts = fetch_parts(
-        first + EIGHTH, 3 * EIGHTH, diag, face, diag_rest, face_rest, arrived
-    )
     fill_local(lookup, rounded)
-
-    def apply_some(begin, diag_of, face_of):
-        for at in range(EIGHTH):
-            e = begin + at
-            vectors = [lookup[e]]
-            for f in range(FACES):
-                near = neighbours[f, e]
-                vectors.append(
-                    lookup[jnp.where((near < 0) | (near >= CAP), NOTHING, near)]
-                )
-            rows = [face_of[at, f] for f in range(FACES)]
-            apply_as_is(e, vectors, diag_of[at], rows, image, image_rounded)
-
-    apply_some(first, diag_next, face_next)
+    for e in range(CAP // 2, CAP):
+        vectors = [lookup[e]]
+        for f in range(FACES):
+            near = neighbours[f, e]
+            vectors.append(
+                lookup[jnp.where((near < 0) | (near >= CAP), NOTHING, near)]
+            )
+        rows = [face[e, f] for f in range(FACES)]
+        apply_as_is(e, vectors, diag[e], rows, image, image_rounded)
     for run in (2, 3):
         farthest = jnp.int32(-1)
         for e in range(run * UNROLL, (run + 1) * UNROLL):
             for f in range(FACES):
                 farthest = jnp.maximum(farthest, neighbours[f, e])
         ghostly[run] = farthest
-    for begin, place, copies in parts:
-        for copy in copies:
-            copy.wait()
-        apply_some(begin, *place)
-
-
-def late_kernel(diag_next, face_next, diag_rest, face_rest, before, turned, done):
-    transpose_some(CAP // 2, diag_next, face_next, turned)
-    transpose_some(CAP // 2 + EIGHTH, diag_rest, face_rest, turned)
+
+
+def late_kernel(diag, face, before, turned, done):
+    half = pl.ds(CAP // 2, CAP // 2)
+    transpose_some(CAP // 2, diag.at[half], face.at[half], turned)
     done[...] = jnp.zeros_like(done)
 
 
@@ -267,8 +246,7 @@
 
 
 def whole_kernel(
-    neighbours, send_slots, ghostly, turned, diag_next, face_next, diag_rest, face_rest,
-    rounded, from_down, from_up, from_last, from_next, b0, before, before_rounded,
+    neighbours, send_slots, ghostly, turned, diag, face, rounded, from_down, from_up, from_last, from_next, b0, before, before_rounded,
     image, image_rounded, up, down, next_row, last_row, gram_out, lookup,
 ):
     fill_local(lookup, rounded)
@@ -280,13 +258,9 @@
 
     def again(run):
         for e in range(run * UNROLL, (run + 1) * UNROLL):
-            at = e - CAP // 2
-            diag_of, face_of = diag_next, face_next
-            if at >= EIGHTH:
-                at, diag_of, face_of = at - EIGHTH, diag_rest, face_rest
             vectors = [lookup[place] for place in find(e)]
-            rows = [face_of[at, f] for f in range(FACES)]
-            apply_as_is(e, vectors, diag_of[at], rows, image, image_rounded)
+            rows = [face[e, f] for f in range(FACES)]
+            apply_as_is(e, vectors, diag[e], rows, image, image_rounded)
 
     apply_runs(0, 2, find, turned, lookup, (), image, image_rounded)
     for run in (2, 3):
@@ -427,6 +401,7 @@
     neighbours = neighbours.T
     send_slots = send_slots.transpose(1, 0, 2)
     in_place = lambda array: pltpu.with_memory_space_constraint(array, pltpu.HBM)
+    blocks = diag_blocks, face_blocks
     diag_blocks = in_place(diag_blocks)
     face_blocks = in_place(face_blocks)
     packets = [vector_shape(n * SEND, half) for n in (3, 3, 1, 1)]
@@ -465,13 +440,13 @@
         from_up = shifted(down, "gy", -1)
         after = ()
         if power == 0:
-            turned, *blocks, done = pl.pallas_call(
+            turned, done = pl.pallas_call(
                 first_half_kernel,
                 name="first_half",
                 in_specs=[IN_HBM] * 2,
-                out_specs=[IN_VMEM] * 4,
-                out_shape=[turned_shape] + room(EIGHTH) + [gram_shape],
-                scratch_shapes=room(CAP // 2) + [pltpu.SemaphoreType.DMA((5, 2))],
+                out_specs=[IN_VMEM] * 2,
+                out_shape=[turned_shape, gram_shape],
+                scratch_shapes=room(CAP // 2) + [pltpu.SemaphoreType.DMA((4, 2))],
                 compiler_params=params(),
             )(diag_blocks, face_blocks)
             after = (done,)
@@ -487,10 +462,10 @@
             turned, turned_done = pl.pallas_call(
                 late_kernel,
                 name="late",
-                in_specs=[IN_VMEM] * 5,
+                in_specs=[IN_VMEM] * 3,
                 out_specs=[IN_VMEM] * 2,
                 out_shape=[turned_shape, gram_shape],
-                input_output_aliases={4: 0},
+                input_output_aliases={2: 0},
                 compiler_params=params(),
             )(*blocks, turned)
             after = (done, turned_done)
@@ -516,25 +491,23 @@
         from_next = shifted(send_last, "gx", -1)
         received = (from_down, from_up, from_last, from_next)
         if power == 0:
-            image, image_rounded, *rest, ghostly = pl.pallas_call(
+            image, image_rounded, ghostly = pl.pallas_call(
                 second_half_kernel,
                 name="second_half",
-                in_specs=[IN_SMEM] + [IN_HBM] * 2 + [IN_VMEM] * 3,
-                out_specs=[IN_VMEM] * 4 + [IN_SMEM],
-                out_shape=[full, narrow] + room(3 * EIGHTH)
-                + [pltpu.SMEM((8,), jnp.int32)],
-                scratch_shapes=[pltpu.SemaphoreType.DMA((3, 2)), lookup],
-                compiler_params=params(),
-            )(neighbours, diag_blocks, face_blocks, *blocks, rounded)
-            blocks = blocks + rest
+                in_specs=[IN_SMEM] + [IN_VMEM] * 3,
+                out_specs=[IN_VMEM] * 2 + [IN_SMEM],
+                out_shape=[full, narrow, pltpu.SMEM((8,), jnp.int32)],
+                scratch_shapes=[lookup],
+                compiler_params=params(),
+            )(neighbours, *blocks, rounded)
             outs = pl.pallas_call(
                 whole_kernel,
                 name="whole",
-                in_specs=[IN_SMEM] * 3 + [IN_VMEM] * 13,
+                in_specs=[IN_SMEM] * 3 + [IN_VMEM] * 11,
                 out_specs=[IN_VMEM] * 7,
                 out_shape=[full, narrow] + packets + [gram_shape],
                 scratch_shapes=[lookup],
-                input_output_aliases={14: 0, 15: 1},
+                input_output_aliases={12: 0, 13: 1},
                 compiler_params=params(),
             )(
                 neighbours, send_slots, ghostly, turned, *blocks, rounded, *received,

time: 92.3 us -> 91.6 us (level)
  Pallas kernels: 18.2 us -> 17.1 us
    pallas_call x1, Pallas kernels: 3.34 us -> 1.73 us  [per_device(): pl.pallas_call(second_half_kernel, name='second_half', in_specs=[IN_SMEM]...]
  transfers between devices with their start and end apart: 16 -> 16, of which waited for: 6 -> 6; matrix products, arithmetic and copies ran while one was open for 0% -> 0% of each run, Pallas kernels for 12% -> 10%
where the time goes in v10:
time: 91.6 us; the launch traced here: 91.5 us
  starting transfers between devices  35.2 us (38%)
  blocking collectives  29.4 us (32%)
  Pallas kernels  17.1 us (19%)
  waiting for transfers between devices  8.1 us (9%)
  between operations  1.73 us (2%)
    ppermute x16, starting transfers between devices, shifted(): lax.ppermute(block, axis, [(i, (i + distance) % SIDE) for i in range(SIDE)])  35.2 us
    all_to_all x1, blocking collectives, per_device(): gathered = lax.all_to_all(gram, ('gx', 'gy'), 0, 0, tiled=True)  29.4 us
    ppermute x16, waiting for transfers between devices, shifted(): lax.ppermute(block, axis, [(i, (i + distance) % SIDE) for i in range(SIDE)])  8.1 us
    pallas_call x3, Pallas kernels, per_device(): pl.pallas_call(functools.partial(ghost_kernel, power), name=f'ghost{power...  3.49 us
    pallas_call x3, Pallas kernels, per_device(): pl.pallas_call(functools.partial(local_kernel, power), name=f'local{power...  3.32 us
    pallas_call x1, Pallas kernels, per_device(): pl.pallas_call(first_half_kernel, name='first_half', in_specs=[IN_HBM] *...  2.96 us
  transfers between devices with their start and end apart: 16, of which 6 were waited for; matrix products, arithmetic and copies ran while one was open for 0% of the time, Pallas kernels for 10%

profile of v10, /device:TPU:1, one launch (start us, length us, event | category | flops | bytes accessed | tf_op | source)
XLA Modules:
  0.0 91.5 jit_solution(7705261116972405414)
XLA Ops:
  1.4 1.6 %start.1 = (f32[64,8,128]{2,1,0:T(8,128)S(1)}, bf16[64,8,128]{2,1,0:T(8,128)(2,1)S(1)}, bf16[48,8,128]{2,1,0:T(8,128)(2,1)S(1)}, bf16[48,8,128]{2,1,0:T(8,128)(2...) custom-call(s32[4,64]{1,0:T(4,128)} %bitcast.9, ...), custom_call_target="tpu_custom_call" | custom-call | tf_op jit(solution)/shard_map/start/pallas_call | solution.py:421
  3.1 2.2 %collective-permute-start = (bf16[48,8,128]{2,1,0:T(8,128)(2,1)S(1)}, bf16[48,8,128]{2,1,0:T(8,128)(2,1)S(1)}, u32[]{:S(2)}, u32[]{:S(2)}) collective-permute-start(bf16[48,8,128]{2,1,0:T(8,128)(2,1)S(1)} %get-tuple-element.66), channel_id=1, source_target_pairs={{0,1},{1,2},{2,3},{3,4},{4,5},{5,6},{6,7},{7,8},{8,9},{9,10},{10,1... | collective-permute-start | bytes 294920 | tf_op jit(solution)/shard_map/ppermute | solution.py:396
  5.3 3.7 %collective-permute-start.1 = (bf16[48,8,128]{2,1,0:T(8,128)(2,1)S(1)}, bf16[48,8,128]{2,1,0:T(8,128)(2,1)S(1)}, u32[]{:S(2)}, u32[]{:S(2)}) collective-permute-start(bf16[48,8,128]{2,1,0:T(8,128)(2,1)S(1)} %get-tuple-element.67), channel_id=1, source_target_pairs={{0,15},{1,0},{2,1},{3,2},{4,3},{5,4},{6,5},{7,6},{8,7},{9,8},{10,9... | collective-permute-start | bytes 294920 | tf_op jit(solution)/shard_map/ppermute | solution.py:396
  9.0 3.0 %first_half.1 = (bf16[64,640,128]{2,1,0:T(8,128)(2,1)S(1)}, f32[8,128]{1,0:T(8,128)S(1)}) custom-call(bf16[64,128,128]{2,1,0:T(8,128)(2,1)} %diag.7, bf16[64,4,128,128]{3,2,1,0:T(8,128)(2,1)} %face.7), custom_call_target="tpu_custom_call" | custom-call | tf_op jit(solution)/shard_map/first_half/pallas_call | solution.py:443
  12.0 2.5 %collective-permute-start.2 = (bf16[48,8,128]{2,1,0:T(8,128)(2,1)S(1)}, bf16[48,8,128]{2,1,0:T(8,128)(2,1)S(1)}, u32[]{:S(2)}, u32[]{:S(2)}) collective-permute-start(bf16[48,8,128]{2,1,0:T(8,128)(2,1)S(1)} %get-tuple-element.71), channel_id=1, source_target_pairs={{0,16},{16,32},{32,48},{48,64},{64,80},{80,96},{96,112},{112,128},... | collective-permute-start | bytes 294920 | tf_op jit(solution)/shard_map/ppermute | solution.py:396
  14.5 0.2 collective-permute-start.3
  14.8 1.7 %second_half.1 = (f32[64,8,128]{2,1,0:T(8,128)S(1)}, bf16[64,8,128]{2,1,0:T(8,128)(2,1)S(1)}, s32[8]{0:T(128)S(4)}) custom-call(s32[4,64]{1,0:T(4,128)S(4)} %get-tuple-element.59.neighbours, bf16[64,128,128]{2,1,0:T(8,128)(2,1)S(1)} %copy-done.1, bf16[64,4,128,128]{3,2,1,0:T(8,128)(2,1)S(1)} %copy-done, bf16[64,8,128]{2,1,0:T(8,128)(2,1)S(1)} %get-tuple-element.64.rounded), custom_call_target="tpu_custom_call" | custom-call | tf_op jit(solution)/shard_map/second_half/pallas_call | solution.py:494
  16.5 2.4 %collective-permute-done.3.from_next = bf16[48,8,128]{2,1,0:T(8,128)(2,1)S(1)} collective-permute-done((bf16[48,8,128]{2,1,0:T(8,128)(2,1)S(1)}, bf16[48,8,128]{2,1,0:T(8,128)(2,1)S(1)}, u32[]{:S(2)}, u32[]{:S(2)}) %collective-permute-start.3) | collective-permute-done | bytes 98336 | tf_op jit(solution)/shard_map/ppermute | solution.py:396
  18.9 1.3 %whole.1 = (f32[64,8,128]{2,1,0:T(8,128)S(1)}, bf16[64,8,128]{2,1,0:T(8,128)(2,1)S(1)}, bf16[48,8,128]{2,1,0:T(8,128)(2,1)S(1)}, bf16[48,8,128]{2,1,0:T(8,128)(2...) custom-call(s32[4,64]{1,0:T(4,128)S(4)} %get-tuple-element.59.neighb, ...), custom_call_target="tpu_custom_call", output_to_operand_aliasing={{0}: (12, {}), {1}: (13, {})} | custom-call | tf_op jit(solution)/shard_map/whole/pallas_call | solution.py:503
  20.2 4.8 %collective-permute-start.5 = (bf16[48,8,128]{2,1,0:T(8,128)(2,1)S(1)}, bf16[48,8,128]{2,1,0:T(8,128)(2,1)S(1)}, u32[]{:S(2)}, u32[]{:S(2)}) collective-permute-start(bf16[48,8,128]{2,1,0:T(8,128)(2,1)S(1)} %get-tuple-element.78), channel_id=1, source_target_pairs={{0,15},{1,0},{2,1},{3,2},{4,3},{5,4},{6,5},{7,6},{8,7},{9,8},{10,9... | collective-permute-start | bytes 294920 | tf_op jit(solution)/shard_map/ppermute | solution.py:396
  25.0 1.6 %late.1 = (bf16[64,640,128]{2,1,0:T(8,128)(2,1)S(1)}, f32[8,128]{1,0:T(8,128)S(1)}) custom-call(bf16[64,128,128]{2,1,0:T(8,128)(2,1)S(1)} %copy-done.1, bf16[64,4,128,128]{3,2,1,0:T(8,128)(2,1)S(1)} %copy-done, bf16[64,640,128]{2,1,0:T(8,128)(2,1)S(1)} %get-tuple-element.62.before.turned), custom_call_target="tpu_custom_call", output_to_operand_aliasing={{0}: (2, {})} | custom-call | tf_op jit(solution)/shard_map/late/pallas_call | solution.py:462
  26.6 0.4 collective-permute-done.4.refs_0_.refs_3_
  27.0 0.9 collective-permute-start.6
  27.9 1.7 %collective-permute-start.7 = (bf16[48,8,128]{2,1,0:T(8,128)(2,1)S(1)}, bf16[48,8,128]{2,1,0:T(8,128)(2,1)S(1)}, u32[]{:S(2)}, u32[]{:S(2)}) collective-permute-start(bf16[48,8,128]{2,1,0:T(8,128)(2,1)S(1)} %get-tuple-element.84), channel_id=1, source_target_pairs={{0,240},{16,0},{32,16},{48,32},{64,48},{80,64},{96,80},{112,96},{1... | collective-permute-start | bytes 294920 | tf_op jit(solution)/shard_map/ppermute | solution.py:396
  29.6 1.0 %local1.1 = (f32[64,8,128]{2,1,0:T(8,128)S(1)}, bf16[64,8,128]{2,1,0:T(8,128)(2,1)S(1)}, f32[8,128]{1,0:T(8,128)S(1)}) custom-call(s32[544]{0:T(1024)S(4)} %get-tuple-element.61.refs_0_, bf16[64,640,128]{2,1,0:T(8,128)(2,1)S(1)} %get-tuple-element.63.refs_1_, bf16[64,8,128]{2,1,0:T(8,128)(2,1)S(1)} %get-tuple-element.76.refs_2_, ...), custom_call_target="tpu_custom_call" | custom-call | tf_op jit(solution)/shard_map/local1/pallas_call | solution.py:473
  30.6 1.3 %collective-permute-done.7.refs_6_ = bf16[48,8,128]{2,1,0:T(8,128)(2,1)S(1)} collective-permute-done((bf16[48,8,128]{2,1,0:T(8,128)(2,1)S(1)}, bf16[48,8,128]{2,1,0:T(8,128)(2,1)S(1)}, u32[]{:S(2)}, u32[]{:S(2)}) %collective-permute-start.7) | collective-permute-done | bytes 98336 | tf_op jit(solution)/shard_map/ppermute | solution.py:396
  31.9 1.1 %ghost1.1 = (f32[64,8,128]{2,1,0:T(8,128)S(1)}, bf16[64,8,128]{2,1,0:T(8,128)(2,1)S(1)}, bf16[48,8,128]{2,1,0:T(8,128)(2,1)S(1)}, bf16[48,8,128]{2,1,0:T(8,128)(...) custom-call(s32[544]{0:T(1024)S(4)} %get-tuple-element.61.refs_0_, ...), custom_call_target="tpu_custom_call", output_to_operand_aliasing={{0}: (10, {}), {1}: (11, {})} | custom-call | tf_op jit(solution)/shard_map/ghost1/pallas_call | solution.py:518
  33.1 5.4 %collective-permute-start.9 = (bf16[48,8,128]{2,1,0:T(8,128)(2,1)S(1)}, bf16[48,8,128]{2,1,0:T(8,128)(2,1)S(1)}, u32[]{:S(2)}, u32[]{:S(2)}) collective-permute-start(bf16[48,8,128]{2,1,0:T(8,128)(2,1)S(1)} %get-tuple-element.92), channel_id=1, source_target_pairs={{0,15},{1,0},{2,1},{3,2},{4,3},{5,4},{6,5},{7,6},{8,7},{9,8},{10,9... | collective-permute-start | bytes 294920 | tf_op jit(solution)/shard_map/ppermute | solution.py:396
  38.6 1.9 %collective-permute-done.8.refs_0_.refs_3_ = bf16[48,8,128]{2,1,0:T(8,128)(2,1)S(1)} collective-permute-done((bf16[48,8,128]{2,1,0:T(8,128)(2,1)S(1)}, bf16[48,8,128]{2,1,0:T(8,128)(2,1)S(1)}, u32[]{:S(2)}, u32[]{:S(2)}) %collective-permute-start.8) | collective-permute-done | bytes 98336 | tf_op jit(solution)/shard_map/ppermute | solution.py:396
  40.5 0.9 collective-permute-start.10
  41.4 2.6 %collective-permute-start.11 = (bf16[48,8,128]{2,1,0:T(8,128)(2,1)S(1)}, bf16[48,8,128]{2,1,0:T(8,128)(2,1)S(1)}, u32[]{:S(2)}, u32[]{:S(2)}) collective-permute-start(bf16[48,8,128]{2,1,0:T(8,128)(2,1)S(1)} %get-tuple-element.96), channel_id=1, source_target_pairs={{0,240},{16,0},{32,16},{48,32},{64,48},{80,64},{96,80},{112,96},{1... | collective-permute-start | bytes 294920 | tf_op jit(solution)/shard_map/ppermute | solution.py:396
  44.0 1.2 %local2.1 = (f32[64,8,128]{2,1,0:T(8,128)S(1)}, bf16[64,8,128]{2,1,0:T(8,128)(2,1)S(1)}, f32[8,128]{1,0:T(8,128)S(1)}) custom-call(s32[544]{0:T(1024)S(4)} %get-tuple-element.61.refs_0_, bf16[64,640,128]{2,1,0:T(8,128)(2,1)S(1)} %get-tuple-element.63.refs_1_, bf16[64,8,128]{2,1,0:T(8,128)(2,1)S(1)} %get-tuple-element.90.refs_2_, ...), custom_call_target="tpu_custom_call" | custom-call | tf_op jit(solution)/shard_map/local2/pallas_call | solution.py:473
  45.3 0.2 collective-permute-done.11.refs_6_
  45.5 1.1 %ghost2.1 = (f32[64,8,128]{2,1,0:T(8,128)S(1)}, bf16[64,8,128]{2,1,0:T(8,128)(2,1)S(1)}, bf16[48,8,128]{2,1,0:T(8,128)(2,1)S(1)}, bf16[48,8,128]{2,1,0:T(8,128)(...) custom-call(s32[544]{0:T(1024)S(4)} %get-tuple-element.61.refs_0_, ...), custom_call_target="tpu_custom_call", output_to_operand_aliasing={{0}: (11, {}), {1}: (12, {})} | custom-call | tf_op jit(solution)/shard_map/ghost2/pallas_call | solution.py:518
  46.7 5.2 %collective-permute-start.13 = (bf16[48,8,128]{2,1,0:T(8,128)(2,1)S(1)}, bf16[48,8,128]{2,1,0:T(8,128)(2,1)S(1)}, u32[]{:S(2)}, u32[]{:S(2)}) collective-permute-start(bf16[48,8,128]{2,1,0:T(8,128)(2,1)S(1)} %get-tuple-element.104), channel_id=1, source_target_pairs={{0,15},{1,0},{2,1},{3,2},{4,3},{5,4},{6,5},{7,6},{8,7},{9,8},{10,9... | collective-permute-start | bytes 294920 | tf_op jit(solution)/shard_map/ppermute | solution.py:396
  51.9 1.9 %collective-permute-done.12.refs_0_.refs_3_ = bf16[48,8,128]{2,1,0:T(8,128)(2,1)S(1)} collective-permute-done((bf16[48,8,128]{2,1,0:T(8,128)(2,1)S(1)}, bf16[48,8,128]{2,1,0:T(8,128)(2,1)S(1)}, u32[]{:S(2)}, u32[]{:S(2)}) %collective-permute-start.12) | collective-permute-done | bytes 98336 | tf_op jit(solution)/shard_map/ppermute | solution.py:396
  53.9 0.9 collective-permute-start.14
  54.7 3.8 %collective-permute-start.15 = (bf16[48,8,128]{2,1,0:T(8,128)(2,1)S(1)}, bf16[48,8,128]{2,1,0:T(8,128)(2,1)S(1)}, u32[]{:S(2)}, u32[]{:S(2)}) collective-permute-start(bf16[48,8,128]{2,1,0:T(8,128)(2,1)S(1)} %get-tuple-element.108), channel_id=1, source_target_pairs={{0,240},{16,0},{32,16},{48,32},{64,48},{80,64},{96,80},{112,96},{1... | collective-permute-start | bytes 294920 | tf_op jit(solution)/shard_map/ppermute | solution.py:396
  58.6 1.1 %local3.1 = (f32[64,8,128]{2,1,0:T(8,128)S(1)}, bf16[64,8,128]{2,1,0:T(8,128)(2,1)S(1)}, f32[8,128]{1,0:T(8,128)S(1)}) custom-call(s32[544]{0:T(1024)S(4)} %get-tuple-element.61.refs_0_, bf16[64,640,128]{2,1,0:T(8,128)(2,1)S(1)} %get-tuple-element.63.refs_1_, bf16[64,8,128]{2,1,0:T(8,128)(2,1)S(1)} %get-tuple-element.102.refs_2_, ...), custom_call_target="tpu_custom_call" | custom-call | tf_op jit(solution)/shard_map/local3/pallas_call | solution.py:473
  59.7 1.2 %ghost3.1 = (f32[64,8,128]{2,1,0:T(8,128)S(1)}, bf16[64,8,128]{2,1,0:T(8,128)(2,1)S(1)}, f32[256,128]{1,0:T(8,128)S(1)}) custom-call(s32[544]{0:T(1024)S(4)} %get-tuple-element.61.refs_0_, bf16[64,640,128]{2,1,0:T(8,128)(2,1)S(1)} %get-tuple-element.63.refs_1_, ...), custom_call_target="tpu_custom_call", output_to_operand_aliasing={{0}: (12, {}), {1}: (13, {})} | custom-call | tf_op jit(solution)/shard_map/ghost3/pallas_call | solution.py:518
  60.9 29.4 %all_to_all.11 = f32[256,1,128]{2,1,0:T(1,128)S(1)} all-to-all(f32[256,1,128]{2,1,0:T(1,128)S(1)} %bitcast.7), channel_id=1, replica_groups=mesh['gx'=16,'gy'=16] {'gx','gy'}, dimensions={0} | all-to-all | bytes 262144 | tf_op jit(solution)/shard_map/all_to_all | solution.py:535
  90.2 1.1 %finish.1 = (f32[64,8,128]{2,1,0:T(8,128)}, f32[64,8,128]{2,1,0:T(8,128)}) custom-call(f32[256,128]{1,0:T(8,128)S(1)} %bitcast.6, f32[64,8,128]{2,1,0:T(8,128)S(1)} %get-tuple-element.73.b0.refs_4_.refs_8_, f32[64,8,128]{2,1,0:T(8,128)S(1)} %get-tuple-element.86.refs_5_.refs_9_.b1, f32[64,8,128]{2,1,0:T(8,128)S(1)} %get-tuple-element.98.refs_6_.refs_10_.b2, ...), custom_call_target="tpu_custom_call" | custom-call | tf_op jit(solution)/shard_map/finish/pallas_call | solution.py:536
  (22 shorter events, 0.3 us)
Async XLA Ops:
  0.6 14.1 %copy-start = (bf16[64,4,128,128]{3,2,1,0:T(8,128)(2,1)S(1)}, bf16[64,4,128,128]{3,2,1,0:T(8,128)(2,1)}, u32[]{:S(2)}) copy-start(bf16[64,4,128,128]{3,2,1,0:T(8,128)(2,1)} %face.7) | copy-start | bytes 25165828
  0.6 14.1 %copy-start.1 = (bf16[64,128,128]{2,1,0:T(8,128)(2,1)S(1)}, bf16[64,128,128]{2,1,0:T(8,128)(2,1)}, u32[]{:S(2)}) copy-start(bf16[64,128,128]{2,1,0:T(8,128)(2,1)} %diag.7) | copy-start | bytes 6291460
  3.1 8.9 %collective-permute-start = (bf16[48,8,128]{2,1,0:T(8,128)(2,1)S(1)}, bf16[48,8,128]{2,1,0:T(8,128)(2,1)S(1)}, u32[]{:S(2)}, u32[]{:S(2)}) collective-permute-start(bf16[48,8,128]{2,1,0:T(8,128)(2,1)S(1)} %get-tuple-element.66), channel_id=1, source_target_pairs={{0,1},{1,2},{2,3},{3,4},{4,5},{5,6},{6,7},{7,8},{8,9},{9,10},{10,1... | collective-permute-start | bytes 294920 | tf_op jit(solution)/shard_map/ppermute | solution.py:396
  5.3 6.7 %collective-permute-start.1 = (bf16[48,8,128]{2,1,0:T(8,128)(2,1)S(1)}, bf16[48,8,128]{2,1,0:T(8,128)(2,1)S(1)}, u32[]{:S(2)}, u32[]{:S(2)}) collective-permute-start(bf16[48,8,128]{2,1,0:T(8,128)(2,1)S(1)} %get-tuple-element.67), channel_id=1, source_target_pairs={{0,15},{1,0},{2,1},{3,2},{4,3},{5,4},{6,5},{7,6},{8,7},{9,8},{10,9... | collective-permute-start | bytes 294920 | tf_op jit(solution)/shard_map/ppermute | solution.py:396
  12.0 4.5 %collective-permute-start.2 = (bf16[48,8,128]{2,1,0:T(8,128)(2,1)S(1)}, bf16[48,8,128]{2,1,0:T(8,128)(2,1)S(1)}, u32[]{:S(2)}, u32[]{:S(2)}) collective-permute-start(bf16[48,8,128]{2,1,0:T(8,128)(2,1)S(1)} %get-tuple-element.71), channel_id=1, source_target_pairs={{0,16},{16,32},{32,48},{48,64},{64,80},{80,96},{96,112},{112,128},... | collective-permute-start | bytes 294920 | tf_op jit(solution)/shard_map/ppermute | solution.py:396
  14.5 4.3 %collective-permute-start.3 = (bf16[48,8,128]{2,1,0:T(8,128)(2,1)S(1)}, bf16[48,8,128]{2,1,0:T(8,128)(2,1)S(1)}, u32[]{:S(2)}, u32[]{:S(2)}) collective-permute-start(bf16[48,8,128]{2,1,0:T(8,128)(2,1)S(1)} %get-tuple-element.72), channel_id=1, source_target_pairs={{0,240},{16,0},{32,16},{48,32},{64,48},{80,64},{96,80},{112,96},{1... | collective-permute-start | bytes 294920 | tf_op jit(solution)/shard_map/ppermute | solution.py:396
  20.2 6.8 %collective-permute-start.4 = (bf16[48,8,128]{2,1,0:T(8,128)(2,1)S(1)}, bf16[48,8,128]{2,1,0:T(8,128)(2,1)S(1)}, u32[]{:S(2)}, u32[]{:S(2)}) collective-permute-start(bf16[48,8,128]{2,1,0:T(8,128)(2,1)S(1)} %get-tuple-element.77), channel_id=1, source_target_pairs={{0,1},{1,2},{2,3},{3,4},{4,5},{5,6},{6,7},{7,8},{8,9},{9,10},{10,1... | collective-permute-start | bytes 294920 | tf_op jit(solution)/shard_map/ppermute | solution.py:396
  20.2 6.8 %collective-permute-start.5 = (bf16[48,8,128]{2,1,0:T(8,128)(2,1)S(1)}, bf16[48,8,128]{2,1,0:T(8,128)(2,1)S(1)}, u32[]{:S(2)}, u32[]{:S(2)}) collective-permute-start(bf16[48,8,128]{2,1,0:T(8,128)(2,1)S(1)} %get-tuple-element.78), channel_id=1, source_target_pairs={{0,15},{1,0},{2,1},{3,2},{4,3},{5,4},{6,5},{7,6},{8,7},{9,8},{10,9... | collective-permute-start | bytes 294920 | tf_op jit(solution)/shard_map/ppermute | solution.py:396
  27.0 3.6 %collective-permute-start.6 = (bf16[48,8,128]{2,1,0:T(8,128)(2,1)S(1)}, bf16[48,8,128]{2,1,0:T(8,128)(2,1)S(1)}, u32[]{:S(2)}, u32[]{:S(2)}) collective-permute-start(bf16[48,8,128]{2,1,0:T(8,128)(2,1)S(1)} %get-tuple-element.83), channel_id=1, source_target_pairs={{0,16},{16,32},{32,48},{48,64},{64,80},{80,96},{96,112},{112,128},... | collective-permute-start | bytes 294920 | tf_op jit(solution)/shard_map/ppermute | solution.py:396
  27.9 4.0 %collective-permute-start.7 = (bf16[48,8,128]{2,1,0:T(8,128)(2,1)S(1)}, bf16[48,8,128]{2,1,0:T(8,128)(2,1)S(1)}, u32[]{:S(2)}, u32[]{:S(2)}) collective-permute-start(bf16[48,8,128]{2,1,0:T(8,128)(2,1)S(1)} %get-tuple-element.84), channel_id=1, source_target_pairs={{0,240},{16,0},{32,16},{48,32},{64,48},{80,64},{96,80},{112,96},{1... | collective-permute-start | bytes 294920 | tf_op jit(solution)/shard_map/ppermute | solution.py:396
  33.0 7.5 %collective-permute-start.8 = (bf16[48,8,128]{2,1,0:T(8,128)(2,1)S(1)}, bf16[48,8,128]{2,1,0:T(8,128)(2,1)S(1)}, u32[]{:S(2)}, u32[]{:S(2)}) collective-permute-start(bf16[48,8,128]{2,1,0:T(8,128)(2,1)S(1)} %get-tuple-element.91), channel_id=1, source_target_pairs={{0,1},{1,2},{2,3},{3,4},{4,5},{5,6},{6,7},{7,8},{8,9},{9,10},{10,1... | collective-permute-start | bytes 294920 | tf_op jit(solution)/shard_map/ppermute | solution.py:396
  33.1 7.4 %collective-permute-start.9 = (bf16[48,8,128]{2,1,0:T(8,128)(2,1)S(1)}, bf16[48,8,128]{2,1,0:T(8,128)(2,1)S(1)}, u32[]{:S(2)}, u32[]{:S(2)}) collective-permute-start(bf16[48,8,128]{2,1,0:T(8,128)(2,1)S(1)} %get-tuple-element.92), channel_id=1, source_target_pairs={{0,15},{1,0},{2,1},{3,2},{4,3},{5,4},{6,5},{7,6},{8,7},{9,8},{10,9... | collective-permute-start | bytes 294920 | tf_op jit(solution)/shard_map/ppermute | solution.py:396
  40.5 4.7 %collective-permute-start.10 = (bf16[48,8,128]{2,1,0:T(8,128)(2,1)S(1)}, bf16[48,8,128]{2,1,0:T(8,128)(2,1)S(1)}, u32[]{:S(2)}, u32[]{:S(2)}) collective-permute-start(bf16[48,8,128]{2,1,0:T(8,128)(2,1)S(1)} %get-tuple-element.95), channel_id=1, source_target_pairs={{0,16},{16,32},{32,48},{48,64},{64,80},{80,96},{96,112},{112,128},... | collective-permute-start | bytes 294920 | tf_op jit(solution)/shard_map/ppermute | solution.py:396
  41.4 4.0 %collective-permute-start.11 = (bf16[48,8,128]{2,1,0:T(8,128)(2,1)S(1)}, bf16[48,8,128]{2,1,0:T(8,128)(2,1)S(1)}, u32[]{:S(2)}, u32[]{:S(2)}) collective-permute-start(bf16[48,8,128]{2,1,0:T(8,128)(2,1)S(1)} %get-tuple-element.96), channel_id=1, source_target_pairs={{0,240},{16,0},{32,16},{48,32},{64,48},{80,64},{96,80},{112,96},{1... | collective-permute-start | bytes 294920 | tf_op jit(solution)/shard_map/ppermute | solution.py:396
  46.6 7.2 %collective-permute-start.12 = (bf16[48,8,128]{2,1,0:T(8,128)(2,1)S(1)}, bf16[48,8,128]{2,1,0:T(8,128)(2,1)S(1)}, u32[]{:S(2)}, u32[]{:S(2)}) collective-permute-start(bf16[48,8,128]{2,1,0:T(8,128)(2,1)S(1)} %get-tuple-element.103), channel_id=1, source_target_pairs={{0,1},{1,2},{2,3},{3,4},{4,5},{5,6},{6,7},{7,8},{8,9},{9,10},{10,1... | collective-permute-start | bytes 294920 | tf_op jit(solution)/shard_map/ppermute | solution.py:396
  46.7 7.1 %collective-permute-start.13 = (bf16[48,8,128]{2,1,0:T(8,128)(2,1)S(1)}, bf16[48,8,128]{2,1,0:T(8,128)(2,1)S(1)}, u32[]{:S(2)}, u32[]{:S(2)}) collective-permute-start(bf16[48,8,128]{2,1,0:T(8,128)(2,1)S(1)} %get-tuple-element.104), channel_id=1, source_target_pairs={{0,15},{1,0},{2,1},{3,2},{4,3},{5,4},{6,5},{7,6},{8,7},{9,8},{10,9... | collective-permute-start | bytes 294920 | tf_op jit(solution)/shard_map/ppermute | solution.py:396
  53.9 5.8 %collective-permute-start.14 = (bf16[48,8,128]{2,1,0:T(8,128)(2,1)S(1)}, bf16[48,8,128]{2,1,0:T(8,128)(2,1)S(1)}, u32[]{:S(2)}, u32[]{:S(2)}) collective-permute-start(bf16[48,8,128]{2,1,0:T(8,128)(2,1)S(1)} %get-tuple-element.107), channel_id=1, source_target_pairs={{0,16},{16,32},{32,48},{48,64},{64,80},{80,96},{96,112},{112,128},... | collective-permute-start | bytes 294920 | tf_op jit(solution)/shard_map/ppermute | solution.py:396
  54.7 4.9 %collective-permute-start.15 = (bf16[48,8,128]{2,1,0:T(8,128)(2,1)S(1)}, bf16[48,8,128]{2,1,0:T(8,128)(2,1)S(1)}, u32[]{:S(2)}, u32[]{:S(2)}) collective-permute-start(bf16[48,8,128]{2,1,0:T(8,128)(2,1)S(1)} %get-tuple-element.108), channel_id=1, source_target_pairs={{0,240},{16,0},{32,16},{48,32},{64,48},{80,64},{96,80},{112,96},{1... | collective-permute-start | bytes 294920 | tf_op jit(solution)/shard_map/ppermute | solution.py:396

commit v11 on v10

--- a/solution.py
+++ b/solution.py
@@ -16,7 +16,8 @@
 ROWS = 128
 LOOKUP = CAP + 9 * SEND
 NOTHING = CAP + 4 * SEND
-UNROLL = 16
+UNROLL = 32
+RUN = 16
 BLOCKS = FACES + 1
 QUARTER = CAP // 4
 EIGHTH = CAP // 8
@@ -171,7 +172,7 @@
         apply_as_is(e, vectors, diag[e], rows, image, image_rounded)
     for run in (2, 3):
         farthest = jnp.int32(-1)
-        for e in range(run * UNROLL, (run + 1) * UNROLL):
+        for e in range(run * RUN, (run + 1) * RUN):
             for f in range(FACES):
                 farthest = jnp.maximum(farthest, neighbours[f, e])
         ghostly[run] = farthest
@@ -257,12 +258,12 @@
         return [e] + [jnp.where(a < 0, NOTHING, a) for a in at]
 
     def again(run):
-        for e in range(run * UNROLL, (run + 1) * UNROLL):
+        for e in range(run * RUN, (run + 1) * RUN):
             vectors = [lookup[place] for place in find(e)]
             rows = [face[e, f] for f in range(FACES)]
             apply_as_is(e, vectors, diag[e], rows, image, image_rounded)
 
-    apply_runs(0, 2, find, turned, lookup, (), image, image_rounded)
+    apply_runs(0, CAP // 2 // UNROLL, find, turned, lookup, (), image, image_rounded)
     for run in (2, 3):
         pl.when(ghostly[run] >= CAP)(functools.partial(again, run))
     pack(listed(send_slots), image_rounded, up, down, next_row, last_row)

time: 91.6 us -> 91.2 us (level)
  Pallas kernels: 17.1 us -> 16.1 us
where the time goes in v11:
time: 91.2 us; the launch traced here: 91.1 us
  starting transfers between devices  35.5 us (39%)
  blocking collectives  29.4 us (32%)
  Pallas kernels  16.1 us (18%)
  waiting for transfers between devices  8.31 us (9%)
  between operations  1.73 us (2%)
    ppermute x16, starting transfers between devices, shifted(): lax.ppermute(block, axis, [(i, (i + distance) % SIDE) for i in range(SIDE)])  35.5 us
    all_to_all x1, blocking collectives, per_device(): gathered = lax.all_to_all(gram, ('gx', 'gy'), 0, 0, tiled=True)  29.4 us
    ppermute x16, waiting for transfers between devices, shifted(): lax.ppermute(block, axis, [(i, (i + distance) % SIDE) for i in range(SIDE)])  8.31 us
    pallas_call x3, Pallas kernels, per_device(): pl.pallas_call(functools.partial(ghost_kernel, power), name=f'ghost{power...  3.15 us
    pallas_call x1, Pallas kernels, per_device(): pl.pallas_call(first_half_kernel, name='first_half', in_specs=[IN_HBM] *...  2.96 us
    pallas_call x3, Pallas kernels, per_device(): pl.pallas_call(functools.partial(local_kernel, power), name=f'local{power...  2.8 us
  transfers between devices with their start and end apart: 16, of which 6 were waited for; matrix products, arithmetic and copies ran while one was open for 0% of the time, Pallas kernels for 10%

profile of v11, /device:TPU:1, one launch (start us, length us, event | category | flops | bytes accessed | tf_op | source)
XLA Modules:
  0.0 91.1 jit_solution(13105106792051955212)
XLA Ops:
  1.4 1.6 %start.1 = (f32[64,8,128]{2,1,0:T(8,128)S(1)}, bf16[64,8,128]{2,1,0:T(8,128)(2,1)S(1)}, bf16[48,8,128]{2,1,0:T(8,128)(2,1)S(1)}, bf16[48,8,128]{2,1,0:T(8,128)(2...) custom-call(s32[4,64]{1,0:T(4,128)} %bitcast.9, ...), custom_call_target="tpu_custom_call" | custom-call | tf_op jit(solution)/shard_map/start/pallas_call | solution.py:422
  3.1 2.2 %collective-permute-start = (bf16[48,8,128]{2,1,0:T(8,128)(2,1)S(1)}, bf16[48,8,128]{2,1,0:T(8,128)(2,1)S(1)}, u32[]{:S(2)}, u32[]{:S(2)}) collective-permute-start(bf16[48,8,128]{2,1,0:T(8,128)(2,1)S(1)} %get-tuple-element.66), channel_id=1, source_target_pairs={{0,1},{1,2},{2,3},{3,4},{4,5},{5,6},{6,7},{7,8},{8,9},{9,10},{10,1... | collective-permute-start | bytes 294920 | tf_op jit(solution)/shard_map/ppermute | solution.py:397
  5.3 3.7 %collective-permute-start.1 = (bf16[48,8,128]{2,1,0:T(8,128)(2,1)S(1)}, bf16[48,8,128]{2,1,0:T(8,128)(2,1)S(1)}, u32[]{:S(2)}, u32[]{:S(2)}) collective-permute-start(bf16[48,8,128]{2,1,0:T(8,128)(2,1)S(1)} %get-tuple-element.67), channel_id=1, source_target_pairs={{0,15},{1,0},{2,1},{3,2},{4,3},{5,4},{6,5},{7,6},{8,7},{9,8},{10,9... | collective-permute-start | bytes 294920 | tf_op jit(solution)/shard_map/ppermute | solution.py:397
  9.0 3.0 %first_half.1 = (bf16[64,640,128]{2,1,0:T(8,128)(2,1)S(1)}, f32[8,128]{1,0:T(8,128)S(1)}) custom-call(bf16[64,128,128]{2,1,0:T(8,128)(2,1)} %diag.7, bf16[64,4,128,128]{3,2,1,0:T(8,128)(2,1)} %face.7), custom_call_target="tpu_custom_call" | custom-call | tf_op jit(solution)/shard_map/first_half/pallas_call | solution.py:444
  12.0 2.5 %collective-permute-start.2 = (bf16[48,8,128]{2,1,0:T(8,128)(2,1)S(1)}, bf16[48,8,128]{2,1,0:T(8,128)(2,1)S(1)}, u32[]{:S(2)}, u32[]{:S(2)}) collective-permute-start(bf16[48,8,128]{2,1,0:T(8,128)(2,1)S(1)} %get-tuple-element.71), channel_id=1, source_target_pairs={{0,16},{16,32},{32,48},{48,64},{64,80},{80,96},{96,112},{112,128},... | collective-permute-start | bytes 294920 | tf_op jit(solution)/shard_map/ppermute | solution.py:397
  14.5 0.2 collective-permute-start.3
  14.8 1.7 %second_half.1 = (f32[64,8,128]{2,1,0:T(8,128)S(1)}, bf16[64,8,128]{2,1,0:T(8,128)(2,1)S(1)}, s32[8]{0:T(128)S(4)}) custom-call(s32[4,64]{1,0:T(4,128)S(4)} %get-tuple-element.59.neighbours, bf16[64,128,128]{2,1,0:T(8,128)(2,1)S(1)} %copy-done.1, bf16[64,4,128,128]{3,2,1,0:T(8,128)(2,1)S(1)} %copy-done, bf16[64,8,128]{2,1,0:T(8,128)(2,1)S(1)} %get-tuple-element.64.rounded), custom_call_target="tpu_custom_call" | custom-call | tf_op jit(solution)/shard_map/second_half/pallas_call | solution.py:495
  16.5 2.4 %collective-permute-done.3.from_next = bf16[48,8,128]{2,1,0:T(8,128)(2,1)S(1)} collective-permute-done((bf16[48,8,128]{2,1,0:T(8,128)(2,1)S(1)}, bf16[48,8,128]{2,1,0:T(8,128)(2,1)S(1)}, u32[]{:S(2)}, u32[]{:S(2)}) %collective-permute-start.3) | collective-permute-done | bytes 98336 | tf_op jit(solution)/shard_map/ppermute | solution.py:397
  18.9 1.2 %whole.1 = (f32[64,8,128]{2,1,0:T(8,128)S(1)}, bf16[64,8,128]{2,1,0:T(8,128)(2,1)S(1)}, bf16[48,8,128]{2,1,0:T(8,128)(2,1)S(1)}, bf16[48,8,128]{2,1,0:T(8,128)(2...) custom-call(s32[4,64]{1,0:T(4,128)S(4)} %get-tuple-element.59.neighb, ...), custom_call_target="tpu_custom_call", output_to_operand_aliasing={{0}: (12, {}), {1}: (13, {})} | custom-call | tf_op jit(solution)/shard_map/whole/pallas_call | solution.py:504
  20.1 4.8 %collective-permute-start.5 = (bf16[48,8,128]{2,1,0:T(8,128)(2,1)S(1)}, bf16[48,8,128]{2,1,0:T(8,128)(2,1)S(1)}, u32[]{:S(2)}, u32[]{:S(2)}) collective-permute-start(bf16[48,8,128]{2,1,0:T(8,128)(2,1)S(1)} %get-tuple-element.78), channel_id=1, source_target_pairs={{0,15},{1,0},{2,1},{3,2},{4,3},{5,4},{6,5},{7,6},{8,7},{9,8},{10,9... | collective-permute-start | bytes 294920 | tf_op jit(solution)/shard_map/ppermute | solution.py:397
  24.8 1.6 %late.1 = (bf16[64,640,128]{2,1,0:T(8,128)(2,1)S(1)}, f32[8,128]{1,0:T(8,128)S(1)}) custom-call(bf16[64,128,128]{2,1,0:T(8,128)(2,1)S(1)} %copy-done.1, bf16[64,4,128,128]{3,2,1,0:T(8,128)(2,1)S(1)} %copy-done, bf16[64,640,128]{2,1,0:T(8,128)(2,1)S(1)} %get-tuple-element.62.before.turned), custom_call_target="tpu_custom_call", output_to_operand_aliasing={{0}: (2, {})} | custom-call | tf_op jit(solution)/shard_map/late/pallas_call | solution.py:463
  26.4 0.4 collective-permute-done.4.refs_0_.refs_3_
  26.9 0.9 collective-permute-start.6
  27.7 1.7 %collective-permute-start.7 = (bf16[48,8,128]{2,1,0:T(8,128)(2,1)S(1)}, bf16[48,8,128]{2,1,0:T(8,128)(2,1)S(1)}, u32[]{:S(2)}, u32[]{:S(2)}) collective-permute-start(bf16[48,8,128]{2,1,0:T(8,128)(2,1)S(1)} %get-tuple-element.84), channel_id=1, source_target_pairs={{0,240},{16,0},{32,16},{48,32},{64,48},{80,64},{96,80},{112,96},{1... | collective-permute-start | bytes 294920 | tf_op jit(solution)/shard_map/ppermute | solution.py:397
  29.5 0.9 %local1.1 = (f32[64,8,128]{2,1,0:T(8,128)S(1)}, bf16[64,8,128]{2,1,0:T(8,128)(2,1)S(1)}, f32[8,128]{1,0:T(8,128)S(1)}) custom-call(s32[544]{0:T(1024)S(4)} %get-tuple-element.61.refs_0_, bf16[64,640,128]{2,1,0:T(8,128)(2,1)S(1)} %get-tuple-element.63.refs_1_, bf16[64,8,128]{2,1,0:T(8,128)(2,1)S(1)} %get-tuple-element.76.refs_2_, ...), custom_call_target="tpu_custom_call" | custom-call | tf_op jit(solution)/shard_map/local1/pallas_call | solution.py:474
  30.4 1.4 %collective-permute-done.7.refs_6_ = bf16[48,8,128]{2,1,0:T(8,128)(2,1)S(1)} collective-permute-done((bf16[48,8,128]{2,1,0:T(8,128)(2,1)S(1)}, bf16[48,8,128]{2,1,0:T(8,128)(2,1)S(1)}, u32[]{:S(2)}, u32[]{:S(2)}) %collective-permute-start.7) | collective-permute-done | bytes 98336 | tf_op jit(solution)/shard_map/ppermute | solution.py:397
  31.8 1.0 %ghost1.1 = (f32[64,8,128]{2,1,0:T(8,128)S(1)}, bf16[64,8,128]{2,1,0:T(8,128)(2,1)S(1)}, bf16[48,8,128]{2,1,0:T(8,128)(2,1)S(1)}, bf16[48,8,128]{2,1,0:T(8,128)(...) custom-call(s32[544]{0:T(1024)S(4)} %get-tuple-element.61.refs_0_, ...), custom_call_target="tpu_custom_call", output_to_operand_aliasing={{0}: (10, {}), {1}: (11, {})} | custom-call | tf_op jit(solution)/shard_map/ghost1/pallas_call | solution.py:519
  32.9 5.6 %collective-permute-start.9 = (bf16[48,8,128]{2,1,0:T(8,128)(2,1)S(1)}, bf16[48,8,128]{2,1,0:T(8,128)(2,1)S(1)}, u32[]{:S(2)}, u32[]{:S(2)}) collective-permute-start(bf16[48,8,128]{2,1,0:T(8,128)(2,1)S(1)} %get-tuple-element.92), channel_id=1, source_target_pairs={{0,15},{1,0},{2,1},{3,2},{4,3},{5,4},{6,5},{7,6},{8,7},{9,8},{10,9... | collective-permute-start | bytes 294920 | tf_op jit(solution)/shard_map/ppermute | solution.py:397
  38.5 1.7 %collective-permute-done.8.refs_0_.refs_3_ = bf16[48,8,128]{2,1,0:T(8,128)(2,1)S(1)} collective-permute-done((bf16[48,8,128]{2,1,0:T(8,128)(2,1)S(1)}, bf16[48,8,128]{2,1,0:T(8,128)(2,1)S(1)}, u32[]{:S(2)}, u32[]{:S(2)}) %collective-permute-start.8) | collective-permute-done | bytes 98336 | tf_op jit(solution)/shard_map/ppermute | solution.py:397
  40.3 0.9 collective-permute-start.10
  41.1 2.6 %collective-permute-start.11 = (bf16[48,8,128]{2,1,0:T(8,128)(2,1)S(1)}, bf16[48,8,128]{2,1,0:T(8,128)(2,1)S(1)}, u32[]{:S(2)}, u32[]{:S(2)}) collective-permute-start(bf16[48,8,128]{2,1,0:T(8,128)(2,1)S(1)} %get-tuple-element.96), channel_id=1, source_target_pairs={{0,240},{16,0},{32,16},{48,32},{64,48},{80,64},{96,80},{112,96},{1... | collective-permute-start | bytes 294920 | tf_op jit(solution)/shard_map/ppermute | solution.py:397
  43.8 0.9 %local2.1 = (f32[64,8,128]{2,1,0:T(8,128)S(1)}, bf16[64,8,128]{2,1,0:T(8,128)(2,1)S(1)}, f32[8,128]{1,0:T(8,128)S(1)}) custom-call(s32[544]{0:T(1024)S(4)} %get-tuple-element.61.refs_0_, bf16[64,640,128]{2,1,0:T(8,128)(2,1)S(1)} %get-tuple-element.63.refs_1_, bf16[64,8,128]{2,1,0:T(8,128)(2,1)S(1)} %get-tuple-element.90.refs_2_, ...), custom_call_target="tpu_custom_call" | custom-call | tf_op jit(solution)/shard_map/local2/pallas_call | solution.py:474
  44.7 0.5 collective-permute-done.11.refs_6_
  45.2 1.0 %ghost2.1 = (f32[64,8,128]{2,1,0:T(8,128)S(1)}, bf16[64,8,128]{2,1,0:T(8,128)(2,1)S(1)}, bf16[48,8,128]{2,1,0:T(8,128)(2,1)S(1)}, bf16[48,8,128]{2,1,0:T(8,128)(...) custom-call(s32[544]{0:T(1024)S(4)} %get-tuple-element.61.refs_0_, ...), custom_call_target="tpu_custom_call", output_to_operand_aliasing={{0}: (11, {}), {1}: (12, {})} | custom-call | tf_op jit(solution)/shard_map/ghost2/pallas_call | solution.py:519
  46.3 5.4 %collective-permute-start.13 = (bf16[48,8,128]{2,1,0:T(8,128)(2,1)S(1)}, bf16[48,8,128]{2,1,0:T(8,128)(2,1)S(1)}, u32[]{:S(2)}, u32[]{:S(2)}) collective-permute-start(bf16[48,8,128]{2,1,0:T(8,128)(2,1)S(1)} %get-tuple-element.104), channel_id=1, source_target_pairs={{0,15},{1,0},{2,1},{3,2},{4,3},{5,4},{6,5},{7,6},{8,7},{9,8},{10,9... | collective-permute-start | bytes 294920 | tf_op jit(solution)/shard_map/ppermute | solution.py:397
  51.7 1.9 %collective-permute-done.12.refs_0_.refs_3_ = bf16[48,8,128]{2,1,0:T(8,128)(2,1)S(1)} collective-permute-done((bf16[48,8,128]{2,1,0:T(8,128)(2,1)S(1)}, bf16[48,8,128]{2,1,0:T(8,128)(2,1)S(1)}, u32[]{:S(2)}, u32[]{:S(2)}) %collective-permute-start.12) | collective-permute-done | bytes 98336 | tf_op jit(solution)/shard_map/ppermute | solution.py:397
  53.7 0.9 collective-permute-start.14
  54.5 3.8 %collective-permute-start.15 = (bf16[48,8,128]{2,1,0:T(8,128)(2,1)S(1)}, bf16[48,8,128]{2,1,0:T(8,128)(2,1)S(1)}, u32[]{:S(2)}, u32[]{:S(2)}) collective-permute-start(bf16[48,8,128]{2,1,0:T(8,128)(2,1)S(1)} %get-tuple-element.108), channel_id=1, source_target_pairs={{0,240},{16,0},{32,16},{48,32},{64,48},{80,64},{96,80},{112,96},{1... | collective-permute-start | bytes 294920 | tf_op jit(solution)/shard_map/ppermute | solution.py:397
  58.4 0.9 %local3.1 = (f32[64,8,128]{2,1,0:T(8,128)S(1)}, bf16[64,8,128]{2,1,0:T(8,128)(2,1)S(1)}, f32[8,128]{1,0:T(8,128)S(1)}) custom-call(s32[544]{0:T(1024)S(4)} %get-tuple-element.61.refs_0_, bf16[64,640,128]{2,1,0:T(8,128)(2,1)S(1)} %get-tuple-element.63.refs_1_, bf16[64,8,128]{2,1,0:T(8,128)(2,1)S(1)} %get-tuple-element.102.refs_2_, ...), custom_call_target="tpu_custom_call" | custom-call | tf_op jit(solution)/shard_map/local3/pallas_call | solution.py:474
  59.3 1.1 %ghost3.1 = (f32[64,8,128]{2,1,0:T(8,128)S(1)}, bf16[64,8,128]{2,1,0:T(8,128)(2,1)S(1)}, f32[256,128]{1,0:T(8,128)S(1)}) custom-call(s32[544]{0:T(1024)S(4)} %get-tuple-element.61.refs_0_, bf16[64,640,128]{2,1,0:T(8,128)(2,1)S(1)} %get-tuple-element.63.refs_1_, ...), custom_call_target="tpu_custom_call", output_to_operand_aliasing={{0}: (12, {}), {1}: (13, {})} | custom-call | tf_op jit(solution)/shard_map/ghost3/pallas_call | solution.py:519
  60.5 29.4 %all_to_all.11 = f32[256,1,128]{2,1,0:T(1,128)S(1)} all-to-all(f32[256,1,128]{2,1,0:T(1,128)S(1)} %bitcast.7), channel_id=1, replica_groups=mesh['gx'=16,'gy'=16] {'gx','gy'}, dimensions={0} | all-to-all | bytes 262144 | tf_op jit(solution)/shard_map/all_to_all | solution.py:536
  89.8 1.1 %finish.1 = (f32[64,8,128]{2,1,0:T(8,128)}, f32[64,8,128]{2,1,0:T(8,128)}) custom-call(f32[256,128]{1,0:T(8,128)S(1)} %bitcast.6, f32[64,8,128]{2,1,0:T(8,128)S(1)} %get-tuple-element.73.b0.refs_4_.refs_8_, f32[64,8,128]{2,1,0:T(8,128)S(1)} %get-tuple-element.86.refs_5_.refs_9_.b1, f32[64,8,128]{2,1,0:T(8,128)S(1)} %get-tuple-element.98.refs_6_.refs_10_.b2, ...), custom_call_target="tpu_custom_call" | custom-call | tf_op jit(solution)/shard_map/finish/pallas_call | solution.py:537
  (22 shorter events, 0.3 us)
Async XLA Ops:
  0.6 14.1 %copy-start = (bf16[64,4,128,128]{3,2,1,0:T(8,128)(2,1)S(1)}, bf16[64,4,128,128]{3,2,1,0:T(8,128)(2,1)}, u32[]{:S(2)}) copy-start(bf16[64,4,128,128]{3,2,1,0:T(8,128)(2,1)} %face.7) | copy-start | bytes 25165828
  0.6 14.1 %copy-start.1 = (bf16[64,128,128]{2,1,0:T(8,128)(2,1)S(1)}, bf16[64,128,128]{2,1,0:T(8,128)(2,1)}, u32[]{:S(2)}) copy-start(bf16[64,128,128]{2,1,0:T(8,128)(2,1)} %diag.7) | copy-start | bytes 6291460
  3.1 8.9 %collective-permute-start = (bf16[48,8,128]{2,1,0:T(8,128)(2,1)S(1)}, bf16[48,8,128]{2,1,0:T(8,128)(2,1)S(1)}, u32[]{:S(2)}, u32[]{:S(2)}) collective-permute-start(bf16[48,8,128]{2,1,0:T(8,128)(2,1)S(1)} %get-tuple-element.66), channel_id=1, source_target_pairs={{0,1},{1,2},{2,3},{3,4},{4,5},{5,6},{6,7},{7,8},{8,9},{9,10},{10,1... | collective-permute-start | bytes 294920 | tf_op jit(solution)/shard_map/ppermute | solution.py:397
  5.3 6.7 %collective-permute-start.1 = (bf16[48,8,128]{2,1,0:T(8,128)(2,1)S(1)}, bf16[48,8,128]{2,1,0:T(8,128)(2,1)S(1)}, u32[]{:S(2)}, u32[]{:S(2)}) collective-permute-start(bf16[48,8,128]{2,1,0:T(8,128)(2,1)S(1)} %get-tuple-element.67), channel_id=1, source_target_pairs={{0,15},{1,0},{2,1},{3,2},{4,3},{5,4},{6,5},{7,6},{8,7},{9,8},{10,9... | collective-permute-start | bytes 294920 | tf_op jit(solution)/shard_map/ppermute | solution.py:397
  12.0 4.5 %collective-permute-start.2 = (bf16[48,8,128]{2,1,0:T(8,128)(2,1)S(1)}, bf16[48,8,128]{2,1,0:T(8,128)(2,1)S(1)}, u32[]{:S(2)}, u32[]{:S(2)}) collective-permute-start(bf16[48,8,128]{2,1,0:T(8,128)(2,1)S(1)} %get-tuple-element.71), channel_id=1, source_target_pairs={{0,16},{16,32},{32,48},{48,64},{64,80},{80,96},{96,112},{112,128},... | collective-permute-start | bytes 294920 | tf_op jit(solution)/shard_map/ppermute | solution.py:397
  14.5 4.3 %collective-permute-start.3 = (bf16[48,8,128]{2,1,0:T(8,128)(2,1)S(1)}, bf16[48,8,128]{2,1,0:T(8,128)(2,1)S(1)}, u32[]{:S(2)}, u32[]{:S(2)}) collective-permute-start(bf16[48,8,128]{2,1,0:T(8,128)(2,1)S(1)} %get-tuple-element.72), channel_id=1, source_target_pairs={{0,240},{16,0},{32,16},{48,32},{64,48},{80,64},{96,80},{112,96},{1... | collective-permute-start | bytes 294920 | tf_op jit(solution)/shard_map/ppermute | solution.py:397
  20.0 6.8 %collective-permute-start.4 = (bf16[48,8,128]{2,1,0:T(8,128)(2,1)S(1)}, bf16[48,8,128]{2,1,0:T(8,128)(2,1)S(1)}, u32[]{:S(2)}, u32[]{:S(2)}) collective-permute-start(bf16[48,8,128]{2,1,0:T(8,128)(2,1)S(1)} %get-tuple-element.77), channel_id=1, source_target_pairs={{0,1},{1,2},{2,3},{3,4},{4,5},{5,6},{6,7},{7,8},{8,9},{9,10},{10,1... | collective-permute-start | bytes 294920 | tf_op jit(solution)/shard_map/ppermute | solution.py:397
  20.1 6.8 %collective-permute-start.5 = (bf16[48,8,128]{2,1,0:T(8,128)(2,1)S(1)}, bf16[48,8,128]{2,1,0:T(8,128)(2,1)S(1)}, u32[]{:S(2)}, u32[]{:S(2)}) collective-permute-start(bf16[48,8,128]{2,1,0:T(8,128)(2,1)S(1)} %get-tuple-element.78), channel_id=1, source_target_pairs={{0,15},{1,0},{2,1},{3,2},{4,3},{5,4},{6,5},{7,6},{8,7},{9,8},{10,9... | collective-permute-start | bytes 294920 | tf_op jit(solution)/shard_map/ppermute | solution.py:397
  26.9 3.5 %collective-permute-start.6 = (bf16[48,8,128]{2,1,0:T(8,128)(2,1)S(1)}, bf16[48,8,128]{2,1,0:T(8,128)(2,1)S(1)}, u32[]{:S(2)}, u32[]{:S(2)}) collective-permute-start(bf16[48,8,128]{2,1,0:T(8,128)(2,1)S(1)} %get-tuple-element.83), channel_id=1, source_target_pairs={{0,16},{16,32},{32,48},{48,64},{64,80},{80,96},{96,112},{112,128},... | collective-permute-start | bytes 294920 | tf_op jit(solution)/shard_map/ppermute | solution.py:397
  27.7 4.0 %collective-permute-start.7 = (bf16[48,8,128]{2,1,0:T(8,128)(2,1)S(1)}, bf16[48,8,128]{2,1,0:T(8,128)(2,1)S(1)}, u32[]{:S(2)}, u32[]{:S(2)}) collective-permute-start(bf16[48,8,128]{2,1,0:T(8,128)(2,1)S(1)} %get-tuple-element.84), channel_id=1, source_target_pairs={{0,240},{16,0},{32,16},{48,32},{64,48},{80,64},{96,80},{112,96},{1... | collective-permute-start | bytes 294920 | tf_op jit(solution)/shard_map/ppermute | solution.py:397
  32.8 7.4 %collective-permute-start.8 = (bf16[48,8,128]{2,1,0:T(8,128)(2,1)S(1)}, bf16[48,8,128]{2,1,0:T(8,128)(2,1)S(1)}, u32[]{:S(2)}, u32[]{:S(2)}) collective-permute-start(bf16[48,8,128]{2,1,0:T(8,128)(2,1)S(1)} %get-tuple-element.91), channel_id=1, source_target_pairs={{0,1},{1,2},{2,3},{3,4},{4,5},{5,6},{6,7},{7,8},{8,9},{9,10},{10,1... | collective-permute-start | bytes 294920 | tf_op jit(solution)/shard_map/ppermute | solution.py:397
  32.9 7.4 %collective-permute-start.9 = (bf16[48,8,128]{2,1,0:T(8,128)(2,1)S(1)}, bf16[48,8,128]{2,1,0:T(8,128)(2,1)S(1)}, u32[]{:S(2)}, u32[]{:S(2)}) collective-permute-start(bf16[48,8,128]{2,1,0:T(8,128)(2,1)S(1)} %get-tuple-element.92), channel_id=1, source_target_pairs={{0,15},{1,0},{2,1},{3,2},{4,3},{5,4},{6,5},{7,6},{8,7},{9,8},{10,9... | collective-permute-start | bytes 294920 | tf_op jit(solution)/shard_map/ppermute | solution.py:397
  40.3 4.5 %collective-permute-start.10 = (bf16[48,8,128]{2,1,0:T(8,128)(2,1)S(1)}, bf16[48,8,128]{2,1,0:T(8,128)(2,1)S(1)}, u32[]{:S(2)}, u32[]{:S(2)}) collective-permute-start(bf16[48,8,128]{2,1,0:T(8,128)(2,1)S(1)} %get-tuple-element.95), channel_id=1, source_target_pairs={{0,16},{16,32},{32,48},{48,64},{64,80},{80,96},{96,112},{112,128},... | collective-permute-start | bytes 294920 | tf_op jit(solution)/shard_map/ppermute | solution.py:397
  41.1 4.0 %collective-permute-start.11 = (bf16[48,8,128]{2,1,0:T(8,128)(2,1)S(1)}, bf16[48,8,128]{2,1,0:T(8,128)(2,1)S(1)}, u32[]{:S(2)}, u32[]{:S(2)}) collective-permute-start(bf16[48,8,128]{2,1,0:T(8,128)(2,1)S(1)} %get-tuple-element.96), channel_id=1, source_target_pairs={{0,240},{16,0},{32,16},{48,32},{64,48},{80,64},{96,80},{112,96},{1... | collective-permute-start | bytes 294920 | tf_op jit(solution)/shard_map/ppermute | solution.py:397
  46.2 7.4 %collective-permute-start.12 = (bf16[48,8,128]{2,1,0:T(8,128)(2,1)S(1)}, bf16[48,8,128]{2,1,0:T(8,128)(2,1)S(1)}, u32[]{:S(2)}, u32[]{:S(2)}) collective-permute-start(bf16[48,8,128]{2,1,0:T(8,128)(2,1)S(1)} %get-tuple-element.103), channel_id=1, source_target_pairs={{0,1},{1,2},{2,3},{3,4},{4,5},{5,6},{6,7},{7,8},{8,9},{9,10},{10,1... | collective-permute-start | bytes 294920 | tf_op jit(solution)/shard_map/ppermute | solution.py:397
  46.3 7.3 %collective-permute-start.13 = (bf16[48,8,128]{2,1,0:T(8,128)(2,1)S(1)}, bf16[48,8,128]{2,1,0:T(8,128)(2,1)S(1)}, u32[]{:S(2)}, u32[]{:S(2)}) collective-permute-start(bf16[48,8,128]{2,1,0:T(8,128)(2,1)S(1)} %get-tuple-element.104), channel_id=1, source_target_pairs={{0,15},{1,0},{2,1},{3,2},{4,3},{5,4},{6,5},{7,6},{8,7},{9,8},{10,9... | collective-permute-start | bytes 294920 | tf_op jit(solution)/shard_map/ppermute | solution.py:397
  53.7 5.7 %collective-permute-start.14 = (bf16[48,8,128]{2,1,0:T(8,128)(2,1)S(1)}, bf16[48,8,128]{2,1,0:T(8,128)(2,1)S(1)}, u32[]{:S(2)}, u32[]{:S(2)}) collective-permute-start(bf16[48,8,128]{2,1,0:T(8,128)(2,1)S(1)} %get-tuple-element.107), channel_id=1, source_target_pairs={{0,16},{16,32},{32,48},{48,64},{64,80},{80,96},{96,112},{112,128},... | collective-permute-start | bytes 294920 | tf_op jit(solution)/shard_map/ppermute | solution.py:397
  54.5 4.8 %collective-permute-start.15 = (bf16[48,8,128]{2,1,0:T(8,128)(2,1)S(1)}, bf16[48,8,128]{2,1,0:T(8,128)(2,1)S(1)}, u32[]{:S(2)}, u32[]{:S(2)}) collective-permute-start(bf16[48,8,128]{2,1,0:T(8,128)(2,1)S(1)} %get-tuple-element.108), channel_id=1, source_target_pairs={{0,240},{16,0},{32,16},{48,32},{64,48},{80,64},{96,80},{112,96},{1... | collective-permute-start | bytes 294920 | tf_op jit(solution)/shard_map/ppermute | solution.py:397
